TPU v7x, 32 devices: a whole 2x2x4 slice. The times are simulated.
32 devices in a mesh: section: 2 (over x), dp: 8 (over z, y), tensor: 2 (over core).
Axes of the slice: x: 2, y: 2, z: 4, core: 2. Of those that a mesh axis runs over, the one named last changes fastest.
Arguments:
- tokens: bfloat16 [2, 4096, 384], P(None, 'dp'), may hold values from -6 to 6
- image_counts: int32 [2], replicated, may hold values from 15 to 20, as said below
- cotangent: bfloat16 [2, 4096, 384], P(None, 'dp'), may hold values from -6 to 6
- norm_gains: bfloat16 [2, 2, 384], P('section', None, 'dp'), may hold values from 0.5 to 1.5
- row_biases: bfloat16 [2, 4, 384], P('section', None, 'dp'), may hold values from -3 to 3
- qkv_weight: bfloat16 [2, 384, 3, 384], P('section', 'dp', None, 'tensor'), may hold values from -0.3125 to 0.3125
- qv_bias: bfloat16 [2, 2, 384], P('section', None, 'tensor'), may hold values from -3 to 3
- out_weight: bfloat16 [2, 384, 384], P('section', 'tensor', 'dp'), may hold values from -1.25 to 1.25
- up_weight: bfloat16 [2, 384, 1536], P('section', 'dp', 'tensor'), may hold values from -0.3125 to 0.3125
- up_bias: bfloat16 [2, 1536], P('section', 'tensor'), may hold values from -3 to 3
- down_weight: bfloat16 [2, 1536, 384], P('section', 'tensor', 'dp'), may hold values from -0.21875 to 0.21875
Outputs:
- layer_outputs: bfloat16 [2, 2, 4096, 384], P('section', None, 'dp')
- input_grads: float32 [2, 2, 4096, 384], P('section', None, 'dp')
- grad_norm_gains: float32 [2, 2, 384], P('section', None, 'dp')
- grad_row_biases: float32 [2, 4, 384], P('section', None, 'dp')
- grad_qkv: float32 [2, 384, 3, 384], P('section', 'dp', None, 'tensor')
- grad_qv_bias: float32 [2, 2, 384], P('section', None, 'tensor')
- grad_out: float32 [2, 384, 384], P('section', 'tensor', 'dp')
- grad_up: float32 [2, 384, 1536], P('section', 'dp', 'tensor')
- grad_up_bias: float32 [2, 1536], P('section', 'tensor')
- grad_down: float32 [2, 1536, 384], P('section', 'tensor', 'dp')
Inputs may be any that keep to these rules, and one draw needn't show every extreme that they name: `image_counts`: number of images in each micro-batch; image i fills rows i * 197 to (i + 1) * 197 - 1 of its micro-batch, later rows are padding; some micro-batch holds 20 images.
All inputs are finite; a program needn't handle non-finite values.
Results may differ from a plain program's by a relative error of at most 0.019.
Values may be sent and summed in bfloat16 or wider, within the bound.
No kernel may reach another device: no remote copies, remote signals or barrier semaphores. Data moves between devices by JAX's collectives and lax.ppermute only.
A program may use at most 128 MiB of HBM per device.

v0:
```python
from functools import partial
import math

import jax
import jax.numpy as jnp
from jax import lax
from jax.sharding import PartitionSpec as P

HD = 64
IMG_LEN = 197
HALO = 256
QBLOCK = 512


EPSILON = 1e-06
NEGATIVE = -1e30


def with_halo(block, sides, width):
    for axis, dim in sides:
        count = lax.axis_size(axis)
        forward = [(i, i + 1) for i in range(count - 1)]
        backward = [(target, source) for source, target in forward]
        low = lax.ppermute(
            lax.slice_in_dim(block, block.shape[dim] - width, None, axis=dim), axis, forward
        )
        high = lax.ppermute(lax.slice_in_dim(block, 0, width, axis=dim), axis, backward)
        block = jnp.concatenate([low, block, high], axis=dim)
    return block


def passed_along(block, axis, distance):
    devices = range(lax.axis_size(axis))
    route = [(i - distance, i) for i in devices if i - distance in devices]
    return lax.ppermute(block, axis, route)


def norm_rows(inputs, gain_row, shift_row):
    centred = inputs - jnp.mean(inputs, -1, keepdims=True)
    inverse = lax.rsqrt(jnp.mean(centred * centred, -1, keepdims=True) + EPSILON)
    normed = centred * inverse
    return (normed * gain_row + shift_row, normed, inverse)


def norm_back(upstream, normed, inverse, gain_row):
    scaled = upstream * gain_row
    return inverse * (
        scaled
        - jnp.mean(scaled, -1, keepdims=True)
        - normed * jnp.mean(scaled * normed, -1, keepdims=True)
    )


def image_masks(image_count, dp_index, local_rows):
    query_rows = dp_index * local_rows + jnp.arange(local_rows, dtype=jnp.int32)
    key_rows = dp_index * local_rows - HALO + jnp.arange(local_rows + 2 * HALO, dtype=jnp.int32)
    query_image = query_rows // IMG_LEN
    key_image = key_rows // IMG_LEN
    valid_rows = (query_image < image_count).astype(jnp.float32)
    same_image = query_image[:, None] == key_image[None, :]
    return (valid_rows, same_image)


def attention_scores(query_heads, key_heads, same_image):
    scores = jnp.einsum(
        "qhd,khd->hqk", query_heads, key_heads, preferred_element_type=jnp.float32
    ) * (1.0 / math.sqrt(HD))
    return jnp.where(same_image[None], scores, NEGATIVE)


def unpack_weights(gathered):
    return (
        gathered[0][0],
        gathered[1][0],
        gathered[2][0],
        gathered[3][0],
        gathered[4][0].astype(jnp.float32),
        gathered[5][0].astype(jnp.float32),
    )


def layer_forward(inputs, weights, qv_shift, up_shift, valid_rows, same_image):
    qkv_matrix, out_matrix, up_matrix, down_matrix, gain_rows, shift_rows = weights
    local_rows = inputs.shape[0]
    width_heads = qkv_matrix.shape[2]
    head_count = width_heads // HD
    block_rows = min(QBLOCK, local_rows)
    normed_in, normed_one, inverse_one = norm_rows(inputs, gain_rows[0], shift_rows[0])
    attn_in = normed_in.astype(jnp.bfloat16)
    projected = jnp.einsum("rd,dch->rch", attn_in, qkv_matrix, preferred_element_type=jnp.float32)
    query_rows = (projected[:, 0] + qv_shift[0]).astype(jnp.bfloat16)
    key_values = jnp.concatenate([projected[:, 1], projected[:, 2] + qv_shift[1]], 1).astype(
        jnp.bfloat16
    )
    widened = with_halo(key_values, (("dp", 0),), HALO)
    key_heads = widened[:, :width_heads].reshape(-1, head_count, HD)
    value_heads = widened[:, width_heads:].reshape(-1, head_count, HD)
    query_heads = query_rows.reshape(local_rows, head_count, HD)
    mixed_list = []
    total_list = []
    for first_row in range(0, local_rows, block_rows):
        window_end = first_row + block_rows + 2 * HALO
        scores = attention_scores(
            query_heads[first_row : first_row + block_rows],
            key_heads[first_row:window_end],
            same_image[first_row : first_row + block_rows, first_row:window_end],
        )
        highest = jnp.max(scores, -1, keepdims=True)
        raised = jnp.exp(scores - highest)
        totals = jnp.sum(raised, -1, keepdims=True)
        attention = raised / totals
        total_list.append(highest + jnp.log(totals))
        mixed_list.append(
            jnp.einsum(
                "hqk,khd->qhd",
                attention.astype(jnp.bfloat16),
                value_heads[first_row:window_end],
                preferred_element_type=jnp.float32,
            )
        )
    log_total = jnp.concatenate(total_list, 1)
    mixed_heads = (
        jnp.concatenate(mixed_list, 0).reshape(local_rows, width_heads).astype(jnp.bfloat16)
    )
    attn_partial = jnp.dot(mixed_heads, out_matrix, preferred_element_type=jnp.float32)
    attn_out = lax.psum(attn_partial.astype(jnp.bfloat16), "tensor").astype(jnp.float32)
    residual = inputs + (attn_out + shift_rows[1])
    normed_mid, normed_two, inverse_two = norm_rows(residual, gain_rows[1], shift_rows[2])
    mlp_in = normed_mid.astype(jnp.bfloat16)
    up_value = jnp.dot(mlp_in, up_matrix, preferred_element_type=jnp.float32) + up_shift
    hidden_value, gelu_back = jax.vjp(partial(jax.nn.gelu, approximate=False), up_value)
    hidden = hidden_value.astype(jnp.bfloat16)
    down_partial = jnp.dot(hidden, down_matrix, preferred_element_type=jnp.float32)
    down_out = lax.psum(down_partial.astype(jnp.bfloat16), "tensor").astype(jnp.float32)
    layer_out = ((residual + (down_out + shift_rows[3])) * valid_rows[:, None]).astype(jnp.bfloat16)
    kept_state = (
        normed_one,
        inverse_one,
        attn_in,
        query_heads,
        key_heads,
        value_heads,
        log_total,
        mixed_heads,
        normed_two,
        inverse_two,
        mlp_in,
        gelu_back,
        hidden,
        valid_rows,
        same_image,
    )
    return (layer_out, kept_state)


def layer_backward(upstream, weights, kept_state):
    qkv_matrix, out_matrix, up_matrix, down_matrix, gain_rows, shift_rows = weights
    (
        normed_one,
        inverse_one,
        attn_in,
        query_heads,
        key_heads,
        value_heads,
        log_total,
        mixed_heads,
        normed_two,
        inverse_two,
        mlp_in,
        gelu_back,
        hidden,
        valid_rows,
        same_image,
    ) = kept_state
    local_rows = upstream.shape[0]
    width_heads = qkv_matrix.shape[2]
    head_count = width_heads // HD
    block_rows = min(QBLOCK, local_rows)
    scale_factor = 1.0 / math.sqrt(HD)
    masked = upstream * valid_rows[:, None]
    down_grad = masked.astype(jnp.bfloat16)
    grad_down = jnp.einsum("rf,rd->fd", hidden, down_grad, preferred_element_type=jnp.float32)
    hidden_grad = jnp.einsum(
        "rd,fd->rf", down_grad, down_matrix, preferred_element_type=jnp.float32
    )
    up_grad = gelu_back(hidden_grad)[0].astype(jnp.bfloat16)
    grad_up_shift = jnp.sum(up_grad.astype(jnp.float32), 0)
    grad_up = jnp.einsum("rd,rf->df", mlp_in, up_grad, preferred_element_type=jnp.float32)
    mlp_partial = jnp.einsum("rf,df->rd", up_grad, up_matrix, preferred_element_type=jnp.float32)
    mlp_in_grad = lax.psum(mlp_partial.astype(jnp.bfloat16), "tensor").astype(jnp.float32)
    residual_grad = masked + norm_back(mlp_in_grad, normed_two, inverse_two, gain_rows[1])
    gain_two = jnp.sum(mlp_in_grad * normed_two, 0)
    shift_two = jnp.sum(mlp_in_grad, 0)
    attn_grad = residual_grad.astype(jnp.bfloat16)
    grad_out = jnp.einsum("rh,rd->hd", mixed_heads, attn_grad, preferred_element_type=jnp.float32)
    mixed_grad = jnp.einsum("rd,hd->rh", attn_grad, out_matrix, preferred_element_type=jnp.float32)
    mixed_grad = mixed_grad.astype(jnp.bfloat16).reshape(local_rows, head_count, HD)
    wide_grad = jnp.zeros((local_rows + 2 * HALO, 2 * width_heads), jnp.float32)
    query_list = []
    for first_row in range(0, local_rows, block_rows):
        window_end = first_row + block_rows + 2 * HALO
        query_block = query_heads[first_row : first_row + block_rows]
        key_block = key_heads[first_row:window_end]
        value_block = value_heads[first_row:window_end]
        grad_block = mixed_grad[first_row : first_row + block_rows]
        scores = attention_scores(
            query_block,
            key_block,
            same_image[first_row : first_row + block_rows, first_row:window_end],
        )
        attention = jnp.exp(scores - log_total[:, first_row : first_row + block_rows])
        value_grad = jnp.einsum(
            "hqk,qhd->khd",
            attention.astype(jnp.bfloat16),
            grad_block,
            preferred_element_type=jnp.float32,
        )
        prob_grad = jnp.einsum(
            "qhd,khd->hqk", grad_block, value_block, preferred_element_type=jnp.float32
        )
        score_grad = (
            attention * (prob_grad - jnp.sum(attention * prob_grad, -1, keepdims=True))
        ).astype(jnp.bfloat16)
        query_list.append(
            jnp.einsum("hqk,khd->qhd", score_grad, key_block, preferred_element_type=jnp.float32)
            * scale_factor
        )
        key_grad = (
            jnp.einsum("hqk,qhd->khd", score_grad, query_block, preferred_element_type=jnp.float32)
            * scale_factor
        )
        window_grad = jnp.concatenate(
            [key_grad.reshape(-1, width_heads), value_grad.reshape(-1, width_heads)], 1
        )
        wide_grad = wide_grad.at[first_row:window_end].add(window_grad)
    query_grad = jnp.concatenate(query_list, 0)
    rim_pair = jnp.concatenate([wide_grad[:HALO], wide_grad[local_rows + HALO :]], 0)
    rim_widened = with_halo(rim_pair.astype(jnp.bfloat16), (("dp", 0),), HALO).astype(
        rim_pair.dtype
    )
    from_lower = rim_widened[:HALO]
    from_upper = rim_widened[3 * HALO :]
    own_grad = wide_grad[HALO : HALO + local_rows]
    own_grad = (
        own_grad
        + jnp.pad(from_lower, ((0, local_rows - HALO), (0, 0)))
        + jnp.pad(from_upper, ((local_rows - HALO, 0), (0, 0)))
    )
    query_low = query_grad.reshape(local_rows, width_heads).astype(jnp.bfloat16)
    key_low = own_grad[:, :width_heads].astype(jnp.bfloat16)
    value_low = own_grad[:, width_heads:].astype(jnp.bfloat16)
    grad_qv_shift = jnp.stack(
        [jnp.sum(query_low.astype(jnp.float32), 0), jnp.sum(value_low.astype(jnp.float32), 0)]
    )
    proj_grad = jnp.stack([query_low, key_low, value_low], 1)
    grad_qkv = jnp.einsum("rd,rch->dch", attn_in, proj_grad, preferred_element_type=jnp.float32)
    attn_in_grad = lax.psum(
        jnp.einsum("rch,dch->rd", proj_grad, qkv_matrix, preferred_element_type=jnp.float32).astype(
            jnp.bfloat16
        ),
        "tensor",
    ).astype(jnp.float32)
    input_grad = residual_grad + norm_back(attn_in_grad, normed_one, inverse_one, gain_rows[0])
    grad_gains = jnp.stack([jnp.sum(attn_in_grad * normed_one, 0), gain_two])
    grad_shifts = jnp.stack(
        [jnp.sum(attn_in_grad, 0), jnp.sum(residual_grad, 0), shift_two, jnp.sum(masked, 0)]
    )
    weight_terms = (
        grad_qkv[None],
        grad_out[None],
        grad_up[None],
        grad_down[None],
        grad_gains[None],
        grad_shifts[None],
    )
    return (input_grad, weight_terms, (grad_qv_shift, grad_up_shift))


def shards(
    tokens,
    image_counts,
    cotangent,
    norm_gains,
    row_biases,
    qkv_weight,
    qv_bias,
    out_weight,
    up_weight,
    up_bias,
    down_weight,
):
    section_index = lax.axis_index("section")
    dp_index = lax.axis_index("dp")
    is_first = section_index == 0
    micro_count = tokens.shape[0]
    local_rows = tokens.shape[1]
    gathered = (
        lax.all_gather(qkv_weight, "dp", axis=1, tiled=True),
        lax.all_gather(out_weight, "dp", axis=2, tiled=True),
        lax.all_gather(up_weight, "dp", axis=1, tiled=True),
        lax.all_gather(down_weight, "dp", axis=2, tiled=True),
        lax.all_gather(norm_gains, "dp", axis=2, tiled=True),
        lax.all_gather(row_biases, "dp", axis=2, tiled=True),
    )
    layer_weights = unpack_weights(gathered)
    qv_shift = qv_bias[0].astype(jnp.float32)
    up_shift = up_bias[0].astype(jnp.float32)
    received = jnp.zeros(tokens.shape[1:], jnp.bfloat16)
    kept_list = []
    output_list = []
    for step_index in range(micro_count + 1):
        batch_index = jnp.clip(step_index - section_index, 0, micro_count - 1)
        valid_rows, same_image = image_masks(image_counts[batch_index], dp_index, local_rows)
        layer_in = jnp.where(is_first, tokens[min(step_index, micro_count - 1)], received).astype(
            jnp.float32
        )
        rounded_out, kept_state = layer_forward(
            layer_in, layer_weights, qv_shift, up_shift, valid_rows, same_image
        )
        output_list.append(rounded_out)
        kept_list.append(kept_state)
        if step_index < micro_count:
            received = passed_along(rounded_out, "section", 1)
    grad_from_next = jnp.zeros(tokens.shape[1:], jnp.float32)
    weight_total = None
    bias_total = None
    input_list = []
    for step_index in range(micro_count + 1):
        kept_state = kept_list[micro_count - step_index]
        if step_index < micro_count:
            from_loss = cotangent[micro_count - 1 - step_index].astype(jnp.float32)
        else:
            from_loss = jnp.zeros(tokens.shape[1:], jnp.float32)
        upstream = jnp.where(is_first, grad_from_next, from_loss)
        input_grad, weight_terms, bias_terms = layer_backward(upstream, layer_weights, kept_state)
        weight_terms = (
            lax.psum_scatter(
                weight_terms[0].astype(jnp.bfloat16), "dp", scatter_dimension=1, tiled=True
            ).astype(jnp.float32),
            lax.psum_scatter(
                weight_terms[1].astype(jnp.bfloat16), "dp", scatter_dimension=2, tiled=True
            ).astype(jnp.float32),
            lax.psum_scatter(
                weight_terms[2].astype(jnp.bfloat16), "dp", scatter_dimension=1, tiled=True
            ).astype(jnp.float32),
            lax.psum_scatter(
                weight_terms[3].astype(jnp.bfloat16), "dp", scatter_dimension=2, tiled=True
            ).astype(jnp.float32),
            lax.psum_scatter(
                weight_terms[4].astype(jnp.bfloat16), "dp", scatter_dimension=2, tiled=True
            ).astype(jnp.float32),
            lax.psum_scatter(
                weight_terms[5].astype(jnp.bfloat16), "dp", scatter_dimension=2, tiled=True
            ).astype(jnp.float32),
        )
        weight_total = (
            weight_terms
            if weight_total is None
            else jax.tree.map(jnp.add, weight_total, weight_terms)
        )
        bias_total = (
            bias_terms if bias_total is None else jax.tree.map(jnp.add, bias_total, bias_terms)
        )
        input_list.append(input_grad)
        if step_index < micro_count:
            grad_from_next = passed_along(input_grad.astype(jnp.bfloat16), "section", -1).astype(
                input_grad.dtype
            )
    bias_sums = lax.psum((bias_total[0], bias_total[1]), "dp")
    layer_outputs = jnp.stack(
        [
            jnp.where(is_first, output_list[batch_number], output_list[batch_number + 1])
            for batch_number in range(micro_count)
        ]
    )[None]
    input_grads = jnp.stack(
        [
            jnp.where(
                is_first,
                input_list[micro_count - batch_number],
                input_list[micro_count - 1 - batch_number],
            )
            for batch_number in range(micro_count)
        ]
    )[None]
    return (
        layer_outputs,
        input_grads,
        weight_total[4],
        weight_total[5],
        weight_total[0],
        bias_sums[0][None],
        weight_total[1],
        weight_total[2],
        bias_sums[1][None],
        weight_total[3],
    )


def solution(mesh):
    in_specs = (
        P(None, "dp", None),
        P(),
        P(None, "dp", None),
        P("section", None, "dp"),
        P("section", None, "dp"),
        P("section", "dp", None, "tensor"),
        P("section", None, "tensor"),
        P("section", "tensor", "dp"),
        P("section", "dp", "tensor"),
        P("section", "tensor"),
        P("section", "tensor", "dp"),
    )
    out_specs = (
        P("section", None, "dp", None),
        P("section", None, "dp", None),
        P("section", None, "dp"),
        P("section", None, "dp"),
        P("section", "dp", None, "tensor"),
        P("section", None, "tensor"),
        P("section", "tensor", "dp"),
        P("section", "dp", "tensor"),
        P("section", "tensor"),
        P("section", "tensor", "dp"),
    )
    return jax.shard_map(shards, mesh=mesh, in_specs=in_specs, out_specs=out_specs, check_vma=False)
```

profile of v0, /device:TPU:0, one launch (start us, length us, event | category | flops | bytes accessed | tf_op | source)
XLA Modules:
  0.0 1637.2 jit_solution(2951071099775499943)
XLA Ops:
  10.5 32.4 %all_gather.18 = bf16[1,2,384]{1,0,2:T(2,128)(2,1)S(1)} all-gather(bf16[1,2,48]{1,0,2:T(2,128)(2,1)S(1)} %copy.86), channel_id=1, replica_groups=mesh['section'=2,'dp'=8,'tensor'=2] {'dp'}, dimensions={2}, use_global_device_ids=true | all-gather | bytes 1728 | tf_op jit(solution)/shard_map/all_gather | solution.py:302
  45.0 30.8 %all_gather.19 = bf16[1,4,384]{1,0,2:T(2,128)(2,1)S(1)} all-gather(bf16[1,4,48]{1,0,2:T(2,128)(2,1)S(1)} %copy.87), channel_id=1, replica_groups=mesh['section'=2,'dp'=8,'tensor'=2] {'dp'}, dimensions={2}, use_global_device_ids=true | all-gather | bytes 3456 | tf_op jit(solution)/shard_map/all_gather | solution.py:303
  76.0 5.1 slice_reduce_fusion
  81.1 31.4 %all_gather.20 = bf16[1,384,3,192]{3,1,2,0:T(8,128)(2,1)S(1)} all-gather(bf16[1,48,3,192]{3,1,2,0:T(8,128)(2,1)S(1)} %copy-done.95), channel_id=1, replica_groups=mesh['section'=2,'dp'=8,'tensor'=2] {'dp'}, dimensions={1}, use_global_device_ids=true | all-gather | bytes 497664 | tf_op jit(solution)/shard_map/all_gather | solution.py:298
  114.4 3.7 collective-permute-start
  119.6 31.6 %all_gather.21 = bf16[1,192,384]{1,2,0:T(8,128)(2,1)S(1)} all-gather(bf16[1,192,48]{1,2,0:T(8,128)(2,1)S(1)} %copy-done.116), channel_id=1, replica_groups=mesh['section'=2,'dp'=8,'tensor'=2] {'dp'}, dimensions={2}, use_global_device_ids=true | all-gather | bytes 165888 | tf_op jit(solution)/shard_map/all_gather | solution.py:299
  158.9 33.7 %all_gather.22 = bf16[1,384,768]{2,1,0:T(8,128)(2,1)} all-gather(bf16[1,48,768]{2,1,0:T(8,128)(2,1)S(1)} %copy-done.96), channel_id=1, replica_groups=mesh['section'=2,'dp'=8,'tensor'=2] {'dp'}, dimensions={1}, use_global_device_ids=true | all-gather | bytes 663552 | tf_op jit(solution)/shard_map/all_gather | solution.py:300
  192.6 31.4 %all_gather.23 = bf16[1,768,384]{1,2,0:T(8,128)(2,1)S(1)} all-gather(bf16[1,768,48]{1,2,0:T(8,128)(2,1)S(1)} %copy-done.97), channel_id=1, replica_groups=mesh['section'=2,'dp'=8,'tensor'=2] {'dp'}, dimensions={2}, use_global_device_ids=true | all-gather | bytes 663552 | tf_op jit(solution)/shard_map/all_gather | solution.py:301
  226.9 5.1 multiply_convert_fusion.5
  235.5 18.6 %all-reduce.27.cloned.1.call-done = bf16[512,384]{1,0:T(8,128)(2,1)} async-done(((bf16[512,384]{1,0:T(8,128)(2,1)}), bf16[512,384]{1,0:T(8,128)(2,1)}) %all-reduce.27.cloned.1.call-update) | async-done | bytes 393232 | tf_op jit(solution)/shard_map/psum | solution.py:134
  255.4 3.7 collective-permute-start.2
  259.1 8.7 collective-permute-done.2
  269.2 3.4 collective-permute-start.3
  276.3 4.1 collective-permute-done.4
  287.7 21.5 %all-reduce.29.cloned.1.call-done = bf16[512,384]{1,0:T(8,128)(2,1)} async-done(((bf16[512,384]{1,0:T(8,128)(2,1)}), bf16[512,384]{1,0:T(8,128)(2,1)}) %all-reduce.29.cloned.1.call-update) | async-done | bytes 393232 | tf_op jit(solution)/shard_map/psum | solution.py:126
  311.8 6.3 multiply_convert_fusion.4
  321.2 19.0 %all-reduce.31.cloned.1.call-done = bf16[512,384]{1,0:T(8,128)(2,1)} async-done(((bf16[512,384]{1,0:T(8,128)(2,1)}), bf16[512,384]{1,0:T(8,128)(2,1)}) %all-reduce.31.cloned.1.call-update) | async-done | bytes 393232 | tf_op jit(solution)/shard_map/psum | solution.py:134
  342.4 3.7 collective-permute-start.5
  346.1 8.7 collective-permute-done.5
  356.2 3.4 collective-permute-start.6
  363.3 4.1 collective-permute-done.7
  375.2 20.8 %all-reduce.33.cloned.1.call-done = bf16[512,384]{1,0:T(8,128)(2,1)} async-done(((bf16[512,384]{1,0:T(8,128)(2,1)}), bf16[512,384]{1,0:T(8,128)(2,1)}) %all-reduce.33.cloned.1.call-update) | async-done | bytes 393232 | tf_op jit(solution)/shard_map/psum | solution.py:126
  398.7 4.8 multiply_convert_fusion.3
  407.5 19.5 %all-reduce.35.cloned.1.call-done = bf16[512,384]{1,0:T(8,128)(2,1)} async-done(((bf16[512,384]{1,0:T(8,128)(2,1)}), bf16[512,384]{1,0:T(8,128)(2,1)}) %all-reduce.35.cloned.1.call-update) | async-done | bytes 393232 | tf_op jit(solution)/shard_map/psum | solution.py:190
  430.7 5.6 multiply_reduce_fusion.2
  440.8 5.3 multiply_convert_fusion.2
  452.5 4.4 collective-permute-start.8
  462.3 3.4 collective-permute-done.9
  470.5 19.8 %all-reduce.37.cloned.1.call-done = bf16[512,384]{1,0:T(8,128)(2,1)} async-done(((bf16[512,384]{1,0:T(8,128)(2,1)}), bf16[512,384]{1,0:T(8,128)(2,1)}) %all-reduce.37.cloned.1.call-update) | async-done | bytes 393232 | tf_op jit(solution)/shard_map/psum | solution.py:257
  495.7 11.9 collective-permute-done.10
  507.6 3.1 convert_reduce_fusion.1
  513.3 18.6 %all-reduce.39.cloned.1.call-done = bf16[512,384]{1,0:T(8,128)(2,1)} async-done(((bf16[512,384]{1,0:T(8,128)(2,1)}), bf16[512,384]{1,0:T(8,128)(2,1)}) %all-reduce.39.cloned.1.call-update) | async-done | bytes 393232 | tf_op jit(solution)/shard_map/psum | solution.py:190
  534.1 2.7 fusion.150
  537.1 5.5 multiply_reduce_fusion.1
  547.2 5.4 multiply_convert_fusion.1
  559.7 4.3 collective-permute-start.11
  569.5 3.5 collective-permute-done.12
  578.1 19.9 %all-reduce.41.cloned.1.call-done = bf16[512,384]{1,0:T(8,128)(2,1)} async-done(((bf16[512,384]{1,0:T(8,128)(2,1)}), bf16[512,384]{1,0:T(8,128)(2,1)}) %all-reduce.41.cloned.1.call-update) | async-done | bytes 393232 | tf_op jit(solution)/shard_map/psum | solution.py:257
  603.3 11.9 collective-permute-done.13
  631.8 2.7 convolution_convert_fusion.9
  644.9 4.9 fusion.6
  649.8 3.5 multiply_reduce_fusion
  654.7 5.4 multiply_convert_fusion
  664.6 4.5 collective-permute-start.14
  674.5 3.8 collective-permute-done.15
  692.4 4.7 copy.107
  697.0 2.8 fusion.39
  709.8 59.3 %reduce-scatter.37.cloned.1.call-done = bf16[48,2]{1,0:T(8,128)(2,1)} async-done(((bf16[384,2]{1,0:T(8,128)(2,1)}), bf16[48,2]{1,0:T(8,128)(2,1)}) %reduce-scatter.37.cloned.1.call-update) | async-done | bytes 208
  770.6 2.7 fusion.40
  773.4 2.7 fusion.43
  776.1 4.8 copy.108
  781.6 48.6 %reduce-scatter.43.cloned.1.call-done = bf16[48,4]{1,0:T(8,128)(2,1)} async-done(((bf16[384,4]{1,0:T(8,128)(2,1)}), bf16[48,4]{1,0:T(8,128)(2,1)}) %reduce-scatter.43.cloned.1.call-update) | async-done | bytes 400
  841.0 53.3 %reduce-scatter.51.cloned.1.call-done = bf16[48,192]{1,0:T(8,128)(2,1)} async-done(((bf16[384,192]{1,0:T(8,128)(2,1)}), bf16[48,192]{1,0:T(8,128)(2,1)}) %reduce-scatter.51.cloned.1.call-update) | async-done | bytes 18448
  895.9 59.9 %reduce-scatter.39.cloned.1.call-done = bf16[48,2]{1,0:T(8,128)(2,1)} async-done(((bf16[384,2]{1,0:T(8,128)(2,1)}), bf16[48,2]{1,0:T(8,128)(2,1)}) %reduce-scatter.39.cloned.1.call-update) | async-done | bytes 208
  959.8 4.7 copy.109
  983.4 55.8 %reduce-scatter.45.cloned.1.call-done = bf16[48,4]{1,0:T(8,128)(2,1)} async-done(((bf16[384,4]{1,0:T(8,128)(2,1)}), bf16[48,4]{1,0:T(8,128)(2,1)}) %reduce-scatter.45.cloned.1.call-update) | async-done | bytes 400
  1040.3 20.3 %all-reduce.9 = (f32[1,2,192]{2,1,0:T(2,128)}, f32[1,768]{1,0:T(1,128)}) all-reduce(f32[1,2,192]{2,1,0:T(2,128)S(1)} %fusion.236, f32[1,768]{1,0:T(1,128)S(1)} %broadcast_in_dim.48), channel_id=1, replica_groups=mesh['section'=2,'dp'=8,'tensor'=2] {'dp'}, use_global_device_ids=true, to_apply=%region_78.79 | all-reduce | flops 1152 | bytes 9216 | tf_op jit(solution)/shard_map/psum | solution.py:369
  1060.7 42.7 %reduce-scatter.53.cloned.1.call-done = bf16[48,192]{1,0:T(8,128)(2,1)} async-done(((bf16[384,192]{1,0:T(8,128)(2,1)}), bf16[48,192]{1,0:T(8,128)(2,1)}) %reduce-scatter.53.cloned.1.call-update) | async-done | bytes 18448
  1105.0 63.4 %reduce-scatter.31.cloned.1.call-done = bf16[1,48,768]{2,1,0:T(8,128)(2,1)} async-done(((bf16[1,384,768]{2,1,0:T(8,128)(2,1)}), bf16[1,48,768]{2,1,0:T(8,128)(2,1)}) %reduce-scatter.31.cloned.1.call-update) | async-done | bytes 73744 | tf_op jit(solution)/shard_map/reduce_scatter | solution.py:343
  1168.4 64.9 %reduce-scatter.33.cloned.1.call-done = bf16[1,48,768]{2,1,0:T(8,128)(2,1)} async-done(((bf16[1,384,768]{2,1,0:T(8,128)(2,1)}), bf16[1,48,768]{2,1,0:T(8,128)(2,1)}) %reduce-scatter.33.cloned.1.call-update) | async-done | bytes 73744 | tf_op jit(solution)/shard_map/reduce_scatter | solution.py:343
  1233.3 65.0 %reduce-scatter.35.cloned.1.call-done = bf16[1,48,768]{2,1,0:T(8,128)(2,1)} async-done(((bf16[1,384,768]{2,1,0:T(8,128)(2,1)}), bf16[1,48,768]{2,1,0:T(8,128)(2,1)}) %reduce-scatter.35.cloned.1.call-update) | async-done | bytes 73744 | tf_op jit(solution)/shard_map/reduce_scatter | solution.py:343
  1305.9 54.1 %reduce-scatter.41.cloned.1.call-done = bf16[48,2]{1,0:T(8,128)(2,1)} async-done(((bf16[384,2]{1,0:T(8,128)(2,1)}), bf16[48,2]{1,0:T(8,128)(2,1)}) %reduce-scatter.41.cloned.1.call-update) | async-done | bytes 208
  1361.3 60.2 %reduce-scatter.47.cloned.1.call-done = bf16[48,4]{1,0:T(8,128)(2,1)} async-done(((bf16[384,4]{1,0:T(8,128)(2,1)}), bf16[48,4]{1,0:T(8,128)(2,1)}) %reduce-scatter.47.cloned.1.call-update) | async-done | bytes 400
  1423.0 203.4 %all-reduce.45.cloned.1.call-done = (bf16[1,384,3,192]{3,2,0,1:T(4,128)(2,1)}, bf16[1,384,3,192]{3,2,0,1:T(4,128)(2,1)}, bf16[1,384,3,192]{3,2,0,1:T(4,128)(2,1)...) async-done(((bf16[1,384,3,192]{3,2,0,1:T(4,128)(2,1)}, bf16[1,384,3,192]{3,2,0,1:T(4,128)(2,1)}, ...) | async-done | bytes 3096592
  (702 shorter events, 240.2 us)
Async XLA Ops:
  7.2 216.8 %all-reduce.25.cloned.1.call-start = ((), (), s32[]{:S(2)}) async-start(), calls=%async_computation.12 | async-start | bytes 786432 | tf_op jit(solution)/shard_map/psum | solution.py:126
  7.2 73.8 %copy-start.95 = (bf16[1,48,3,192]{3,1,2,0:T(8,128)(2,1)S(1)}, bf16[1,48,3,192]{3,1,2,0:T(8,128)(2,1)}, u32[]{:S(2)}) copy-start(bf16[1,48,3,192]{3,1,2,0:T(8,128)(2,1)} %param.28) | copy-start | bytes 165892
  8.4 104.4 %copy-start.101 = (f32[512]{0:T(512)}, f32[512]{0:T(512)S(1)}, u32[]{:S(2)}) copy-start(f32[512]{0:T(512)S(1)} %broadcast_multiply_fusion.17) | copy-start | bytes 6148
  9.7 103.2 %copy-start.117 = (f32[512]{0:T(512)}, f32[512]{0:T(512)S(1)}, u32[]{:S(2)}) copy-start(f32[512]{0:T(512)S(1)} %add_rsqrt_fusion.5) | copy-start | bytes 6148
  44.9 68.0 %copy-start.154 = (bf16[1,2,192]{2,1,0:T(2,128)(2,1)S(1)}, bf16[1,2,192]{2,1,0:T(2,128)(2,1)}, u32[]{:S(2)}) copy-start(bf16[1,2,192]{2,1,0:T(2,128)(2,1)} %param.29) | copy-start | bytes 2308
  44.9 68.0 %copy-start.9 = (bf16[2,512,384]{2,1,0:T(8,128)(2,1)S(1)}, bf16[2,512,384]{2,1,0:T(8,128)(2,1)}, u32[]{:S(2)}) copy-start(bf16[2,512,384]{2,1,0:T(8,128)(2,1)} %param.23) | copy-start | bytes 2359300
  81.1 145.7 %copy-start.162 = (f32[384]{0:T(512)}, f32[384]{0:T(512)S(1)}, u32[]{:S(2)}) copy-start(f32[384]{0:T(512)S(1)} %get-tuple-element.131) | copy-start | bytes 4612
  81.1 187.2 %copy-start.132 = (f32[384]{0:T(512)}, f32[384]{0:T(512)S(1)}, u32[]{:S(2)}) copy-start(f32[384]{0:T(512)S(1)} %get-tuple-element.133) | copy-start | bytes 4612
  81.1 259.1 %copy-start.99 = (f32[384]{0:T(512)}, f32[384]{0:T(512)S(1)}, u32[]{:S(2)}) copy-start(f32[384]{0:T(512)S(1)} %get-tuple-element.130) | copy-start | bytes 4612
  112.9 156.2 %copy-start.135 = (f32[1,1,192]{2,1,0:T(1,128)}, f32[1,1,192]{2,1,0:T(1,128)S(1)}, u32[]{:S(2)}) copy-start(f32[1,1,192]{2,1,0:T(1,128)S(1)} %slice.320) | copy-start | bytes 2308
  114.4 37.2 %collective-permute-start = (bf16[256,384]{0,1:T(8,128)(2,1)}, bf16[256,384]{0,1:T(8,128)(2,1)S(1)}, u32[]{:S(2)}, u32[]{:S(2)}) collective-permute-start(bf16[256,384]{0,1:T(8,128)(2,1)} %get-tuple-element.193), channel_id=1, source_target_pairs={{0,2},{2,4},{4,6},{6,8},{8,10},{10,12},{12,14},{1,3},{3,5},{5,7},{... | collective-permute-start | bytes 589832 | tf_op jit(solution)/shard_map/ppermute | solution.py:24
  118.1 33.5 %collective-permute-start.1 = (bf16[256,384]{0,1:T(8,128)(2,1)S(1)}, bf16[256,384]{0,1:T(8,128)(2,1)S(1)}, u32[]{:S(2)}, u32[]{:S(2)}) collective-permute-start(bf16[256,384]{0,1:T(8,128)(2,1)S(1)} %get-tuple-element.194), channel_id=1, source_target_pairs={{2,0},{4,2},{6,4},{8,6},{10,8},{12,10},{14,12},{3,1},{5,3},{7,5},{... | collective-permute-start | bytes 589832 | tf_op jit(solution)/shard_map/ppermute | solution.py:27
  157.7 66.4 %copy-start.77 = (bf16[3,64,512]{2,1,0:T(8,128)(2,1)}, bf16[3,64,512]{2,1,0:T(8,128)(2,1)S(1)}, u32[]{:S(2)}) copy-start(bf16[3,64,512]{2,1,0:T(8,128)(2,1)S(1)} %fusion.53) | copy-start | bytes 589828
  158.8 95.3 %all-reduce.27.cloned.1.call-start = ((), (), s32[]{:S(2)}) async-start(), calls=%async_computation.13 | async-start | bytes 786432 | tf_op jit(solution)/shard_map/psum | solution.py:134
  192.6 119.2 %copy-start.152 = (f32[768]{0:T(1024)}, f32[768]{0:T(1024)S(1)}, u32[]{:S(2)}) copy-start(f32[768]{0:T(1024)S(1)} %convert_reduce_fusion.12) | copy-start | bytes 9220
  225.5 415.6 %copy-start.105 = (f32[512]{0:T(512)}, f32[512]{0:T(512)S(1)}, u32[]{:S(2)}) copy-start(f32[512]{0:T(512)S(1)} %broadcast_multiply_fusion.16) | copy-start | bytes 6148
  234.2 75.0 %all-reduce.29.cloned.1.call-start = ((), (), s32[]{:S(2)}) async-start(), calls=%async_computation.14 | async-start | bytes 786432 | tf_op jit(solution)/shard_map/psum | solution.py:126
  255.4 12.5 collective-permute-start.2
  269.2 7.1 collective-permute-start.3
  272.6 7.8 collective-permute-start.4
  287.6 52.6 %all-reduce.31.cloned.1.call-start = ((), (), s32[]{:S(2)}) async-start(), calls=%async_computation.15 | async-start | bytes 786432 | tf_op jit(solution)/shard_map/psum | solution.py:134
  310.5 223.6 %copy-start.103 = (f32[512]{0:T(512)}, f32[512]{0:T(512)S(1)}, u32[]{:S(2)}) copy-start(f32[512]{0:T(512)S(1)} %broadcast_multiply_fusion.14) | copy-start | bytes 6148
  320.4 75.7 %all-reduce.33.cloned.1.call-start = ((), (), s32[]{:S(2)}) async-start(), calls=%async_computation.16 | async-start | bytes 786432 | tf_op jit(solution)/shard_map/psum | solution.py:126
  342.4 12.5 collective-permute-start.5
  355.0 137.0 %copy-start.98 = (f32[512]{0:T(512)}, f32[512]{0:T(512)S(1)}, u32[]{:S(2)}) copy-start(f32[512]{0:T(512)S(1)} %broadcast_multiply_fusion.13) | copy-start | bytes 6148
  356.2 7.1 collective-permute-start.6
  359.6 7.8 collective-permute-start.7
  374.5 52.6 %all-reduce.35.cloned.1.call-start = ((), (), s32[]{:S(2)}) async-start(), calls=%async_computation.17 | async-start | bytes 786432 | tf_op jit(solution)/shard_map/psum | solution.py:190
  407.3 83.0 %all-reduce.37.cloned.1.call-start = ((), (), s32[]{:S(2)}) async-start(), calls=%async_computation.18 | async-start | bytes 786432 | tf_op jit(solution)/shard_map/psum | solution.py:257
  452.5 9.8 collective-permute-start.8
  456.9 8.8 collective-permute-start.9
  470.5 61.4 %all-reduce.39.cloned.1.call-start = ((), (), s32[]{:S(2)}) async-start(), calls=%async_computation.19 | async-start | bytes 786432 | tf_op jit(solution)/shard_map/psum | solution.py:190
  494.4 13.2 collective-permute-start.10
  513.0 84.9 %all-reduce.41.cloned.1.call-start = ((), (), s32[]{:S(2)}) async-start(), calls=%async_computation.20 | async-start | bytes 786432 | tf_op jit(solution)/shard_map/psum | solution.py:257
  559.7 9.8 collective-permute-start.11
  564.0 9.0 collective-permute-start.12
  578.0 60.7 %all-reduce.43.cloned.1.call-start = ((), (), s32[]{:S(2)}) async-start(), calls=%async_computation.21 | async-start | bytes 786432 | tf_op jit(solution)/shard_map/psum | solution.py:190
  602.0 13.2 collective-permute-start.13
  619.8 88.5 %reduce-scatter.49.cloned.1.call-start = ((), (), s32[]{:S(2)}) async-start(), calls=%async_computation.31 | async-start | bytes 221184
  623.0 146.2 %reduce-scatter.37.cloned.1.call-start = ((), (), s32[]{:S(2)}) async-start(), calls=%async_computation.25 | async-start | bytes 110592
  624.2 206.0 %reduce-scatter.43.cloned.1.call-start = ((), (), s32[]{:S(2)}) async-start(), calls=%async_computation.28 | async-start | bytes 110592
  625.2 269.2 %reduce-scatter.51.cloned.1.call-start = ((), (), s32[]{:S(2)}) async-start(), calls=%async_computation.32 | async-start | bytes 221184
  631.3 324.5 %reduce-scatter.39.cloned.1.call-start = ((), (), s32[]{:S(2)}) async-start(), calls=%async_computation.26 | async-start | bytes 110592
  636.9 339.2 %all-reduce.47.cloned.1.call-start = ((), (), s32[]{:S(2)}) async-start(), calls=%async_computation.35 | async-start | bytes 1572864 | tf_op jit(solution)/shard_map/psum | solution.py:134
  664.6 9.9 collective-permute-start.14
  669.0 9.3 collective-permute-start.15
  683.1 356.0 %reduce-scatter.45.cloned.1.call-start = ((), (), s32[]{:S(2)}) async-start(), calls=%async_computation.29 | async-start | bytes 110592
  685.6 417.7 %reduce-scatter.53.cloned.1.call-start = ((), (), s32[]{:S(2)}) async-start(), calls=%async_computation.33 | async-start | bytes 221184
  689.7 478.7 %reduce-scatter.31.cloned.1.call-start = ((), (), s32[]{:S(2)}) async-start(), calls=%async_computation.22 | async-start | bytes 663552 | tf_op jit(solution)/shard_map/reduce_scatter | solution.py:343
  699.8 533.5 %reduce-scatter.33.cloned.1.call-start = ((), (), s32[]{:S(2)}) async-start(), calls=%async_computation.23 | async-start | bytes 663552 | tf_op jit(solution)/shard_map/reduce_scatter | solution.py:343
  704.6 66.0 %copy-start.16 = (bf16[512,384]{1,0:T(8,128)(2,1)S(1)}, bf16[512,384]{1,0:T(8,128)(2,1)}, u32[]{:S(2)}) copy-start(bf16[512,384]{1,0:T(8,128)(2,1)} %all-reduce.29.cloned.1.call-done) | copy-start | bytes 1179652
  704.6 66.0 %copy-start.104 = (f32[512]{0:T(512)S(1)}, f32[512]{0:T(512)}, u32[]{:S(2)}) copy-start(f32[512]{0:T(512)} %copy-done.103) | copy-start | bytes 6148
  704.6 66.0 %copy-start.121 = (f32[512]{0:T(512)S(1)}, f32[512]{0:T(512)}, u32[]{:S(2)}) copy-start(f32[512]{0:T(512)} %copy-done.119) | copy-start | bytes 6148
  773.3 525.0 %reduce-scatter.35.cloned.1.call-start = ((), (), s32[]{:S(2)}) async-start(), calls=%async_computation.24 | async-start | bytes 663552 | tf_op jit(solution)/shard_map/reduce_scatter | solution.py:343
  838.0 119.1 %copy-start.92 = (bf16[512,384]{1,0:T(8,128)(2,1)S(1)}, bf16[512,384]{1,0:T(8,128)(2,1)}, u32[]{:S(2)}) copy-start(bf16[512,384]{1,0:T(8,128)(2,1)} %copy-done.91) | copy-start | bytes 1179652
  838.0 119.1 %copy-start.130 = (f32[512]{0:T(512)S(1)}, f32[512]{0:T(512)}, u32[]{:S(2)}) copy-start(f32[512]{0:T(512)} %copy-done.128) | copy-start | bytes 6148
  838.0 521.9 %reduce-scatter.41.cloned.1.call-start = ((), (), s32[]{:S(2)}) async-start(), calls=%async_computation.27 | async-start | bytes 110592
  979.7 441.9 %reduce-scatter.47.cloned.1.call-start = ((), (), s32[]{:S(2)}) async-start(), calls=%async_computation.30 | async-start | bytes 110592
  980.6 645.8 %all-reduce.45.cloned.1.call-start = ((), (), s32[]{:S(2)}) async-start(), calls=%async_computation.34 | async-start | bytes 11796480
  983.3 120.9 %copy-start.93 = (bf16[1,192,48]{2,1,0:T(8,128)(2,1)S(1)}, bf16[1,192,48]{2,1,0:T(8,128)(2,1)}, u32[]{:S(2)}) copy-start(bf16[1,192,48]{2,1,0:T(8,128)(2,1)} %copy.129) | copy-start | bytes 55300
  983.3 120.9 %copy-start.94 = (bf16[1,192,48]{2,1,0:T(8,128)(2,1)S(1)}, bf16[1,192,48]{2,1,0:T(8,128)(2,1)}, u32[]{:S(2)}) copy-start(bf16[1,192,48]{2,1,0:T(8,128)(2,1)} %copy.131) | copy-start | bytes 55300
  983.4 316.6 %copy-start.100 = (f32[384]{0:T(512)S(1)}, f32[384]{0:T(512)}, u32[]{:S(2)}) copy-start(f32[384]{0:T(512)} %copy-done.99) | copy-start | bytes 4612
  983.4 316.6 %copy-start.110 = (f32[512]{0:T(512)S(1)}, f32[512]{0:T(512)}, u32[]{:S(2)}) copy-start(f32[512]{0:T(512)} %copy-done.107) | copy-start | bytes 6148
  1304.6 117.8 %copy-start.151 = (bf16[1,4,48]{2,1,0:T(4,128)(2,1)S(1)}, bf16[1,4,48]{2,1,0:T(4,128)(2,1)}, u32[]{:S(2)}) copy-start(bf16[1,4,48]{2,1,0:T(4,128)(2,1)} %copy.123) | copy-start | bytes 1156
  (162 other events, 2033.2 us)
Sparse Core Ops, SparseCore 0:
  158.9 19.7 all-reduce.24
  234.3 19.7 all-reduce.26
  287.8 21.4 all-reduce.28
  320.5 19.6 all-reduce.30
  374.6 21.3 all-reduce.32
  407.4 19.6 all-reduce.34
  470.6 19.6 all-reduce.36
  513.1 18.7 all-reduce.38
  578.1 19.7 all-reduce.40
  619.9 18.7 all-reduce.42
  641.9 65.6 reduce-scatter.48
  711.3 57.7 reduce-scatter.36
  772.4 57.7 reduce-scatter.42
  833.3 61.0 reduce-scatter.50
  898.0 57.7 reduce-scatter.38
  958.0 18.0 all-reduce.46
  979.2 59.8 reduce-scatter.44
  1042.3 61.0 reduce-scatter.52
  1106.6 61.7 reduce-scatter.30
  1171.5 61.6 reduce-scatter.32
  1236.6 61.7 reduce-scatter.34
  1302.2 57.7 reduce-scatter.40
  1363.8 57.7 reduce-scatter.46
  1425.8 200.5 all-reduce.44
where the time goes:
time: 1650 us; the launch traced here: 1640 us
  waiting for transfers between devices  1060 us (64%)
  blocking collectives  212 us (13%)
  matrix products  114 us (7%)
  local copies, waits for them, and re-layouts  98.2 us (6%)
  other arithmetic  94 us (6%)
  starting transfers between devices  44.1 us (3%)
  between operations  18 us (1%)
    unnamed x34, waiting for transfers between devices  638 us
    reduce_scatter x3, waiting for transfers between devices, shards(): lax.psum_scatter(weight_terms[2].astype(jnp.bfloat16), 'dp', scatter_dime...  193 us
    psum x3, waiting for transfers between devices, layer_forward(): lax.psum(attn_partial.astype(jnp.bfloat16), 'tensor').astype(jnp.float32)  42.4 us
    unnamed x414, local copies, waits for them, and re-layouts  41.9 us
    ppermute x4, waiting for transfers between devices, passed_along(): return lax.ppermute(block, axis, route)  41.2 us
    psum x3, waiting for transfers between devices, layer_forward(): lax.psum(down_partial.astype(jnp.bfloat16), 'tensor').astype(jnp.float32)  40.1 us
    psum x3, waiting for transfers between devices, layer_backward(): lax.psum(mlp_partial.astype(jnp.bfloat16), 'tensor').astype(jnp.float32)  39.8 us
    psum x2, waiting for transfers between devices, layer_backward(): lax.psum(jnp.einsum('rch,dch->rd', proj_grad, qkv_matrix, preferred_eleme...  39.7 us
  transfers between devices with their start and end apart: 40, of which 33 were waited for; matrix products, arithmetic and copies ran while one was open for 9% of the time, Pallas kernels for 0%

commit v1 on v0

v1 whole, which is shorter than its diff:
```python
import math

import jax
import jax.numpy as jnp
from jax import lax
from jax.sharding import PartitionSpec as P

IMG_LEN = 197
IMG_PAD = 208
HD = 64
EPSILON = 1e-06
NEGATIVE = -1e30
MISC = 128
F32 = jnp.float32
BF16 = jnp.bfloat16


def mm(a, b, dims):
    return lax.dot_general(a, b, (dims, ((), ())), preferred_element_type=F32)


def nn(a, b):
    return mm(a, b, ((1,), (0,)))


def nt(a, b):
    return mm(a, b, ((1,), (1,)))


def tn(a, b):
    return mm(a, b, ((0,), (0,)))


def normed(x):
    centred = x - jnp.mean(x, -1, keepdims=True)
    inverse = lax.rsqrt(jnp.mean(centred * centred, -1, keepdims=True) + EPSILON)
    return centred * inverse, inverse


def norm_back(grad, xhat, inverse, gain):
    t = grad * gain
    return inverse * (
        t - jnp.mean(t, -1, keepdims=True) - xhat * jnp.mean(t * xhat, -1, keepdims=True)
    )


def gelu_parts(u):
    cdf = 0.5 * (1.0 + lax.erf(u * math.sqrt(0.5)))
    pdf = jnp.exp(-0.5 * u * u) * (1.0 / math.sqrt(2.0 * math.pi))
    return u * cdf, cdf + u * pdf


def layer_fwd(x, w, rows):
    wq, wk, wv, wo, wu, wd = w
    gain1, gain2, bias0, bias1, bias2, bias3, qb, vb, ub = rows
    total, width = x.shape
    xhat1, inv1 = normed(x)
    attn_in = (xhat1 * gain1 + bias0).astype(BF16)
    q = ((nn(attn_in, wq) + qb) * (1.0 / math.sqrt(HD))).astype(BF16)
    k = nn(attn_in, wk).astype(BF16)
    v = (nn(attn_in, wv) + vb).astype(BF16)
    low = lax.broadcasted_iota(jnp.int32, (1, 128), 1) < HD
    real = lax.broadcasted_iota(jnp.int32, (1, IMG_PAD), 1) < IMG_LEN
    probs = []
    mixed_rows = []
    for n in range(total // IMG_PAD):
        r = slice(n * IMG_PAD, (n + 1) * IMG_PAD)
        cols = []
        for b in range(width // 128):
            c = slice(b * 128, (b + 1) * 128)
            qq, kk, vv = q[r, c], k[r, c], v[r, c]
            outs = []
            for side in (low, ~low):
                s = jnp.where(real, nt(jnp.where(side, qq, 0), kk), NEGATIVE)
                e = jnp.exp(s - jnp.max(s, -1, keepdims=True))
                p = (e / jnp.sum(e, -1, keepdims=True)).astype(BF16)
                probs.append(p)
                outs.append(nn(p, vv))
            cols.append(jnp.where(low, outs[0], outs[1]))
        mixed_rows.append(jnp.concatenate(cols, 1))
    mixed = jnp.concatenate(mixed_rows, 0).astype(BF16)
    residual = x + (nt(mixed, wo) + bias1)
    xhat2, inv2 = normed(residual)
    mlp_in = (xhat2 * gain2 + bias2).astype(BF16)
    hidden, slope = gelu_parts(nn(mlp_in, wu) + ub)
    hidden = hidden.astype(BF16)
    out = residual + (nt(hidden, wd) + bias3)
    kept = (xhat1, inv1, attn_in, q, k, v, probs, mixed, xhat2, inv2, mlp_in, slope.astype(BF16), hidden)
    return out, kept


def layer_bwd(masked, w, rows, kept):
    wq, wk, wv, wo, wu, wd = w
    gain1, gain2 = rows[0], rows[1]
    xhat1, inv1, attn_in, q, k, v, probs, mixed, xhat2, inv2, mlp_in, slope, hidden = kept
    total, width = masked.shape

    def rsum(a):
        return jnp.sum(a.astype(F32), 0, keepdims=True)

    dg = masked.astype(BF16)
    g_down = tn(dg, hidden)
    up_grad = (nn(dg, wd) * slope).astype(BF16)
    g_up = tn(mlp_in, up_grad)
    mg = nt(up_grad, wu)
    res = masked + norm_back(mg, xhat2, inv2, gain2)
    ag = res.astype(BF16)
    g_out = tn(ag, mixed)
    xg = nn(ag, wo).astype(BF16)
    low = lax.broadcasted_iota(jnp.int32, (1, 128), 1) < HD
    out_rows = []
    at = 0
    for n in range(total // IMG_PAD):
        r = slice(n * IMG_PAD, (n + 1) * IMG_PAD)
        qs, ks, vs = [], [], []
        for b in range(width // 128):
            c = slice(b * 128, (b + 1) * 128)
            qq, kk, vv, gg = q[r, c], k[r, c], v[r, c], xg[r, c]
            dq, dk, dv = [], [], []
            for side in (low, ~low):
                p = probs[at].astype(F32)
                dp = nt(jnp.where(side, gg, 0), vv)
                ds = (p * (dp - jnp.sum(p * dp, -1, keepdims=True))).astype(BF16)
                dv.append(tn(probs[at], gg))
                dq.append(nn(ds, kk) * (1.0 / math.sqrt(HD)))
                dk.append(tn(ds, qq))
                at += 1
            qs.append(jnp.where(low, *dq))
            ks.append(jnp.where(low, *dk))
            vs.append(jnp.where(low, *dv))
        out_rows.append([jnp.concatenate(a, 1).astype(BF16) for a in (qs, ks, vs)])
    dq, dk, dv = [jnp.concatenate([o[i] for o in out_rows], 0) for i in range(3)]
    g_q, g_k, g_v = tn(attn_in, dq), tn(attn_in, dk), tn(attn_in, dv)
    ig = nt(dq, wq) + nt(dk, wk) + nt(dv, wv)
    inp = res + norm_back(ig, xhat1, inv1, gain1)
    row_grads = (
        rsum(ig * xhat1), rsum(mg * xhat2), rsum(ig), rsum(res), rsum(mg), rsum(masked),
        rsum(dq), rsum(dv), rsum(up_grad),
    )
    return inp, (g_q, g_k, g_v, g_out, g_up, g_down), row_grads


def shards(tokens, image_counts, cotangent, norm_gains, row_biases, qkv_weight, qv_bias, out_weight,
           up_weight, up_bias, down_weight):
    sec = lax.axis_index("section")
    dp = lax.axis_index("dp")
    ten = lax.axis_index("tensor")
    n_dp = lax.axis_size("dp")
    m = n_dp // 2
    zi, yi = dp // 2, dp % 2
    local_rows, width = tokens.shape[1:]
    images = local_rows * n_dp // IMG_LEN
    piece = width // n_dp
    heads = qkv_weight.shape[3]
    ff = up_weight.shape[2]
    cols = 4 * heads + 2 * ff
    full = cols + MISC

    def pt(a):
        return lax.ppermute(a, "tensor", [(0, 1), (1, 0)])

    def px(a):
        return lax.ppermute(a, "section", [(0, 1), (1, 0)])

    def py(a):
        return lax.ppermute(a, "dp", [(i, i ^ 1) for i in range(n_dp)])

    def pz(a, k):
        return lax.ppermute(a, "dp", [(2 * z + y, 2 * ((z + k) % m) + y) for z in range(m) for y in range(2)])

    batch_tokens = lax.dynamic_index_in_dim(tokens, sec, 0, keepdims=False)
    batch_cot = lax.dynamic_index_in_dim(cotangent, sec, 0, keepdims=False)
    count = lax.dynamic_index_in_dim(image_counts, sec, 0, keepdims=False)
    first = jnp.minimum((dp * local_rows + IMG_LEN - 1) // IMG_LEN, images)
    last = jnp.minimum(((dp + 1) * local_rows + IMG_LEN - 1) // IMG_LEN, images)
    held = last - first
    slots = -(-(-(-local_rows // IMG_LEN)) // 2)
    lower = held // 2
    own_first = jnp.where(ten == 0, first, first + lower)
    own_count = jnp.where(ten == 0, lower, held - lower)
    total = slots * IMG_PAD
    row = lax.broadcasted_iota(jnp.int32, (total, 1), 0)
    slot, inside = row // IMG_PAD, row % IMG_PAD
    exists = (inside < IMG_LEN) & (slot < own_count)
    valid = (exists & (own_first + slot < count)).astype(F32)
    target = (own_first + slot) * IMG_LEN + inside - dp * local_rows
    canvas_rows = local_rows + IMG_PAD
    select = ((lax.broadcasted_iota(jnp.int32, (total, canvas_rows), 1) == target) & exists).astype(BF16)

    both = jnp.stack([batch_tokens, batch_cot])
    halo = lax.ppermute(both[:, :IMG_PAD], "dp", [(i + 1, i) for i in range(n_dp - 1)])
    both = jnp.concatenate([both, halo], 1)
    x0 = nn(select, both[0])
    cot = nn(select, both[1])

    extra = jnp.concatenate([qv_bias[0].reshape(-1), up_bias[0]])
    extra = extra.reshape(-1, width)
    extra = lax.dynamic_slice_in_dim(extra, dp * piece, piece, 1)
    misc = jnp.concatenate([norm_gains[0], row_biases[0], extra], 0)
    misc = jnp.pad(misc, ((0, MISC - misc.shape[0]), (0, 0))).T
    own = jnp.concatenate(
        [qkv_weight[0].reshape(piece, 3 * heads), out_weight[0].T, up_weight[0], down_weight[0].T, misc], 1
    )
    ring = jnp.stack([own] + [pz(own, k) for k in range(1, m)])
    ring = ring[::-1]
    quad = lax.dynamic_slice_in_dim(jnp.concatenate([ring, ring]), m - 1 - zi, m, 0)
    half = full // 256 * 128
    qx, qy = px(quad), py(quad)
    qd = jnp.concatenate([px(qy[..., :half]), py(qx[..., half:])], -1)

    def order(flag, a, b, axis):
        return jnp.where(flag == 0, jnp.stack([a, b], axis), jnp.stack([b, a], axis))

    mine = order(yi, quad, qy, 1)
    other = order(yi, qx, qd, 1)
    layers = order(sec, mine, other, 0)
    theirs = pt(layers)
    layers = order(ten, layers, theirs, 1).reshape(2, 2, width, full)

    def unpack(l):
        a = layers[l]

        def part(lo, size):
            return jnp.concatenate([a[0, :, lo:lo + size], a[1, :, lo:lo + size]], 1)

        w = [part(i * heads, heads) for i in range(4)] + [part(4 * heads, ff), part(4 * heads + ff, ff)]
        ext = a[:, :, cols:].swapaxes(1, 2).astype(F32)
        rows = [ext[0, i:i + 1] for i in range(6)]
        n_ext = (2 * heads + ff) // width
        tail = ext[:, 6:6 + n_ext].reshape(2, -1)
        rows.append(tail[:, :heads].reshape(1, -1))
        rows.append(tail[:, heads:2 * heads].reshape(1, -1))
        rows.append(tail[:, 2 * heads:].reshape(1, -1))
        return w, rows

    w0, r0 = unpack(0)
    w1, r1 = unpack(1)
    out0, kept0 = layer_fwd(x0, w0, r0)
    low0 = (out0 * valid).astype(BF16)
    out1, kept1 = layer_fwd(low0.astype(F32), w1, r1)
    low1 = (out1 * valid).astype(BF16)
    in1, g1, rg1 = layer_bwd(cot * valid, w1, r1, kept1)
    in0, g0, rg0 = layer_bwd(in1 * valid, w0, r0, kept0)

    def pack(g, rg):
        by_core = []
        small = jnp.concatenate(rg[:6], 0)
        small = jnp.pad(small, ((0, MISC - 6), (0, 0))).T
        for t in range(2):
            parts = [a[:, t * heads:(t + 1) * heads] for a in g[:4]]
            parts += [a[:, t * ff:(t + 1) * ff] for a in g[4:]]
            by_core.append(jnp.concatenate(parts + [small], 1).astype(BF16))
        return jnp.stack(by_core)

    def pack_rows(rg):
        return jnp.stack([
            jnp.concatenate([rg[6][0, t * heads:(t + 1) * heads], rg[7][0, t * heads:(t + 1) * heads],
                             rg[8][0, t * ff:(t + 1) * ff]]) for t in range(2)])

    def pick(a, i, axis):
        return lax.dynamic_index_in_dim(a, i, axis, keepdims=False)

    def plus(a, b):
        return (a.astype(F32) + b.astype(F32)).astype(BF16)

    grads = jnp.stack([pack(g0, rg0), pack(g1, rg1)]).reshape(2, 2, m, 2, piece, full)
    grads = plus(pick(grads, ten, 1), pt(pick(grads, 1 - ten, 1)))
    near, far = pick(grads, sec, 0), pick(grads, 1 - sec, 0)
    g_own, g_y = pick(near, yi, 1), pick(near, 1 - yi, 1)
    g_x, g_d = pick(far, yi, 1), pick(far, 1 - yi, 1)
    via_x, via_y = px(g_d[..., :half]), py(g_d[..., half:])
    g_y = jnp.concatenate([plus(g_y[..., :half], via_x), g_y[..., half:]], -1)
    g_x = jnp.concatenate([g_x[..., :half], plus(g_x[..., half:], via_y)], -1)
    g_own = g_own.astype(F32) + px(g_x).astype(F32) + py(g_y).astype(F32)
    g_low = g_own.astype(BF16)
    final = pick(g_own, zi, 0)
    for k in range(1, m):
        final = final + pz(pick(g_low, (zi + k) % m, 0), k).astype(F32)

    small = jnp.stack([pack_rows(rg0), pack_rows(rg1)])
    small = pick(small, ten, 1) + pt(pick(small, 1 - ten, 1))
    small = pick(small, sec, 0) + px(pick(small, 1 - sec, 0))
    small = small + py(small)
    small = sum([pz(small, k) for k in range(1, m)], small)

    def settle(a):
        canvas = tn(select, a.astype(BF16)).astype(BF16)
        return canvas

    def gathered(a):
        a = a + pt(a)
        spill = lax.ppermute(a[..., local_rows:, :], "dp", [(i, i + 1) for i in range(n_dp - 1)])
        return jnp.concatenate([a[..., :IMG_PAD, :] + spill, a[..., IMG_PAD:local_rows, :]], -2)

    def exchange(a0, a1):
        keep = jnp.where(sec == 0, a0, a1)
        got = px(jnp.where(sec == 0, a1, a0))
        return jnp.where(sec == 0, jnp.stack([keep, got]), jnp.stack([got, keep]))

    block = gathered(jnp.stack([settle(low0), settle(low1), settle(in0), settle(in1)]))
    moved = exchange(block[0::2], block[1::2])
    layer_outputs = moved[:, 0][None]
    input_grads = moved[:, 1].astype(F32)[None]

    g_gain = final[:, cols:cols + 2].T[None]
    g_bias = final[:, cols + 2:cols + 6].T[None]
    return (
        layer_outputs,
        input_grads,
        g_gain,
        g_bias,
        final[:, :3 * heads].reshape(1, piece, 3, heads),
        small[:2 * heads].reshape(1, 2, heads),
        final[:, 3 * heads:4 * heads].T[None],
        final[:, 4 * heads:4 * heads + ff][None],
        small[2 * heads:][None],
        final[:, 4 * heads + ff:cols].T[None],
    )


def solution(mesh):
    in_specs = (
        P(None, "dp", None),
        P(),
        P(None, "dp", None),
        P("section", None, "dp"),
        P("section", None, "dp"),
        P("section", "dp", None, "tensor"),
        P("section", None, "tensor"),
        P("section", "tensor", "dp"),
        P("section", "dp", "tensor"),
        P("section", "tensor"),
        P("section", "tensor", "dp"),
    )
    out_specs = (
        P("section", None, "dp", None),
        P("section", None, "dp", None),
        P("section", None, "dp"),
        P("section", None, "dp"),
        P("section", "dp", None, "tensor"),
        P("section", None, "tensor"),
        P("section", "tensor", "dp"),
        P("section", "dp", "tensor"),
        P("section", "tensor"),
        P("section", "tensor", "dp"),
    )
    return jax.shard_map(shards, mesh=mesh, in_specs=in_specs, out_specs=out_specs, check_vma=False)
```

time: 1650 us -> 394 us (0.24)
  the two profiles are of different devices: /device:TPU:0 before, /device:TPU:8 now
where the time goes in v1:
time: 394 us; the launch traced here: 388 us
  waiting for transfers between devices  118 us (30%)
  matrix products  96 us (24%)
  local copies, waits for them, and re-layouts  80.7 us (20%)
  other arithmetic  54.1 us (14%)
  starting transfers between devices  32.5 us (8%)
  between operations  6.62 us (2%)
    dot_general x185, matrix products, mm(): return lax.dot_general(a, b, (dims, ((), ())), preferred_element_type=F32)  96 us
    ppermute x6, waiting for transfers between devices, px(): return lax.ppermute(a, 'section', [(0, 1), (1, 0)])  48 us
    ppermute x9, waiting for transfers between devices, pz(): lax.ppermute(a, 'dp', [(2 * z + y, 2 * ((z + k) % m) + y) for z in range(...  37.1 us
    slice x24, local copies, waits for them, and re-layouts, pack(): parts = [a[:, t * heads:(t + 1) * heads] for a in g[:4]]  17.6 us
    unnamed x705, local copies, waits for them, and re-layouts  15.6 us
    concatenate x4, local copies, waits for them, and re-layouts, pack(): by_core.append(jnp.concatenate(parts + [small], 1).astype(BF16))  14.6 us
    ppermute x5, waiting for transfers between devices, py(): return lax.ppermute(a, 'dp', [(i, i ^ 1) for i in range(n_dp)])  14.2 us
    ppermute x9, starting transfers between devices, pz(): lax.ppermute(a, 'dp', [(2 * z + y, 2 * ((z + k) % m) + y) for z in range(...  11 us
  transfers between devices with their start and end apart: 26, of which 17 were waited for; matrix products, arithmetic and copies ran while one was open for 9% of the time, Pallas kernels for 0%

profile of v1, /device:TPU:8, one launch (start us, length us, event | category | flops | bytes accessed | tf_op | source)
XLA Modules:
  0.0 387.5 jit_solution(10805662446205462107)
XLA Ops:
  5.1 1.6 collective-permute-start.1
  7.9 1.9 collective-permute-start.3
  9.8 13.0 %collective-permute-done.1 = bf16[48,2432]{1,0:T(8,128)(2,1)S(1)} collective-permute-done((bf16[48,2432]{1,0:T(8,128)(2,1)S(1)}, bf16[48,2432]{1,0:T(8,128)(2,1)S(1)}, u32[]{:S(2)}, u32[]{:S(2)}) %collective-permute-start.1) | collective-permute-done | bytes 233504 | tf_op jit(solution)/shard_map/ppermute | solution.py:169
  22.8 3.9 collective-permute-done.2
  26.7 1.8 collective-permute-done.3
  30.1 1.5 collective-permute-start.5
  31.6 1.5 collective-permute-start.4
  33.5 19.4 %collective-permute-done.5 = bf16[4,48,2432]{2,1,0:T(8,128)(2,1)S(1)} collective-permute-done((bf16[4,48,2432]{2,1,0:T(8,128)(2,1)}, bf16[4,48,2432]{2,1,0:T(8,128)(2,1)S(1)}, u32[]{:S(2)}, u32[]{:S(2)}) %collective-permute-start.5) | collective-permute-done | bytes 933920 | tf_op jit(solution)/shard_map/ppermute | solution.py:163
  52.9 1.6 collective-permute-start.7
  54.6 1.6 collective-permute-start.6
  56.7 8.9 %collective-permute-done.6 = bf16[4,48,1152]{2,1,0:T(8,128)(2,1)S(1)} collective-permute-done((bf16[4,48,1152]{2,1,0:T(8,128)(2,1)S(1)}, bf16[4,48,1152]{2,1,0:T(8,128)(2,1)S(1)}, u32[]{:S(2)}, u32[]{:S(2)}) %collective-permute-start.6) | collective-permute-done | bytes 442400 | tf_op jit(solution)/shard_map/ppermute | solution.py:163
  66.0 2.2 maximum_select_fusion.2
  70.9 1.9 collective-permute-start
  74.3 8.8 %collective-permute-done = bf16[2,208,384]{2,1,0:T(8,128)(2,1)} collective-permute-done((bf16[2,208,384]{2,1,0:T(8,128)(2,1)}, bf16[2,208,384]{2,1,0:T(8,128)(2,1)}, u32[]{:S(2)}, u32[]{:S(2)}) %collective-permute-start) | collective-permute-done | bytes 319520 | tf_op jit(solution)/shard_map/ppermute | solution.py:191
  87.7 5.2 %maximum_select_fusion = bf16[2,2,4,2,48,2432]{5,4,3,2,1,0:T(8,128)(2,1)S(1)} fusion(bf16[2,1,4,2,48,2432]{5,4,3,2,1,0:T(8,128)(2,1)} %bitcast.19, bf16[2,1,4,2,48,2432]{5,4,3,2,1,0:T(8,128)(2,1)S(1)} %maximum_select_fusion.1, pred[]{:T(512)S(6)} %eq.31), kind=kLoop, calls=%fused_computation | loop fusion | flops 11206656 | bytes 14942209 | tf_op jit(solution)/shard_map/jit(_where)/select_n | solution.py:212
  92.9 2.4 fusion.727
  95.4 1.5 slice_bitcast_fusion.25
  105.9 3.0 slice_bitcast_fusion.17
  113.4 1.6 fusion.47
  123.6 3.8 multiply_convert_fusion.1
  130.6 1.6 fusion.49
  135.6 1.5 fusion.766
  137.1 1.5 fusion.765
  143.3 1.6 slice_bitcast_fusion.3
  149.3 1.6 fusion.50
  161.6 3.4 multiply_convert_fusion
  165.0 2.4 convert_reduce_fusion
  186.2 2.5 convert_reduce_fusion.1
  195.3 1.9 convolution_convert_fusion.2
  197.3 2.0 convolution_convert_fusion.3
  207.5 2.0 convolution_convert_fusion.1
  214.6 1.6 fusion.43
  222.6 2.5 fusion.728
  241.9 2.1 convolution_convert_fusion
  248.5 2.7 concatenate.403
  251.2 4.0 %concatenate.410 = bf16[1,1,4,2,48,2432]{5,4,3,2,1,0:T(8,128)(2,1)} concatenate(bf16[1,1,4,2,48,192]{5,4,3,2,1,0:T(8,128)(2,1)} %bitcast.344, bf16[1,1,4,2,48,192]{5,4,3,2,1,0:T(8,128)(2,1)} %bitcast.343, bf16[1,1,4,2,48,192]{5,4,3,2,1,0:T(8,128)(2,1)} %bitcast.341, bf16[1,1,4,2,48,192]{5,4,3,2,1,0:T(8,128)(2,1)} %bitcast.340, bf16[1,1,4,2,48,768]{5,4,3,2,1,0:T(8,128)(2,1)} %bitcast.323, ...), dimensions={5} | concatenate | bytes 3735552 | tf_op jit(solution)/shard_map/concatenate | solution.py:252
  255.1 4.0 %concatenate.419 = bf16[1,1,4,2,48,2432]{5,4,3,2,1,0:T(8,128)(2,1)} concatenate(bf16[1,1,4,2,48,192]{5,4,3,2,1,0:T(8,128)(2,1)} %bitcast.348, bf16[1,1,4,2,48,192]{5,4,3,2,1,0:T(8,128)(2,1)} %bitcast.347, bf16[1,1,4,2,48,192]{5,4,3,2,1,0:T(8,128)(2,1)} %bitcast.346, bf16[1,1,4,2,48,192]{5,4,3,2,1,0:T(8,128)(2,1)} %bitcast.345, bf16[1,1,4,2,48,768]{5,4,3,2,1,0:T(8,128)(2,1)} %bitcast.327, ...), dimensions={5} | concatenate | bytes 3735552 | tf_op jit(solution)/shard_map/concatenate | solution.py:252
  259.1 4.0 %concatenate.426 = bf16[1,1,4,2,48,2432]{5,4,3,2,1,0:T(8,128)(2,1)} concatenate(bf16[1,1,4,2,48,192]{5,4,3,2,1,0:T(8,128)(2,1)} %bitcast.352, bf16[1,1,4,2,48,192]{5,4,3,2,1,0:T(8,128)(2,1)} %bitcast.351, bf16[1,1,4,2,48,192]{5,4,3,2,1,0:T(8,128)(2,1)} %bitcast.350, bf16[1,1,4,2,48,192]{5,4,3,2,1,0:T(8,128)(2,1)} %bitcast.349, bf16[1,1,4,2,48,768]{5,4,3,2,1,0:T(8,128)(2,1)} %bitcast.326, ...), dimensions={5} | concatenate | bytes 3735552 | tf_op jit(solution)/shard_map/concatenate | solution.py:252
  263.1 3.6 maximum_maximum_fusion
  266.8 2.1 dynamic-slice_bitcast_fusion
  268.8 2.1 copy-done
  271.0 1.6 fusion.34
  272.6 1.9 fusion.40
  274.5 3.5 fusion.37
  278.0 3.4 pad_maximum_fusion
  287.4 2.8 fusion.715
  290.4 4.3 %collective-permute-start.10 = (bf16[4,208,384]{2,1,0:T(8,128)(2,1)S(1)}, bf16[4,208,384]{2,1,0:T(8,128)(2,1)S(1)}, u32[]{:S(2)}, u32[]{:S(2)}) collective-permute-start(bf16[4,208,384]{2,1,0:T(8,128)(2,1)S(1)} %slice.806), channel_id=1, source_target_pairs={{0,2},{2,4},{4,6},{6,8},{8,10},{10,12},{12,14},{1,3},{3,5},{5,7},{... | collective-permute-start | bytes 1916936 | tf_op jit(solution)/shard_map/ppermute | solution.py:292
  294.7 2.9 fusion
  297.9 1.6 copy-done.4
  299.5 1.6 collective-permute-start.15
  301.1 8.4 %collective-permute-done.10 = bf16[4,208,384]{2,1,0:T(8,128)(2,1)S(1)} collective-permute-done((bf16[4,208,384]{2,1,0:T(8,128)(2,1)S(1)}, bf16[4,208,384]{2,1,0:T(8,128)(2,1)S(1)}, u32[]{:S(2)}, u32[]{:S(2)}) %collective-permute-start.10) | collective-permute-done | bytes 639008 | tf_op jit(solution)/shard_map/ppermute | solution.py:292
  314.7 11.7 %collective-permute-done.13 = bf16[4,48,1280]{2,1,0:T(8,128)(2,1)S(1)} collective-permute-done((bf16[4,48,1280]{2,1,0:T(8,128)(2,1)S(1)}, bf16[4,48,1280]{2,1,0:T(8,128)(2,1)S(1)}, u32[]{:S(2)}, u32[]{:S(2)}) %collective-permute-start.13) | collective-permute-done | bytes 491552 | tf_op jit(solution)/shard_map/ppermute | solution.py:166
  328.6 1.5 collective-permute-start.21
  330.1 19.7 %collective-permute-done.21 = f32[1152]{0:T(1024)S(1)} collective-permute-done((f32[1152]{0:T(1024)S(1)}, f32[1152]{0:T(1024)S(1)}, u32[]{:S(2)}, u32[]{:S(2)}) %collective-permute-start.21) | collective-permute-done | bytes 4640 | tf_op jit(solution)/shard_map/ppermute | solution.py:163
  351.0 2.5 collective-permute-done.22
  354.6 2.4 collective-permute-done.23
  359.2 1.5 collective-permute-done.25
  362.3 2.1 fusion.722
  365.7 1.8 collective-permute-start.18
  367.5 1.5 collective-permute-start.19
  369.0 1.6 fusion.113
  370.6 8.1 %collective-permute-done.17 = bf16[48,2432]{1,0:T(8,128)(2,1)S(1)} collective-permute-done((bf16[48,2432]{1,0:T(8,128)(2,1)S(1)}, bf16[48,2432]{1,0:T(8,128)(2,1)S(1)}, u32[]{:S(2)}, u32[]{:S(2)}) %collective-permute-start.17) | collective-permute-done | bytes 233504 | tf_op jit(solution)/shard_map/ppermute | solution.py:169
  378.7 2.5 collective-permute-done.18
  381.2 2.4 collective-permute-done.19
  (1149 shorter events, 152.1 us)
Async XLA Ops:
  5.1 17.7 %collective-permute-start.1 = (bf16[48,2432]{1,0:T(8,128)(2,1)S(1)}, bf16[48,2432]{1,0:T(8,128)(2,1)S(1)}, u32[]{:S(2)}, u32[]{:S(2)}) collective-permute-start(bf16[48,2432]{1,0:T(8,128)(2,1)S(1)} %concatenate.355), channel_id=1, source_target_pairs={{0,4},{2,6},{4,8},{6,10},{8,12},{10,14},{12,0},{14,2},{1,5},{3,7},... | collective-permute-start | bytes 700424 | tf_op jit(solution)/shard_map/ppermute | solution.py:169
  6.8 20.0 %collective-permute-start.2 = (bf16[48,2432]{1,0:T(8,128)(2,1)S(1)}, bf16[48,2432]{1,0:T(8,128)(2,1)S(1)}, u32[]{:S(2)}, u32[]{:S(2)}) collective-permute-start(bf16[48,2432]{1,0:T(8,128)(2,1)S(1)} %concatenate.355), channel_id=1, source_target_pairs={{0,8},{2,10},{4,12},{6,14},{8,0},{10,2},{12,4},{14,6},{1,9},{3,11}... | collective-permute-start | bytes 700424 | tf_op jit(solution)/shard_map/ppermute | solution.py:169
  7.9 20.7 %collective-permute-start.3 = (bf16[48,2432]{1,0:T(8,128)(2,1)S(1)}, bf16[48,2432]{1,0:T(8,128)(2,1)S(1)}, u32[]{:S(2)}, u32[]{:S(2)}) collective-permute-start(bf16[48,2432]{1,0:T(8,128)(2,1)S(1)} %concatenate.355), channel_id=1, source_target_pairs={{0,12},{2,14},{4,0},{6,2},{8,4},{10,6},{12,8},{14,10},{1,13},{3,15... | collective-permute-start | bytes 700424 | tf_op jit(solution)/shard_map/ppermute | solution.py:169
  30.1 22.8 %collective-permute-start.5 = (bf16[4,48,2432]{2,1,0:T(8,128)(2,1)}, bf16[4,48,2432]{2,1,0:T(8,128)(2,1)S(1)}, u32[]{:S(2)}, u32[]{:S(2)}) collective-permute-start(bf16[4,48,2432]{2,1,0:T(8,128)(2,1)} %fusion.112), channel_id=1, source_target_pairs={{0,16},{16,0},{1,17},{17,1},{2,18},{18,2},{3,19},{19,3},{4,20},{20... | collective-permute-start | bytes 2801672 | tf_op jit(solution)/shard_map/ppermute | solution.py:163
  31.6 23.0 %collective-permute-start.4 = (bf16[4,48,2432]{2,1,0:T(8,128)(2,1)}, bf16[4,48,2432]{2,1,0:T(8,128)(2,1)S(1)}, u32[]{:S(2)}, u32[]{:S(2)}) collective-permute-start(bf16[4,48,2432]{2,1,0:T(8,128)(2,1)} %fusion.112), channel_id=1, source_target_pairs={{0,2},{2,0},{4,6},{6,4},{8,10},{10,8},{12,14},{14,12},{1,3},{3,1},... | collective-permute-start | bytes 2801672 | tf_op jit(solution)/shard_map/ppermute | solution.py:166
  52.9 12.7 %collective-permute-start.7 = (bf16[4,48,1280]{2,1,0:T(8,128)(2,1)S(1)}, bf16[4,48,1280]{2,1,0:T(8,128)(2,1)S(1)}, u32[]{:S(2)}, u32[]{:S(2)}) collective-permute-start(bf16[4,48,1280]{2,1,0:T(8,128)(2,1)S(1)} %slice.707), channel_id=1, source_target_pairs={{0,2},{2,0},{4,6},{6,4},{8,10},{10,8},{12,14},{14,12},{1,3},{3,1},... | collective-permute-start | bytes 1474568 | tf_op jit(solution)/shard_map/ppermute | solution.py:166
  54.6 11.0 %collective-permute-start.6 = (bf16[4,48,1152]{2,1,0:T(8,128)(2,1)S(1)}, bf16[4,48,1152]{2,1,0:T(8,128)(2,1)S(1)}, u32[]{:S(2)}, u32[]{:S(2)}) collective-permute-start(bf16[4,48,1152]{2,1,0:T(8,128)(2,1)S(1)} %slice.706), channel_id=1, source_target_pairs={{0,16},{16,0},{1,17},{17,1},{2,18},{18,2},{3,19},{19,3},{4,20},{20... | collective-permute-start | bytes 1327112 | tf_op jit(solution)/shard_map/ppermute | solution.py:163
  68.2 19.5 %collective-permute-start.8 = (bf16[2,4,2,48,2432]{4,3,2,1,0:T(8,128)(2,1)}, bf16[2,4,2,48,2432]{4,3,2,1,0:T(8,128)(2,1)}, u32[]{:S(2)}, u32[]{:S(2)}) collective-permute-start(bf16[2,4,2,48,2432]{4,3,2,1,0:T(8,128)(2,1)} %maximum_select_fusion.2), channel_id=1, source_target_pairs={{0,1},{1,0},{2,3},{3,2},{4,5},{5,4},{6,7},{7,6},{8,9},{9,8},{10,11... | collective-permute-start | bytes 11206664 | tf_op jit(solution)/shard_map/ppermute | solution.py:160
  70.9 12.1 %collective-permute-start = (bf16[2,208,384]{2,1,0:T(8,128)(2,1)}, bf16[2,208,384]{2,1,0:T(8,128)(2,1)}, u32[]{:S(2)}, u32[]{:S(2)}) collective-permute-start(bf16[2,208,384]{2,1,0:T(8,128)(2,1)} %pad_maximum_fusion.22), channel_id=1, source_target_pairs={{2,0},{4,2},{6,4},{8,6},{10,8},{12,10},{14,12},{3,1},{5,3},{7,5},{... | collective-permute-start | bytes 958472 | tf_op jit(solution)/shard_map/ppermute | solution.py:191
  73.5 30.7 %copy-start.342 = (pred[208]{0:T(512)(128)(4,1)}, pred[208]{0:T(512)(128)(4,1)S(1)}, u32[]{:S(2)}) copy-start(pred[208]{0:T(512)(128)(4,1)S(1)} %iota_compare_fusion.1) | copy-start | bytes 628
  84.9 14.2 %copy-start.209 = (f32[416]{0:T(512)}, f32[416]{0:T(512)S(1)}, u32[]{:S(2)}) copy-start(f32[416]{0:T(512)S(1)} %broadcast_multiply_fusion.11) | copy-start | bytes 4996
  85.2 14.0 %copy-start.309 = (f32[416]{0:T(512)}, f32[416]{0:T(512)S(1)}, u32[]{:S(2)}) copy-start(f32[416]{0:T(512)S(1)} %add_rsqrt_fusion.3) | copy-start | bytes 4996
  100.8 12.3 %copy-start.25 = (f32[208,208]{0,1:T(8,128)}, f32[208,208]{0,1:T(8,128)S(1)}, u32[]{:S(2)}) copy-start(f32[208,208]{0,1:T(8,128)S(1)} %get-tuple-element.182) | copy-start | bytes 519172
  102.2 14.0 %copy-start.21 = (f32[208,208]{0,1:T(8,128)}, f32[208,208]{0,1:T(8,128)S(1)}, u32[]{:S(2)}) copy-start(f32[208,208]{0,1:T(8,128)S(1)} %get-tuple-element.178) | copy-start | bytes 519172
  103.0 14.7 %copy-start.19 = (f32[208,208]{0,1:T(8,128)}, f32[208,208]{0,1:T(8,128)S(1)}, u32[]{:S(2)}) copy-start(f32[208,208]{0,1:T(8,128)S(1)} %get-tuple-element.176) | copy-start | bytes 519172
  103.2 15.9 %copy-start.17 = (f32[208,208]{0,1:T(8,128)}, f32[208,208]{0,1:T(8,128)S(1)}, u32[]{:S(2)}) copy-start(f32[208,208]{0,1:T(8,128)S(1)} %get-tuple-element.174) | copy-start | bytes 519172
  103.2 15.9 %copy-start.220 = (f32[208]{0:T(256)}, f32[208]{0:T(256)S(1)}, u32[]{:S(2)}) copy-start(f32[208]{0:T(256)S(1)} %get-tuple-element.173) | copy-start | bytes 2500
  103.5 15.8 %copy-start.15 = (f32[208,208]{0,1:T(8,128)}, f32[208,208]{0,1:T(8,128)S(1)}, u32[]{:S(2)}) copy-start(f32[208,208]{0,1:T(8,128)S(1)} %get-tuple-element.172) | copy-start | bytes 519172
  103.5 15.8 %copy-start.218 = (f32[208]{0:T(256)}, f32[208]{0:T(256)S(1)}, u32[]{:S(2)}) copy-start(f32[208]{0:T(256)S(1)} %get-tuple-element.171) | copy-start | bytes 2500
  103.7 15.9 %copy-start.13 = (f32[208,208]{0,1:T(8,128)}, f32[208,208]{0,1:T(8,128)S(1)}, u32[]{:S(2)}) copy-start(f32[208,208]{0,1:T(8,128)S(1)} %get-tuple-element.170) | copy-start | bytes 519172
  103.7 15.9 %copy-start.216 = (f32[208]{0:T(256)}, f32[208]{0:T(256)S(1)}, u32[]{:S(2)}) copy-start(f32[208]{0:T(256)S(1)} %get-tuple-element.169) | copy-start | bytes 2500
  104.0 15.9 %copy-start.11 = (f32[208,208]{0,1:T(8,128)}, f32[208,208]{0,1:T(8,128)S(1)}, u32[]{:S(2)}) copy-start(f32[208,208]{0,1:T(8,128)S(1)} %get-tuple-element.168) | copy-start | bytes 519172
  104.0 15.9 %copy-start.214 = (f32[208]{0:T(256)}, f32[208]{0:T(256)S(1)}, u32[]{:S(2)}) copy-start(f32[208]{0:T(256)S(1)} %get-tuple-element.167) | copy-start | bytes 2500
  128.8 20.5 %copy-start.318 = (f32[416]{0:T(512)}, f32[416]{0:T(512)S(1)}, u32[]{:S(2)}) copy-start(f32[416]{0:T(512)S(1)} %add_rsqrt_fusion.1) | copy-start | bytes 4996
  130.6 12.5 %copy-start.106 = (bf16[416,384]{1,0:T(8,128)(2,1)}, bf16[416,384]{1,0:T(8,128)(2,1)S(1)}, u32[]{:S(2)}) copy-start(bf16[416,384]{1,0:T(8,128)(2,1)S(1)} %convolution_convert_fusion.10) | copy-start | bytes 958468
  132.9 12.8 %copy-start.49 = (f32[208,208]{0,1:T(8,128)}, f32[208,208]{0,1:T(8,128)S(1)}, u32[]{:S(2)}) copy-start(f32[208,208]{0,1:T(8,128)S(1)} %get-tuple-element.214) | copy-start | bytes 519172
  132.9 12.8 %copy-start.279 = (f32[208]{0:T(256)}, f32[208]{0:T(256)S(1)}, u32[]{:S(2)}) copy-start(f32[208]{0:T(256)S(1)} %get-tuple-element.213) | copy-start | bytes 2500
  133.9 13.7 %copy-start.275 = (f32[208]{0:T(256)}, f32[208]{0:T(256)S(1)}, u32[]{:S(2)}) copy-start(f32[208]{0:T(256)S(1)} %get-tuple-element.211) | copy-start | bytes 2500
  134.1 14.6 %copy-start.46 = (f32[208,208]{0,1:T(8,128)}, f32[208,208]{0,1:T(8,128)S(1)}, u32[]{:S(2)}) copy-start(f32[208,208]{0,1:T(8,128)S(1)} %get-tuple-element.210) | copy-start | bytes 519172
  134.1 14.6 %copy-start.271 = (f32[208]{0:T(256)}, f32[208]{0:T(256)S(1)}, u32[]{:S(2)}) copy-start(f32[208]{0:T(256)S(1)} %get-tuple-element.209) | copy-start | bytes 2500
  142.3 14.6 %copy-start.35 = (f32[208,208]{0,1:T(8,128)}, f32[208,208]{0,1:T(8,128)S(1)}, u32[]{:S(2)}) copy-start(f32[208,208]{0,1:T(8,128)S(1)} %get-tuple-element.198) | copy-start | bytes 519172
  143.1 15.1 %copy-start.33 = (f32[208,208]{0,1:T(8,128)}, f32[208,208]{0,1:T(8,128)S(1)}, u32[]{:S(2)}) copy-start(f32[208,208]{0,1:T(8,128)S(1)} %get-tuple-element.196) | copy-start | bytes 519172
  143.3 15.5 %copy-start.31 = (f32[208,208]{0,1:T(8,128)}, f32[208,208]{0,1:T(8,128)S(1)}, u32[]{:S(2)}) copy-start(f32[208,208]{0,1:T(8,128)S(1)} %get-tuple-element.194) | copy-start | bytes 519172
  143.3 15.5 %copy-start.256 = (f32[208]{0:T(256)}, f32[208]{0:T(256)S(1)}, u32[]{:S(2)}) copy-start(f32[208]{0:T(256)S(1)} %get-tuple-element.193) | copy-start | bytes 2500
  174.7 36.0 %copy-start.143 = (bf16[208,128]{1,0:T(8,128)(2,1)}, bf16[208,128]{1,0:T(8,128)(2,1)S(1)}, u32[]{:S(2)}) copy-start(bf16[208,128]{1,0:T(8,128)(2,1)S(1)} %fusion.94) | copy-start | bytes 159748
  174.9 35.8 %copy-start.145 = (bf16[208,128]{1,0:T(8,128)(2,1)}, bf16[208,128]{1,0:T(8,128)(2,1)S(1)}, u32[]{:S(2)}) copy-start(bf16[208,128]{1,0:T(8,128)(2,1)S(1)} %fusion.95) | copy-start | bytes 159748
  175.1 35.6 %copy-start.147 = (bf16[208,128]{1,0:T(8,128)(2,1)}, bf16[208,128]{1,0:T(8,128)(2,1)S(1)}, u32[]{:S(2)}) copy-start(bf16[208,128]{1,0:T(8,128)(2,1)S(1)} %fusion.96) | copy-start | bytes 159748
  175.3 35.4 %copy-start.149 = (bf16[208,128]{1,0:T(8,128)(2,1)}, bf16[208,128]{1,0:T(8,128)(2,1)S(1)}, u32[]{:S(2)}) copy-start(bf16[208,128]{1,0:T(8,128)(2,1)S(1)} %fusion.97) | copy-start | bytes 159748
  175.4 35.2 %copy-start.151 = (bf16[208,128]{1,0:T(8,128)(2,1)}, bf16[208,128]{1,0:T(8,128)(2,1)S(1)}, u32[]{:S(2)}) copy-start(bf16[208,128]{1,0:T(8,128)(2,1)S(1)} %fusion.98) | copy-start | bytes 159748
  175.7 35.0 %copy-start.153 = (bf16[208,128]{1,0:T(8,128)(2,1)}, bf16[208,128]{1,0:T(8,128)(2,1)S(1)}, u32[]{:S(2)}) copy-start(bf16[208,128]{1,0:T(8,128)(2,1)S(1)} %fusion.99) | copy-start | bytes 159748
  176.6 36.7 %copy-start.154 = (bf16[208,128]{1,0:T(8,128)(2,1)}, bf16[208,128]{1,0:T(8,128)(2,1)S(1)}, u32[]{:S(2)}) copy-start(bf16[208,128]{1,0:T(8,128)(2,1)S(1)} %fusion.75) | copy-start | bytes 159748
  177.5 35.8 %copy-start.155 = (bf16[208,128]{1,0:T(8,128)(2,1)}, bf16[208,128]{1,0:T(8,128)(2,1)S(1)}, u32[]{:S(2)}) copy-start(bf16[208,128]{1,0:T(8,128)(2,1)S(1)} %fusion.74) | copy-start | bytes 159748
  178.4 34.9 %copy-start.156 = (bf16[208,128]{1,0:T(8,128)(2,1)}, bf16[208,128]{1,0:T(8,128)(2,1)S(1)}, u32[]{:S(2)}) copy-start(bf16[208,128]{1,0:T(8,128)(2,1)S(1)} %fusion.73) | copy-start | bytes 159748
  179.2 34.1 %copy-start.157 = (bf16[208,128]{1,0:T(8,128)(2,1)}, bf16[208,128]{1,0:T(8,128)(2,1)S(1)}, u32[]{:S(2)}) copy-start(bf16[208,128]{1,0:T(8,128)(2,1)S(1)} %fusion.72) | copy-start | bytes 159748
  180.1 33.2 %copy-start.158 = (bf16[208,128]{1,0:T(8,128)(2,1)}, bf16[208,128]{1,0:T(8,128)(2,1)S(1)}, u32[]{:S(2)}) copy-start(bf16[208,128]{1,0:T(8,128)(2,1)S(1)} %fusion.71) | copy-start | bytes 159748
  180.9 32.4 %copy-start.159 = (bf16[208,128]{1,0:T(8,128)(2,1)}, bf16[208,128]{1,0:T(8,128)(2,1)S(1)}, u32[]{:S(2)}) copy-start(bf16[208,128]{1,0:T(8,128)(2,1)S(1)} %fusion.70) | copy-start | bytes 159748
  270.9 23.7 %collective-permute-start.12 = (bf16[2,4,2,48,2432]{4,3,2,1,0:T(8,128)(2,1)}, bf16[2,4,2,48,2432]{4,3,2,1,0:T(8,128)(2,1)}, u32[]{:S(2)}, u32[]{:S(2)}) collective-permute-start(bf16[2,4,2,48,2432]{4,3,2,1,0:T(8,128)(2,1)} %dynamic-slice_bitcast_fusion), channel_id=1, source_target_pairs={{0,1},{1,0},{2,3},{3,2},{4,5},{5,4},{6,7},{7,6},{8,9},{9,8},{10,11... | collective-permute-start | bytes 11206664 | tf_op jit(solution)/shard_map/ppermute | solution.py:160
  278.0 16.6 %slice-start = ((s8[7471104]{0:T(1024)(128)(4,1)}), s8[3276800]{0:T(1024)(128)(4,1)S(1)}, s32[]{:S(2)}) async-start(s8[7471104]{0:T(1024)(128)(4,1)} %bitcast.311), calls=%async_computation | async-start | bytes 6553600
  281.4 6.0 %collective-permute-start.9 = (bf16[4,720,384]{2,1,0:T(8,128)(2,1)}, bf16[4,720,384]{2,1,0:T(8,128)(2,1)}, u32[]{:S(2)}, u32[]{:S(2)}) collective-permute-start(bf16[4,720,384]{2,1,0:T(8,128)(2,1)} %pad_maximum_fusion), channel_id=1, source_target_pairs={{0,1},{1,0},{2,3},{3,2},{4,5},{5,4},{6,7},{7,6},{8,9},{9,8},{10,11... | collective-permute-start | bytes 6635528 | tf_op jit(solution)/shard_map/ppermute | solution.py:160
  290.4 19.1 %collective-permute-start.10 = (bf16[4,208,384]{2,1,0:T(8,128)(2,1)S(1)}, bf16[4,208,384]{2,1,0:T(8,128)(2,1)S(1)}, u32[]{:S(2)}, u32[]{:S(2)}) collective-permute-start(bf16[4,208,384]{2,1,0:T(8,128)(2,1)S(1)} %slice.806), channel_id=1, source_target_pairs={{0,2},{2,4},{4,6},{6,8},{8,10},{10,12},{12,14},{1,3},{3,5},{5,7},{... | collective-permute-start | bytes 1916936 | tf_op jit(solution)/shard_map/ppermute | solution.py:292
  299.5 14.1 %collective-permute-start.15 = (bf16[4,48,1152]{2,1,0:T(8,128)(2,1)S(1)}, bf16[4,48,1152]{2,1,0:T(8,128)(2,1)S(1)}, u32[]{:S(2)}, u32[]{:S(2)}) collective-permute-start(bf16[4,48,1152]{2,1,0:T(8,128)(2,1)S(1)} %slice.838), channel_id=1, source_target_pairs={{0,16},{16,0},{1,17},{17,1},{2,18},{18,2},{3,19},{19,3},{4,20},{20... | collective-permute-start | bytes 1327112 | tf_op jit(solution)/shard_map/ppermute | solution.py:163
  310.7 51.3 %collective-permute-start.11 = (bf16[2,512,384]{2,1,0:T(8,128)(2,1)}, bf16[2,512,384]{2,1,0:T(8,128)(2,1)S(1)}, u32[]{:S(2)}, u32[]{:S(2)}) collective-permute-start(bf16[2,512,384]{2,1,0:T(8,128)(2,1)} %get-tuple-element.116), channel_id=1, source_target_pairs={{0,16},{16,0},{1,17},{17,1},{2,18},{18,2},{3,19},{19,3},{4,20},{20... | collective-permute-start | bytes 2359304 | tf_op jit(solution)/shard_map/ppermute | solution.py:163
  312.2 14.2 %collective-permute-start.13 = (bf16[4,48,1280]{2,1,0:T(8,128)(2,1)S(1)}, bf16[4,48,1280]{2,1,0:T(8,128)(2,1)S(1)}, u32[]{:S(2)}, u32[]{:S(2)}) collective-permute-start(bf16[4,48,1280]{2,1,0:T(8,128)(2,1)S(1)} %slice.836), channel_id=1, source_target_pairs={{0,2},{2,0},{4,6},{6,4},{8,10},{10,8},{12,14},{14,12},{1,3},{3,1},... | collective-permute-start | bytes 1474568 | tf_op jit(solution)/shard_map/ppermute | solution.py:166
  313.8 48.5 %collective-permute-start.16 = (bf16[4,48,2432]{2,1,0:T(8,128)(2,1)S(1)}, bf16[4,48,2432]{2,1,0:T(8,128)(2,1)}, u32[]{:S(2)}, u32[]{:S(2)}) collective-permute-start(bf16[4,48,2432]{2,1,0:T(8,128)(2,1)S(1)} %pad_maximum_fusion.11), channel_id=1, source_target_pairs={{0,2},{2,0},{4,6},{6,4},{8,10},{10,8},{12,14},{14,12},{1,3},{3,1},... | collective-permute-start | bytes 2801672 | tf_op jit(solution)/shard_map/ppermute | solution.py:166
  326.6 35.7 %collective-permute-start.14 = (bf16[4,48,2432]{2,1,0:T(8,128)(2,1)S(1)}, bf16[4,48,2432]{2,1,0:T(8,128)(2,1)}, u32[]{:S(2)}, u32[]{:S(2)}) collective-permute-start(bf16[4,48,2432]{2,1,0:T(8,128)(2,1)S(1)} %pad_maximum_fusion.10), channel_id=1, source_target_pairs={{0,16},{16,0},{1,17},{17,1},{2,18},{18,2},{3,19},{19,3},{4,20},{20... | collective-permute-start | bytes 2801672 | tf_op jit(solution)/shard_map/ppermute | solution.py:163
  327.3 1.2 collective-permute-start.20
  328.6 21.2 %collective-permute-start.21 = (f32[1152]{0:T(1024)S(1)}, f32[1152]{0:T(1024)S(1)}, u32[]{:S(2)}, u32[]{:S(2)}) collective-permute-start(f32[1152]{0:T(1024)S(1)} %get-tuple-element.68), channel_id=1, source_target_pairs={{0,16},{16,0},{1,17},{17,1},{2,18},{18,2},{3,19},{19,3},{4,20},{20... | collective-permute-start | bytes 13832 | tf_op jit(solution)/shard_map/ppermute | solution.py:163
  349.8 3.7 collective-permute-start.22
  353.4 3.7 collective-permute-start.23
  354.6 4.5 %collective-permute-start.24 = (f32[1152]{0:T(1024)S(1)}, f32[1152]{0:T(1024)S(1)}, u32[]{:S(2)}, u32[]{:S(2)}) collective-permute-start(f32[1152]{0:T(1024)S(1)} %add.546), channel_id=1, source_target_pairs={{0,8},{2,10},{4,12},{6,14},{8,0},{10,2},{12,4},{14,6},{1,9},{3,11}... | collective-permute-start | bytes 13832 | tf_op jit(solution)/shard_map/ppermute | solution.py:169
  357.1 3.7 collective-permute-start.25
  364.5 14.2 %collective-permute-start.17 = (bf16[48,2432]{1,0:T(8,128)(2,1)S(1)}, bf16[48,2432]{1,0:T(8,128)(2,1)S(1)}, u32[]{:S(2)}, u32[]{:S(2)}) collective-permute-start(bf16[48,2432]{1,0:T(8,128)(2,1)S(1)} %get-tuple-element.125), channel_id=1, source_target_pairs={{0,4},{2,6},{4,8},{6,10},{8,12},{10,14},{12,0},{14,2},{1,5},{3,7},... | collective-permute-start | bytes 700424 | tf_op jit(solution)/shard_map/ppermute | solution.py:169
  365.7 15.4 %collective-permute-start.18 = (bf16[48,2432]{1,0:T(8,128)(2,1)S(1)}, bf16[48,2432]{1,0:T(8,128)(2,1)S(1)}, u32[]{:S(2)}, u32[]{:S(2)}) collective-permute-start(bf16[48,2432]{1,0:T(8,128)(2,1)S(1)} %get-tuple-element.127), channel_id=1, source_target_pairs={{0,8},{2,10},{4,12},{6,14},{8,0},{10,2},{12,4},{14,6},{1,9},{3,11}... | collective-permute-start | bytes 700424 | tf_op jit(solution)/shard_map/ppermute | solution.py:169
  367.5 16.0 %collective-permute-start.19 = (bf16[48,2432]{1,0:T(8,128)(2,1)S(1)}, bf16[48,2432]{1,0:T(8,128)(2,1)S(1)}, u32[]{:S(2)}, u32[]{:S(2)}) collective-permute-start(bf16[48,2432]{1,0:T(8,128)(2,1)S(1)} %get-tuple-element.126), channel_id=1, source_target_pairs={{0,12},{2,14},{4,0},{6,2},{8,4},{10,6},{12,8},{14,10},{1,13},{3,15... | collective-permute-start | bytes 700424 | tf_op jit(solution)/shard_map/ppermute | solution.py:169
  (312 other events, 961.3 us)

commit v2 on v1

v2 whole, which is shorter than its diff:
```python
import math

import jax
import jax.numpy as jnp
from jax import lax
from jax.experimental import pallas as pl
from jax.experimental.pallas import tpu as pltpu
from jax.sharding import PartitionSpec as P

IMG_LEN = 197
IMG_PAD = 208
HD = 64
EPSILON = 1e-06
NEGATIVE = -1e30
F32 = jnp.float32
BF16 = jnp.bfloat16
BLOCK = 128
HALF = 1280
SCALE = 1.0 / math.sqrt(HD)


def mm(a, b, dims):
    return lax.dot_general(a, b, (dims, ((), ())), preferred_element_type=F32)


def nn(a, b):
    return mm(a, b, ((1,), (0,)))


def nt(a, b):
    return mm(a, b, ((1,), (1,)))


def tn(a, b):
    return mm(a, b, ((0,), (0,)))


def normed(x):
    centred = x - jnp.mean(x, -1, keepdims=True)
    inverse = lax.rsqrt(jnp.mean(centred * centred, -1, keepdims=True) + EPSILON)
    return centred * inverse, inverse


def norm_back(grad, xhat, inverse, gain):
    t = grad * gain
    return inverse * (
        t - jnp.mean(t, -1, keepdims=True) - xhat * jnp.mean(t * xhat, -1, keepdims=True)
    )


def gelu_parts(u):
    cdf = 0.5 * (1.0 + lax.erf(u * math.sqrt(0.5)))
    pdf = jnp.exp(-0.5 * u * u) * (1.0 / math.sqrt(2.0 * math.pi))
    return u * cdf, cdf + u * pdf


ATT = 640
OUT = 512
MISC = 768
UP0 = 896
DOWN = 384
ROWSB = 1152
CHUNK = 384


def up_at(w, t, j):
    return w[t, 0, :, UP0:] if j == 0 else w[t, 1, :, :CHUNK]


def down_at(w, t, j):
    return w[t, 1, :, DOWN + j * CHUNK:DOWN + (j + 1) * CHUNK]


def low_lanes():
    return lax.broadcasted_iota(jnp.int32, (1, BLOCK), 1) < HD


def turn(a):
    return jnp.concatenate([a[:, HD:], a[:, :HD]], 1)


def valid_rows(sc, n):
    row = lax.broadcasted_iota(jnp.int32, (IMG_PAD, 1), 0)
    return jnp.where((row < IMG_LEN) & (n < sc[0]), 1.0, 0.0)


def image_rows(n):
    return pl.ds(pl.multiple_of(n * IMG_PAD, 16), IMG_PAD)


def forward_image(n, sc, x_ref, w, vec, brow, out_ref, kept):
    r = image_rows(n)
    x = x_ref[r, :].astype(F32)
    xhat, inv = normed(x)
    attn_in = (xhat * vec[0:1, :] + vec[2:3, :]).astype(BF16)
    kept["xh1"][r, :] = xhat
    kept["inv1"][r, :] = jnp.broadcast_to(inv, (IMG_PAD, BLOCK))
    kept["ain"][r, :] = attn_in
    residual = x + vec[3:4, :]
    low = low_lanes()
    lane = lax.broadcasted_iota(jnp.int32, (1, ATT), 1)
    factor = jnp.where(lane < 192, SCALE, jnp.where(lane < 576, 1.0, 0.0))
    real = lax.broadcasted_iota(jnp.int32, (1, IMG_PAD), 1) < IMG_LEN
    for t in range(2):
        bias = jnp.concatenate([brow[t, i:i + 1, :] for i in range(5)], 1)
        p = ((nn(attn_in, w[t, 0, :, :ATT]) + bias) * factor).astype(BF16)
        kept["qkv"][t, r, :] = p
        q, qk, k, v, vx = [p[:, i * BLOCK:(i + 1) * BLOCK] for i in range(5)]
        kq, xv = turn(qk), turn(vx)
        outs = []
        for i, (qq, kk, vv) in enumerate(
                [(jnp.where(low, q, 0), k, v), (jnp.where(low, 0, q), k, v), (jnp.where(low, qk, 0), kq, xv)]):
            s = jnp.where(real, nt(qq, kk), NEGATIVE)
            e = jnp.exp(s - jnp.max(s, -1, keepdims=True))
            pr = (e * (1.0 / jnp.sum(e, -1, keepdims=True))).astype(BF16)
            kept["pr"][n * 6 + t * 3 + i] = pr
            outs.append(nn(pr, vv))
        mixed = jnp.concatenate([outs[2], jnp.where(low, outs[0], outs[1])], 1).astype(BF16)
        kept["mx"][t, r, :] = mixed
        residual = residual + nt(mixed, w[t, 0, :, OUT:MISC])
    xhat, inv = normed(residual)
    mlp_in = (xhat * vec[1:2, :] + vec[4:5, :]).astype(BF16)
    kept["xh2"][r, :] = xhat
    kept["inv2"][r, :] = jnp.broadcast_to(inv, (IMG_PAD, BLOCK))
    kept["min"][r, :] = mlp_in
    out = residual + vec[5:6, :]
    for t in range(2):
        for j in range(2):
            bias = jnp.concatenate([brow[t, 5 + j * 3 + i:6 + j * 3 + i, :] for i in range(3)], 1)
            hidden, slope = gelu_parts(nn(mlp_in, up_at(w, t, j)) + bias)
            c = slice((t * 2 + j) * CHUNK, (t * 2 + j + 1) * CHUNK)
            hidden = hidden.astype(BF16)
            kept["hd"][r, c] = hidden
            kept["sl"][r, c] = slope.astype(BF16)
            out = out + nt(hidden, down_at(w, t, j))
    out_ref[r, :] = (out * valid_rows(sc, n)).astype(BF16)


def backward_image(n, sc, u_ref, w, vec, in_ref, kept, grad, sums, bsum):
    r = image_rows(n)

    def rsum(a):
        return jnp.sum(a, 0, keepdims=True)

    masked = u_ref[r, :].astype(F32) * valid_rows(sc, n)
    sums[5:6, :] += rsum(masked)
    dg = masked.astype(BF16)
    grad["dg"][r, :] = dg
    mg = jnp.zeros(masked.shape, F32)
    for t in range(2):
        for j in range(2):
            c = slice((t * 2 + j) * CHUNK, (t * 2 + j + 1) * CHUNK)
            up = nn(dg, down_at(w, t, j)) * kept["sl"][r, c].astype(F32)
            up = up.astype(BF16)
            grad["up"][r, c] = up
            total = rsum(up.astype(F32))
            for i in range(3):
                bsum[t, 5 + j * 3 + i:6 + j * 3 + i, :] += total[:, i * BLOCK:(i + 1) * BLOCK]
            mg = mg + nt(up, up_at(w, t, j))
    xhat = kept["xh2"][r, :]
    sums[4:5, :] += rsum(mg)
    sums[1:2, :] += rsum(mg * xhat)
    res = masked + norm_back(mg, xhat, kept["inv2"][r, :1], vec[1:2, :])
    sums[3:4, :] += rsum(res)
    ag = res.astype(BF16)
    grad["ag"][r, :] = ag
    low = low_lanes()
    ig = jnp.zeros(masked.shape, F32)
    for t in range(2):
        xg = nn(ag, w[t, 0, :, OUT:MISC]).astype(BF16)
        gx = jnp.where(low, 0, xg[:, :BLOCK])
        g = xg[:, BLOCK:]
        p = kept["qkv"][t, r, :]
        q, qk, k, v, vx = [p[:, i * BLOCK:(i + 1) * BLOCK] for i in range(5)]
        kq, xv = turn(qk), turn(vx)
        dq, dk, dv = [], [], []
        for i, (qq, kk, vv, gm, gg) in enumerate(
                [(q, k, v, jnp.where(low, g, 0), g), (q, k, v, jnp.where(low, 0, g), g), (qk, kq, xv, gx, turn(gx))]):
            pb = kept["pr"][n * 6 + t * 3 + i]
            pf = pb.astype(F32)
            dp = nt(gm, vv)
            ds = (pf * (dp - jnp.sum(pf * dp, -1, keepdims=True))).astype(BF16)
            dv.append(tn(pb, gg))
            dq.append(nn(ds, kk) * SCALE)
            dk.append(tn(ds, kq if i == 2 else qq))
        blocks = [
            jnp.where(low, dq[0], dq[1]), jnp.where(low, dq[2], dk[2]), jnp.where(low, dk[0], dk[1]),
            jnp.where(low, dv[0], dv[1]), dv[2],
        ]
        d = jnp.concatenate(blocks, 1).astype(BF16)
        grad["qkv"][t, r, :] = d
        total = rsum(d.astype(F32))
        for i in range(5):
            bsum[t, i:i + 1, :] += total[:, i * BLOCK:(i + 1) * BLOCK]
        ig = ig + nt(d, w[t, 0, :, :ATT])
    xhat = kept["xh1"][r, :]
    sums[2:3, :] += rsum(ig)
    sums[0:1, :] += rsum(ig * xhat)
    in_ref[r, :] = res + norm_back(ig, xhat, kept["inv1"][r, :1], vec[0:1, :])


def weight_grads(t, piece, kept, grad, small, bsum, g):
    width = small.shape[0]
    ag, dg = grad["ag"][...], grad["dg"][...]
    ain, mlp_in = kept["ain"][...], kept["min"][...]
    high = jnp.where(low_lanes(), 0.0, 1.0)
    d = grad["qkv"][t]
    g[t, 0, :, :OUT] = tn(ain, d[:, :OUT]).astype(BF16)
    out = tn(ag, kept["mx"][t])
    g[t, 0, :, OUT:ATT] = (tn(ain, d[:, OUT:]) + out[:, :BLOCK] * high).astype(BF16)
    g[t, 0, :, ATT:MISC] = out[:, BLOCK:].astype(BF16)
    g[t, 0, :, MISC:UP0] = small
    for j in range(2):
        c = pl.ds(pl.multiple_of((t * 2 + j) * CHUNK, BLOCK), CHUNK)
        up = tn(mlp_in, grad["up"][:, c]).astype(BF16)
        if j == 0:
            g[t, 0, :, UP0:] = up
        else:
            g[t, 1, :, :CHUNK] = up
        g[t, 1, :, DOWN + j * CHUNK:DOWN + (j + 1) * CHUNK] = tn(dg, kept["hd"][:, c]).astype(BF16)
    if piece % 16 == 0:
        rows = jnp.concatenate([bsum[t], jnp.zeros((piece - 16, BLOCK), F32)], 0).astype(BF16)
        for i in range(width // piece):
            g[t, 1, i * piece:(i + 1) * piece, ROWSB:] = rows


KEPT = ("xh1", "inv1", "ain", "qkv", "pr", "mx", "xh2", "inv2", "min", "sl", "hd")


def kept_shapes(total, width, ff):
    images = total // IMG_PAD
    return dict(
        xh1=((total, width), F32), inv1=((total, BLOCK), F32), ain=((total, width), BF16), qkv=((2, total, ATT), BF16),
        pr=((images * 6, IMG_PAD, IMG_PAD), BF16), mx=((2, total, 2 * BLOCK), BF16), xh2=((total, width), F32),
        inv2=((total, BLOCK), F32), min=((total, width), BF16), sl=((total, ff), BF16), hd=((total, ff), BF16))


def grad_shapes(total, width, ff):
    return dict(dg=((total, width), BF16), up=((total, ff), BF16), ag=((total, width), BF16),
                qkv=((2, total, ATT), BF16))


def layer_call(sources, load, store, out_shapes, scalars, x, u, kept_in, ff, piece):
    forward, backward = x is not None, u is not None
    total, width = (x if forward else u).shape
    ks = kept_shapes(total, width, ff)
    gs = grad_shapes(total, width, ff)
    vmem = pl.BlockSpec(memory_space=pltpu.VMEM)
    anywhere = pl.BlockSpec(memory_space=pl.ANY)
    ins, in_specs = [scalars], [pl.BlockSpec(memory_space=pltpu.SMEM)]
    outs, out_specs = [], []
    keep_out = forward and not backward
    keep_in = backward and not forward
    for a in (x, u):
        if a is not None:
            ins.append(a)
            in_specs.append(vmem)
    if keep_in:
        ins += [kept_in[k] for k in KEPT]
        in_specs += [vmem] * len(KEPT)
    ins += sources
    in_specs += [anywhere] * len(sources)
    if forward:
        outs.append(((total, width), BF16))
        out_specs.append(vmem)
    if backward:
        outs += [((total, width), F32), ((2, 16, BLOCK), F32)] + out_shapes
        out_specs += [vmem, vmem] + [anywhere] * len(out_shapes)
    if keep_out:
        outs += [ks[k] for k in KEPT]
        out_specs += [vmem] * len(KEPT)
    scratch = [pltpu.VMEM((2, 2, width, HALF), BF16), pltpu.VMEM((8, width), F32), pltpu.VMEM((2, 16, BLOCK), F32),
               pltpu.SemaphoreType.DMA]
    if backward:
        scratch += [pltpu.VMEM(*gs[k]) for k in gs]
        scratch += [pltpu.VMEM((8, width), F32), pltpu.VMEM((2, 2, width, HALF), BF16)]
    if forward and backward:
        scratch += [pltpu.VMEM(*ks[k]) for k in KEPT]

    def body(*refs):
        refs = list(refs)

        def take(n):
            got = refs[:n]
            del refs[:n]
            return got

        sc = take(1)[0]
        x_ref = take(1)[0] if forward else None
        u_ref = take(1)[0] if backward else None
        if keep_in:
            kept = dict(zip(KEPT, take(len(KEPT))))
        src = take(len(sources))
        if forward:
            out_ref = take(1)[0]
        if backward:
            in_ref, bsum = take(2)
            dst = take(len(out_shapes))
        if keep_out:
            kept = dict(zip(KEPT, take(len(KEPT))))
        w, vec, brow, sem = take(4)
        if backward:
            grad = dict(zip(gs, take(len(gs))))
            sums, g = take(2)
        if forward and backward:
            kept = dict(zip(KEPT, take(len(KEPT))))
        copies = load(sc, src, w, sem)
        for c in copies:
            c.start()
        for c in copies:
            c.wait()
        vec[...] = w[0, 0, :, MISC:UP0].astype(F32).T[:8, :]
        for t in range(2):
            brow[t] = w[t, 1, :16, ROWSB:].astype(F32)
        if forward:
            def step(n, carry):
                forward_image(n, sc, x_ref, w, vec, brow, out_ref, kept)
                return carry
            lax.fori_loop(0, total // IMG_PAD, step, 0)
        if backward:
            sums[...] = jnp.zeros_like(sums)
            bsum[...] = jnp.zeros_like(bsum)

            def back(n, carry):
                backward_image(n, sc, u_ref, w, vec, in_ref, kept, grad, sums, bsum)
                return carry
            lax.fori_loop(0, total // IMG_PAD, back, 0)
            small = jnp.concatenate([sums[...], jnp.zeros((BLOCK - 8, width), F32)], 0).T.astype(BF16)
            copies = []
            for side in range(2):
                t = jnp.where(sc[1] == 0, 1 - side, side)
                weight_grads(t, piece, kept, grad, small, bsum, g)
                out = store(sc, side, t, g, dst, sem)
                for c in out:
                    c.start()
                copies += out
            for c in copies:
                c.wait()

    got = pl.pallas_call(
        body,
        out_shape=[jax.ShapeDtypeStruct(*o) for o in outs],
        in_specs=in_specs,
        out_specs=out_specs,
        scratch_shapes=scratch,
        compiler_params=pltpu.CompilerParams(vmem_limit_bytes=56 * 2 ** 20),
    )(*ins)
    got = list(got)
    res = {}
    if forward:
        res["out"] = got.pop(0)
    if backward:
        res["in"], res["bias"] = got[:2]
        res["g"] = got[2:2 + len(out_shapes)]
        del got[:2 + len(out_shapes)]
    if keep_out:
        res["kept"] = dict(zip(KEPT, got))
    return res


def shards(tokens, image_counts, cotangent, norm_gains, row_biases, qkv_weight, qv_bias, out_weight,
           up_weight, up_bias, down_weight):
    sec = lax.axis_index("section")
    dp = lax.axis_index("dp")
    ten = lax.axis_index("tensor")
    n_dp = lax.axis_size("dp")
    m = n_dp // 2
    zi, yi = dp // 2, dp % 2
    local_rows, width = tokens.shape[1:]
    images = local_rows * n_dp // IMG_LEN
    piece = width // n_dp
    ff = 2 * up_weight.shape[2]
    direct = piece % 16 == 0

    def pt(a):
        return lax.ppermute(a, "tensor", [(0, 1), (1, 0)])

    def px(a):
        return lax.ppermute(a, "section", [(0, 1), (1, 0)])

    def py(a):
        return lax.ppermute(a, "dp", [(i, i ^ 1) for i in range(n_dp)])

    def pd(a):
        return lax.ppermute(a, ("section", "dp"), [(i, (i + n_dp) % (2 * n_dp) ^ 1) for i in range(2 * n_dp)])

    def pz(a, k):
        return lax.ppermute(a, "dp", [(2 * z + y, 2 * ((z + k) % m) + y) for z in range(m) for y in range(2)])

    def plus(*a):
        return sum(b.astype(F32) for b in a)

    batch_tokens = lax.dynamic_index_in_dim(tokens, sec, 0, keepdims=False)
    batch_cot = lax.dynamic_index_in_dim(cotangent, sec, 0, keepdims=False)
    count = lax.dynamic_index_in_dim(image_counts, sec, 0, keepdims=False)
    first = jnp.minimum((dp * local_rows + IMG_LEN - 1) // IMG_LEN, images)
    last = jnp.minimum(((dp + 1) * local_rows + IMG_LEN - 1) // IMG_LEN, images)
    held = last - first
    slots = -(-(-(-local_rows // IMG_LEN)) // 2)
    lower = held // 2
    own_first = jnp.where(ten == 0, first, first + lower)
    own_count = jnp.where(ten == 0, lower, held - lower)
    total = slots * IMG_PAD
    row = lax.broadcasted_iota(jnp.int32, (total, 1), 0)
    slot, inside = row // IMG_PAD, row % IMG_PAD
    exists = (inside < IMG_LEN) & (slot < own_count)
    target = (own_first + slot) * IMG_LEN + inside - dp * local_rows
    canvas_rows = local_rows + IMG_PAD
    select = ((lax.broadcasted_iota(jnp.int32, (total, canvas_rows), 1) == target) & exists).astype(BF16)
    scalars = jnp.stack([jnp.minimum(own_count, jnp.maximum(count - own_first, 0)), ten, sec, zi, yi]).astype(jnp.int32)

    both = jnp.stack([batch_tokens, batch_cot])
    halo = lax.ppermute(both[:, :IMG_PAD], "dp", [(i + 1, i) for i in range(n_dp - 1)])
    both = jnp.concatenate([both, halo], 1)
    x0 = nn(select, both[0]).astype(BF16)
    cot = nn(select, both[1]).astype(BF16)

    q, k, v = [[qkv_weight[0, :, i, h * HD:(h + 1) * HD] for h in range(3)] for i in range(3)]
    o = out_weight[0].T
    o = [o[:, h * HD:(h + 1) * HD] for h in range(3)]
    misc = jnp.concatenate([norm_gains[0], row_biases[0]], 0).T
    misc = jnp.pad(misc, ((0, 0), (0, BLOCK - misc.shape[1])))
    gap = jnp.zeros((HD,), BF16)
    rows = jnp.concatenate([qv_bias[0, 0], gap, gap, gap, qv_bias[0, 1], gap, up_bias[0]]).reshape(-1, BLOCK)
    rows = jnp.pad(rows, ((0, piece - rows.shape[0]), (0, 0)))
    up, down = up_weight[0], down_weight[0].T
    part0 = jnp.concatenate(
        [q[0], q[1], q[2], k[2], k[0], k[1], v[0], v[1], v[2], o[2], o[0], o[1], misc, up[:, :CHUNK]], 1)
    part1 = jnp.concatenate([up[:, CHUNK:], down, rows], 1)

    if direct:
        keep = jnp.where(sec == 0, part0, part1)
        give = jnp.where(sec == 0, part1, part0)
        got = px(give)
        start = [jnp.where(sec == 0, keep, got), jnp.where(sec == 0, got, keep)]
        half = HALF // 2

        def load(sc, src, w, sem):
            copies = []
            for side in range(2):
                t = jnp.where(sc[1] == 0, side, 1 - side)
                quad, qx, qy, qd0, qd1 = src[side * 5:side * 5 + 5]
                for kk in range(m):
                    z = lax.rem(sc[3] - kk + m, m)
                    near = pl.ds(pl.multiple_of((2 * z + sc[4]) * piece, 16), piece)
                    far = pl.ds(pl.multiple_of((2 * z + 1 - sc[4]) * piece, 16), piece)
                    for a, h, r, c in (
                            (quad, sc[2], near, slice(0, HALF)), (qx, 1 - sc[2], near, slice(0, HALF)),
                            (qy, sc[2], far, slice(0, HALF)), (qd0, 1 - sc[2], far, slice(0, half)),
                            (qd1, 1 - sc[2], far, slice(half, HALF))):
                        copies.append(pltpu.make_async_copy(a.at[kk], w.at[t, h, r, c], sem))
            return copies

        def store(sc, side, t, g, dst, sem):
            copies = []
            for hr in range(2):
                h = jnp.where(sc[2] == 0, hr, 1 - hr)
                for yr in range(2):
                    y = jnp.where(sc[4] == 0, yr, 1 - yr)
                    for kk in range(m):
                        z = lax.rem(sc[3] + kk, m)
                        r = pl.ds(pl.multiple_of((2 * z + y) * piece, 16), piece)
                        out = dst[0].at[hr, yr, kk] if side == 0 else dst[1 + hr * 2 + yr].at[kk]
                        copies.append(pltpu.make_async_copy(g.at[t, h, r, :], out, sem))
            return copies

        out_shapes = [((2, 2, m, piece, HALF), BF16)] + [((m, piece, HALF), BF16)] * 4

        def spread(a):
            quad = jnp.stack([a] + [pz(a, kk) for kk in range(1, m)])
            qx, qy = px(quad), py(quad)
            qd0, qd1 = px(qy[..., :half]), py(qx[..., half:])
            mine = [quad, qx, qy, qd0, qd1]
            return mine + [pt(b) for b in mine]

        sources = [spread(a) for a in start]
    else:
        def load(sc, src, w, sem):
            return [pltpu.make_async_copy(src[0], w, sem)]

        def store(sc, side, t, g, dst, sem):
            return [pltpu.make_async_copy(g.at[t], dst[0].at[t], sem)]

        out_shapes = [((2, 2, width, HALF), BF16)]
        a = lax.all_gather(jnp.stack([part0, part1]), "dp", axis=1, tiled=True)
        a = lax.all_gather(lax.all_gather(a, "tensor"), "section")
        sources = [[a[0]], [a[1]]]

    def call(l, x, u, kept):
        return layer_call(sources[l], load, store, out_shapes, scalars, x, u, kept, ff, piece)

    r0 = call(0, x0, None, None)
    r1 = call(1, r0["out"], cot, None)
    b0 = call(0, None, r1["in"], r0["kept"])

    if direct:
        def gather_in(g):
            theirs, keep, to_y, to_x, to_d = g
            got = pt(theirs)
            to_y = plus(to_y, got[0, 1]).astype(BF16)
            to_x = plus(to_x, got[1, 0]).astype(BF16)
            to_d = plus(to_d, got[1, 1]).astype(BF16)
            quad = plus(keep, got[0, 0], py(to_y), px(to_x), pd(to_d))
            low = quad.astype(BF16)
            return plus(quad[0], *[pz(low[kk], kk) for kk in range(1, m)])

        done = [gather_in(r1["g"]), gather_in(b0["g"])]
        mine = jnp.where(sec == 0, done[1], done[0])
        other = px(jnp.where(sec == 0, done[0], done[1]).astype(BF16)).astype(F32)
        final0 = jnp.where(sec == 0, mine, other)
        final1 = jnp.where(sec == 0, other, mine)
        small = final1[:, ROWSB:]
    else:
        g = jnp.stack([b0["g"][0], r1["g"][0]])
        g = lax.psum_scatter(g.astype(F32), "section", scatter_dimension=0)
        g = lax.psum_scatter(g, "tensor", scatter_dimension=0)
        g = lax.psum_scatter(g, "dp", scatter_dimension=1, tiled=True)
        final0, final1 = g[0], g[1]
        small = lax.psum(jnp.stack([b0["bias"], r1["bias"]]), ("section", "tensor", "dp"))
        small = lax.dynamic_index_in_dim(lax.dynamic_index_in_dim(small, sec, 0, False), ten, 0, False)

    def settled(a0, a1):
        keep = jnp.where(sec == 0, a0, a1)
        got = px(jnp.where(sec == 0, a1, a0))
        a = jnp.where(sec == 0, jnp.stack([keep, got]), jnp.stack([got, keep]))
        a = jnp.stack([tn(select, a[0]), tn(select, a[1])]).astype(BF16)
        a = a + pt(a)
        spill = lax.ppermute(a[:, local_rows:], "dp", [(i, i + 1) for i in range(n_dp - 1)])
        return jnp.concatenate([a[:, :IMG_PAD] + spill, a[:, IMG_PAD:local_rows]], 1)

    layer_outputs = settled(r0["out"], r1["out"])[None]
    input_grads = settled(b0["in"].astype(BF16), r1["in"].astype(BF16)).astype(F32)[None]

    def heads(*starts):
        return [final0[:, s * HD:(s + 1) * HD] for s in starts]

    small = small.reshape(-1)
    qkv = jnp.concatenate(heads(0, 1, 2, 4, 5, 3, 6, 7, 8), 1).reshape(1, piece, 3, 3 * HD)
    return (
        layer_outputs,
        input_grads,
        final0[:, MISC:MISC + 2].T[None],
        final0[:, MISC + 2:MISC + 6].T[None],
        qkv,
        jnp.stack([small[:3 * HD], small[6 * HD:9 * HD]])[None],
        jnp.concatenate(heads(10, 11, 9), 1).T[None],
        jnp.concatenate([final0[:, UP0:], final1[:, :DOWN]], 1)[None],
        small[ATT:ATT + ff // 2][None],
        final1[:, DOWN:ROWSB].T[None],
    )


def solution(mesh):
    in_specs = (
        P(None, "dp", None),
        P(),
        P(None, "dp", None),
        P("section", None, "dp"),
        P("section", None, "dp"),
        P("section", "dp", None, "tensor"),
        P("section", None, "tensor"),
        P("section", "tensor", "dp"),
        P("section", "dp", "tensor"),
        P("section", "tensor"),
        P("section", "tensor", "dp"),
    )
    out_specs = (
        P("section", None, "dp", None),
        P("section", None, "dp", None),
        P("section", None, "dp"),
        P("section", None, "dp"),
        P("section", "dp", None, "tensor"),
        P("section", None, "tensor"),
        P("section", "tensor", "dp"),
        P("section", "dp", "tensor"),
        P("section", "tensor"),
        P("section", "tensor", "dp"),
    )
    return jax.shard_map(shards, mesh=mesh, in_specs=in_specs, out_specs=out_specs, check_vma=False)
```

time: 394 us -> 248 us (0.63)
  the two profiles are of different devices: /device:TPU:8 before, /device:TPU:0 now
where the time goes in v2:
time: 248 us; the launch traced here: 247 us
  waiting for transfers between devices  79.3 us (32%)
  starting transfers between devices  73.8 us (30%)
  Pallas kernels  56.4 us (23%)
  local copies, waits for them, and re-layouts  17.2 us (7%)
  other arithmetic  12.3 us (5%)
  matrix products  5.81 us (2%)
    pallas_call x3, Pallas kernels, layer_call(): pl.pallas_call(body, out_shape=[jax.ShapeDtypeStruct(*o) for o in outs],...  56.4 us
    ppermute x6, waiting for transfers between devices, py(): return lax.ppermute(a, 'dp', [(i, i ^ 1) for i in range(n_dp)])  26.4 us
    ppermute x10, waiting for transfers between devices, px(): return lax.ppermute(a, 'section', [(0, 1), (1, 0)])  22.1 us
    ppermute x12, starting transfers between devices, pz(): lax.ppermute(a, 'dp', [(2 * z + y, 2 * ((z + k) % m) + y) for z in range(...  21.7 us
    ppermute x12, waiting for transfers between devices, pz(): lax.ppermute(a, 'dp', [(2 * z + y, 2 * ((z + k) % m) + y) for z in range(...  13.9 us
    ppermute x10, starting transfers between devices, px(): return lax.ppermute(a, 'section', [(0, 1), (1, 0)])  13.2 us
    ppermute x6, starting transfers between devices, py(): return lax.ppermute(a, 'dp', [(i, i ^ 1) for i in range(n_dp)])  12.8 us
    ppermute x2, starting transfers between devices, settled(): lax.ppermute(a[:, local_rows:], 'dp', [(i, i + 1) for i in range(n_dp - 1)])  12 us
  transfers between devices with their start and end apart: 47, of which 19 were waited for; matrix products, arithmetic and copies ran while one was open for 8% of the time, Pallas kernels for 5%

profile of v2, /device:TPU:0, one launch (start us, length us, event | category | flops | bytes accessed | tf_op | source)
XLA Modules:
  0.0 247.0 jit_solution(13466622428682734643)
XLA Ops:
  2.1 0.9 slice_bitcast_fusion.33
  3.0 0.8 fusion.78
  4.6 0.8 slice_reduce_fusion
  6.4 0.9 broadcast_select_fusion.5
  7.3 3.0 %collective-permute-start.1 = (bf16[48,1280]{1,0:T(8,128)(2,1)S(1)}, bf16[48,1280]{1,0:T(8,128)(2,1)S(1)}, u32[]{:S(2)}, u32[]{:S(2)}) collective-permute-start(bf16[48,1280]{1,0:T(8,128)(2,1)S(1)} %broadcast_select_fusion.5), channel_id=1, source_target_pairs={{0,16},{16,0},{1,17},{17,1},{2,18},{18,2},{3,19},{19,3},{4,20},{20... | collective-permute-start | bytes 368648 | tf_op jit(solution)/shard_map/ppermute | solution.py:379
  10.3 3.3 %collective-permute-done.1 = bf16[48,1280]{1,0:T(8,128)(2,1)S(1)} collective-permute-done((bf16[48,1280]{1,0:T(8,128)(2,1)S(1)}, bf16[48,1280]{1,0:T(8,128)(2,1)S(1)}, u32[]{:S(2)}, u32[]{:S(2)}) %collective-permute-start.1) | collective-permute-done | bytes 122912 | tf_op jit(solution)/shard_map/ppermute | solution.py:379
  13.7 1.9 collective-permute-start.2
  15.6 2.6 %collective-permute-start.3 = (bf16[48,1280]{1,0:T(8,128)(2,1)S(1)}, bf16[48,1280]{1,0:T(8,128)(2,1)S(1)}, u32[]{:S(2)}, u32[]{:S(2)}) collective-permute-start(bf16[48,1280]{1,0:T(8,128)(2,1)S(1)} %get-tuple-element.118), channel_id=1, source_target_pairs={{0,8},{2,10},{4,12},{6,14},{8,0},{10,2},{12,4},{14,6},{1,9},{3,11}... | collective-permute-start | bytes 368648 | tf_op jit(solution)/shard_map/ppermute | solution.py:388
  18.2 1.3 collective-permute-start.4
  20.5 1.4 collective-permute-done.2
  21.9 3.2 %collective-permute-start.16 = (bf16[48,1280]{1,0:T(8,128)(2,1)S(1)}, bf16[48,1280]{1,0:T(8,128)(2,1)S(1)}, u32[]{:S(2)}, u32[]{:S(2)}) collective-permute-start(bf16[48,1280]{1,0:T(8,128)(2,1)S(1)} %get-tuple-element.117), channel_id=1, source_target_pairs={{0,12},{2,14},{4,0},{6,2},{8,4},{10,6},{12,8},{14,10},{1,13},{3,15... | collective-permute-start | bytes 368648 | tf_op jit(solution)/shard_map/ppermute | solution.py:388
  25.1 3.9 %collective-permute-done.3 = bf16[48,1280]{1,0:T(8,128)(2,1)S(1)} collective-permute-done((bf16[48,1280]{1,0:T(8,128)(2,1)S(1)}, bf16[48,1280]{1,0:T(8,128)(2,1)S(1)}, u32[]{:S(2)}, u32[]{:S(2)}) %collective-permute-start.3) | collective-permute-done | bytes 122912 | tf_op jit(solution)/shard_map/ppermute | solution.py:388
  29.1 1.5 collective-permute-start.6
  30.6 1.5 collective-permute-start.5
  32.1 3.9 %collective-permute-done.15 = bf16[48,1280]{1,0:T(8,128)(2,1)S(1)} collective-permute-done((bf16[48,1280]{1,0:T(8,128)(2,1)S(1)}, bf16[48,1280]{1,0:T(8,128)(2,1)S(1)}, u32[]{:S(2)}, u32[]{:S(2)}) %collective-permute-start.15) | collective-permute-done | bytes 122912 | tf_op jit(solution)/shard_map/ppermute | solution.py:388
  36.0 1.6 collective-permute-start.18
  37.7 1.5 collective-permute-start.17
  39.2 1.2 constant_dynamic-slice_fusion
  40.4 0.8 pad_maximum_fusion.5
  41.9 1.3 collective-permute-start
  43.9 1.9 collective-permute-start.7
  46.5 10.4 %collective-permute-done.18.refs_5_ = bf16[4,48,1280]{2,1,0:T(8,128)(2,1)} collective-permute-done((bf16[4,48,1280]{2,1,0:T(8,128)(2,1)S(1)}, bf16[4,48,1280]{2,1,0:T(8,128)(2,1)}, u32[]{:S(2)}, u32[]{:S(2)}) %collective-permute-start.18) | collective-permute-done | bytes 491552 | tf_op jit(solution)/shard_map/ppermute | solution.py:382
  56.9 2.6 %collective-permute-start.8 = (bf16[4,48,640]{2,1,0:T(8,128)(2,1)}, bf16[4,48,640]{2,1,0:T(8,128)(2,1)}, u32[]{:S(2)}, u32[]{:S(2)}) collective-permute-start(bf16[4,48,640]{2,1,0:T(8,128)(2,1)} %slice.272), channel_id=1, source_target_pairs={{0,2},{2,0},{4,6},{6,4},{8,10},{10,8},{12,14},{14,12},{1,3},{3,1},... | collective-permute-start | bytes 737288 | tf_op jit(solution)/shard_map/ppermute | solution.py:382
  59.5 1.7 slice.274
  61.2 1.5 collective-permute-start.19
  64.5 1.0 slice.275
  66.3 1.4 collective-permute-done.19.refs_6_
  67.7 1.1 pad_maximum_fusion
  68.8 3.0 %collective-permute-done.20.refs_7_ = bf16[4,48,640]{2,1,0:T(8,128)(2,1)S(1)} collective-permute-done((bf16[4,48,640]{2,1,0:T(8,128)(2,1)S(1)}, bf16[4,48,640]{2,1,0:T(8,128)(2,1)S(1)}, u32[]{:S(2)}, u32[]{:S(2)}) %collective-permute-start.20) | collective-permute-done | bytes 245792 | tf_op jit(solution)/shard_map/ppermute | solution.py:382
  72.4 1.3 fusion.21.refs_1_
  74.2 1.3 fusion.24.refs_2_
  75.5 12.9 %shard_map.186 = (bf16[416,384]{1,0:T(8,128)(2,1)}, f32[416,384]{1,0:T(8,128)}, f32[416,128]{1,0:T(8,128)}, bf16[416,384]{1,0:T(8,128)(2,1)}, bf16[2,416,640]{2,...) custom-call(s32[5]{0:T(128)} %stack.119.refs_0_, ...), custom_call_target="tpu_custom_call" | custom-call | tf_op jit(solution)/shard_map/pallas_call | solution.py:340
  89.7 24.4 %shard_map.187 = (bf16[416,384]{1,0:T(8,128)(2,1)}, f32[416,384]{1,0:T(8,128)}, f32[2,16,128]{2,1,0:T(8,128)}, bf16[2,2,4,48,1280]{4,3,2,1,0:T(8,128)(2,1)}, bf1...) custom-call(s32[5]{0:T(128)} %stack.119.refs_0_, ...), custom_call_target="tpu_custom_call" | custom-call | tf_op jit(solution)/shard_map/pallas_call | solution.py:340
  114.1 19.1 %shard_map.188 = (f32[416,384]{1,0:T(8,128)}, f32[2,16,128]{2,1,0:T(8,128)}, bf16[2,2,4,48,1280]{4,3,2,1,0:T(8,128)(2,1)}, bf16[4,48,1280]{2,1,0:T(8,128)(2,1)},...) custom-call(s32[5]{0:T(128)} %stack.119.refs_0_, ...), custom_call_target="tpu_custom_call" | custom-call | tf_op jit(solution)/shard_map/pallas_call | solution.py:340
  133.3 1.2 select_bitcast_fusion
  135.2 1.6 collective-permute-start.26
  136.7 8.2 %collective-permute-done.29 = bf16[416,384]{1,0:T(8,128)(2,1)S(1)} collective-permute-done((bf16[416,384]{1,0:T(8,128)(2,1)S(1)}, bf16[416,384]{1,0:T(8,128)(2,1)S(1)}, u32[]{:S(2)}, u32[]{:S(2)}) %collective-permute-start.29) | collective-permute-done | bytes 319520 | tf_op jit(solution)/shard_map/ppermute | solution.py:379
  145.1 0.8 fusion.15
  145.9 0.8 fusion.18
  147.0 4.3 %collective-permute-done.26 = bf16[416,384]{1,0:T(8,128)(2,1)S(1)} collective-permute-done((bf16[416,384]{1,0:T(8,128)(2,1)S(1)}, bf16[416,384]{1,0:T(8,128)(2,1)S(1)}, u32[]{:S(2)}, u32[]{:S(2)}) %collective-permute-start.26) | collective-permute-done | bytes 319520 | tf_op jit(solution)/shard_map/ppermute | solution.py:379
  151.4 0.8 fusion.9
  152.2 0.8 fusion.12
  153.8 1.0 copy-done.29
  155.0 1.9 collective-permute-start.31
  157.2 10.1 %collective-permute-start.28 = (bf16[2,208,384]{2,1,0:T(8,128)(2,1)S(1)}, bf16[2,208,384]{2,1,0:T(8,128)(2,1)S(1)}, u32[]{:S(2)}, u32[]{:S(2)}) collective-permute-start(bf16[2,208,384]{2,1,0:T(8,128)(2,1)S(1)} %slice.279), channel_id=1, source_target_pairs={{0,2},{2,4},{4,6},{6,8},{8,10},{10,12},{12,14},{1,3},{3,5},{5,7},{... | collective-permute-start | bytes 958472 | tf_op jit(solution)/shard_map/ppermute | solution.py:528
  167.5 7.0 %collective-permute-done.28 = bf16[2,208,384]{2,1,0:T(8,128)(2,1)S(1)} collective-permute-done((bf16[2,208,384]{2,1,0:T(8,128)(2,1)S(1)}, bf16[2,208,384]{2,1,0:T(8,128)(2,1)S(1)}, u32[]{:S(2)}, u32[]{:S(2)}) %collective-permute-start.28) | collective-permute-done | bytes 319520 | tf_op jit(solution)/shard_map/ppermute | solution.py:528
  174.9 5.0 %collective-permute-start.40 = (bf16[4,48,1280]{2,1,0:T(8,128)(2,1)S(1)}, bf16[4,48,1280]{2,1,0:T(8,128)(2,1)S(1)}, u32[]{:S(2)}, u32[]{:S(2)}) collective-permute-start(bf16[4,48,1280]{2,1,0:T(8,128)(2,1)S(1)} %get-tuple-element.99), channel_id=1, source_target_pairs={{0,2},{2,0},{4,6},{6,4},{8,10},{10,8},{12,14},{14,12},{1,3},{3,1},... | collective-permute-start | bytes 1474568 | tf_op jit(solution)/shard_map/ppermute | solution.py:382
  180.5 1.0 collective-permute-start.42
  181.9 2.0 collective-permute-start.33
  184.4 8.7 %collective-permute-done.40 = bf16[4,48,1280]{2,1,0:T(8,128)(2,1)S(1)} collective-permute-done((bf16[4,48,1280]{2,1,0:T(8,128)(2,1)S(1)}, bf16[4,48,1280]{2,1,0:T(8,128)(2,1)S(1)}, u32[]{:S(2)}, u32[]{:S(2)}) %collective-permute-start.40) | collective-permute-done | bytes 491552 | tf_op jit(solution)/shard_map/ppermute | solution.py:382
  193.1 9.9 %collective-permute-start.35 = (bf16[4,48,1280]{2,1,0:T(8,128)(2,1)S(1)}, bf16[4,48,1280]{2,1,0:T(8,128)(2,1)S(1)}, u32[]{:S(2)}, u32[]{:S(2)}) collective-permute-start(bf16[4,48,1280]{2,1,0:T(8,128)(2,1)S(1)} %get-tuple-element.103), channel_id=1, source_target_pairs={{0,18},{2,16},{4,22},{6,20},{8,26},{10,24},{12,30},{14,28},{16,2},... | collective-permute-start | bytes 1474568 | tf_op jit(solution)/shard_map/ppermute | solution.py:385
  203.0 1.1 collective-permute-done.42
  204.5 3.9 %collective-permute-start.43 = (bf16[48,1280]{1,0:T(8,128)(2,1)S(1)}, bf16[48,1280]{1,0:T(8,128)(2,1)S(1)}, u32[]{:S(2)}, u32[]{:S(2)}) collective-permute-start(bf16[48,1280]{1,0:T(8,128)(2,1)S(1)} %get-tuple-element.111), channel_id=1, source_target_pairs={{0,4},{2,6},{4,8},{6,10},{8,12},{10,14},{12,0},{14,2},{1,5},{3,7},... | collective-permute-start | bytes 368648 | tf_op jit(solution)/shard_map/ppermute | solution.py:388
  208.4 3.7 %collective-permute-done.33 = bf16[4,48,1280]{2,1,0:T(8,128)(2,1)S(1)} collective-permute-done((bf16[4,48,1280]{2,1,0:T(8,128)(2,1)S(1)}, bf16[4,48,1280]{2,1,0:T(8,128)(2,1)S(1)}, u32[]{:S(2)}, u32[]{:S(2)}) %collective-permute-start.33) | collective-permute-done | bytes 491552 | tf_op jit(solution)/shard_map/ppermute | solution.py:382
  212.1 1.6 collective-permute-start.45
  213.7 1.4 collective-permute-done.34
  215.2 8.7 %collective-permute-done.35 = bf16[4,48,1280]{2,1,0:T(8,128)(2,1)S(1)} collective-permute-done((bf16[4,48,1280]{2,1,0:T(8,128)(2,1)S(1)}, bf16[4,48,1280]{2,1,0:T(8,128)(2,1)S(1)}, u32[]{:S(2)}, u32[]{:S(2)}) %collective-permute-start.35) | collective-permute-done | bytes 491552 | tf_op jit(solution)/shard_map/ppermute | solution.py:385
  224.3 3.6 %collective-permute-start.36 = (bf16[48,1280]{1,0:T(8,128)(2,1)S(1)}, bf16[48,1280]{1,0:T(8,128)(2,1)S(1)}, u32[]{:S(2)}, u32[]{:S(2)}) collective-permute-start(bf16[48,1280]{1,0:T(8,128)(2,1)S(1)} %get-tuple-element.114), channel_id=1, source_target_pairs={{0,4},{2,6},{4,8},{6,10},{8,12},{10,14},{12,0},{14,2},{1,5},{3,7},... | collective-permute-start | bytes 368648 | tf_op jit(solution)/shard_map/ppermute | solution.py:388
  227.9 2.4 collective-permute-start.38
  230.3 1.2 maximum_convert_fusion
  231.6 0.7 collective-permute-done.36
  232.3 4.0 %collective-permute-done.37 = bf16[48,1280]{1,0:T(8,128)(2,1)S(1)} collective-permute-done((bf16[48,1280]{1,0:T(8,128)(2,1)S(1)}, bf16[48,1280]{1,0:T(8,128)(2,1)S(1)}, u32[]{:S(2)}, u32[]{:S(2)}) %collective-permute-start.37) | collective-permute-done | bytes 122912 | tf_op jit(solution)/shard_map/ppermute | solution.py:388
  237.0 1.0 maximum_bitcast_fusion
  238.0 3.4 %collective-permute-done.46 = bf16[48,1280]{1,0:T(8,128)(2,1)S(1)} collective-permute-done((bf16[48,1280]{1,0:T(8,128)(2,1)S(1)}, bf16[48,1280]{1,0:T(8,128)(2,1)S(1)}, u32[]{:S(2)}, u32[]{:S(2)}) %collective-permute-start.46) | collective-permute-done | bytes 122912 | tf_op jit(solution)/shard_map/ppermute | solution.py:379
  (176 shorter events, 22.0 us)
Async XLA Ops:
  0.6 13.0 %copy-start.25 = (bf16[1,768,48]{1,2,0:T(8,128)(2,1)S(1)}, bf16[1,768,48]{1,2,0:T(8,128)(2,1)}, u32[]{:S(2)}) copy-start(bf16[1,768,48]{1,2,0:T(8,128)(2,1)} %param.21) | copy-start | bytes 221188
  7.3 6.4 %collective-permute-start.1 = (bf16[48,1280]{1,0:T(8,128)(2,1)S(1)}, bf16[48,1280]{1,0:T(8,128)(2,1)S(1)}, u32[]{:S(2)}, u32[]{:S(2)}) collective-permute-start(bf16[48,1280]{1,0:T(8,128)(2,1)S(1)} %broadcast_select_fusion.5), channel_id=1, source_target_pairs={{0,16},{16,0},{1,17},{17,1},{2,18},{18,2},{3,19},{19,3},{4,20},{20... | collective-permute-start | bytes 368648 | tf_op jit(solution)/shard_map/ppermute | solution.py:379
  13.7 8.2 %collective-permute-start.2 = (bf16[48,1280]{1,0:T(8,128)(2,1)S(1)}, bf16[48,1280]{1,0:T(8,128)(2,1)S(1)}, u32[]{:S(2)}, u32[]{:S(2)}) collective-permute-start(bf16[48,1280]{1,0:T(8,128)(2,1)S(1)} %get-tuple-element.118), channel_id=1, source_target_pairs={{0,4},{2,6},{4,8},{6,10},{8,12},{10,14},{12,0},{14,2},{1,5},{3,7},... | collective-permute-start | bytes 368648 | tf_op jit(solution)/shard_map/ppermute | solution.py:388
  15.6 13.5 %collective-permute-start.3 = (bf16[48,1280]{1,0:T(8,128)(2,1)S(1)}, bf16[48,1280]{1,0:T(8,128)(2,1)S(1)}, u32[]{:S(2)}, u32[]{:S(2)}) collective-permute-start(bf16[48,1280]{1,0:T(8,128)(2,1)S(1)} %get-tuple-element.118), channel_id=1, source_target_pairs={{0,8},{2,10},{4,12},{6,14},{8,0},{10,2},{12,4},{14,6},{1,9},{3,11}... | collective-permute-start | bytes 368648 | tf_op jit(solution)/shard_map/ppermute | solution.py:388
  18.2 10.9 %collective-permute-start.4 = (bf16[48,1280]{1,0:T(8,128)(2,1)S(1)}, bf16[48,1280]{1,0:T(8,128)(2,1)S(1)}, u32[]{:S(2)}, u32[]{:S(2)}) collective-permute-start(bf16[48,1280]{1,0:T(8,128)(2,1)S(1)} %get-tuple-element.118), channel_id=1, source_target_pairs={{0,12},{2,14},{4,0},{6,2},{8,4},{10,6},{12,8},{14,10},{1,13},{3,15... | collective-permute-start | bytes 368648 | tf_op jit(solution)/shard_map/ppermute | solution.py:388
  19.5 12.6 %collective-permute-start.14 = (bf16[48,1280]{1,0:T(8,128)(2,1)S(1)}, bf16[48,1280]{1,0:T(8,128)(2,1)S(1)}, u32[]{:S(2)}, u32[]{:S(2)}) collective-permute-start(bf16[48,1280]{1,0:T(8,128)(2,1)S(1)} %get-tuple-element.117), channel_id=1, source_target_pairs={{0,4},{2,6},{4,8},{6,10},{8,12},{10,14},{12,0},{14,2},{1,5},{3,7},... | collective-permute-start | bytes 368648 | tf_op jit(solution)/shard_map/ppermute | solution.py:388
  20.2 15.8 %collective-permute-start.15 = (bf16[48,1280]{1,0:T(8,128)(2,1)S(1)}, bf16[48,1280]{1,0:T(8,128)(2,1)S(1)}, u32[]{:S(2)}, u32[]{:S(2)}) collective-permute-start(bf16[48,1280]{1,0:T(8,128)(2,1)S(1)} %get-tuple-element.117), channel_id=1, source_target_pairs={{0,8},{2,10},{4,12},{6,14},{8,0},{10,2},{12,4},{14,6},{1,9},{3,11}... | collective-permute-start | bytes 368648 | tf_op jit(solution)/shard_map/ppermute | solution.py:388
  21.9 14.1 %collective-permute-start.16 = (bf16[48,1280]{1,0:T(8,128)(2,1)S(1)}, bf16[48,1280]{1,0:T(8,128)(2,1)S(1)}, u32[]{:S(2)}, u32[]{:S(2)}) collective-permute-start(bf16[48,1280]{1,0:T(8,128)(2,1)S(1)} %get-tuple-element.117), channel_id=1, source_target_pairs={{0,12},{2,14},{4,0},{6,2},{8,4},{10,6},{12,8},{14,10},{1,13},{3,15... | collective-permute-start | bytes 368648 | tf_op jit(solution)/shard_map/ppermute | solution.py:388
  29.1 11.2 %copy-start.1 = (bf16[4,48,1280]{2,1,0:T(8,128)(2,1)}, bf16[4,48,1280]{2,1,0:T(8,128)(2,1)S(1)}, u32[]{:S(2)}) copy-start(bf16[4,48,1280]{2,1,0:T(8,128)(2,1)S(1)} %pad_maximum_fusion.3.refs_2_.refs_13_) | copy-start | bytes 1474564
  29.1 12.7 %collective-permute-start.6 = (bf16[4,48,1280]{2,1,0:T(8,128)(2,1)S(1)}, bf16[4,48,1280]{2,1,0:T(8,128)(2,1)S(1)}, u32[]{:S(2)}, u32[]{:S(2)}) collective-permute-start(bf16[4,48,1280]{2,1,0:T(8,128)(2,1)S(1)} %pad_maximum_fusion.3.refs_2_.refs_13_), channel_id=1, source_target_pairs={{0,2},{2,0},{4,6},{6,4},{8,10},{10,8},{12,14},{14,12},{1,3},{3,1},... | collective-permute-start | bytes 1474568 | tf_op jit(solution)/shard_map/ppermute | solution.py:382
  30.6 13.3 %collective-permute-start.5 = (bf16[4,48,1280]{2,1,0:T(8,128)(2,1)S(1)}, bf16[4,48,1280]{2,1,0:T(8,128)(2,1)S(1)}, u32[]{:S(2)}, u32[]{:S(2)}) collective-permute-start(bf16[4,48,1280]{2,1,0:T(8,128)(2,1)S(1)} %pad_maximum_fusion.3.refs_2_.refs_13_), channel_id=1, source_target_pairs={{0,16},{16,0},{1,17},{17,1},{2,18},{18,2},{3,19},{19,3},{4,20},{20... | collective-permute-start | bytes 1474568 | tf_op jit(solution)/shard_map/ppermute | solution.py:379
  36.0 35.8 %copy-start.6 = (bf16[4,48,1280]{2,1,0:T(8,128)(2,1)}, bf16[4,48,1280]{2,1,0:T(8,128)(2,1)S(1)}, u32[]{:S(2)}) copy-start(bf16[4,48,1280]{2,1,0:T(8,128)(2,1)S(1)} %pad_maximum_fusion.4.refs_3_) | copy-start | bytes 1474564
  36.0 20.8 %collective-permute-start.18 = (bf16[4,48,1280]{2,1,0:T(8,128)(2,1)S(1)}, bf16[4,48,1280]{2,1,0:T(8,128)(2,1)}, u32[]{:S(2)}, u32[]{:S(2)}) collective-permute-start(bf16[4,48,1280]{2,1,0:T(8,128)(2,1)S(1)} %pad_maximum_fusion.4.refs_3_), channel_id=1, source_target_pairs={{0,2},{2,0},{4,6},{6,4},{8,10},{10,8},{12,14},{14,12},{1,3},{3,1},... | collective-permute-start | bytes 1474568 | tf_op jit(solution)/shard_map/ppermute | solution.py:382
  37.7 23.5 %collective-permute-start.17 = (bf16[4,48,1280]{2,1,0:T(8,128)(2,1)S(1)}, bf16[4,48,1280]{2,1,0:T(8,128)(2,1)}, u32[]{:S(2)}, u32[]{:S(2)}) collective-permute-start(bf16[4,48,1280]{2,1,0:T(8,128)(2,1)S(1)} %pad_maximum_fusion.4.refs_3_), channel_id=1, source_target_pairs={{0,16},{16,0},{1,17},{17,1},{2,18},{18,2},{3,19},{19,3},{4,20},{20... | collective-permute-start | bytes 1474568 | tf_op jit(solution)/shard_map/ppermute | solution.py:379
  39.2 26.4 %collective-permute-start.9 = (bf16[4,48,1280]{2,1,0:T(8,128)(2,1)S(1)}, bf16[4,48,1280]{2,1,0:T(8,128)(2,1)S(1)}, u32[]{:S(2)}, u32[]{:S(2)}) collective-permute-start(bf16[4,48,1280]{2,1,0:T(8,128)(2,1)S(1)} %pad_maximum_fusion.3.refs_2_.refs_13_), channel_id=1, source_target_pairs={{0,1},{1,0},{2,3},{3,2},{4,5},{5,4},{6,7},{7,6},{8,9},{9,8},{10,11... | collective-permute-start | bytes 1474568 | tf_op jit(solution)/shard_map/ppermute | solution.py:376
  40.4 22.3 %copy-start.31 = (s32[2]{0:T(128)S(1)}, s32[2]{0:T(128)}, u32[]{:S(2)}) copy-start(s32[2]{0:T(128)} %param.12) | copy-start | bytes 28
  41.9 26.9 %copy-start.2 = (bf16[4,48,1280]{2,1,0:T(8,128)(2,1)}, bf16[4,48,1280]{2,1,0:T(8,128)(2,1)S(1)}, u32[]{:S(2)}) copy-start(bf16[4,48,1280]{2,1,0:T(8,128)(2,1)S(1)} %collective-permute-done.6.refs_4_.refs_15_) | copy-start | bytes 1474564
  41.9 23.7 %collective-permute-start = (bf16[2,208,384]{2,1,0:T(8,128)(2,1)}, bf16[2,208,384]{2,1,0:T(8,128)(2,1)}, u32[]{:S(2)}, u32[]{:S(2)}) collective-permute-start(bf16[2,208,384]{2,1,0:T(8,128)(2,1)} %pad_maximum_fusion.5), channel_id=1, source_target_pairs={{2,0},{4,2},{6,4},{8,6},{10,8},{12,10},{14,12},{3,1},{5,3},{7,5},{... | collective-permute-start | bytes 958472 | tf_op jit(solution)/shard_map/ppermute | solution.py:413
  43.9 24.9 %copy-start.3 = (bf16[4,48,1280]{2,1,0:T(8,128)(2,1)}, bf16[4,48,1280]{2,1,0:T(8,128)(2,1)S(1)}, u32[]{:S(2)}) copy-start(bf16[4,48,1280]{2,1,0:T(8,128)(2,1)S(1)} %collective-permute-done.5.refs_3_.refs_14_) | copy-start | bytes 1474564
  43.9 21.8 %collective-permute-start.7 = (bf16[4,48,640]{2,1,0:T(8,128)(2,1)}, bf16[4,48,640]{2,1,0:T(8,128)(2,1)S(1)}, u32[]{:S(2)}, u32[]{:S(2)}) collective-permute-start(bf16[4,48,640]{2,1,0:T(8,128)(2,1)} %slice.271), channel_id=1, source_target_pairs={{0,16},{16,0},{1,17},{17,1},{2,18},{18,2},{3,19},{19,3},{4,20},{20... | collective-permute-start | bytes 737288 | tf_op jit(solution)/shard_map/ppermute | solution.py:379
  56.9 9.3 %collective-permute-start.8 = (bf16[4,48,640]{2,1,0:T(8,128)(2,1)}, bf16[4,48,640]{2,1,0:T(8,128)(2,1)}, u32[]{:S(2)}, u32[]{:S(2)}) collective-permute-start(bf16[4,48,640]{2,1,0:T(8,128)(2,1)} %slice.272), channel_id=1, source_target_pairs={{0,2},{2,0},{4,6},{6,4},{8,10},{10,8},{12,14},{14,12},{1,3},{3,1},... | collective-permute-start | bytes 737288 | tf_op jit(solution)/shard_map/ppermute | solution.py:382
  61.2 6.5 %collective-permute-start.19 = (bf16[4,48,640]{2,1,0:T(8,128)(2,1)}, bf16[4,48,640]{2,1,0:T(8,128)(2,1)}, u32[]{:S(2)}, u32[]{:S(2)}) collective-permute-start(bf16[4,48,640]{2,1,0:T(8,128)(2,1)} %slice.274), channel_id=1, source_target_pairs={{0,16},{16,0},{1,17},{17,1},{2,18},{18,2},{3,19},{19,3},{4,20},{20... | collective-permute-start | bytes 737288 | tf_op jit(solution)/shard_map/ppermute | solution.py:379
  65.5 6.3 %collective-permute-start.20 = (bf16[4,48,640]{2,1,0:T(8,128)(2,1)S(1)}, bf16[4,48,640]{2,1,0:T(8,128)(2,1)S(1)}, u32[]{:S(2)}, u32[]{:S(2)}) collective-permute-start(bf16[4,48,640]{2,1,0:T(8,128)(2,1)S(1)} %slice.275), channel_id=1, source_target_pairs={{0,2},{2,0},{4,6},{6,4},{8,10},{10,8},{12,14},{14,12},{1,3},{3,1},... | collective-permute-start | bytes 737288 | tf_op jit(solution)/shard_map/ppermute | solution.py:382
  65.6 8.0 %collective-permute-start.10 = (bf16[4,48,1280]{2,1,0:T(8,128)(2,1)S(1)}, bf16[4,48,1280]{2,1,0:T(8,128)(2,1)S(1)}, u32[]{:S(2)}, u32[]{:S(2)}) collective-permute-start(bf16[4,48,1280]{2,1,0:T(8,128)(2,1)S(1)} %collective-permute-done.5.refs_3_.refs_14_), channel_id=1, source_target_pairs={{0,1},{1,0},{2,3},{3,2},{4,5},{5,4},{6,7},{7,6},{8,9},{9,8},{10,11... | collective-permute-start | bytes 1474568 | tf_op jit(solution)/shard_map/ppermute | solution.py:376
  65.7 8.4 %collective-permute-start.11 = (bf16[4,48,1280]{2,1,0:T(8,128)(2,1)S(1)}, bf16[4,48,1280]{2,1,0:T(8,128)(2,1)S(1)}, u32[]{:S(2)}, u32[]{:S(2)}) collective-permute-start(bf16[4,48,1280]{2,1,0:T(8,128)(2,1)S(1)} %collective-permute-done.6.refs_4_.refs_15_), channel_id=1, source_target_pairs={{0,1},{1,0},{2,3},{3,2},{4,5},{5,4},{6,7},{7,6},{8,9},{9,8},{10,11... | collective-permute-start | bytes 1474568 | tf_op jit(solution)/shard_map/ppermute | solution.py:376
  66.2 5.6 %collective-permute-start.12 = (bf16[4,48,640]{2,1,0:T(8,128)(2,1)S(1)}, bf16[4,48,640]{2,1,0:T(8,128)(2,1)S(1)}, u32[]{:S(2)}, u32[]{:S(2)}) collective-permute-start(bf16[4,48,640]{2,1,0:T(8,128)(2,1)S(1)} %collective-permute-done.7.refs_5_.refs_16_), channel_id=1, source_target_pairs={{0,1},{1,0},{2,3},{3,2},{4,5},{5,4},{6,7},{7,6},{8,9},{9,8},{10,11... | collective-permute-start | bytes 737288 | tf_op jit(solution)/shard_map/ppermute | solution.py:376
  67.7 4.6 %collective-permute-start.13 = (bf16[4,48,640]{2,1,0:T(8,128)(2,1)}, bf16[4,48,640]{2,1,0:T(8,128)(2,1)S(1)}, u32[]{:S(2)}, u32[]{:S(2)}) collective-permute-start(bf16[4,48,640]{2,1,0:T(8,128)(2,1)} %collective-permute-done.8.refs_6_.refs_17_), channel_id=1, source_target_pairs={{0,1},{1,0},{2,3},{3,2},{4,5},{5,4},{6,7},{7,6},{8,9},{9,8},{10,11... | collective-permute-start | bytes 737288 | tf_op jit(solution)/shard_map/ppermute | solution.py:376
  71.8 16.6 %collective-permute-start.21 = (bf16[4,48,1280]{2,1,0:T(8,128)(2,1)S(1)}, bf16[4,48,1280]{2,1,0:T(8,128)(2,1)S(1)}, u32[]{:S(2)}, u32[]{:S(2)}) collective-permute-start(bf16[4,48,1280]{2,1,0:T(8,128)(2,1)S(1)} %pad_maximum_fusion.4.refs_3_), channel_id=1, source_target_pairs={{0,1},{1,0},{2,3},{3,2},{4,5},{5,4},{6,7},{7,6},{8,9},{9,8},{10,11... | collective-permute-start | bytes 1474568 | tf_op jit(solution)/shard_map/ppermute | solution.py:376
  71.8 16.7 %collective-permute-start.22 = (bf16[4,48,1280]{2,1,0:T(8,128)(2,1)}, bf16[4,48,1280]{2,1,0:T(8,128)(2,1)S(1)}, u32[]{:S(2)}, u32[]{:S(2)}) collective-permute-start(bf16[4,48,1280]{2,1,0:T(8,128)(2,1)} %collective-permute-done.17.refs_4_), channel_id=1, source_target_pairs={{0,1},{1,0},{2,3},{3,2},{4,5},{5,4},{6,7},{7,6},{8,9},{9,8},{10,11... | collective-permute-start | bytes 1474568 | tf_op jit(solution)/shard_map/ppermute | solution.py:376
  72.3 16.2 %collective-permute-start.23 = (bf16[4,48,1280]{2,1,0:T(8,128)(2,1)}, bf16[4,48,1280]{2,1,0:T(8,128)(2,1)S(1)}, u32[]{:S(2)}, u32[]{:S(2)}) collective-permute-start(bf16[4,48,1280]{2,1,0:T(8,128)(2,1)} %collective-permute-done.18.refs_5_), channel_id=1, source_target_pairs={{0,1},{1,0},{2,3},{3,2},{4,5},{5,4},{6,7},{7,6},{8,9},{9,8},{10,11... | collective-permute-start | bytes 1474568 | tf_op jit(solution)/shard_map/ppermute | solution.py:376
  73.7 14.8 %collective-permute-start.24 = (bf16[4,48,640]{2,1,0:T(8,128)(2,1)}, bf16[4,48,640]{2,1,0:T(8,128)(2,1)S(1)}, u32[]{:S(2)}, u32[]{:S(2)}) collective-permute-start(bf16[4,48,640]{2,1,0:T(8,128)(2,1)} %collective-permute-done.19.refs_6_), channel_id=1, source_target_pairs={{0,1},{1,0},{2,3},{3,2},{4,5},{5,4},{6,7},{7,6},{8,9},{9,8},{10,11... | collective-permute-start | bytes 737288 | tf_op jit(solution)/shard_map/ppermute | solution.py:376
  74.1 14.4 %collective-permute-start.25 = (bf16[4,48,640]{2,1,0:T(8,128)(2,1)S(1)}, bf16[4,48,640]{2,1,0:T(8,128)(2,1)S(1)}, u32[]{:S(2)}, u32[]{:S(2)}) collective-permute-start(bf16[4,48,640]{2,1,0:T(8,128)(2,1)S(1)} %collective-permute-done.20.refs_7_), channel_id=1, source_target_pairs={{0,1},{1,0},{2,3},{3,2},{4,5},{5,4},{6,7},{7,6},{8,9},{9,8},{10,11... | collective-permute-start | bytes 737288 | tf_op jit(solution)/shard_map/ppermute | solution.py:376
  114.1 19.2 %copy-start.4 = (f32[416,384]{1,0:T(8,128)S(1)}, f32[416,384]{1,0:T(8,128)}, u32[]{:S(2)}) copy-start(f32[416,384]{1,0:T(8,128)} %get-tuple-element.37.refs_1_) | copy-start | bytes 1916932
  134.5 10.5 %collective-permute-start.29 = (bf16[416,384]{1,0:T(8,128)(2,1)S(1)}, bf16[416,384]{1,0:T(8,128)(2,1)S(1)}, u32[]{:S(2)}, u32[]{:S(2)}) collective-permute-start(bf16[416,384]{1,0:T(8,128)(2,1)S(1)} %get-tuple-element.106), channel_id=1, source_target_pairs={{0,16},{16,0},{1,17},{17,1},{2,18},{18,2},{3,19},{19,3},{4,20},{20... | collective-permute-start | bytes 958472 | tf_op jit(solution)/shard_map/ppermute | solution.py:379
  135.2 16.1 %collective-permute-start.26 = (bf16[416,384]{1,0:T(8,128)(2,1)S(1)}, bf16[416,384]{1,0:T(8,128)(2,1)S(1)}, u32[]{:S(2)}, u32[]{:S(2)}) collective-permute-start(bf16[416,384]{1,0:T(8,128)(2,1)S(1)} %get-tuple-element.108), channel_id=1, source_target_pairs={{0,16},{16,0},{1,17},{17,1},{2,18},{18,2},{3,19},{19,3},{4,20},{20... | collective-permute-start | bytes 958472 | tf_op jit(solution)/shard_map/ppermute | solution.py:379
  146.9 7.9 %collective-permute-start.30 = (bf16[2,720,384]{2,1,0:T(8,128)(2,1)S(1)}, bf16[2,720,384]{2,1,0:T(8,128)(2,1)S(1)}, u32[]{:S(2)}, u32[]{:S(2)}) collective-permute-start(bf16[2,720,384]{2,1,0:T(8,128)(2,1)S(1)} %pad_maximum_fusion.2), channel_id=1, source_target_pairs={{0,1},{1,0},{2,3},{3,2},{4,5},{5,4},{6,7},{7,6},{8,9},{9,8},{10,11... | collective-permute-start | bytes 3317768 | tf_op jit(solution)/shard_map/ppermute | solution.py:376
  153.2 3.8 %collective-permute-start.27 = (bf16[2,720,384]{2,1,0:T(8,128)(2,1)S(1)}, bf16[2,720,384]{2,1,0:T(8,128)(2,1)S(1)}, u32[]{:S(2)}, u32[]{:S(2)}) collective-permute-start(bf16[2,720,384]{2,1,0:T(8,128)(2,1)S(1)} %pad_maximum_fusion.1), channel_id=1, source_target_pairs={{0,1},{1,0},{2,3},{3,2},{4,5},{5,4},{6,7},{7,6},{8,9},{9,8},{10,11... | collective-permute-start | bytes 3317768 | tf_op jit(solution)/shard_map/ppermute | solution.py:376
  153.8 20.7 %collective-permute-start.39 = (bf16[2,2,4,48,1280]{4,3,2,1,0:T(8,128)(2,1)S(1)}, bf16[2,2,4,48,1280]{4,3,2,1,0:T(8,128)(2,1)S(1)}, u32[]{:S(2)}, u32[]{:S(2)}) collective-permute-start(bf16[2,2,4,48,1280]{4,3,2,1,0:T(8,128)(2,1)S(1)} %copy-done.30), channel_id=1, source_target_pairs={{0,1},{1,0},{2,3},{3,2},{4,5},{5,4},{6,7},{7,6},{8,9},{9,8},{10,11... | collective-permute-start | bytes 5898248 | tf_op jit(solution)/shard_map/ppermute | solution.py:376
  154.8 26.7 %collective-permute-start.32 = (bf16[2,2,4,48,1280]{4,3,2,1,0:T(8,128)(2,1)S(1)}, bf16[2,2,4,48,1280]{4,3,2,1,0:T(8,128)(2,1)S(1)}, u32[]{:S(2)}, u32[]{:S(2)}) collective-permute-start(bf16[2,2,4,48,1280]{4,3,2,1,0:T(8,128)(2,1)S(1)} %copy-done.29), channel_id=1, source_target_pairs={{0,1},{1,0},{2,3},{3,2},{4,5},{5,4},{6,7},{7,6},{8,9},{9,8},{10,11... | collective-permute-start | bytes 5898248 | tf_op jit(solution)/shard_map/ppermute | solution.py:376
  155.0 12.4 %collective-permute-start.31 = (bf16[2,208,384]{2,1,0:T(8,128)(2,1)S(1)}, bf16[2,208,384]{2,1,0:T(8,128)(2,1)S(1)}, u32[]{:S(2)}, u32[]{:S(2)}) collective-permute-start(bf16[2,208,384]{2,1,0:T(8,128)(2,1)S(1)} %slice.284), channel_id=1, source_target_pairs={{0,2},{2,4},{4,6},{6,8},{8,10},{10,12},{12,14},{1,3},{3,5},{5,7},{... | collective-permute-start | bytes 958472 | tf_op jit(solution)/shard_map/ppermute | solution.py:528
  157.2 17.3 %copy-start = (bf16[2,720,384]{2,1,0:T(8,128)(2,1)}, bf16[2,720,384]{2,1,0:T(8,128)(2,1)S(1)}, u32[]{:S(2)}) copy-start(bf16[2,720,384]{2,1,0:T(8,128)(2,1)S(1)} %fusion.68) | copy-start | bytes 3317764
  157.2 17.3 %collective-permute-start.28 = (bf16[2,208,384]{2,1,0:T(8,128)(2,1)S(1)}, bf16[2,208,384]{2,1,0:T(8,128)(2,1)S(1)}, u32[]{:S(2)}, u32[]{:S(2)}) collective-permute-start(bf16[2,208,384]{2,1,0:T(8,128)(2,1)S(1)} %slice.279), channel_id=1, source_target_pairs={{0,2},{2,4},{4,6},{6,8},{8,10},{10,12},{12,14},{1,3},{3,5},{5,7},{... | collective-permute-start | bytes 958472 | tf_op jit(solution)/shard_map/ppermute | solution.py:528
  167.4 7.1 %copy-start.18 = (bf16[4,48,1280]{2,1,0:T(8,128)(2,1)S(1)}, bf16[4,48,1280]{2,1,0:T(8,128)(2,1)}, u32[]{:S(2)}) copy-start(bf16[4,48,1280]{2,1,0:T(8,128)(2,1)} %get-tuple-element.57) | copy-start | bytes 1474564
  167.4 7.1 %copy-start.19 = (bf16[4,48,1280]{2,1,0:T(8,128)(2,1)S(1)}, bf16[4,48,1280]{2,1,0:T(8,128)(2,1)}, u32[]{:S(2)}) copy-start(bf16[4,48,1280]{2,1,0:T(8,128)(2,1)} %get-tuple-element.58) | copy-start | bytes 1474564
  167.4 7.1 %copy-start.20 = (bf16[4,48,1280]{2,1,0:T(8,128)(2,1)S(1)}, bf16[4,48,1280]{2,1,0:T(8,128)(2,1)}, u32[]{:S(2)}) copy-start(bf16[4,48,1280]{2,1,0:T(8,128)(2,1)} %get-tuple-element.59) | copy-start | bytes 1474564
  174.6 6.9 %copy-start.15 = (bf16[4,48,1280]{2,1,0:T(8,128)(2,1)S(1)}, bf16[4,48,1280]{2,1,0:T(8,128)(2,1)}, u32[]{:S(2)}) copy-start(bf16[4,48,1280]{2,1,0:T(8,128)(2,1)} %get-tuple-element.52) | copy-start | bytes 1474564
  174.6 6.9 %copy-start.16 = (bf16[4,48,1280]{2,1,0:T(8,128)(2,1)S(1)}, bf16[4,48,1280]{2,1,0:T(8,128)(2,1)}, u32[]{:S(2)}) copy-start(bf16[4,48,1280]{2,1,0:T(8,128)(2,1)} %get-tuple-element.53) | copy-start | bytes 1474564
  174.6 6.9 %copy-start.17 = (bf16[4,48,1280]{2,1,0:T(8,128)(2,1)S(1)}, bf16[4,48,1280]{2,1,0:T(8,128)(2,1)}, u32[]{:S(2)}) copy-start(bf16[4,48,1280]{2,1,0:T(8,128)(2,1)} %get-tuple-element.54) | copy-start | bytes 1474564
  174.9 18.2 %collective-permute-start.40 = (bf16[4,48,1280]{2,1,0:T(8,128)(2,1)S(1)}, bf16[4,48,1280]{2,1,0:T(8,128)(2,1)S(1)}, u32[]{:S(2)}, u32[]{:S(2)}) collective-permute-start(bf16[4,48,1280]{2,1,0:T(8,128)(2,1)S(1)} %get-tuple-element.99), channel_id=1, source_target_pairs={{0,2},{2,0},{4,6},{6,4},{8,10},{10,8},{12,14},{14,12},{1,3},{3,1},... | collective-permute-start | bytes 1474568 | tf_op jit(solution)/shard_map/ppermute | solution.py:382
  180.0 23.1 %collective-permute-start.41 = (bf16[4,48,1280]{2,1,0:T(8,128)(2,1)S(1)}, bf16[4,48,1280]{2,1,0:T(8,128)(2,1)S(1)}, u32[]{:S(2)}, u32[]{:S(2)}) collective-permute-start(bf16[4,48,1280]{2,1,0:T(8,128)(2,1)S(1)} %get-tuple-element.101), channel_id=1, source_target_pairs={{0,16},{16,0},{1,17},{17,1},{2,18},{18,2},{3,19},{19,3},{4,20},{20... | collective-permute-start | bytes 1474568 | tf_op jit(solution)/shard_map/ppermute | solution.py:379
  180.5 23.6 %collective-permute-start.42 = (bf16[4,48,1280]{2,1,0:T(8,128)(2,1)S(1)}, bf16[4,48,1280]{2,1,0:T(8,128)(2,1)S(1)}, u32[]{:S(2)}, u32[]{:S(2)}) collective-permute-start(bf16[4,48,1280]{2,1,0:T(8,128)(2,1)S(1)} %get-tuple-element.100), channel_id=1, source_target_pairs={{0,18},{2,16},{4,22},{6,20},{8,26},{10,24},{12,30},{14,28},{16,2},... | collective-permute-start | bytes 1474568 | tf_op jit(solution)/shard_map/ppermute | solution.py:385
  181.5 22.6 %copy-start.14 = (bf16[4,48,1280]{2,1,0:T(8,128)(2,1)S(1)}, bf16[4,48,1280]{2,1,0:T(8,128)(2,1)}, u32[]{:S(2)}) copy-start(bf16[4,48,1280]{2,1,0:T(8,128)(2,1)} %get-tuple-element.55) | copy-start | bytes 1474564
  181.9 30.2 %collective-permute-start.33 = (bf16[4,48,1280]{2,1,0:T(8,128)(2,1)S(1)}, bf16[4,48,1280]{2,1,0:T(8,128)(2,1)S(1)}, u32[]{:S(2)}, u32[]{:S(2)}) collective-permute-start(bf16[4,48,1280]{2,1,0:T(8,128)(2,1)S(1)} %get-tuple-element.102), channel_id=1, source_target_pairs={{0,2},{2,0},{4,6},{6,4},{8,10},{10,8},{12,14},{14,12},{1,3},{3,1},... | collective-permute-start | bytes 1474568 | tf_op jit(solution)/shard_map/ppermute | solution.py:382
  183.9 31.3 %collective-permute-start.34 = (bf16[4,48,1280]{2,1,0:T(8,128)(2,1)S(1)}, bf16[4,48,1280]{2,1,0:T(8,128)(2,1)S(1)}, u32[]{:S(2)}, u32[]{:S(2)}) collective-permute-start(bf16[4,48,1280]{2,1,0:T(8,128)(2,1)S(1)} %get-tuple-element.104), channel_id=1, source_target_pairs={{0,16},{16,0},{1,17},{17,1},{2,18},{18,2},{3,19},{19,3},{4,20},{20... | collective-permute-start | bytes 1474568 | tf_op jit(solution)/shard_map/ppermute | solution.py:379
  193.1 30.8 %collective-permute-start.35 = (bf16[4,48,1280]{2,1,0:T(8,128)(2,1)S(1)}, bf16[4,48,1280]{2,1,0:T(8,128)(2,1)S(1)}, u32[]{:S(2)}, u32[]{:S(2)}) collective-permute-start(bf16[4,48,1280]{2,1,0:T(8,128)(2,1)S(1)} %get-tuple-element.103), channel_id=1, source_target_pairs={{0,18},{2,16},{4,22},{6,20},{8,26},{10,24},{12,30},{14,28},{16,2},... | collective-permute-start | bytes 1474568 | tf_op jit(solution)/shard_map/ppermute | solution.py:385
  204.1 19.7 %copy-start.13 = (bf16[4,48,1280]{2,1,0:T(8,128)(2,1)S(1)}, bf16[4,48,1280]{2,1,0:T(8,128)(2,1)}, u32[]{:S(2)}) copy-start(bf16[4,48,1280]{2,1,0:T(8,128)(2,1)} %get-tuple-element.50) | copy-start | bytes 1474564
  204.5 23.4 %collective-permute-start.43 = (bf16[48,1280]{1,0:T(8,128)(2,1)S(1)}, bf16[48,1280]{1,0:T(8,128)(2,1)S(1)}, u32[]{:S(2)}, u32[]{:S(2)}) collective-permute-start(bf16[48,1280]{1,0:T(8,128)(2,1)S(1)} %get-tuple-element.111), channel_id=1, source_target_pairs={{0,4},{2,6},{4,8},{6,10},{8,12},{10,14},{12,0},{14,2},{1,5},{3,7},... | collective-permute-start | bytes 368648 | tf_op jit(solution)/shard_map/ppermute | solution.py:388
  208.4 23.2 %collective-permute-start.44 = (bf16[48,1280]{1,0:T(8,128)(2,1)S(1)}, bf16[48,1280]{1,0:T(8,128)(2,1)S(1)}, u32[]{:S(2)}, u32[]{:S(2)}) collective-permute-start(bf16[48,1280]{1,0:T(8,128)(2,1)S(1)} %get-tuple-element.113), channel_id=1, source_target_pairs={{0,8},{2,10},{4,12},{6,14},{8,0},{10,2},{12,4},{14,6},{1,9},{3,11}... | collective-permute-start | bytes 368648 | tf_op jit(solution)/shard_map/ppermute | solution.py:388
  212.1 19.5 %collective-permute-start.45 = (bf16[48,1280]{1,0:T(8,128)(2,1)S(1)}, bf16[48,1280]{1,0:T(8,128)(2,1)S(1)}, u32[]{:S(2)}, u32[]{:S(2)}) collective-permute-start(bf16[48,1280]{1,0:T(8,128)(2,1)S(1)} %get-tuple-element.112), channel_id=1, source_target_pairs={{0,12},{2,14},{4,0},{6,2},{8,4},{10,6},{12,8},{14,10},{1,13},{3,15... | collective-permute-start | bytes 368648 | tf_op jit(solution)/shard_map/ppermute | solution.py:388
  224.3 8.1 %collective-permute-start.36 = (bf16[48,1280]{1,0:T(8,128)(2,1)S(1)}, bf16[48,1280]{1,0:T(8,128)(2,1)S(1)}, u32[]{:S(2)}, u32[]{:S(2)}) collective-permute-start(bf16[48,1280]{1,0:T(8,128)(2,1)S(1)} %get-tuple-element.114), channel_id=1, source_target_pairs={{0,4},{2,6},{4,8},{6,10},{8,12},{10,14},{12,0},{14,2},{1,5},{3,7},... | collective-permute-start | bytes 368648 | tf_op jit(solution)/shard_map/ppermute | solution.py:388
  227.9 8.4 %collective-permute-start.37 = (bf16[48,1280]{1,0:T(8,128)(2,1)S(1)}, bf16[48,1280]{1,0:T(8,128)(2,1)S(1)}, u32[]{:S(2)}, u32[]{:S(2)}) collective-permute-start(bf16[48,1280]{1,0:T(8,128)(2,1)S(1)} %get-tuple-element.116), channel_id=1, source_target_pairs={{0,8},{2,10},{4,12},{6,14},{8,0},{10,2},{12,4},{14,6},{1,9},{3,11}... | collective-permute-start | bytes 368648 | tf_op jit(solution)/shard_map/ppermute | solution.py:388
  227.9 8.4 %collective-permute-start.38 = (bf16[48,1280]{1,0:T(8,128)(2,1)S(1)}, bf16[48,1280]{1,0:T(8,128)(2,1)S(1)}, u32[]{:S(2)}, u32[]{:S(2)}) collective-permute-start(bf16[48,1280]{1,0:T(8,128)(2,1)S(1)} %get-tuple-element.115), channel_id=1, source_target_pairs={{0,12},{2,14},{4,0},{6,2},{8,4},{10,6},{12,8},{14,10},{1,13},{3,15... | collective-permute-start | bytes 368648 | tf_op jit(solution)/shard_map/ppermute | solution.py:388
  231.6 5.5 %slice-start = ((bf16[2,720,384]{2,1,0:T(8,128)(2,1)}), bf16[2,304,384]{2,1,0:T(8,128)(2,1)S(1)}, s32[]{:S(2)}) async-start(bf16[2,720,384]{2,1,0:T(8,128)(2,1)} %copy-done), calls=%async_computation | async-start | bytes 933888 | tf_op jit(solution)/shard_map/slice | solution.py:529
  236.4 4.9 %collective-permute-start.46 = (bf16[48,1280]{1,0:T(8,128)(2,1)S(1)}, bf16[48,1280]{1,0:T(8,128)(2,1)S(1)}, u32[]{:S(2)}, u32[]{:S(2)}) collective-permute-start(bf16[48,1280]{1,0:T(8,128)(2,1)S(1)} %get-tuple-element.92), channel_id=1, source_target_pairs={{0,16},{16,0},{1,17},{17,1},{2,18},{18,2},{3,19},{19,3},{4,20},{20... | collective-permute-start | bytes 368648 | tf_op jit(solution)/shard_map/ppermute | solution.py:379
  (16 other events, 31.8 us)

commit v3 on v2

--- a/solution.py
+++ b/solution.py
@@ -16,6 +16,7 @@
 BF16 = jnp.bfloat16
 BLOCK = 128
 HALF = 1280
+COST = 10 ** 10
 SCALE = 1.0 / math.sqrt(HD)
 
 
@@ -136,11 +137,12 @@
     out_ref[r, :] = (out * valid_rows(sc, n)).astype(BF16)
 
 
-def backward_image(n, sc, u_ref, w, vec, in_ref, kept, grad, sums, bsum):
+def rsum(a):
+    return jnp.sum(a, 0, keepdims=True)
+
+
+def backward_mlp(n, sc, u_ref, w, vec, kept, grad, sums, bsum):
     r = image_rows(n)
-
-    def rsum(a):
-        return jnp.sum(a, 0, keepdims=True)
 
     masked = u_ref[r, :].astype(F32) * valid_rows(sc, n)
     sums[5:6, :] += rsum(masked)
@@ -162,10 +164,16 @@
     sums[1:2, :] += rsum(mg * xhat)
     res = masked + norm_back(mg, xhat, kept["inv2"][r, :1], vec[1:2, :])
     sums[3:4, :] += rsum(res)
+    grad["res"][r, :] = res
+
+
+def backward_attention(n, w, vec, in_ref, kept, grad, sums, bsum):
+    r = image_rows(n)
+    res = grad["res"][r, :]
     ag = res.astype(BF16)
     grad["ag"][r, :] = ag
     low = low_lanes()
-    ig = jnp.zeros(masked.shape, F32)
+    ig = jnp.zeros(res.shape, F32)
     for t in range(2):
         xg = nn(ag, w[t, 0, :, OUT:MISC]).astype(BF16)
         gx = jnp.where(low, 0, xg[:, :BLOCK])
@@ -188,7 +196,7 @@
             jnp.where(low, dv[0], dv[1]), dv[2],
         ]
         d = jnp.concatenate(blocks, 1).astype(BF16)
-        grad["qkv"][t, r, :] = d
+        grad["dqkv"][t, r, :] = d
         total = rsum(d.astype(F32))
         for i in range(5):
             bsum[t, i:i + 1, :] += total[:, i * BLOCK:(i + 1) * BLOCK]
@@ -204,7 +212,7 @@
     ag, dg = grad["ag"][...], grad["dg"][...]
     ain, mlp_in = kept["ain"][...], kept["min"][...]
     high = jnp.where(low_lanes(), 0.0, 1.0)
-    d = grad["qkv"][t]
+    d = grad["dqkv"][t]
     g[t, 0, :, :OUT] = tn(ain, d[:, :OUT]).astype(BF16)
     out = tn(ag, kept["mx"][t])
     g[t, 0, :, OUT:ATT] = (tn(ain, d[:, OUT:]) + out[:, :BLOCK] * high).astype(BF16)
@@ -224,9 +232,6 @@
             g[t, 1, i * piece:(i + 1) * piece, ROWSB:] = rows
 
 
-KEPT = ("xh1", "inv1", "ain", "qkv", "pr", "mx", "xh2", "inv2", "min", "sl", "hd")
-
-
 def kept_shapes(total, width, ff):
     images = total // IMG_PAD
     return dict(
@@ -236,46 +241,41 @@
 
 
 def grad_shapes(total, width, ff):
-    return dict(dg=((total, width), BF16), up=((total, ff), BF16), ag=((total, width), BF16),
-                qkv=((2, total, ATT), BF16))
-
-
-def layer_call(sources, load, store, out_shapes, scalars, x, u, kept_in, ff, piece):
-    forward, backward = x is not None, u is not None
-    total, width = (x if forward else u).shape
+    return dict(dg=((total, width), BF16), up=((total, ff), BF16), res=((total, width), F32), sums=((8, width), F32),
+                bsum=((2, 16, BLOCK), F32))
+
+
+def layer_call(phases, sources, load, store, out_shapes, scalars, given, total, width, ff, piece):
     ks = kept_shapes(total, width, ff)
     gs = grad_shapes(total, width, ff)
+    need = {
+        "forward": ["x"], "mlp": ["u", "sl", "xh2", "inv2"],
+        "attention": list(gs) + ["ain", "qkv", "pr", "mx", "xh1", "inv1", "min", "hd"],
+    }
+    gives = {"forward": {"out": ((total, width), BF16), **ks}, "mlp": gs, "attention": {"in": ((total, width), F32)}}
+    made = {}
+    for p in phases:
+        made.update(gives[p])
+    inputs = [n for p in phases for n in need[p] if n not in made]
+    inputs = list(dict.fromkeys(inputs))
+    last = phases[-1]
+    shown = {"forward": list(gives["forward"]), "mlp": list(gs), "attention": ["in"]}[last]
+    if last != "forward" and "forward" in phases:
+        shown = ["out"] + shown
+    if last == "mlp" and "forward" in phases:
+        shown += [n for n in ks if n in need["attention"]]
+    inner = [n for n in made if n not in shown]
+    end = last == "attention"
     vmem = pl.BlockSpec(memory_space=pltpu.VMEM)
     anywhere = pl.BlockSpec(memory_space=pl.ANY)
-    ins, in_specs = [scalars], [pl.BlockSpec(memory_space=pltpu.SMEM)]
-    outs, out_specs = [], []
-    keep_out = forward and not backward
-    keep_in = backward and not forward
-    for a in (x, u):
-        if a is not None:
-            ins.append(a)
-            in_specs.append(vmem)
-    if keep_in:
-        ins += [kept_in[k] for k in KEPT]
-        in_specs += [vmem] * len(KEPT)
-    ins += sources
-    in_specs += [anywhere] * len(sources)
-    if forward:
-        outs.append(((total, width), BF16))
-        out_specs.append(vmem)
-    if backward:
-        outs += [((total, width), F32), ((2, 16, BLOCK), F32)] + out_shapes
-        out_specs += [vmem, vmem] + [anywhere] * len(out_shapes)
-    if keep_out:
-        outs += [ks[k] for k in KEPT]
-        out_specs += [vmem] * len(KEPT)
+    ends = out_shapes if end else []
     scratch = [pltpu.VMEM((2, 2, width, HALF), BF16), pltpu.VMEM((8, width), F32), pltpu.VMEM((2, 16, BLOCK), F32),
-               pltpu.SemaphoreType.DMA]
-    if backward:
-        scratch += [pltpu.VMEM(*gs[k]) for k in gs]
-        scratch += [pltpu.VMEM((8, width), F32), pltpu.VMEM((2, 2, width, HALF), BF16)]
-    if forward and backward:
-        scratch += [pltpu.VMEM(*ks[k]) for k in KEPT]
+               pltpu.SemaphoreType.DMA] + [pltpu.VMEM(*made[n]) for n in inner]
+    if end:
+        scratch += [pltpu.VMEM((total, width), BF16), pltpu.VMEM((2, total, ATT), BF16),
+                    pltpu.VMEM((2, 2, width, HALF), BF16)]
+        if "mlp" not in phases:
+            scratch += [pltpu.VMEM(*gs["sums"]), pltpu.VMEM(*gs["bsum"])]
 
     def body(*refs):
         refs = list(refs)
@@ -286,24 +286,21 @@
             return got
 
         sc = take(1)[0]
-        x_ref = take(1)[0] if forward else None
-        u_ref = take(1)[0] if backward else None
-        if keep_in:
-            kept = dict(zip(KEPT, take(len(KEPT))))
+        at = dict(zip(inputs, take(len(inputs))))
         src = take(len(sources))
-        if forward:
-            out_ref = take(1)[0]
-        if backward:
-            in_ref, bsum = take(2)
-            dst = take(len(out_shapes))
-        if keep_out:
-            kept = dict(zip(KEPT, take(len(KEPT))))
+        at.update(zip(shown, take(len(shown))))
+        if end:
+            bias = take(1)[0]
+        dst = take(len(ends))
         w, vec, brow, sem = take(4)
-        if backward:
-            grad = dict(zip(gs, take(len(gs))))
-            sums, g = take(2)
-        if forward and backward:
-            kept = dict(zip(KEPT, take(len(KEPT))))
+        at.update(zip(inner, take(len(inner))))
+        if end:
+            at["ag"], at["dqkv"], g = take(3)
+            if "mlp" not in phases:
+                sums, bsum = take(2)
+                sums[...] = at["sums"][...]
+                bsum[...] = at["bsum"][...]
+                at["sums"], at["bsum"] = sums, bsum
         copies = load(sc, src, w, sem)
         for c in copies:
             c.start()
@@ -312,24 +309,32 @@
         vec[...] = w[0, 0, :, MISC:UP0].astype(F32).T[:8, :]
         for t in range(2):
             brow[t] = w[t, 1, :16, ROWSB:].astype(F32)
-        if forward:
+        if "forward" in phases:
             def step(n, carry):
-                forward_image(n, sc, x_ref, w, vec, brow, out_ref, kept)
+                forward_image(n, sc, at["x"], w, vec, brow, at["out"], at)
                 return carry
             lax.fori_loop(0, total // IMG_PAD, step, 0)
-        if backward:
-            sums[...] = jnp.zeros_like(sums)
-            bsum[...] = jnp.zeros_like(bsum)
+        if "mlp" in phases:
+            at["sums"][...] = jnp.zeros_like(at["sums"])
+            at["bsum"][...] = jnp.zeros_like(at["bsum"])
+
+            def back_mlp(n, carry):
+                backward_mlp(n, sc, at["u"], w, vec, at, at, at["sums"], at["bsum"])
+                return carry
+            lax.fori_loop(0, total // IMG_PAD, back_mlp, 0)
+        if end:
+            sums, bsum = at["sums"], at["bsum"]
 
             def back(n, carry):
-                backward_image(n, sc, u_ref, w, vec, in_ref, kept, grad, sums, bsum)
+                backward_attention(n, w, vec, at["in"], at, at, sums, bsum)
                 return carry
             lax.fori_loop(0, total // IMG_PAD, back, 0)
+            bias[...] = bsum[...]
             small = jnp.concatenate([sums[...], jnp.zeros((BLOCK - 8, width), F32)], 0).T.astype(BF16)
             copies = []
             for side in range(2):
                 t = jnp.where(sc[1] == 0, 1 - side, side)
-                weight_grads(t, piece, kept, grad, small, bsum, g)
+                weight_grads(t, piece, at, at, small, bsum, g)
                 out = store(sc, side, t, g, dst, sem)
                 for c in out:
                     c.start()
@@ -337,24 +342,22 @@
             for c in copies:
                 c.wait()
 
+    outs = [made[n] for n in shown] + ([gs["bsum"]] if end else []) + ends
     got = pl.pallas_call(
         body,
         out_shape=[jax.ShapeDtypeStruct(*o) for o in outs],
-        in_specs=in_specs,
-        out_specs=out_specs,
+        in_specs=[pl.BlockSpec(memory_space=pltpu.SMEM)] + [vmem] * len(inputs) + [anywhere] * len(sources),
+        out_specs=[vmem] * (len(outs) - len(ends)) + [anywhere] * len(ends),
         scratch_shapes=scratch,
         compiler_params=pltpu.CompilerParams(vmem_limit_bytes=56 * 2 ** 20),
-    )(*ins)
+        cost_estimate=pl.CostEstimate(flops=COST * len(phases), transcendentals=0, bytes_accessed=2 ** 23),
+    )(scalars, *[given[n] for n in inputs], *sources)
     got = list(got)
-    res = {}
-    if forward:
-        res["out"] = got.pop(0)
-    if backward:
-        res["in"], res["bias"] = got[:2]
-        res["g"] = got[2:2 + len(out_shapes)]
-        del got[:2 + len(out_shapes)]
-    if keep_out:
-        res["kept"] = dict(zip(KEPT, got))
+    res = dict(zip(shown, got))
+    del got[:len(shown)]
+    if end:
+        res["bias"] = got.pop(0)
+        res["g"] = got
     return res
 
 
@@ -387,8 +390,23 @@
     def pz(a, k):
         return lax.ppermute(a, "dp", [(2 * z + y, 2 * ((z + k) % m) + y) for z in range(m) for y in range(2)])
 
+    def after(a, *b):
+        return lax.optimization_barrier((a, *b))
+
     def plus(*a):
         return sum(b.astype(F32) for b in a)
+
+    def add_pair(g, got):
+        keep, to_y, to_x, to_d = [plus(a, b) for a, b in zip(g[1:], (got[0, 0], got[0, 1], got[1, 0], got[1, 1]))]
+        return [keep, to_y.astype(BF16), to_x.astype(BF16), to_d.astype(BF16)]
+
+    def across(sent):
+        return [sent[0], py(sent[1]), px(sent[2]), pd(sent[3])]
+
+    def along(quad):
+        quad = plus(*quad)
+        low = quad.astype(BF16)
+        return plus(quad[0], *[pz(low[kk], kk) for kk in range(1, m)])
 
     batch_tokens = lax.dynamic_index_in_dim(tokens, sec, 0, keepdims=False)
     batch_cot = lax.dynamic_index_in_dim(cotangent, sec, 0, keepdims=False)
@@ -433,22 +451,18 @@
         give = jnp.where(sec == 0, part1, part0)
         got = px(give)
         start = [jnp.where(sec == 0, keep, got), jnp.where(sec == 0, got, keep)]
-        half = HALF // 2
 
         def load(sc, src, w, sem):
             copies = []
             for side in range(2):
                 t = jnp.where(sc[1] == 0, side, 1 - side)
-                quad, qx, qy, qd0, qd1 = src[side * 5:side * 5 + 5]
+                quad, qx, qy, qd = src[side * 4:side * 4 + 4]
                 for kk in range(m):
                     z = lax.rem(sc[3] - kk + m, m)
                     near = pl.ds(pl.multiple_of((2 * z + sc[4]) * piece, 16), piece)
                     far = pl.ds(pl.multiple_of((2 * z + 1 - sc[4]) * piece, 16), piece)
-                    for a, h, r, c in (
-                            (quad, sc[2], near, slice(0, HALF)), (qx, 1 - sc[2], near, slice(0, HALF)),
-                            (qy, sc[2], far, slice(0, HALF)), (qd0, 1 - sc[2], far, slice(0, half)),
-                            (qd1, 1 - sc[2], far, slice(half, HALF))):
-                        copies.append(pltpu.make_async_copy(a.at[kk], w.at[t, h, r, c], sem))
+                    for a, h, r in ((quad, sc[2], near), (qx, 1 - sc[2], near), (qy, sc[2], far), (qd, 1 - sc[2], far)):
+                        copies.append(pltpu.make_async_copy(a.at[kk], w.at[t, h, r, :], sem))
             return copies
 
         def store(sc, side, t, g, dst, sem):
@@ -466,14 +480,12 @@
 
         out_shapes = [((2, 2, m, piece, HALF), BF16)] + [((m, piece, HALF), BF16)] * 4
 
-        def spread(a):
-            quad = jnp.stack([a] + [pz(a, kk) for kk in range(1, m)])
-            qx, qy = px(quad), py(quad)
-            qd0, qd1 = px(qy[..., :half]), py(qx[..., half:])
-            mine = [quad, qx, qy, qd0, qd1]
-            return mine + [pt(b) for b in mine]
-
-        sources = [spread(a) for a in start]
+        quads = [jnp.stack([a] + [pz(a, kk) for kk in range(1, m)]) for a in start]
+        mine = [quads[0], px(quads[0]), py(quads[0]), pd(quads[0])]
+        quads[1], mine[1] = after(quads[1], mine[1])
+        sources = [mine + [pt(b) for b in mine]]
+        mine = [quads[1], px(quads[1]), py(quads[1]), pd(quads[1])]
+        sources.append(mine)
     else:
         def load(sc, src, w, sem):
             return [pltpu.make_async_copy(src[0], w, sem)]
@@ -486,25 +498,32 @@
         a = lax.all_gather(lax.all_gather(a, "tensor"), "section")
         sources = [[a[0]], [a[1]]]
 
-    def call(l, x, u, kept):
-        return layer_call(sources[l], load, store, out_shapes, scalars, x, u, kept, ff, piece)
-
-    r0 = call(0, x0, None, None)
-    r1 = call(1, r0["out"], cot, None)
-    b0 = call(0, None, r1["in"], r0["kept"])
-
+    def call(l, phases, **given):
+        return layer_call(phases, sources[l], load, store, out_shapes, scalars, given, total, width, ff, piece)
+
+    r0 = call(0, ["forward"], x=x0)
     if direct:
-        def gather_in(g):
-            theirs, keep, to_y, to_x, to_d = g
-            got = pt(theirs)
-            to_y = plus(to_y, got[0, 1]).astype(BF16)
-            to_x = plus(to_x, got[1, 0]).astype(BF16)
-            to_d = plus(to_d, got[1, 1]).astype(BF16)
-            quad = plus(keep, got[0, 0], py(to_y), px(to_x), pd(to_d))
-            low = quad.astype(BF16)
-            return plus(quad[0], *[pz(low[kk], kk) for kk in range(1, m)])
-
-        done = [gather_in(r1["g"]), gather_in(b0["g"])]
+        low0, *mine = after(r0["out"], *sources[1])
+        sources[1] = mine + [pt(b) for b in mine]
+    else:
+        low0 = r0["out"]
+    r1 = call(1, ["forward", "mlp", "attention"], x=low0, u=cot)
+    if direct:
+        got1 = pt(r1["g"][0])
+    m0 = call(0, ["mlp"], **{**r0, "u": r1["in"]})
+    if direct:
+        m0["res"], got1 = after(m0["res"], got1)
+        sent1 = add_pair(r1["g"], got1)
+        m0["res"], *sent1 = after(m0["res"], *sent1)
+        quad1 = across(sent1)
+    b0 = call(0, ["attention"], **{**r0, **m0})
+
+    if direct:
+        out0, *quad1 = after(b0["g"][0], *quad1)
+        got0 = pt(out0)
+        sent0 = add_pair(b0["g"], got0)
+        b0["in"], *sent0 = after(b0["in"], *sent0)
+        done = [along(quad1), along(across(sent0))]
         mine = jnp.where(sec == 0, done[1], done[0])
         other = px(jnp.where(sec == 0, done[0], done[1]).astype(BF16)).astype(F32)
         final0 = jnp.where(sec == 0, mine, other)

time: 248 us -> 244 us (0.984)
  starting transfers between devices: 73.8 us -> 62.2 us
  Pallas kernels: 56.4 us -> 61.5 us
    ppermute x6 -> x4, waiting for transfers between devices: 26.4 us -> 11.8 us  [py(): return lax.ppermute(a, 'dp', [(i, i ^ 1) for i in range(n_dp)])]
    ppermute x12, starting transfers between devices: 21.7 us -> 30.8 us  [pz(): lax.ppermute(a, 'dp', [(2 * z + y, 2 * ((z + k) % m) + y) for z in range(...]
    ppermute x2 -> x4, waiting for transfers between devices: 9.83 us -> 16.7 us  [pd(): lax.ppermute(a, ('section', 'dp'), [(i, (i + n_dp) % (2 * n_dp) ^ 1) for...]
    ppermute x6 -> x4, starting transfers between devices: 12.8 us -> 5.89 us  [py(): return lax.ppermute(a, 'dp', [(i, i ^ 1) for i in range(n_dp)])]
    ppermute x12, waiting for transfers between devices: 13.9 us -> 20.4 us  [pz(): lax.ppermute(a, 'dp', [(2 * z + y, 2 * ((z + k) % m) + y) for z in range(...]
    ppermute x10 -> x8, waiting for transfers between devices: 22.1 us -> 16.7 us  [px(): return lax.ppermute(a, 'section', [(0, 1), (1, 0)])]
    pallas_call x3 -> x4, Pallas kernels: 56.4 us -> 61.5 us  [layer_call(): pl.pallas_call(body, out_shape=[jax.ShapeDtypeStruct(*o) for o in outs],...]
    ppermute x2, starting transfers between devices: 12 us -> 7.04 us  [settled(): lax.ppermute(a[:, local_rows:], 'dp', [(i, i + 1) for i in range(n_dp - 1)])]
  transfers between devices with their start and end apart: 47 -> 43, of which waited for: 19 -> 22; matrix products, arithmetic and copies ran while one was open for 8% -> 10% of each run, Pallas kernels for 5% -> 15%
where the time goes in v3:
time: 244 us; the launch traced here: 243 us
  waiting for transfers between devices  79.4 us (33%)
  starting transfers between devices  62.2 us (25%)
  Pallas kernels  61.5 us (25%)
  local copies, waits for them, and re-layouts  19.4 us (8%)
  other arithmetic  12.9 us (5%)
  matrix products  5.83 us (2%)
    pallas_call x4, Pallas kernels, layer_call(): pl.pallas_call(body, out_shape=[jax.ShapeDtypeStruct(*o) for o in outs],...  61.5 us
    ppermute x12, starting transfers between devices, pz(): lax.ppermute(a, 'dp', [(2 * z + y, 2 * ((z + k) % m) + y) for z in range(...  30.8 us
    ppermute x12, waiting for transfers between devices, pz(): lax.ppermute(a, 'dp', [(2 * z + y, 2 * ((z + k) % m) + y) for z in range(...  20.4 us
    ppermute x8, waiting for transfers between devices, px(): return lax.ppermute(a, 'section', [(0, 1), (1, 0)])  16.7 us
    ppermute x4, waiting for transfers between devices, pd(): lax.ppermute(a, ('section', 'dp'), [(i, (i + n_dp) % (2 * n_dp) ^ 1) for...  16.7 us
    ppermute x4, waiting for transfers between devices, py(): return lax.ppermute(a, 'dp', [(i, i ^ 1) for i in range(n_dp)])  11.8 us
    ppermute x2, waiting for transfers between devices, settled(): lax.ppermute(a[:, local_rows:], 'dp', [(i, i + 1) for i in range(n_dp - 1)])  11.1 us
    ppermute x8, starting transfers between devices, px(): return lax.ppermute(a, 'section', [(0, 1), (1, 0)])  9.11 us
  transfers between devices with their start and end apart: 43, of which 22 were waited for; matrix products, arithmetic and copies ran while one was open for 10% of the time, Pallas kernels for 15%

profile of v3, /device:TPU:0, one launch (start us, length us, event | category | flops | bytes accessed | tf_op | source)
XLA Modules:
  0.0 243.2 jit_solution(13530548018576957474)
XLA Ops:
  3.7 0.8 fusion.70
  4.5 0.9 slice_bitcast_fusion.29
  6.4 1.0 broadcast_select_fusion.5
  7.4 3.0 %collective-permute-start.1 = (bf16[48,1280]{1,0:T(8,128)(2,1)S(1)}, bf16[48,1280]{1,0:T(8,128)(2,1)S(1)}, u32[]{:S(2)}, u32[]{:S(2)}) collective-permute-start(bf16[48,1280]{1,0:T(8,128)(2,1)S(1)} %broadcast_select_fusion.5), channel_id=1, source_target_pairs={{0,16},{16,0},{1,17},{17,1},{2,18},{18,2},{3,19},{19,3},{4,20},{20... | collective-permute-start | bytes 368648 | tf_op jit(solution)/shard_map/ppermute | solution.py:382
  10.4 3.3 %collective-permute-done.1 = bf16[48,1280]{1,0:T(8,128)(2,1)S(1)} collective-permute-done((bf16[48,1280]{1,0:T(8,128)(2,1)S(1)}, bf16[48,1280]{1,0:T(8,128)(2,1)S(1)}, u32[]{:S(2)}, u32[]{:S(2)}) %collective-permute-start.1) | collective-permute-done | bytes 122912 | tf_op jit(solution)/shard_map/ppermute | solution.py:382
  13.8 3.9 %collective-permute-start.4 = (bf16[48,1280]{1,0:T(8,128)(2,1)S(1)}, bf16[48,1280]{1,0:T(8,128)(2,1)S(1)}, u32[]{:S(2)}, u32[]{:S(2)}) collective-permute-start(bf16[48,1280]{1,0:T(8,128)(2,1)S(1)} %get-tuple-element.178), channel_id=1, source_target_pairs={{0,12},{2,14},{4,0},{6,2},{8,4},{10,6},{12,8},{14,10},{1,13},{3,15... | collective-permute-start | bytes 368648 | tf_op jit(solution)/shard_map/ppermute | solution.py:391
  17.7 1.0 collective-permute-start.2
  18.7 2.8 %collective-permute-start.7 = (bf16[48,1280]{1,0:T(8,128)(2,1)S(1)}, bf16[48,1280]{1,0:T(8,128)(2,1)S(1)}, u32[]{:S(2)}, u32[]{:S(2)}) collective-permute-start(bf16[48,1280]{1,0:T(8,128)(2,1)S(1)} %get-tuple-element.177), channel_id=1, source_target_pairs={{0,12},{2,14},{4,0},{6,2},{8,4},{10,6},{12,8},{14,10},{1,13},{3,15... | collective-permute-start | bytes 368648 | tf_op jit(solution)/shard_map/ppermute | solution.py:391
  21.5 7.2 %collective-permute-done.3 = bf16[48,1280]{1,0:T(8,128)(2,1)S(1)} collective-permute-done((bf16[48,1280]{1,0:T(8,128)(2,1)S(1)}, bf16[48,1280]{1,0:T(8,128)(2,1)S(1)}, u32[]{:S(2)}, u32[]{:S(2)}) %collective-permute-start.3) | collective-permute-done | bytes 122912 | tf_op jit(solution)/shard_map/ppermute | solution.py:391
  28.9 2.5 %collective-permute-start.10 = (bf16[4,48,1280]{2,1,0:T(8,128)(2,1)S(1)}, bf16[4,48,1280]{2,1,0:T(8,128)(2,1)}, u32[]{:S(2)}, u32[]{:S(2)}) collective-permute-start(bf16[4,48,1280]{2,1,0:T(8,128)(2,1)S(1)} %pad_maximum_fusion.3.refs_2_.refs_5_.refs_14_), channel_id=1, source_target_pairs={{0,18},{2,16},{4,22},{6,20},{8,26},{10,24},{12,30},{14,28},{16,2},... | collective-permute-start | bytes 1474568 | tf_op jit(solution)/shard_map/ppermute | solution.py:388
  32.6 4.0 %collective-permute-start.6 = (bf16[48,1280]{1,0:T(8,128)(2,1)S(1)}, bf16[48,1280]{1,0:T(8,128)(2,1)S(1)}, u32[]{:S(2)}, u32[]{:S(2)}) collective-permute-start(bf16[48,1280]{1,0:T(8,128)(2,1)S(1)} %get-tuple-element.177), channel_id=1, source_target_pairs={{0,8},{2,10},{4,12},{6,14},{8,0},{10,2},{12,4},{14,6},{1,9},{3,11}... | collective-permute-start | bytes 368648 | tf_op jit(solution)/shard_map/ppermute | solution.py:391
  38.5 5.7 %collective-permute-done.6 = bf16[48,1280]{1,0:T(8,128)(2,1)S(1)} collective-permute-done((bf16[48,1280]{1,0:T(8,128)(2,1)S(1)}, bf16[48,1280]{1,0:T(8,128)(2,1)S(1)}, u32[]{:S(2)}, u32[]{:S(2)}) %collective-permute-start.6) | collective-permute-done | bytes 122912 | tf_op jit(solution)/shard_map/ppermute | solution.py:391
  44.1 1.3 collective-permute-start
  45.6 6.4 %collective-permute-done.8.refs_3_.refs_6_.refs_15_ = bf16[4,48,1280]{2,1,0:T(8,128)(2,1)} collective-permute-done((bf16[4,48,1280]{2,1,0:T(8,128)(2,1)S(1)}, bf16[4,48,1280]{2,1,0:T(8,128)(2,1)}, u32[]{:S(2)}, u32[]{:S(2)}) %collective-permute-start.8) | collective-permute-done | bytes 491552 | tf_op jit(solution)/shard_map/ppermute | solution.py:382
  52.6 5.2 %collective-permute-done.9.refs_4_.refs_7_.refs_16_ = bf16[4,48,1280]{2,1,0:T(8,128)(2,1)} collective-permute-done((bf16[4,48,1280]{2,1,0:T(8,128)(2,1)S(1)}, bf16[4,48,1280]{2,1,0:T(8,128)(2,1)}, u32[]{:S(2)}, u32[]{:S(2)}) %collective-permute-start.9) | collective-permute-done | bytes 491552 | tf_op jit(solution)/shard_map/ppermute | solution.py:385
  57.8 0.9 collective-permute-done
  58.8 1.3 fusion.21.refs_1_
  60.1 1.9 collective-permute-start.17
  62.0 1.1 collective-permute-start.16
  64.4 0.8 copy-done.18
  65.2 12.8 %shard_map.186 = (bf16[416,384]{1,0:T(8,128)(2,1)}, f32[416,384]{1,0:T(8,128)}, f32[416,128]{1,0:T(8,128)}, bf16[416,384]{1,0:T(8,128)(2,1)}, bf16[2,416,640]{2,...) custom-call(s32[5]{0:T(128)} %stack.119.refs_0_, ...), custom_call_target="tpu_custom_call" | custom-call | flops 10000000000 | bytes 8388608 | tf_op jit(solution)/shard_map/pallas_call | solution.py:346
  78.0 6.7 %collective-permute-done.16.refs_5_ = bf16[4,48,1280]{2,1,0:T(8,128)(2,1)S(1)} collective-permute-done((bf16[4,48,1280]{2,1,0:T(8,128)(2,1)S(1)}, bf16[4,48,1280]{2,1,0:T(8,128)(2,1)S(1)}, u32[]{:S(2)}, u32[]{:S(2)}) %collective-permute-start.16) | collective-permute-done | bytes 491552 | tf_op jit(solution)/shard_map/ppermute | solution.py:385
  86.5 1.3 fusion.24.refs_2_
  89.5 0.8 copy-done.27
  90.3 24.8 %shard_map.187 = (bf16[416,384]{1,0:T(8,128)(2,1)}, f32[416,384]{1,0:T(8,128)}, f32[2,16,128]{2,1,0:T(8,128)}, bf16[2,2,4,48,1280]{4,3,2,1,0:T(8,128)(2,1)}, bf1...) custom-call(s32[5]{0:T(128)} %stack.119.refs_0_, ...), custom_call_target="tpu_custom_call" | custom-call | flops 30000001024 | bytes 8388608 | tf_op jit(solution)/shard_map/pallas_call | solution.py:346
  115.3 1.0 select_bitcast_fusion.1
  116.3 0.9 collective-permute-start.22
  117.2 7.9 %shard_map.188 = (bf16[416,384]{1,0:T(8,128)(2,1)}, bf16[416,1536]{1,0:T(8,128)(2,1)}, f32[416,384]{1,0:T(8,128)}, f32[8,384]{1,0:T(8,128)}, f32[2,16,128]{2,1,0:T(8,128)}) custom-call(s32[5]{0:T(128)} %stack.119.refs_0_, f32[416,384]{1,0:T(8,128)} %get-tuple-element.73.refs_1_, bf16[416,1536]{1,0:T(8,128)(2,1)} %get-tuple-element.74.refs_2_, ...), custom_call_target="tpu_custom_call" | custom-call | flops 10000000000 | bytes 8388608 | tf_op jit(solution)/shard_map/pallas_call | solution.py:346
  125.1 1.1 collective-permute-done.22
  126.4 0.8 fusion.12
  127.2 0.8 fusion.9
  130.0 1.2 collective-permute-start.26
  131.1 0.9 collective-permute-start.27
  132.1 1.4 collective-permute-start.28
  133.5 16.0 %shard_map.189 = (f32[416,384]{1,0:T(8,128)}, f32[2,16,128]{2,1,0:T(8,128)}, bf16[2,2,4,48,1280]{4,3,2,1,0:T(8,128)(2,1)}, bf16[4,48,1280]{2,1,0:T(8,128)(2,1)},...) custom-call(s32[5]{0:T(128)} %stack.119.refs_0_, ...), custom_call_target="tpu_custom_call" | custom-call | flops 10000000000 | bytes 8388608 | tf_op jit(solution)/shard_map/pallas_call | solution.py:346
  149.5 4.9 %collective-permute-done.28 = bf16[4,48,1280]{2,1,0:T(8,128)(2,1)S(1)} collective-permute-done((bf16[4,48,1280]{2,1,0:T(8,128)(2,1)S(1)}, bf16[4,48,1280]{2,1,0:T(8,128)(2,1)S(1)}, u32[]{:S(2)}, u32[]{:S(2)}) %collective-permute-start.28) | collective-permute-done | bytes 491552 | tf_op jit(solution)/shard_map/ppermute | solution.py:388
  154.6 3.3 %collective-permute-start.24 = (bf16[2,208,384]{2,1,0:T(8,128)(2,1)S(1)}, bf16[2,208,384]{2,1,0:T(8,128)(2,1)S(1)}, u32[]{:S(2)}, u32[]{:S(2)}) collective-permute-start(bf16[2,208,384]{2,1,0:T(8,128)(2,1)S(1)} %slice.259), channel_id=1, source_target_pairs={{0,2},{2,4},{4,6},{6,8},{8,10},{10,12},{12,14},{1,3},{3,5},{5,7},{... | collective-permute-start | bytes 958472 | tf_op jit(solution)/shard_map/ppermute | solution.py:547
  158.0 7.2 %collective-permute-done.24 = bf16[2,208,384]{2,1,0:T(8,128)(2,1)S(1)} collective-permute-done((bf16[2,208,384]{2,1,0:T(8,128)(2,1)S(1)}, bf16[2,208,384]{2,1,0:T(8,128)(2,1)S(1)}, u32[]{:S(2)}, u32[]{:S(2)}) %collective-permute-start.24) | collective-permute-done | bytes 319520 | tf_op jit(solution)/shard_map/ppermute | solution.py:547
  165.2 1.0 maximum_bitcast_fusion
  166.4 0.8 copy-done.5
  169.0 1.0 collective-permute-start.30
  170.0 3.1 %collective-permute-start.33 = (bf16[4,48,1280]{2,1,0:T(8,128)(2,1)S(1)}, bf16[4,48,1280]{2,1,0:T(8,128)(2,1)S(1)}, u32[]{:S(2)}, u32[]{:S(2)}) collective-permute-start(bf16[4,48,1280]{2,1,0:T(8,128)(2,1)S(1)} %get-tuple-element.111), channel_id=1, source_target_pairs={{0,2},{2,0},{4,6},{6,4},{8,10},{10,8},{12,14},{14,12},{1,3},{3,1},... | collective-permute-start | bytes 1474568 | tf_op jit(solution)/shard_map/ppermute | solution.py:385
  173.1 1.2 collective-permute-start.34
  174.6 4.0 %collective-permute-start.39 = (bf16[48,1280]{1,0:T(8,128)(2,1)S(1)}, bf16[48,1280]{1,0:T(8,128)(2,1)S(1)}, u32[]{:S(2)}, u32[]{:S(2)}) collective-permute-start(bf16[48,1280]{1,0:T(8,128)(2,1)S(1)} %get-tuple-element.171), channel_id=1, source_target_pairs={{0,4},{2,6},{4,8},{6,10},{8,12},{10,14},{12,0},{14,2},{1,5},{3,7},... | collective-permute-start | bytes 368648 | tf_op jit(solution)/shard_map/ppermute | solution.py:391
  178.6 0.9 collective-permute-done.30
  179.4 6.5 %collective-permute-start.41 = (bf16[48,1280]{1,0:T(8,128)(2,1)S(1)}, bf16[48,1280]{1,0:T(8,128)(2,1)S(1)}, u32[]{:S(2)}, u32[]{:S(2)}) collective-permute-start(bf16[48,1280]{1,0:T(8,128)(2,1)S(1)} %get-tuple-element.172), channel_id=1, source_target_pairs={{0,12},{2,14},{4,0},{6,2},{8,4},{10,6},{12,8},{14,10},{1,13},{3,15... | collective-permute-start | bytes 368648 | tf_op jit(solution)/shard_map/ppermute | solution.py:391
  186.0 0.8 fusion.18
  186.8 2.6 %collective-permute-start.40 = (bf16[48,1280]{1,0:T(8,128)(2,1)S(1)}, bf16[48,1280]{1,0:T(8,128)(2,1)S(1)}, u32[]{:S(2)}, u32[]{:S(2)}) collective-permute-start(bf16[48,1280]{1,0:T(8,128)(2,1)S(1)} %get-tuple-element.173), channel_id=1, source_target_pairs={{0,8},{2,10},{4,12},{6,14},{8,0},{10,2},{12,4},{14,6},{1,9},{3,11}... | collective-permute-start | bytes 368648 | tf_op jit(solution)/shard_map/ppermute | solution.py:391
  190.0 11.9 %collective-permute-done.35 = bf16[4,48,1280]{2,1,0:T(8,128)(2,1)S(1)} collective-permute-done((bf16[4,48,1280]{2,1,0:T(8,128)(2,1)S(1)}, bf16[4,48,1280]{2,1,0:T(8,128)(2,1)S(1)}, u32[]{:S(2)}, u32[]{:S(2)}) %collective-permute-start.35) | collective-permute-done | bytes 491552 | tf_op jit(solution)/shard_map/ppermute | solution.py:388
  202.1 2.6 %collective-permute-start.36 = (bf16[48,1280]{1,0:T(8,128)(2,1)S(1)}, bf16[48,1280]{1,0:T(8,128)(2,1)S(1)}, u32[]{:S(2)}, u32[]{:S(2)}) collective-permute-start(bf16[48,1280]{1,0:T(8,128)(2,1)S(1)} %get-tuple-element.174), channel_id=1, source_target_pairs={{0,4},{2,6},{4,8},{6,10},{8,12},{10,14},{12,0},{14,2},{1,5},{3,7},... | collective-permute-start | bytes 368648 | tf_op jit(solution)/shard_map/ppermute | solution.py:391
  204.7 1.3 collective-permute-start.38
  206.0 2.3 collective-permute-start.37
  208.2 0.8 fusion.15
  209.1 1.2 collective-permute-done.36
  210.6 5.9 %collective-permute-done.37 = bf16[48,1280]{1,0:T(8,128)(2,1)S(1)} collective-permute-done((bf16[48,1280]{1,0:T(8,128)(2,1)S(1)}, bf16[48,1280]{1,0:T(8,128)(2,1)S(1)}, u32[]{:S(2)}, u32[]{:S(2)}) %collective-permute-start.37) | collective-permute-done | bytes 122912 | tf_op jit(solution)/shard_map/ppermute | solution.py:391
  216.7 1.0 collective-permute-start.42
  217.8 3.7 %collective-permute-done.42 = bf16[48,1280]{1,0:T(8,128)(2,1)S(1)} collective-permute-done((bf16[48,1280]{1,0:T(8,128)(2,1)S(1)}, bf16[48,1280]{1,0:T(8,128)(2,1)S(1)}, u32[]{:S(2)}, u32[]{:S(2)}) %collective-permute-start.42) | collective-permute-done | bytes 122912 | tf_op jit(solution)/shard_map/ppermute | solution.py:382
  226.3 1.0 reshape.126
  228.0 1.4 maximum_bitcast_fusion.2
  229.4 1.6 maximum_bitcast_fusion.1
  231.7 1.6 slice_bitcast_fusion.19
  233.5 3.8 %collective-permute-start.32 = (bf16[2,208,384]{2,1,0:T(8,128)(2,1)S(1)}, bf16[2,208,384]{2,1,0:T(8,128)(2,1)S(1)}, u32[]{:S(2)}, u32[]{:S(2)}) collective-permute-start(bf16[2,208,384]{2,1,0:T(8,128)(2,1)S(1)} %slice.268), channel_id=1, source_target_pairs={{0,2},{2,4},{4,6},{6,8},{8,10},{10,12},{12,14},{1,3},{3,5},{5,7},{... | collective-permute-start | bytes 958472 | tf_op jit(solution)/shard_map/ppermute | solution.py:547
  237.9 4.0 %collective-permute-done.32 = bf16[2,208,384]{2,1,0:T(8,128)(2,1)S(1)} collective-permute-done((bf16[2,208,384]{2,1,0:T(8,128)(2,1)S(1)}, bf16[2,208,384]{2,1,0:T(8,128)(2,1)S(1)}, u32[]{:S(2)}, u32[]{:S(2)}) %collective-permute-start.32) | collective-permute-done | bytes 319520 | tf_op jit(solution)/shard_map/ppermute | solution.py:547
  241.9 1.2 maximum_convert_fusion
  (158 shorter events, 25.6 us)
Async XLA Ops:
  0.6 13.1 %copy-start.14 = (bf16[1,768,48]{1,2,0:T(8,128)(2,1)S(1)}, bf16[1,768,48]{1,2,0:T(8,128)(2,1)}, u32[]{:S(2)}) copy-start(bf16[1,768,48]{1,2,0:T(8,128)(2,1)} %param.21) | copy-start | bytes 221188
  6.2 26.2 %copy-start.15 = (bf16[2,512,384]{2,1,0:T(8,128)(2,1)S(1)}, bf16[2,512,384]{2,1,0:T(8,128)(2,1)}, u32[]{:S(2)}) copy-start(bf16[2,512,384]{2,1,0:T(8,128)(2,1)} %param.13) | copy-start | bytes 2359300
  6.2 26.2 %copy-start.16 = (bf16[2,512,384]{2,1,0:T(8,128)(2,1)S(1)}, bf16[2,512,384]{2,1,0:T(8,128)(2,1)}, u32[]{:S(2)}) copy-start(bf16[2,512,384]{2,1,0:T(8,128)(2,1)} %param.11) | copy-start | bytes 2359300
  7.4 6.4 %collective-permute-start.1 = (bf16[48,1280]{1,0:T(8,128)(2,1)S(1)}, bf16[48,1280]{1,0:T(8,128)(2,1)S(1)}, u32[]{:S(2)}, u32[]{:S(2)}) collective-permute-start(bf16[48,1280]{1,0:T(8,128)(2,1)S(1)} %broadcast_select_fusion.5), channel_id=1, source_target_pairs={{0,16},{16,0},{1,17},{17,1},{2,18},{18,2},{3,19},{19,3},{4,20},{20... | collective-permute-start | bytes 368648 | tf_op jit(solution)/shard_map/ppermute | solution.py:382
  13.8 7.7 %collective-permute-start.4 = (bf16[48,1280]{1,0:T(8,128)(2,1)S(1)}, bf16[48,1280]{1,0:T(8,128)(2,1)S(1)}, u32[]{:S(2)}, u32[]{:S(2)}) collective-permute-start(bf16[48,1280]{1,0:T(8,128)(2,1)S(1)} %get-tuple-element.178), channel_id=1, source_target_pairs={{0,12},{2,14},{4,0},{6,2},{8,4},{10,6},{12,8},{14,10},{1,13},{3,15... | collective-permute-start | bytes 368648 | tf_op jit(solution)/shard_map/ppermute | solution.py:391
  17.7 11.1 %collective-permute-start.3 = (bf16[48,1280]{1,0:T(8,128)(2,1)S(1)}, bf16[48,1280]{1,0:T(8,128)(2,1)S(1)}, u32[]{:S(2)}, u32[]{:S(2)}) collective-permute-start(bf16[48,1280]{1,0:T(8,128)(2,1)S(1)} %get-tuple-element.178), channel_id=1, source_target_pairs={{0,8},{2,10},{4,12},{6,14},{8,0},{10,2},{12,4},{14,6},{1,9},{3,11}... | collective-permute-start | bytes 368648 | tf_op jit(solution)/shard_map/ppermute | solution.py:391
  17.7 11.1 %collective-permute-start.2 = (bf16[48,1280]{1,0:T(8,128)(2,1)S(1)}, bf16[48,1280]{1,0:T(8,128)(2,1)S(1)}, u32[]{:S(2)}, u32[]{:S(2)}) collective-permute-start(bf16[48,1280]{1,0:T(8,128)(2,1)S(1)} %get-tuple-element.178), channel_id=1, source_target_pairs={{0,4},{2,6},{4,8},{6,10},{8,12},{10,14},{12,0},{14,2},{1,5},{3,7},... | collective-permute-start | bytes 368648 | tf_op jit(solution)/shard_map/ppermute | solution.py:391
  18.7 17.8 %collective-permute-start.7 = (bf16[48,1280]{1,0:T(8,128)(2,1)S(1)}, bf16[48,1280]{1,0:T(8,128)(2,1)S(1)}, u32[]{:S(2)}, u32[]{:S(2)}) collective-permute-start(bf16[48,1280]{1,0:T(8,128)(2,1)S(1)} %get-tuple-element.177), channel_id=1, source_target_pairs={{0,12},{2,14},{4,0},{6,2},{8,4},{10,6},{12,8},{14,10},{1,13},{3,15... | collective-permute-start | bytes 368648 | tf_op jit(solution)/shard_map/ppermute | solution.py:391
  28.8 7.8 %copy-start.28 = (s32[2]{0:T(128)S(1)}, s32[2]{0:T(128)}, u32[]{:S(2)}) copy-start(s32[2]{0:T(128)} %param.12) | copy-start | bytes 28
  28.8 16.6 %copy-start.3 = (bf16[4,48,1280]{2,1,0:T(8,128)(2,1)}, bf16[4,48,1280]{2,1,0:T(8,128)(2,1)S(1)}, u32[]{:S(2)}) copy-start(bf16[4,48,1280]{2,1,0:T(8,128)(2,1)S(1)} %pad_maximum_fusion.3.refs_2_.refs_5_.refs_14_) | copy-start | bytes 1474564
  28.9 23.2 %collective-permute-start.10 = (bf16[4,48,1280]{2,1,0:T(8,128)(2,1)S(1)}, bf16[4,48,1280]{2,1,0:T(8,128)(2,1)}, u32[]{:S(2)}, u32[]{:S(2)}) collective-permute-start(bf16[4,48,1280]{2,1,0:T(8,128)(2,1)S(1)} %pad_maximum_fusion.3.refs_2_.refs_5_.refs_14_), channel_id=1, source_target_pairs={{0,18},{2,16},{4,22},{6,20},{8,26},{10,24},{12,30},{14,28},{16,2},... | collective-permute-start | bytes 1474568 | tf_op jit(solution)/shard_map/ppermute | solution.py:388
  31.4 26.4 %collective-permute-start.9 = (bf16[4,48,1280]{2,1,0:T(8,128)(2,1)S(1)}, bf16[4,48,1280]{2,1,0:T(8,128)(2,1)}, u32[]{:S(2)}, u32[]{:S(2)}) collective-permute-start(bf16[4,48,1280]{2,1,0:T(8,128)(2,1)S(1)} %pad_maximum_fusion.3.refs_2_.refs_5_.refs_14_), channel_id=1, source_target_pairs={{0,2},{2,0},{4,6},{6,4},{8,10},{10,8},{12,14},{14,12},{1,3},{3,1},... | collective-permute-start | bytes 1474568 | tf_op jit(solution)/shard_map/ppermute | solution.py:385
  31.9 20.2 %collective-permute-start.8 = (bf16[4,48,1280]{2,1,0:T(8,128)(2,1)S(1)}, bf16[4,48,1280]{2,1,0:T(8,128)(2,1)}, u32[]{:S(2)}, u32[]{:S(2)}) collective-permute-start(bf16[4,48,1280]{2,1,0:T(8,128)(2,1)S(1)} %pad_maximum_fusion.3.refs_2_.refs_5_.refs_14_), channel_id=1, source_target_pairs={{0,16},{16,0},{1,17},{17,1},{2,18},{18,2},{3,19},{19,3},{4,20},{20... | collective-permute-start | bytes 1474568 | tf_op jit(solution)/shard_map/ppermute | solution.py:382
  32.6 11.6 %collective-permute-start.6 = (bf16[48,1280]{1,0:T(8,128)(2,1)S(1)}, bf16[48,1280]{1,0:T(8,128)(2,1)S(1)}, u32[]{:S(2)}, u32[]{:S(2)}) collective-permute-start(bf16[48,1280]{1,0:T(8,128)(2,1)S(1)} %get-tuple-element.177), channel_id=1, source_target_pairs={{0,8},{2,10},{4,12},{6,14},{8,0},{10,2},{12,4},{14,6},{1,9},{3,11}... | collective-permute-start | bytes 368648 | tf_op jit(solution)/shard_map/ppermute | solution.py:391
  36.5 8.9 %collective-permute-start.5 = (bf16[48,1280]{1,0:T(8,128)(2,1)S(1)}, bf16[48,1280]{1,0:T(8,128)(2,1)S(1)}, u32[]{:S(2)}, u32[]{:S(2)}) collective-permute-start(bf16[48,1280]{1,0:T(8,128)(2,1)S(1)} %get-tuple-element.177), channel_id=1, source_target_pairs={{0,4},{2,6},{4,8},{6,10},{8,12},{10,14},{12,0},{14,2},{1,5},{3,7},... | collective-permute-start | bytes 368648 | tf_op jit(solution)/shard_map/ppermute | solution.py:391
  44.1 14.6 %collective-permute-start = (bf16[2,208,384]{2,1,0:T(8,128)(2,1)S(1)}, bf16[2,208,384]{2,1,0:T(8,128)(2,1)S(1)}, u32[]{:S(2)}, u32[]{:S(2)}) collective-permute-start(bf16[2,208,384]{2,1,0:T(8,128)(2,1)S(1)} %pad_maximum_fusion.5), channel_id=1, source_target_pairs={{2,0},{4,2},{6,4},{8,6},{10,8},{12,10},{14,12},{3,1},{5,3},{7,5},{... | collective-permute-start | bytes 958472 | tf_op jit(solution)/shard_map/ppermute | solution.py:431
  45.4 16.6 %collective-permute-start.11 = (bf16[4,48,1280]{2,1,0:T(8,128)(2,1)S(1)}, bf16[4,48,1280]{2,1,0:T(8,128)(2,1)S(1)}, u32[]{:S(2)}, u32[]{:S(2)}) collective-permute-start(bf16[4,48,1280]{2,1,0:T(8,128)(2,1)S(1)} %pad_maximum_fusion.3.refs_2_.refs_5_.refs_14_), channel_id=1, source_target_pairs={{0,1},{1,0},{2,3},{3,2},{4,5},{5,4},{6,7},{7,6},{8,9},{9,8},{10,11... | collective-permute-start | bytes 1474568 | tf_op jit(solution)/shard_map/ppermute | solution.py:379
  45.6 39.8 %copy-start.4 = (bf16[4,48,1280]{2,1,0:T(8,128)(2,1)}, bf16[4,48,1280]{2,1,0:T(8,128)(2,1)S(1)}, u32[]{:S(2)}) copy-start(bf16[4,48,1280]{2,1,0:T(8,128)(2,1)S(1)} %pad_maximum_fusion.4.refs_3_) | copy-start | bytes 1474564
  52.0 11.6 %collective-permute-start.12 = (bf16[4,48,1280]{2,1,0:T(8,128)(2,1)}, bf16[4,48,1280]{2,1,0:T(8,128)(2,1)S(1)}, u32[]{:S(2)}, u32[]{:S(2)}) collective-permute-start(bf16[4,48,1280]{2,1,0:T(8,128)(2,1)} %collective-permute-done.8.refs_3_.refs_6_.refs_15_), channel_id=1, source_target_pairs={{0,1},{1,0},{2,3},{3,2},{4,5},{5,4},{6,7},{7,6},{8,9},{9,8},{10,11... | collective-permute-start | bytes 1474568 | tf_op jit(solution)/shard_map/ppermute | solution.py:379
  52.1 11.0 %collective-permute-start.14 = (bf16[4,48,1280]{2,1,0:T(8,128)(2,1)}, bf16[4,48,1280]{2,1,0:T(8,128)(2,1)S(1)}, u32[]{:S(2)}, u32[]{:S(2)}) collective-permute-start(bf16[4,48,1280]{2,1,0:T(8,128)(2,1)} %collective-permute-done.10.refs_5_.refs_8_.refs_17_), channel_id=1, source_target_pairs={{0,1},{1,0},{2,3},{3,2},{4,5},{5,4},{6,7},{7,6},{8,9},{9,8},{10,11... | collective-permute-start | bytes 1474568 | tf_op jit(solution)/shard_map/ppermute | solution.py:379
  57.7 5.9 %collective-permute-start.13 = (bf16[4,48,1280]{2,1,0:T(8,128)(2,1)}, bf16[4,48,1280]{2,1,0:T(8,128)(2,1)S(1)}, u32[]{:S(2)}, u32[]{:S(2)}) collective-permute-start(bf16[4,48,1280]{2,1,0:T(8,128)(2,1)} %collective-permute-done.9.refs_4_.refs_7_.refs_16_), channel_id=1, source_target_pairs={{0,1},{1,0},{2,3},{3,2},{4,5},{5,4},{6,7},{7,6},{8,9},{9,8},{10,11... | collective-permute-start | bytes 1474568 | tf_op jit(solution)/shard_map/ppermute | solution.py:379
  60.1 17.9 %collective-permute-start.17 = (bf16[4,48,1280]{2,1,0:T(8,128)(2,1)S(1)}, bf16[4,48,1280]{2,1,0:T(8,128)(2,1)S(1)}, u32[]{:S(2)}, u32[]{:S(2)}) collective-permute-start(bf16[4,48,1280]{2,1,0:T(8,128)(2,1)S(1)} %pad_maximum_fusion.4.refs_3_), channel_id=1, source_target_pairs={{0,18},{2,16},{4,22},{6,20},{8,26},{10,24},{12,30},{14,28},{16,2},... | collective-permute-start | bytes 1474568 | tf_op jit(solution)/shard_map/ppermute | solution.py:388
  62.0 1.6 copy-start.17
  62.0 22.7 %collective-permute-start.16 = (bf16[4,48,1280]{2,1,0:T(8,128)(2,1)S(1)}, bf16[4,48,1280]{2,1,0:T(8,128)(2,1)S(1)}, u32[]{:S(2)}, u32[]{:S(2)}) collective-permute-start(bf16[4,48,1280]{2,1,0:T(8,128)(2,1)S(1)} %pad_maximum_fusion.4.refs_3_), channel_id=1, source_target_pairs={{0,2},{2,0},{4,6},{6,4},{8,10},{10,8},{12,14},{14,12},{1,3},{3,1},... | collective-permute-start | bytes 1474568 | tf_op jit(solution)/shard_map/ppermute | solution.py:385
  63.1 22.3 %collective-permute-start.15 = (bf16[4,48,1280]{2,1,0:T(8,128)(2,1)S(1)}, bf16[4,48,1280]{2,1,0:T(8,128)(2,1)S(1)}, u32[]{:S(2)}, u32[]{:S(2)}) collective-permute-start(bf16[4,48,1280]{2,1,0:T(8,128)(2,1)S(1)} %pad_maximum_fusion.4.refs_3_), channel_id=1, source_target_pairs={{0,16},{16,0},{1,17},{17,1},{2,18},{18,2},{3,19},{19,3},{4,20},{20... | collective-permute-start | bytes 1474568 | tf_op jit(solution)/shard_map/ppermute | solution.py:382
  78.0 11.4 %copy-start.21 = (bf16[4,48,1280]{2,1,0:T(8,128)(2,1)}, bf16[4,48,1280]{2,1,0:T(8,128)(2,1)S(1)}, u32[]{:S(2)}) copy-start(bf16[4,48,1280]{2,1,0:T(8,128)(2,1)S(1)} %collective-permute-done.17.refs_6_) | copy-start | bytes 1474564
  84.7 4.7 %copy-start.22 = (bf16[4,48,1280]{2,1,0:T(8,128)(2,1)}, bf16[4,48,1280]{2,1,0:T(8,128)(2,1)S(1)}, u32[]{:S(2)}) copy-start(bf16[4,48,1280]{2,1,0:T(8,128)(2,1)S(1)} %collective-permute-done.16.refs_5_) | copy-start | bytes 1474564
  85.4 4.0 %copy-start.23 = (bf16[4,48,1280]{2,1,0:T(8,128)(2,1)}, bf16[4,48,1280]{2,1,0:T(8,128)(2,1)S(1)}, u32[]{:S(2)}) copy-start(bf16[4,48,1280]{2,1,0:T(8,128)(2,1)S(1)} %collective-permute-done.15.refs_4_) | copy-start | bytes 1474564
  85.4 2.3 collective-permute-start.18
  85.4 2.6 %collective-permute-start.19 = (bf16[4,48,1280]{2,1,0:T(8,128)(2,1)S(1)}, bf16[4,48,1280]{2,1,0:T(8,128)(2,1)S(1)}, u32[]{:S(2)}, u32[]{:S(2)}) collective-permute-start(bf16[4,48,1280]{2,1,0:T(8,128)(2,1)S(1)} %collective-permute-done.15.refs_4_), channel_id=1, source_target_pairs={{0,1},{1,0},{2,3},{3,2},{4,5},{5,4},{6,7},{7,6},{8,9},{9,8},{10,11... | collective-permute-start | bytes 1474568 | tf_op jit(solution)/shard_map/ppermute | solution.py:379
  85.9 2.8 %collective-permute-start.20 = (bf16[4,48,1280]{2,1,0:T(8,128)(2,1)S(1)}, bf16[4,48,1280]{2,1,0:T(8,128)(2,1)S(1)}, u32[]{:S(2)}, u32[]{:S(2)}) collective-permute-start(bf16[4,48,1280]{2,1,0:T(8,128)(2,1)S(1)} %collective-permute-done.16.refs_5_), channel_id=1, source_target_pairs={{0,1},{1,0},{2,3},{3,2},{4,5},{5,4},{6,7},{7,6},{8,9},{9,8},{10,11... | collective-permute-start | bytes 1474568 | tf_op jit(solution)/shard_map/ppermute | solution.py:379
  86.0 3.4 %collective-permute-start.21 = (bf16[4,48,1280]{2,1,0:T(8,128)(2,1)S(1)}, bf16[4,48,1280]{2,1,0:T(8,128)(2,1)S(1)}, u32[]{:S(2)}, u32[]{:S(2)}) collective-permute-start(bf16[4,48,1280]{2,1,0:T(8,128)(2,1)S(1)} %collective-permute-done.17.refs_6_), channel_id=1, source_target_pairs={{0,1},{1,0},{2,3},{3,2},{4,5},{5,4},{6,7},{7,6},{8,9},{9,8},{10,11... | collective-permute-start | bytes 1474568 | tf_op jit(solution)/shard_map/ppermute | solution.py:379
  87.7 27.6 %copy-start.13 = (bf16[416,384]{1,0:T(8,128)(2,1)S(1)}, bf16[416,384]{1,0:T(8,128)(2,1)}, u32[]{:S(2)}) copy-start(bf16[416,384]{1,0:T(8,128)(2,1)} %get-tuple-element.67.refs_1_) | copy-start | bytes 958468
  87.7 1.7 copy-start.24
  88.0 1.4 copy-start.25
  115.1 13.1 %collective-permute-start.25 = (bf16[2,2,4,48,1280]{4,3,2,1,0:T(8,128)(2,1)}, bf16[2,2,4,48,1280]{4,3,2,1,0:T(8,128)(2,1)S(1)}, u32[]{:S(2)}, u32[]{:S(2)}) collective-permute-start(bf16[2,2,4,48,1280]{4,3,2,1,0:T(8,128)(2,1)} %get-tuple-element.80), channel_id=1, source_target_pairs={{0,1},{1,0},{2,3},{3,2},{4,5},{5,4},{6,7},{7,6},{8,9},{9,8},{10,11... | collective-permute-start | bytes 5898248 | tf_op jit(solution)/shard_map/ppermute | solution.py:379
  116.3 9.9 %collective-permute-start.22 = (bf16[416,384]{1,0:T(8,128)(2,1)S(1)}, bf16[416,384]{1,0:T(8,128)(2,1)S(1)}, u32[]{:S(2)}, u32[]{:S(2)}) collective-permute-start(bf16[416,384]{1,0:T(8,128)(2,1)S(1)} %get-tuple-element.168), channel_id=1, source_target_pairs={{0,16},{16,0},{1,17},{17,1},{2,18},{18,2},{3,19},{19,3},{4,20},{20... | collective-permute-start | bytes 958472 | tf_op jit(solution)/shard_map/ppermute | solution.py:382
  128.0 1.2 copy-start.10
  128.0 1.3 copy-start.11
  128.0 1.5 copy-start.12
  128.2 26.2 %collective-permute-start.23 = (bf16[2,720,384]{2,1,0:T(8,128)(2,1)S(1)}, bf16[2,720,384]{2,1,0:T(8,128)(2,1)S(1)}, u32[]{:S(2)}, u32[]{:S(2)}) collective-permute-start(bf16[2,720,384]{2,1,0:T(8,128)(2,1)S(1)} %pad_maximum_fusion.1), channel_id=1, source_target_pairs={{0,1},{1,0},{2,3},{3,2},{4,5},{5,4},{6,7},{7,6},{8,9},{9,8},{10,11... | collective-permute-start | bytes 3317768 | tf_op jit(solution)/shard_map/ppermute | solution.py:379
  130.0 19.5 %collective-permute-start.26 = (bf16[4,48,1280]{2,1,0:T(8,128)(2,1)S(1)}, bf16[4,48,1280]{2,1,0:T(8,128)(2,1)S(1)}, u32[]{:S(2)}, u32[]{:S(2)}) collective-permute-start(bf16[4,48,1280]{2,1,0:T(8,128)(2,1)S(1)} %get-tuple-element.102), channel_id=1, source_target_pairs={{0,2},{2,0},{4,6},{6,4},{8,10},{10,8},{12,14},{14,12},{1,3},{3,1},... | collective-permute-start | bytes 1474568 | tf_op jit(solution)/shard_map/ppermute | solution.py:385
  131.1 18.4 %collective-permute-start.27 = (bf16[4,48,1280]{2,1,0:T(8,128)(2,1)S(1)}, bf16[4,48,1280]{2,1,0:T(8,128)(2,1)S(1)}, u32[]{:S(2)}, u32[]{:S(2)}) collective-permute-start(bf16[4,48,1280]{2,1,0:T(8,128)(2,1)S(1)} %get-tuple-element.103), channel_id=1, source_target_pairs={{0,16},{16,0},{1,17},{17,1},{2,18},{18,2},{3,19},{19,3},{4,20},{20... | collective-permute-start | bytes 1474568 | tf_op jit(solution)/shard_map/ppermute | solution.py:382
  132.1 22.3 %collective-permute-start.28 = (bf16[4,48,1280]{2,1,0:T(8,128)(2,1)S(1)}, bf16[4,48,1280]{2,1,0:T(8,128)(2,1)S(1)}, u32[]{:S(2)}, u32[]{:S(2)}) collective-permute-start(bf16[4,48,1280]{2,1,0:T(8,128)(2,1)S(1)} %get-tuple-element.104), channel_id=1, source_target_pairs={{0,18},{2,16},{4,22},{6,20},{8,26},{10,24},{12,30},{14,28},{16,2},... | collective-permute-start | bytes 1474568 | tf_op jit(solution)/shard_map/ppermute | solution.py:388
  154.4 12.0 %collective-permute-start.29 = (bf16[2,2,4,48,1280]{4,3,2,1,0:T(8,128)(2,1)}, bf16[2,2,4,48,1280]{4,3,2,1,0:T(8,128)(2,1)S(1)}, u32[]{:S(2)}, u32[]{:S(2)}) collective-permute-start(bf16[2,2,4,48,1280]{4,3,2,1,0:T(8,128)(2,1)} %get-tuple-element.105), channel_id=1, source_target_pairs={{0,1},{1,0},{2,3},{3,2},{4,5},{5,4},{6,7},{7,6},{8,9},{9,8},{10,11... | collective-permute-start | bytes 5898248 | tf_op jit(solution)/shard_map/ppermute | solution.py:379
  154.6 10.5 %collective-permute-start.24 = (bf16[2,208,384]{2,1,0:T(8,128)(2,1)S(1)}, bf16[2,208,384]{2,1,0:T(8,128)(2,1)S(1)}, u32[]{:S(2)}, u32[]{:S(2)}) collective-permute-start(bf16[2,208,384]{2,1,0:T(8,128)(2,1)S(1)} %slice.259), channel_id=1, source_target_pairs={{0,2},{2,4},{4,6},{6,8},{8,10},{10,12},{12,14},{1,3},{3,5},{5,7},{... | collective-permute-start | bytes 958472 | tf_op jit(solution)/shard_map/ppermute | solution.py:547
  166.1 1.2 copy-start.6
  166.1 1.3 copy-start.7
  166.1 1.5 copy-start.8
  167.6 1.3 copy-start.2
  169.0 10.5 %collective-permute-start.30 = (bf16[416,384]{1,0:T(8,128)(2,1)S(1)}, bf16[416,384]{1,0:T(8,128)(2,1)S(1)}, u32[]{:S(2)}, u32[]{:S(2)}) collective-permute-start(bf16[416,384]{1,0:T(8,128)(2,1)S(1)} %get-tuple-element.166), channel_id=1, source_target_pairs={{0,16},{16,0},{1,17},{17,1},{2,18},{18,2},{3,19},{19,3},{4,20},{20... | collective-permute-start | bytes 958472 | tf_op jit(solution)/shard_map/ppermute | solution.py:382
  170.0 16.9 %collective-permute-start.33 = (bf16[4,48,1280]{2,1,0:T(8,128)(2,1)S(1)}, bf16[4,48,1280]{2,1,0:T(8,128)(2,1)S(1)}, u32[]{:S(2)}, u32[]{:S(2)}) collective-permute-start(bf16[4,48,1280]{2,1,0:T(8,128)(2,1)S(1)} %get-tuple-element.111), channel_id=1, source_target_pairs={{0,2},{2,0},{4,6},{6,4},{8,10},{10,8},{12,14},{14,12},{1,3},{3,1},... | collective-permute-start | bytes 1474568 | tf_op jit(solution)/shard_map/ppermute | solution.py:385
  173.1 16.9 %collective-permute-start.34 = (bf16[4,48,1280]{2,1,0:T(8,128)(2,1)S(1)}, bf16[4,48,1280]{2,1,0:T(8,128)(2,1)S(1)}, u32[]{:S(2)}, u32[]{:S(2)}) collective-permute-start(bf16[4,48,1280]{2,1,0:T(8,128)(2,1)S(1)} %get-tuple-element.112), channel_id=1, source_target_pairs={{0,16},{16,0},{1,17},{17,1},{2,18},{18,2},{3,19},{19,3},{4,20},{20... | collective-permute-start | bytes 1474568 | tf_op jit(solution)/shard_map/ppermute | solution.py:382
  174.3 27.6 %collective-permute-start.35 = (bf16[4,48,1280]{2,1,0:T(8,128)(2,1)S(1)}, bf16[4,48,1280]{2,1,0:T(8,128)(2,1)S(1)}, u32[]{:S(2)}, u32[]{:S(2)}) collective-permute-start(bf16[4,48,1280]{2,1,0:T(8,128)(2,1)S(1)} %get-tuple-element.113), channel_id=1, source_target_pairs={{0,18},{2,16},{4,22},{6,20},{8,26},{10,24},{12,30},{14,28},{16,2},... | collective-permute-start | bytes 1474568 | tf_op jit(solution)/shard_map/ppermute | solution.py:388
  174.6 31.4 %collective-permute-start.39 = (bf16[48,1280]{1,0:T(8,128)(2,1)S(1)}, bf16[48,1280]{1,0:T(8,128)(2,1)S(1)}, u32[]{:S(2)}, u32[]{:S(2)}) collective-permute-start(bf16[48,1280]{1,0:T(8,128)(2,1)S(1)} %get-tuple-element.171), channel_id=1, source_target_pairs={{0,4},{2,6},{4,8},{6,10},{8,12},{10,14},{12,0},{14,2},{1,5},{3,7},... | collective-permute-start | bytes 368648 | tf_op jit(solution)/shard_map/ppermute | solution.py:391
  179.4 29.6 %collective-permute-start.41 = (bf16[48,1280]{1,0:T(8,128)(2,1)S(1)}, bf16[48,1280]{1,0:T(8,128)(2,1)S(1)}, u32[]{:S(2)}, u32[]{:S(2)}) collective-permute-start(bf16[48,1280]{1,0:T(8,128)(2,1)S(1)} %get-tuple-element.172), channel_id=1, source_target_pairs={{0,12},{2,14},{4,0},{6,2},{8,4},{10,6},{12,8},{14,10},{1,13},{3,15... | collective-permute-start | bytes 368648 | tf_op jit(solution)/shard_map/ppermute | solution.py:391
  186.8 22.2 %collective-permute-start.40 = (bf16[48,1280]{1,0:T(8,128)(2,1)S(1)}, bf16[48,1280]{1,0:T(8,128)(2,1)S(1)}, u32[]{:S(2)}, u32[]{:S(2)}) collective-permute-start(bf16[48,1280]{1,0:T(8,128)(2,1)S(1)} %get-tuple-element.173), channel_id=1, source_target_pairs={{0,8},{2,10},{4,12},{6,14},{8,0},{10,2},{12,4},{14,6},{1,9},{3,11}... | collective-permute-start | bytes 368648 | tf_op jit(solution)/shard_map/ppermute | solution.py:391
  202.1 8.2 %collective-permute-start.36 = (bf16[48,1280]{1,0:T(8,128)(2,1)S(1)}, bf16[48,1280]{1,0:T(8,128)(2,1)S(1)}, u32[]{:S(2)}, u32[]{:S(2)}) collective-permute-start(bf16[48,1280]{1,0:T(8,128)(2,1)S(1)} %get-tuple-element.174), channel_id=1, source_target_pairs={{0,4},{2,6},{4,8},{6,10},{8,12},{10,14},{12,0},{14,2},{1,5},{3,7},... | collective-permute-start | bytes 368648 | tf_op jit(solution)/shard_map/ppermute | solution.py:391
  204.7 5.9 %collective-permute-start.38 = (bf16[48,1280]{1,0:T(8,128)(2,1)S(1)}, bf16[48,1280]{1,0:T(8,128)(2,1)S(1)}, u32[]{:S(2)}, u32[]{:S(2)}) collective-permute-start(bf16[48,1280]{1,0:T(8,128)(2,1)S(1)} %get-tuple-element.175), channel_id=1, source_target_pairs={{0,12},{2,14},{4,0},{6,2},{8,4},{10,6},{12,8},{14,10},{1,13},{3,15... | collective-permute-start | bytes 368648 | tf_op jit(solution)/shard_map/ppermute | solution.py:391
  206.0 10.6 %collective-permute-start.37 = (bf16[48,1280]{1,0:T(8,128)(2,1)S(1)}, bf16[48,1280]{1,0:T(8,128)(2,1)S(1)}, u32[]{:S(2)}, u32[]{:S(2)}) collective-permute-start(bf16[48,1280]{1,0:T(8,128)(2,1)S(1)} %get-tuple-element.176), channel_id=1, source_target_pairs={{0,8},{2,10},{4,12},{6,14},{8,0},{10,2},{12,4},{14,6},{1,9},{3,11}... | collective-permute-start | bytes 368648 | tf_op jit(solution)/shard_map/ppermute | solution.py:391
  216.7 4.9 %collective-permute-start.42 = (bf16[48,1280]{1,0:T(8,128)(2,1)S(1)}, bf16[48,1280]{1,0:T(8,128)(2,1)S(1)}, u32[]{:S(2)}, u32[]{:S(2)}) collective-permute-start(bf16[48,1280]{1,0:T(8,128)(2,1)S(1)} %get-tuple-element.150), channel_id=1, source_target_pairs={{0,16},{16,0},{1,17},{17,1},{2,18},{18,2},{3,19},{19,3},{4,20},{20... | collective-permute-start | bytes 368648 | tf_op jit(solution)/shard_map/ppermute | solution.py:382
  217.8 15.5 %collective-permute-start.31 = (bf16[2,720,384]{2,1,0:T(8,128)(2,1)S(1)}, bf16[2,720,384]{2,1,0:T(8,128)(2,1)S(1)}, u32[]{:S(2)}, u32[]{:S(2)}) collective-permute-start(bf16[2,720,384]{2,1,0:T(8,128)(2,1)S(1)} %pad_maximum_fusion.2), channel_id=1, source_target_pairs={{0,1},{1,0},{2,3},{3,2},{4,5},{5,4},{6,7},{7,6},{8,9},{9,8},{10,11... | collective-permute-start | bytes 3317768 | tf_op jit(solution)/shard_map/ppermute | solution.py:379
  221.6 2.1 copy-start
  233.5 8.4 %collective-permute-start.32 = (bf16[2,208,384]{2,1,0:T(8,128)(2,1)S(1)}, bf16[2,208,384]{2,1,0:T(8,128)(2,1)S(1)}, u32[]{:S(2)}, u32[]{:S(2)}) collective-permute-start(bf16[2,208,384]{2,1,0:T(8,128)(2,1)S(1)} %slice.268), channel_id=1, source_target_pairs={{0,2},{2,4},{4,6},{6,8},{8,10},{10,12},{12,14},{1,3},{3,5},{5,7},{... | collective-permute-start | bytes 958472 | tf_op jit(solution)/shard_map/ppermute | solution.py:547
  (8 other events, 7.1 us)

commit v4 on v3

--- a/solution.py
+++ b/solution.py
@@ -408,6 +408,24 @@
         low = quad.astype(BF16)
         return plus(quad[0], *[pz(low[kk], kk) for kk in range(1, m)])
 
+    def pn(a, flip):
+        other = n_dp if flip else 0
+        pairs = [(i, (i + other) % (2 * n_dp) + 1) for i in range(2 * n_dp) if i % n_dp < n_dp - 1]
+        return lax.ppermute(a, ("section", "dp"), pairs)
+
+    def send_rows(a0, a1):
+        keep, give = jnp.where(sec == 0, a0, a1), jnp.where(sec == 0, a1, a0)
+        tail = select[:, local_rows:]
+        return [keep, px(give), pn(tn(tail, keep).astype(BF16), False), pn(tn(tail, give).astype(BF16), True)]
+
+    def place_rows(keep, got, tail, got_tail):
+        def place(a, b):
+            a = tn(select[:, :local_rows], a).astype(BF16)
+            return jnp.concatenate([a[:IMG_PAD] + b, a[IMG_PAD:]], 0)
+
+        near, far = place(keep, tail), place(got, got_tail)
+        return jnp.where(sec == 0, jnp.stack([near, far]), jnp.stack([far, near]))
+
     batch_tokens = lax.dynamic_index_in_dim(tokens, sec, 0, keepdims=False)
     batch_cot = lax.dynamic_index_in_dim(cotangent, sec, 0, keepdims=False)
     count = lax.dynamic_index_in_dim(image_counts, sec, 0, keepdims=False)
@@ -429,10 +447,6 @@
 
     both = jnp.stack([batch_tokens, batch_cot])
     halo = lax.ppermute(both[:, :IMG_PAD], "dp", [(i + 1, i) for i in range(n_dp - 1)])
-    both = jnp.concatenate([both, halo], 1)
-    x0 = nn(select, both[0]).astype(BF16)
-    cot = nn(select, both[1]).astype(BF16)
-
     q, k, v = [[qkv_weight[0, :, i, h * HD:(h + 1) * HD] for h in range(3)] for i in range(3)]
     o = out_weight[0].T
     o = [o[:, h * HD:(h + 1) * HD] for h in range(3)]
@@ -449,6 +463,7 @@
     if direct:
         keep = jnp.where(sec == 0, part0, part1)
         give = jnp.where(sec == 0, part1, part0)
+        give, halo = after(give, halo)
         got = px(give)
         start = [jnp.where(sec == 0, keep, got), jnp.where(sec == 0, got, keep)]
 
@@ -498,6 +513,10 @@
         a = lax.all_gather(lax.all_gather(a, "tensor"), "section")
         sources = [[a[0]], [a[1]]]
 
+    both = jnp.concatenate([both, halo], 1)
+    x0 = nn(select, both[0]).astype(BF16)
+    cot = nn(select, both[1]).astype(BF16)
+
     def call(l, phases, **given):
         return layer_call(phases, sources[l], load, store, out_shapes, scalars, given, total, width, ff, piece)
 
@@ -510,26 +529,40 @@
     r1 = call(1, ["forward", "mlp", "attention"], x=low0, u=cot)
     if direct:
         got1 = pt(r1["g"][0])
+    rows = send_rows(r0["out"], r1["out"])
     m0 = call(0, ["mlp"], **{**r0, "u": r1["in"]})
     if direct:
+        m0["res"], *rows = after(m0["res"], *rows)
         m0["res"], got1 = after(m0["res"], got1)
         sent1 = add_pair(r1["g"], got1)
-        m0["res"], *sent1 = after(m0["res"], *sent1)
+        placed = place_rows(*rows)
+        m0["res"], placed, *sent1 = after(m0["res"], placed, *sent1)
+        other_core = pt(placed)
         quad1 = across(sent1)
+    else:
+        placed = place_rows(*rows)
+        other_core = pt(placed)
     b0 = call(0, ["attention"], **{**r0, **m0})
+    layer_outputs = (placed + other_core)[None]
 
     if direct:
         out0, *quad1 = after(b0["g"][0], *quad1)
         got0 = pt(out0)
+        rows = send_rows(b0["in"].astype(BF16), r1["in"].astype(BF16))
+        got0, *rows = after(got0, *rows)
+        placed = place_rows(*rows)
         sent0 = add_pair(b0["g"], got0)
-        b0["in"], *sent0 = after(b0["in"], *sent0)
-        done = [along(quad1), along(across(sent0))]
+        placed, *sent0 = after(placed, *sent0)
+        other_core, *quad0 = after(pt(placed), *across(sent0))
+        done = [along(quad1), along(quad0)]
         mine = jnp.where(sec == 0, done[1], done[0])
         other = px(jnp.where(sec == 0, done[0], done[1]).astype(BF16)).astype(F32)
         final0 = jnp.where(sec == 0, mine, other)
         final1 = jnp.where(sec == 0, other, mine)
         small = final1[:, ROWSB:]
     else:
+        placed = place_rows(*send_rows(b0["in"].astype(BF16), r1["in"].astype(BF16)))
+        other_core = pt(placed)
         g = jnp.stack([b0["g"][0], r1["g"][0]])
         g = lax.psum_scatter(g.astype(F32), "section", scatter_dimension=0)
         g = lax.psum_scatter(g, "tensor", scatter_dimension=0)
@@ -538,17 +571,7 @@
         small = lax.psum(jnp.stack([b0["bias"], r1["bias"]]), ("section", "tensor", "dp"))
         small = lax.dynamic_index_in_dim(lax.dynamic_index_in_dim(small, sec, 0, False), ten, 0, False)
 
-    def settled(a0, a1):
-        keep = jnp.where(sec == 0, a0, a1)
-        got = px(jnp.where(sec == 0, a1, a0))
-        a = jnp.where(sec == 0, jnp.stack([keep, got]), jnp.stack([got, keep]))
-        a = jnp.stack([tn(select, a[0]), tn(select, a[1])]).astype(BF16)
-        a = a + pt(a)
-        spill = lax.ppermute(a[:, local_rows:], "dp", [(i, i + 1) for i in range(n_dp - 1)])
-        return jnp.concatenate([a[:, :IMG_PAD] + spill, a[:, IMG_PAD:local_rows]], 1)
-
-    layer_outputs = settled(r0["out"], r1["out"])[None]
-    input_grads = settled(b0["in"].astype(BF16), r1["in"].astype(BF16)).astype(F32)[None]
+    input_grads = (placed + other_core).astype(F32)[None]
 
     def heads(*starts):
         return [final0[:, s * HD:(s + 1) * HD] for s in starts]

time: 244 us -> 230 us (0.943)
  local copies, waits for them, and re-layouts: 19.4 us -> 11.6 us
  starting transfers between devices: 62.2 us -> 55.4 us
  waiting for transfers between devices: 79.4 us -> 83.1 us
  other arithmetic: 12.9 us -> 9.44 us
    ppermute x12, starting transfers between devices: 30.8 us -> 18.3 us  [pz(): lax.ppermute(a, 'dp', [(2 * z + y, 2 * ((z + k) % m) + y) for z in range(...]
    ppermute x4, waiting for transfers between devices: 11.8 us -> 22.8 us  [py(): return lax.ppermute(a, 'dp', [(i, i ^ 1) for i in range(n_dp)])]
    ppermute x1, waiting for transfers between devices: 0.93 us -> 10.5 us  [shards(): lax.ppermute(both[:, :IMG_PAD], 'dp', [(i + 1, i) for i in range(n_dp - 1)])]
    ppermute x8, waiting for transfers between devices: 16.7 us -> 7.36 us  [px(): return lax.ppermute(a, 'section', [(0, 1), (1, 0)])]
    ppermute x2 -> x4, starting transfers between devices: 7.04 us -> 15.2 us  [pn(): return lax.ppermute(a, ('section', 'dp'), pairs)]
    ppermute x2 -> x4, waiting for transfers between devices: 11.1 us -> 6.97 us  [pn(): return lax.ppermute(a, ('section', 'dp'), pairs)]
    ppermute x4, starting transfers between devices: 6.11 us -> 2.49 us  [pd(): lax.ppermute(a, ('section', 'dp'), [(i, (i + n_dp) % (2 * n_dp) ^ 1) for...]
    ppermute x12, waiting for transfers between devices: 20.4 us -> 16.8 us  [pz(): lax.ppermute(a, 'dp', [(2 * z + y, 2 * ((z + k) % m) + y) for z in range(...]
  transfers between devices with their start and end apart: 43 -> 45, of which waited for: 22 -> 23; matrix products, arithmetic and copies ran while one was open for 10% -> 6% of each run, Pallas kernels for 15% -> 16%
where the time goes in v4:
time: 230 us; the launch traced here: 229 us
  waiting for transfers between devices  83.1 us (36%)
  Pallas kernels  61.6 us (27%)
  starting transfers between devices  55.4 us (24%)
  local copies, waits for them, and re-layouts  11.6 us (5%)
  other arithmetic  9.44 us (4%)
  matrix products  5.96 us (3%)
    pallas_call x4, Pallas kernels, layer_call(): pl.pallas_call(body, out_shape=[jax.ShapeDtypeStruct(*o) for o in outs],...  61.6 us
    ppermute x4, waiting for transfers between devices, py(): return lax.ppermute(a, 'dp', [(i, i ^ 1) for i in range(n_dp)])  22.8 us
    ppermute x12, starting transfers between devices, pz(): lax.ppermute(a, 'dp', [(2 * z + y, 2 * ((z + k) % m) + y) for z in range(...  18.3 us
    ppermute x4, waiting for transfers between devices, pd(): lax.ppermute(a, ('section', 'dp'), [(i, (i + n_dp) % (2 * n_dp) ^ 1) for...  17.3 us
    ppermute x12, waiting for transfers between devices, pz(): lax.ppermute(a, 'dp', [(2 * z + y, 2 * ((z + k) % m) + y) for z in range(...  16.8 us
    ppermute x4, starting transfers between devices, pn(): return lax.ppermute(a, ('section', 'dp'), pairs)  15.2 us
    ppermute x1, waiting for transfers between devices, shards(): lax.ppermute(both[:, :IMG_PAD], 'dp', [(i + 1, i) for i in range(n_dp - 1)])  10.5 us
    ppermute x8, starting transfers between devices, px(): return lax.ppermute(a, 'section', [(0, 1), (1, 0)])  9.76 us
  transfers between devices with their start and end apart: 45, of which 23 were waited for; matrix products, arithmetic and copies ran while one was open for 6% of the time, Pallas kernels for 16%

profile of v4, /device:TPU:0, one launch (start us, length us, event | category | flops | bytes accessed | tf_op | source)
XLA Modules:
  0.0 229.3 jit_solution(13744286597417708754)
XLA Ops:
  0.7 1.3 constant_dynamic-slice_fusion
  2.1 1.3 collective-permute-start
  4.0 10.5 %collective-permute-done = bf16[2,208,384]{2,1,0:T(8,128)(2,1)S(1)} collective-permute-done((bf16[2,208,384]{2,1,0:T(8,128)(2,1)S(1)}, bf16[2,208,384]{2,1,0:T(8,128)(2,1)S(1)}, u32[]{:S(2)}, u32[]{:S(2)}) %collective-permute-start) | collective-permute-done | bytes 319520 | tf_op jit(solution)/shard_map/ppermute | solution.py:449
  14.5 1.7 collective-permute-start.1
  16.2 3.2 %collective-permute-done.1 = bf16[48,1280]{1,0:T(8,128)(2,1)S(1)} collective-permute-done((bf16[48,1280]{1,0:T(8,128)(2,1)S(1)}, bf16[48,1280]{1,0:T(8,128)(2,1)S(1)}, u32[]{:S(2)}, u32[]{:S(2)}) %collective-permute-start.1) | collective-permute-done | bytes 122912 | tf_op jit(solution)/shard_map/ppermute | solution.py:382
  19.4 1.8 collective-permute-start.2
  21.3 2.6 %collective-permute-start.3 = (bf16[48,1280]{1,0:T(8,128)(2,1)S(1)}, bf16[48,1280]{1,0:T(8,128)(2,1)S(1)}, u32[]{:S(2)}, u32[]{:S(2)}) collective-permute-start(bf16[48,1280]{1,0:T(8,128)(2,1)S(1)} %get-tuple-element.214), channel_id=1, source_target_pairs={{0,8},{2,10},{4,12},{6,14},{8,0},{10,2},{12,4},{14,6},{1,9},{3,11}... | collective-permute-start | bytes 368648 | tf_op jit(solution)/shard_map/ppermute | solution.py:391
  23.9 1.3 collective-permute-start.4
  25.2 2.1 collective-permute-done.2
  27.4 3.2 %collective-permute-done.3 = bf16[48,1280]{1,0:T(8,128)(2,1)S(1)} collective-permute-done((bf16[48,1280]{1,0:T(8,128)(2,1)S(1)}, bf16[48,1280]{1,0:T(8,128)(2,1)S(1)}, u32[]{:S(2)}, u32[]{:S(2)}) %collective-permute-start.3) | collective-permute-done | bytes 122912 | tf_op jit(solution)/shard_map/ppermute | solution.py:391
  30.7 1.7 collective-permute-start.8
  32.3 2.4 %collective-permute-start.9 = (bf16[4,48,1280]{2,1,0:T(8,128)(2,1)S(1)}, bf16[4,48,1280]{2,1,0:T(8,128)(2,1)S(1)}, u32[]{:S(2)}, u32[]{:S(2)}) collective-permute-start(bf16[4,48,1280]{2,1,0:T(8,128)(2,1)S(1)} %pad_maximum_fusion.1.refs_2_.refs_5_.refs_14_), channel_id=1, source_target_pairs={{0,2},{2,0},{4,6},{6,4},{8,10},{10,8},{12,14},{14,12},{1,3},{3,1},... | collective-permute-start | bytes 1474568 | tf_op jit(solution)/shard_map/ppermute | solution.py:385
  34.7 2.3 %collective-permute-start.5 = (bf16[48,1280]{1,0:T(8,128)(2,1)S(1)}, bf16[48,1280]{1,0:T(8,128)(2,1)S(1)}, u32[]{:S(2)}, u32[]{:S(2)}) collective-permute-start(bf16[48,1280]{1,0:T(8,128)(2,1)S(1)} %get-tuple-element.213), channel_id=1, source_target_pairs={{0,4},{2,6},{4,8},{6,10},{8,12},{10,14},{12,0},{14,2},{1,5},{3,7},... | collective-permute-start | bytes 368648 | tf_op jit(solution)/shard_map/ppermute | solution.py:391
  37.1 1.7 collective-permute-start.6
  38.8 2.8 %collective-permute-done.5 = bf16[48,1280]{1,0:T(8,128)(2,1)S(1)} collective-permute-done((bf16[48,1280]{1,0:T(8,128)(2,1)S(1)}, bf16[48,1280]{1,0:T(8,128)(2,1)S(1)}, u32[]{:S(2)}, u32[]{:S(2)}) %collective-permute-start.5) | collective-permute-done | bytes 122912 | tf_op jit(solution)/shard_map/ppermute | solution.py:391
  41.5 1.7 collective-permute-start.7
  45.4 1.2 collective-permute-done.7
  46.8 7.3 %collective-permute-done.9.refs_4_.refs_7_.refs_16_ = bf16[4,48,1280]{2,1,0:T(8,128)(2,1)S(1)} collective-permute-done((bf16[4,48,1280]{2,1,0:T(8,128)(2,1)S(1)}, bf16[4,48,1280]{2,1,0:T(8,128)(2,1)S(1)}, u32[]{:S(2)}, u32[]{:S(2)}) %collective-permute-start.9) | collective-permute-done | bytes 491552 | tf_op jit(solution)/shard_map/ppermute | solution.py:385
  54.0 0.8 collective-permute-done.10.refs_5_.refs_8_.refs_17_
  55.0 1.3 convolution_convert_fusion.5.refs_1_
  56.3 1.5 collective-permute-start.15
  57.8 1.2 collective-permute-start.16
  59.0 1.0 collective-permute-start.17
  60.1 0.8 copy-done.25
  60.8 0.8 copy-done.26
  61.6 12.8 %shard_map.186 = (bf16[416,384]{1,0:T(8,128)(2,1)}, f32[416,384]{1,0:T(8,128)}, f32[416,128]{1,0:T(8,128)}, bf16[416,384]{1,0:T(8,128)(2,1)}, bf16[2,416,640]{2,...) custom-call(s32[5]{0:T(128)} %stack.95.refs_0_, ...), custom_call_target="tpu_custom_call" | custom-call | flops 10000000000 | bytes 8388608 | tf_op jit(solution)/shard_map/pallas_call | solution.py:346
  74.5 5.6 %collective-permute-done.16.refs_5_ = bf16[4,48,1280]{2,1,0:T(8,128)(2,1)S(1)} collective-permute-done((bf16[4,48,1280]{2,1,0:T(8,128)(2,1)S(1)}, bf16[4,48,1280]{2,1,0:T(8,128)(2,1)S(1)}, u32[]{:S(2)}, u32[]{:S(2)}) %collective-permute-start.16) | collective-permute-done | bytes 491552 | tf_op jit(solution)/shard_map/ppermute | solution.py:385
  80.0 1.7 collective-permute-done.17.refs_6_
  83.0 1.3 convolution_convert_fusion.4.refs_2_
  85.0 0.7 collective-permute-done.21.refs_10_
  85.8 0.8 copy-done.33
  86.5 24.8 %shard_map.187 = (bf16[416,384]{1,0:T(8,128)(2,1)}, f32[416,384]{1,0:T(8,128)}, f32[2,16,128]{2,1,0:T(8,128)}, bf16[2,2,4,48,1280]{4,3,2,1,0:T(8,128)(2,1)}, bf1...) custom-call(s32[5]{0:T(128)} %stack.95.refs_0_, ...), custom_call_target="tpu_custom_call" | custom-call | flops 30000001024 | bytes 8388608 | tf_op jit(solution)/shard_map/pallas_call | solution.py:346
  111.4 1.2 broadcast_select_fusion.2
  113.9 3.7 %collective-permute-start.23 = (bf16[208,384]{1,0:T(8,128)(2,1)S(1)}, bf16[208,384]{1,0:T(8,128)(2,1)S(1)}, u32[]{:S(2)}, u32[]{:S(2)}) collective-permute-start(bf16[208,384]{1,0:T(8,128)(2,1)S(1)} %convolution_convert_fusion.9), channel_id=1, source_target_pairs={{0,2},{2,4},{4,6},{6,8},{8,10},{10,12},{12,14},{16,18},{18,20},{20... | collective-permute-start | bytes 479240 | tf_op jit(solution)/shard_map/ppermute | solution.py:414
  117.6 5.7 %collective-permute-start.24 = (bf16[208,384]{1,0:T(8,128)(2,1)S(1)}, bf16[208,384]{1,0:T(8,128)(2,1)S(1)}, u32[]{:S(2)}, u32[]{:S(2)}) collective-permute-start(bf16[208,384]{1,0:T(8,128)(2,1)S(1)} %convolution_convert_fusion.8), channel_id=1, source_target_pairs={{0,18},{2,20},{4,22},{6,24},{8,26},{10,28},{12,30},{16,2},{18,4},{... | collective-permute-start | bytes 479240 | tf_op jit(solution)/shard_map/ppermute | solution.py:414
  123.4 7.9 %shard_map.188 = (bf16[416,384]{1,0:T(8,128)(2,1)}, bf16[416,1536]{1,0:T(8,128)(2,1)}, f32[416,384]{1,0:T(8,128)}, f32[8,384]{1,0:T(8,128)}, f32[2,16,128]{2,1,0:T(8,128)}) custom-call(s32[5]{0:T(128)} %stack.95.refs_0_, f32[416,384]{1,0:T(8,128)} %get-tuple-element.92.refs_1_, bf16[416,1536]{1,0:T(8,128)(2,1)} %get-tuple-element.93.refs_2_, ...), custom_call_target="tpu_custom_call" | custom-call | flops 10000000000 | bytes 8388608 | tf_op jit(solution)/shard_map/pallas_call | solution.py:346
  132.8 0.8 copy-done.7
  134.5 0.9 collective-permute-start.27
  135.4 1.5 collective-permute-start.28
  136.9 1.1 collective-permute-start.29
  138.1 16.0 %shard_map.189 = (f32[416,384]{1,0:T(8,128)}, f32[2,16,128]{2,1,0:T(8,128)}, bf16[2,2,4,48,1280]{4,3,2,1,0:T(8,128)(2,1)}, bf16[4,48,1280]{2,1,0:T(8,128)(2,1)},...) custom-call(s32[5]{0:T(128)} %stack.95.refs_0_, ...), custom_call_target="tpu_custom_call" | custom-call | flops 10000000000 | bytes 8388608 | tf_op jit(solution)/shard_map/pallas_call | solution.py:346
  154.1 5.8 %collective-permute-done.29 = bf16[4,48,1280]{2,1,0:T(8,128)(2,1)S(1)} collective-permute-done((bf16[4,48,1280]{2,1,0:T(8,128)(2,1)S(1)}, bf16[4,48,1280]{2,1,0:T(8,128)(2,1)S(1)}, u32[]{:S(2)}, u32[]{:S(2)}) %collective-permute-start.29) | collective-permute-done | bytes 491552 | tf_op jit(solution)/shard_map/ppermute | solution.py:388
  159.9 1.2 broadcast_select_fusion
  161.1 0.7 collective-permute-start.31
  162.2 3.8 %collective-permute-start.33 = (bf16[208,384]{1,0:T(8,128)(2,1)S(1)}, bf16[208,384]{1,0:T(8,128)(2,1)S(1)}, u32[]{:S(2)}, u32[]{:S(2)}) collective-permute-start(bf16[208,384]{1,0:T(8,128)(2,1)S(1)} %convolution_convert_fusion.6), channel_id=1, source_target_pairs={{0,18},{2,20},{4,22},{6,24},{8,26},{10,28},{12,30},{16,2},{18,4},{... | collective-permute-start | bytes 479240 | tf_op jit(solution)/shard_map/ppermute | solution.py:414
  166.3 2.1 collective-permute-start.32
  168.5 4.3 %collective-permute-done.33 = bf16[208,384]{1,0:T(8,128)(2,1)S(1)} collective-permute-done((bf16[208,384]{1,0:T(8,128)(2,1)S(1)}, bf16[208,384]{1,0:T(8,128)(2,1)S(1)}, u32[]{:S(2)}, u32[]{:S(2)}) %collective-permute-start.33) | collective-permute-done | bytes 159776 | tf_op jit(solution)/shard_map/ppermute | solution.py:414
  172.7 2.7 %collective-permute-done.32 = bf16[208,384]{1,0:T(8,128)(2,1)S(1)} collective-permute-done((bf16[208,384]{1,0:T(8,128)(2,1)S(1)}, bf16[208,384]{1,0:T(8,128)(2,1)S(1)}, u32[]{:S(2)}, u32[]{:S(2)}) %collective-permute-start.32) | collective-permute-done | bytes 159776 | tf_op jit(solution)/shard_map/ppermute | solution.py:414
  176.9 0.8 copy-done.3
  178.7 2.5 %collective-permute-start.35 = (bf16[4,48,1280]{2,1,0:T(8,128)(2,1)S(1)}, bf16[4,48,1280]{2,1,0:T(8,128)(2,1)S(1)}, u32[]{:S(2)}, u32[]{:S(2)}) collective-permute-start(bf16[4,48,1280]{2,1,0:T(8,128)(2,1)S(1)} %get-tuple-element.142), channel_id=1, source_target_pairs={{0,2},{2,0},{4,6},{6,4},{8,10},{10,8},{12,14},{14,12},{1,3},{3,1},... | collective-permute-start | bytes 1474568 | tf_op jit(solution)/shard_map/ppermute | solution.py:385
  181.2 1.2 collective-permute-start.36
  183.0 10.0 %collective-permute-done.35 = bf16[4,48,1280]{2,1,0:T(8,128)(2,1)S(1)} collective-permute-done((bf16[4,48,1280]{2,1,0:T(8,128)(2,1)S(1)}, bf16[4,48,1280]{2,1,0:T(8,128)(2,1)S(1)}, u32[]{:S(2)}, u32[]{:S(2)}) %collective-permute-start.35) | collective-permute-done | bytes 491552 | tf_op jit(solution)/shard_map/ppermute | solution.py:385
  193.0 0.9 collective-permute-start.41
  194.0 1.4 collective-permute-done.36
  195.7 9.0 %collective-permute-done.37 = bf16[4,48,1280]{2,1,0:T(8,128)(2,1)S(1)} collective-permute-done((bf16[4,48,1280]{2,1,0:T(8,128)(2,1)S(1)}, bf16[4,48,1280]{2,1,0:T(8,128)(2,1)S(1)}, u32[]{:S(2)}, u32[]{:S(2)}) %collective-permute-start.37) | collective-permute-done | bytes 491552 | tf_op jit(solution)/shard_map/ppermute | solution.py:388
  205.0 2.1 collective-permute-start.38
  207.6 2.8 %collective-permute-start.40 = (bf16[48,1280]{1,0:T(8,128)(2,1)S(1)}, bf16[48,1280]{1,0:T(8,128)(2,1)S(1)}, u32[]{:S(2)}, u32[]{:S(2)}) collective-permute-start(bf16[48,1280]{1,0:T(8,128)(2,1)S(1)} %get-tuple-element.211), channel_id=1, source_target_pairs={{0,12},{2,14},{4,0},{6,2},{8,4},{10,6},{12,8},{14,10},{1,13},{3,15... | collective-permute-start | bytes 368648 | tf_op jit(solution)/shard_map/ppermute | solution.py:391
  210.4 1.0 add_bitcast_fusion
  211.4 1.2 collective-permute-done.43
  213.2 5.4 %collective-permute-done.39 = bf16[48,1280]{1,0:T(8,128)(2,1)S(1)} collective-permute-done((bf16[48,1280]{1,0:T(8,128)(2,1)S(1)}, bf16[48,1280]{1,0:T(8,128)(2,1)S(1)}, u32[]{:S(2)}, u32[]{:S(2)}) %collective-permute-start.39) | collective-permute-done | bytes 122912 | tf_op jit(solution)/shard_map/ppermute | solution.py:391
  218.7 0.9 collective-permute-start.44
  219.6 1.2 bitcast_convert_fusion
  220.9 2.8 %collective-permute-done.44 = bf16[48,1280]{1,0:T(8,128)(2,1)S(1)} collective-permute-done((bf16[48,1280]{1,0:T(8,128)(2,1)S(1)}, bf16[48,1280]{1,0:T(8,128)(2,1)S(1)}, u32[]{:S(2)}, u32[]{:S(2)}) %collective-permute-start.44) | collective-permute-done | bytes 122912 | tf_op jit(solution)/shard_map/ppermute | solution.py:382
  224.9 0.7 copy.34
  (181 shorter events, 18.6 us)
Async XLA Ops:
  0.7 2.7 %copy-start.15 = (bf16[1,192,48]{1,2,0:T(8,128)(2,1)S(1)}, bf16[1,192,48]{1,2,0:T(8,128)(2,1)}, u32[]{:S(2)}) copy-start(bf16[1,192,48]{1,2,0:T(8,128)(2,1)} %param.18) | copy-start | bytes 55300
  0.7 2.7 %copy-start.13 = (bf16[1,48,3,192]{3,1,2,0:T(8,128)(2,1)S(1)}, bf16[1,48,3,192]{3,1,2,0:T(8,128)(2,1)}, u32[]{:S(2)}) copy-start(bf16[1,48,3,192]{3,1,2,0:T(8,128)(2,1)} %param.16) | copy-start | bytes 165892
  0.7 2.8 %copy-start.14 = (bf16[1,48,768]{2,1,0:T(8,128)(2,1)S(1)}, bf16[1,48,768]{2,1,0:T(8,128)(2,1)}, u32[]{:S(2)}) copy-start(bf16[1,48,768]{2,1,0:T(8,128)(2,1)} %param.19) | copy-start | bytes 221188
  0.7 2.8 %copy-start.18 = (bf16[1,4,48]{2,1,0:T(4,128)(2,1)S(1)}, bf16[1,4,48]{2,1,0:T(4,128)(2,1)}, u32[]{:S(2)}) copy-start(bf16[1,4,48]{2,1,0:T(4,128)(2,1)} %param.15) | copy-start | bytes 1156
  0.7 2.8 %copy-start.19 = (bf16[1,2,48]{2,1,0:T(2,128)(2,1)S(1)}, bf16[1,2,48]{2,1,0:T(2,128)(2,1)}, u32[]{:S(2)}) copy-start(bf16[1,2,48]{2,1,0:T(2,128)(2,1)} %param.14) | copy-start | bytes 580
  0.7 3.0 %copy-start.16 = (bf16[1,2,192]{2,1,0:T(2,128)(2,1)S(1)}, bf16[1,2,192]{2,1,0:T(2,128)(2,1)}, u32[]{:S(2)}) copy-start(bf16[1,2,192]{2,1,0:T(2,128)(2,1)} %param.17) | copy-start | bytes 2308
  0.7 3.0 %copy-start.17 = (bf16[1,768]{1,0:T(2,128)(2,1)S(1)}, bf16[1,768]{1,0:T(2,128)(2,1)}, u32[]{:S(2)}) copy-start(bf16[1,768]{1,0:T(2,128)(2,1)} %param.20) | copy-start | bytes 4612
  2.1 12.4 %collective-permute-start = (bf16[2,208,384]{2,1,0:T(8,128)(2,1)S(1)}, bf16[2,208,384]{2,1,0:T(8,128)(2,1)S(1)}, u32[]{:S(2)}, u32[]{:S(2)}) collective-permute-start(bf16[2,208,384]{2,1,0:T(8,128)(2,1)S(1)} %pad_maximum_fusion.3), channel_id=1, source_target_pairs={{2,0},{4,2},{6,4},{8,6},{10,8},{12,10},{14,12},{3,1},{5,3},{7,5},{... | collective-permute-start | bytes 958472 | tf_op jit(solution)/shard_map/ppermute | solution.py:449
  3.5 39.8 %copy-start.34 = (s32[2]{0:T(128)S(1)}, s32[2]{0:T(128)}, u32[]{:S(2)}) copy-start(s32[2]{0:T(128)} %param.12) | copy-start | bytes 28
  14.5 4.9 %collective-permute-start.1 = (bf16[48,1280]{1,0:T(8,128)(2,1)S(1)}, bf16[48,1280]{1,0:T(8,128)(2,1)S(1)}, u32[]{:S(2)}, u32[]{:S(2)}) collective-permute-start(bf16[48,1280]{1,0:T(8,128)(2,1)S(1)} %broadcast_select_fusion.8), channel_id=1, source_target_pairs={{0,16},{16,0},{1,17},{17,1},{2,18},{18,2},{3,19},{19,3},{4,20},{20... | collective-permute-start | bytes 368648 | tf_op jit(solution)/shard_map/ppermute | solution.py:382
  19.4 7.9 %collective-permute-start.2 = (bf16[48,1280]{1,0:T(8,128)(2,1)S(1)}, bf16[48,1280]{1,0:T(8,128)(2,1)S(1)}, u32[]{:S(2)}, u32[]{:S(2)}) collective-permute-start(bf16[48,1280]{1,0:T(8,128)(2,1)S(1)} %get-tuple-element.214), channel_id=1, source_target_pairs={{0,4},{2,6},{4,8},{6,10},{8,12},{10,14},{12,0},{14,2},{1,5},{3,7},... | collective-permute-start | bytes 368648 | tf_op jit(solution)/shard_map/ppermute | solution.py:391
  21.3 9.3 %collective-permute-start.3 = (bf16[48,1280]{1,0:T(8,128)(2,1)S(1)}, bf16[48,1280]{1,0:T(8,128)(2,1)S(1)}, u32[]{:S(2)}, u32[]{:S(2)}) collective-permute-start(bf16[48,1280]{1,0:T(8,128)(2,1)S(1)} %get-tuple-element.214), channel_id=1, source_target_pairs={{0,8},{2,10},{4,12},{6,14},{8,0},{10,2},{12,4},{14,6},{1,9},{3,11}... | collective-permute-start | bytes 368648 | tf_op jit(solution)/shard_map/ppermute | solution.py:391
  23.9 6.7 %collective-permute-start.4 = (bf16[48,1280]{1,0:T(8,128)(2,1)S(1)}, bf16[48,1280]{1,0:T(8,128)(2,1)S(1)}, u32[]{:S(2)}, u32[]{:S(2)}) collective-permute-start(bf16[48,1280]{1,0:T(8,128)(2,1)S(1)} %get-tuple-element.214), channel_id=1, source_target_pairs={{0,12},{2,14},{4,0},{6,2},{8,4},{10,6},{12,8},{14,10},{1,13},{3,15... | collective-permute-start | bytes 368648 | tf_op jit(solution)/shard_map/ppermute | solution.py:391
  30.6 24.4 %copy-start.1 = (bf16[4,48,1280]{2,1,0:T(8,128)(2,1)}, bf16[4,48,1280]{2,1,0:T(8,128)(2,1)S(1)}, u32[]{:S(2)}) copy-start(bf16[4,48,1280]{2,1,0:T(8,128)(2,1)S(1)} %pad_maximum_fusion.1.refs_2_.refs_5_.refs_14_) | copy-start | bytes 1474564
  30.7 16.0 %collective-permute-start.8 = (bf16[4,48,1280]{2,1,0:T(8,128)(2,1)S(1)}, bf16[4,48,1280]{2,1,0:T(8,128)(2,1)S(1)}, u32[]{:S(2)}, u32[]{:S(2)}) collective-permute-start(bf16[4,48,1280]{2,1,0:T(8,128)(2,1)S(1)} %pad_maximum_fusion.1.refs_2_.refs_5_.refs_14_), channel_id=1, source_target_pairs={{0,16},{16,0},{1,17},{17,1},{2,18},{18,2},{3,19},{19,3},{4,20},{20... | collective-permute-start | bytes 1474568 | tf_op jit(solution)/shard_map/ppermute | solution.py:382
  32.3 21.7 %collective-permute-start.9 = (bf16[4,48,1280]{2,1,0:T(8,128)(2,1)S(1)}, bf16[4,48,1280]{2,1,0:T(8,128)(2,1)S(1)}, u32[]{:S(2)}, u32[]{:S(2)}) collective-permute-start(bf16[4,48,1280]{2,1,0:T(8,128)(2,1)S(1)} %pad_maximum_fusion.1.refs_2_.refs_5_.refs_14_), channel_id=1, source_target_pairs={{0,2},{2,0},{4,6},{6,4},{8,10},{10,8},{12,14},{14,12},{1,3},{3,1},... | collective-permute-start | bytes 1474568 | tf_op jit(solution)/shard_map/ppermute | solution.py:385
  34.7 20.2 %collective-permute-start.10 = (bf16[4,48,1280]{2,1,0:T(8,128)(2,1)S(1)}, bf16[4,48,1280]{2,1,0:T(8,128)(2,1)}, u32[]{:S(2)}, u32[]{:S(2)}) collective-permute-start(bf16[4,48,1280]{2,1,0:T(8,128)(2,1)S(1)} %pad_maximum_fusion.1.refs_2_.refs_5_.refs_14_), channel_id=1, source_target_pairs={{0,18},{2,16},{4,22},{6,20},{8,26},{10,24},{12,30},{14,28},{16,2},... | collective-permute-start | bytes 1474568 | tf_op jit(solution)/shard_map/ppermute | solution.py:388
  34.7 6.8 %collective-permute-start.5 = (bf16[48,1280]{1,0:T(8,128)(2,1)S(1)}, bf16[48,1280]{1,0:T(8,128)(2,1)S(1)}, u32[]{:S(2)}, u32[]{:S(2)}) collective-permute-start(bf16[48,1280]{1,0:T(8,128)(2,1)S(1)} %get-tuple-element.213), channel_id=1, source_target_pairs={{0,4},{2,6},{4,8},{6,10},{8,12},{10,14},{12,0},{14,2},{1,5},{3,7},... | collective-permute-start | bytes 368648 | tf_op jit(solution)/shard_map/ppermute | solution.py:391
  37.1 8.3 %collective-permute-start.6 = (bf16[48,1280]{1,0:T(8,128)(2,1)S(1)}, bf16[48,1280]{1,0:T(8,128)(2,1)S(1)}, u32[]{:S(2)}, u32[]{:S(2)}) collective-permute-start(bf16[48,1280]{1,0:T(8,128)(2,1)S(1)} %get-tuple-element.213), channel_id=1, source_target_pairs={{0,8},{2,10},{4,12},{6,14},{8,0},{10,2},{12,4},{14,6},{1,9},{3,11}... | collective-permute-start | bytes 368648 | tf_op jit(solution)/shard_map/ppermute | solution.py:391
  41.5 5.1 %collective-permute-start.7 = (bf16[48,1280]{1,0:T(8,128)(2,1)S(1)}, bf16[48,1280]{1,0:T(8,128)(2,1)S(1)}, u32[]{:S(2)}, u32[]{:S(2)}) collective-permute-start(bf16[48,1280]{1,0:T(8,128)(2,1)S(1)} %get-tuple-element.213), channel_id=1, source_target_pairs={{0,12},{2,14},{4,0},{6,2},{8,4},{10,6},{12,8},{14,10},{1,13},{3,15... | collective-permute-start | bytes 368648 | tf_op jit(solution)/shard_map/ppermute | solution.py:391
  45.4 12.4 %collective-permute-start.11 = (bf16[4,48,1280]{2,1,0:T(8,128)(2,1)S(1)}, bf16[4,48,1280]{2,1,0:T(8,128)(2,1)S(1)}, u32[]{:S(2)}, u32[]{:S(2)}) collective-permute-start(bf16[4,48,1280]{2,1,0:T(8,128)(2,1)S(1)} %pad_maximum_fusion.1.refs_2_.refs_5_.refs_14_), channel_id=1, source_target_pairs={{0,1},{1,0},{2,3},{3,2},{4,5},{5,4},{6,7},{7,6},{8,9},{9,8},{10,11... | collective-permute-start | bytes 1474568 | tf_op jit(solution)/shard_map/ppermute | solution.py:379
  46.7 35.0 %copy-start.2 = (bf16[4,48,1280]{2,1,0:T(8,128)(2,1)}, bf16[4,48,1280]{2,1,0:T(8,128)(2,1)S(1)}, u32[]{:S(2)}) copy-start(bf16[4,48,1280]{2,1,0:T(8,128)(2,1)S(1)} %pad_maximum_fusion.2.refs_3_) | copy-start | bytes 1474564
  46.7 9.6 %copy-start.21 = (bf16[4,48,1280]{2,1,0:T(8,128)(2,1)}, bf16[4,48,1280]{2,1,0:T(8,128)(2,1)S(1)}, u32[]{:S(2)}) copy-start(bf16[4,48,1280]{2,1,0:T(8,128)(2,1)S(1)} %collective-permute-done.8.refs_3_.refs_6_.refs_15_) | copy-start | bytes 1474564
  46.7 12.3 %collective-permute-start.12 = (bf16[4,48,1280]{2,1,0:T(8,128)(2,1)S(1)}, bf16[4,48,1280]{2,1,0:T(8,128)(2,1)S(1)}, u32[]{:S(2)}, u32[]{:S(2)}) collective-permute-start(bf16[4,48,1280]{2,1,0:T(8,128)(2,1)S(1)} %collective-permute-done.8.refs_3_.refs_6_.refs_15_), channel_id=1, source_target_pairs={{0,1},{1,0},{2,3},{3,2},{4,5},{5,4},{6,7},{7,6},{8,9},{9,8},{10,11... | collective-permute-start | bytes 1474568 | tf_op jit(solution)/shard_map/ppermute | solution.py:379
  54.0 2.3 %copy-start.22 = (bf16[4,48,1280]{2,1,0:T(8,128)(2,1)}, bf16[4,48,1280]{2,1,0:T(8,128)(2,1)S(1)}, u32[]{:S(2)}) copy-start(bf16[4,48,1280]{2,1,0:T(8,128)(2,1)S(1)} %collective-permute-done.9.refs_4_.refs_7_.refs_16_) | copy-start | bytes 1474564
  54.0 6.0 %collective-permute-start.13 = (bf16[4,48,1280]{2,1,0:T(8,128)(2,1)S(1)}, bf16[4,48,1280]{2,1,0:T(8,128)(2,1)S(1)}, u32[]{:S(2)}, u32[]{:S(2)}) collective-permute-start(bf16[4,48,1280]{2,1,0:T(8,128)(2,1)S(1)} %collective-permute-done.9.refs_4_.refs_7_.refs_16_), channel_id=1, source_target_pairs={{0,1},{1,0},{2,3},{3,2},{4,5},{5,4},{6,7},{7,6},{8,9},{9,8},{10,11... | collective-permute-start | bytes 1474568 | tf_op jit(solution)/shard_map/ppermute | solution.py:379
  54.9 5.2 %collective-permute-start.14 = (bf16[4,48,1280]{2,1,0:T(8,128)(2,1)}, bf16[4,48,1280]{2,1,0:T(8,128)(2,1)S(1)}, u32[]{:S(2)}, u32[]{:S(2)}) collective-permute-start(bf16[4,48,1280]{2,1,0:T(8,128)(2,1)} %collective-permute-done.10.refs_5_.refs_8_.refs_17_), channel_id=1, source_target_pairs={{0,1},{1,0},{2,3},{3,2},{4,5},{5,4},{6,7},{7,6},{8,9},{9,8},{10,11... | collective-permute-start | bytes 1474568 | tf_op jit(solution)/shard_map/ppermute | solution.py:379
  56.3 18.1 %collective-permute-start.15 = (bf16[4,48,1280]{2,1,0:T(8,128)(2,1)S(1)}, bf16[4,48,1280]{2,1,0:T(8,128)(2,1)S(1)}, u32[]{:S(2)}, u32[]{:S(2)}) collective-permute-start(bf16[4,48,1280]{2,1,0:T(8,128)(2,1)S(1)} %pad_maximum_fusion.2.refs_3_), channel_id=1, source_target_pairs={{0,16},{16,0},{1,17},{17,1},{2,18},{18,2},{3,19},{19,3},{4,20},{20... | collective-permute-start | bytes 1474568 | tf_op jit(solution)/shard_map/ppermute | solution.py:382
  57.8 2.3 copy-start.23
  57.8 22.2 %collective-permute-start.16 = (bf16[4,48,1280]{2,1,0:T(8,128)(2,1)S(1)}, bf16[4,48,1280]{2,1,0:T(8,128)(2,1)S(1)}, u32[]{:S(2)}, u32[]{:S(2)}) collective-permute-start(bf16[4,48,1280]{2,1,0:T(8,128)(2,1)S(1)} %pad_maximum_fusion.2.refs_3_), channel_id=1, source_target_pairs={{0,2},{2,0},{4,6},{6,4},{8,10},{10,8},{12,14},{14,12},{1,3},{3,1},... | collective-permute-start | bytes 1474568 | tf_op jit(solution)/shard_map/ppermute | solution.py:385
  59.0 22.7 %collective-permute-start.17 = (bf16[4,48,1280]{2,1,0:T(8,128)(2,1)S(1)}, bf16[4,48,1280]{2,1,0:T(8,128)(2,1)S(1)}, u32[]{:S(2)}, u32[]{:S(2)}) collective-permute-start(bf16[4,48,1280]{2,1,0:T(8,128)(2,1)S(1)} %pad_maximum_fusion.2.refs_3_), channel_id=1, source_target_pairs={{0,18},{2,16},{4,22},{6,20},{8,26},{10,24},{12,30},{14,28},{16,2},... | collective-permute-start | bytes 1474568 | tf_op jit(solution)/shard_map/ppermute | solution.py:388
  74.5 11.2 %copy-start.27 = (bf16[4,48,1280]{2,1,0:T(8,128)(2,1)}, bf16[4,48,1280]{2,1,0:T(8,128)(2,1)S(1)}, u32[]{:S(2)}) copy-start(bf16[4,48,1280]{2,1,0:T(8,128)(2,1)S(1)} %collective-permute-done.15.refs_4_) | copy-start | bytes 1474564
  80.0 5.6 %copy-start.28 = (bf16[4,48,1280]{2,1,0:T(8,128)(2,1)}, bf16[4,48,1280]{2,1,0:T(8,128)(2,1)S(1)}, u32[]{:S(2)}) copy-start(bf16[4,48,1280]{2,1,0:T(8,128)(2,1)S(1)} %collective-permute-done.16.refs_5_) | copy-start | bytes 1474564
  81.7 4.0 %copy-start.29 = (bf16[4,48,1280]{2,1,0:T(8,128)(2,1)}, bf16[4,48,1280]{2,1,0:T(8,128)(2,1)S(1)}, u32[]{:S(2)}) copy-start(bf16[4,48,1280]{2,1,0:T(8,128)(2,1)S(1)} %collective-permute-done.17.refs_6_) | copy-start | bytes 1474564
  81.7 2.6 %collective-permute-start.18 = (bf16[4,48,1280]{2,1,0:T(8,128)(2,1)S(1)}, bf16[4,48,1280]{2,1,0:T(8,128)(2,1)S(1)}, u32[]{:S(2)}, u32[]{:S(2)}) collective-permute-start(bf16[4,48,1280]{2,1,0:T(8,128)(2,1)S(1)} %pad_maximum_fusion.2.refs_3_), channel_id=1, source_target_pairs={{0,1},{1,0},{2,3},{3,2},{4,5},{5,4},{6,7},{7,6},{8,9},{9,8},{10,11... | collective-permute-start | bytes 1474568 | tf_op jit(solution)/shard_map/ppermute | solution.py:379
  81.7 2.6 %collective-permute-start.19 = (bf16[4,48,1280]{2,1,0:T(8,128)(2,1)S(1)}, bf16[4,48,1280]{2,1,0:T(8,128)(2,1)S(1)}, u32[]{:S(2)}, u32[]{:S(2)}) collective-permute-start(bf16[4,48,1280]{2,1,0:T(8,128)(2,1)S(1)} %collective-permute-done.15.refs_4_), channel_id=1, source_target_pairs={{0,1},{1,0},{2,3},{3,2},{4,5},{5,4},{6,7},{7,6},{8,9},{9,8},{10,11... | collective-permute-start | bytes 1474568 | tf_op jit(solution)/shard_map/ppermute | solution.py:379
  82.2 2.8 %collective-permute-start.20 = (bf16[4,48,1280]{2,1,0:T(8,128)(2,1)S(1)}, bf16[4,48,1280]{2,1,0:T(8,128)(2,1)S(1)}, u32[]{:S(2)}, u32[]{:S(2)}) collective-permute-start(bf16[4,48,1280]{2,1,0:T(8,128)(2,1)S(1)} %collective-permute-done.16.refs_5_), channel_id=1, source_target_pairs={{0,1},{1,0},{2,3},{3,2},{4,5},{5,4},{6,7},{7,6},{8,9},{9,8},{10,11... | collective-permute-start | bytes 1474568 | tf_op jit(solution)/shard_map/ppermute | solution.py:379
  82.3 3.4 %collective-permute-start.21 = (bf16[4,48,1280]{2,1,0:T(8,128)(2,1)S(1)}, bf16[4,48,1280]{2,1,0:T(8,128)(2,1)S(1)}, u32[]{:S(2)}, u32[]{:S(2)}) collective-permute-start(bf16[4,48,1280]{2,1,0:T(8,128)(2,1)S(1)} %collective-permute-done.17.refs_6_), channel_id=1, source_target_pairs={{0,1},{1,0},{2,3},{3,2},{4,5},{5,4},{6,7},{7,6},{8,9},{9,8},{10,11... | collective-permute-start | bytes 1474568 | tf_op jit(solution)/shard_map/ppermute | solution.py:379
  84.3 27.1 %copy-start.11 = (bf16[416,384]{1,0:T(8,128)(2,1)S(1)}, bf16[416,384]{1,0:T(8,128)(2,1)}, u32[]{:S(2)}) copy-start(bf16[416,384]{1,0:T(8,128)(2,1)} %get-tuple-element.87.refs_1_) | copy-start | bytes 958468
  111.4 11.9 %copy-start.20 = (bf16[2,2,4,48,1280]{4,3,2,1,0:T(8,128)(2,1)S(1)}, bf16[2,2,4,48,1280]{4,3,2,1,0:T(8,128)(2,1)}, u32[]{:S(2)}) copy-start(bf16[2,2,4,48,1280]{4,3,2,1,0:T(8,128)(2,1)} %get-tuple-element.99) | copy-start | bytes 5898244
  112.6 18.8 %collective-permute-start.22 = (bf16[416,384]{1,0:T(8,128)(2,1)S(1)}, bf16[416,384]{1,0:T(8,128)(2,1)S(1)}, u32[]{:S(2)}, u32[]{:S(2)}) collective-permute-start(bf16[416,384]{1,0:T(8,128)(2,1)S(1)} %get-tuple-element.203), channel_id=1, source_target_pairs={{0,16},{16,0},{1,17},{17,1},{2,18},{18,2},{3,19},{19,3},{4,20},{20... | collective-permute-start | bytes 958472 | tf_op jit(solution)/shard_map/ppermute | solution.py:382
  113.9 17.4 %collective-permute-start.23 = (bf16[208,384]{1,0:T(8,128)(2,1)S(1)}, bf16[208,384]{1,0:T(8,128)(2,1)S(1)}, u32[]{:S(2)}, u32[]{:S(2)}) collective-permute-start(bf16[208,384]{1,0:T(8,128)(2,1)S(1)} %convolution_convert_fusion.9), channel_id=1, source_target_pairs={{0,2},{2,4},{4,6},{6,8},{8,10},{10,12},{12,14},{16,18},{18,20},{20... | collective-permute-start | bytes 479240 | tf_op jit(solution)/shard_map/ppermute | solution.py:414
  117.6 13.7 %collective-permute-start.24 = (bf16[208,384]{1,0:T(8,128)(2,1)S(1)}, bf16[208,384]{1,0:T(8,128)(2,1)S(1)}, u32[]{:S(2)}, u32[]{:S(2)}) collective-permute-start(bf16[208,384]{1,0:T(8,128)(2,1)S(1)} %convolution_convert_fusion.8), channel_id=1, source_target_pairs={{0,18},{2,20},{4,22},{6,24},{8,26},{10,28},{12,30},{16,2},{18,4},{... | collective-permute-start | bytes 479240 | tf_op jit(solution)/shard_map/ppermute | solution.py:414
  123.3 9.4 %collective-permute-start.25 = (bf16[2,2,4,48,1280]{4,3,2,1,0:T(8,128)(2,1)S(1)}, bf16[2,2,4,48,1280]{4,3,2,1,0:T(8,128)(2,1)S(1)}, u32[]{:S(2)}, u32[]{:S(2)}) collective-permute-start(bf16[2,2,4,48,1280]{4,3,2,1,0:T(8,128)(2,1)S(1)} %copy-done.20), channel_id=1, source_target_pairs={{0,1},{1,0},{2,3},{3,2},{4,5},{5,4},{6,7},{7,6},{8,9},{9,8},{10,11... | collective-permute-start | bytes 5898248 | tf_op jit(solution)/shard_map/ppermute | solution.py:379
  134.5 19.6 %collective-permute-start.27 = (bf16[4,48,1280]{2,1,0:T(8,128)(2,1)S(1)}, bf16[4,48,1280]{2,1,0:T(8,128)(2,1)S(1)}, u32[]{:S(2)}, u32[]{:S(2)}) collective-permute-start(bf16[4,48,1280]{2,1,0:T(8,128)(2,1)S(1)} %get-tuple-element.126), channel_id=1, source_target_pairs={{0,2},{2,0},{4,6},{6,4},{8,10},{10,8},{12,14},{14,12},{1,3},{3,1},... | collective-permute-start | bytes 1474568 | tf_op jit(solution)/shard_map/ppermute | solution.py:385
  135.4 18.7 %collective-permute-start.28 = (bf16[4,48,1280]{2,1,0:T(8,128)(2,1)S(1)}, bf16[4,48,1280]{2,1,0:T(8,128)(2,1)S(1)}, u32[]{:S(2)}, u32[]{:S(2)}) collective-permute-start(bf16[4,48,1280]{2,1,0:T(8,128)(2,1)S(1)} %get-tuple-element.127), channel_id=1, source_target_pairs={{0,16},{16,0},{1,17},{17,1},{2,18},{18,2},{3,19},{19,3},{4,20},{20... | collective-permute-start | bytes 1474568 | tf_op jit(solution)/shard_map/ppermute | solution.py:382
  136.9 23.0 %collective-permute-start.29 = (bf16[4,48,1280]{2,1,0:T(8,128)(2,1)S(1)}, bf16[4,48,1280]{2,1,0:T(8,128)(2,1)S(1)}, u32[]{:S(2)}, u32[]{:S(2)}) collective-permute-start(bf16[4,48,1280]{2,1,0:T(8,128)(2,1)S(1)} %get-tuple-element.128), channel_id=1, source_target_pairs={{0,18},{2,16},{4,22},{6,20},{8,26},{10,24},{12,30},{14,28},{16,2},... | collective-permute-start | bytes 1474568 | tf_op jit(solution)/shard_map/ppermute | solution.py:388
  138.1 21.9 %copy-start = (f32[416,384]{1,0:T(8,128)S(1)}, f32[416,384]{1,0:T(8,128)}, u32[]{:S(2)}) copy-start(f32[416,384]{1,0:T(8,128)} %get-tuple-element.92.refs_1_) | copy-start | bytes 1916932
  159.9 15.5 %collective-permute-start.30 = (bf16[2,2,4,48,1280]{4,3,2,1,0:T(8,128)(2,1)}, bf16[2,2,4,48,1280]{4,3,2,1,0:T(8,128)(2,1)S(1)}, u32[]{:S(2)}, u32[]{:S(2)}) collective-permute-start(bf16[2,2,4,48,1280]{4,3,2,1,0:T(8,128)(2,1)} %get-tuple-element.129), channel_id=1, source_target_pairs={{0,1},{1,0},{2,3},{3,2},{4,5},{5,4},{6,7},{7,6},{8,9},{9,8},{10,11... | collective-permute-start | bytes 5898248 | tf_op jit(solution)/shard_map/ppermute | solution.py:379
  161.1 14.4 %collective-permute-start.31 = (bf16[416,384]{1,0:T(8,128)(2,1)S(1)}, bf16[416,384]{1,0:T(8,128)(2,1)S(1)}, u32[]{:S(2)}, u32[]{:S(2)}) collective-permute-start(bf16[416,384]{1,0:T(8,128)(2,1)S(1)} %get-tuple-element.201), channel_id=1, source_target_pairs={{0,16},{16,0},{1,17},{17,1},{2,18},{18,2},{3,19},{19,3},{4,20},{20... | collective-permute-start | bytes 958472 | tf_op jit(solution)/shard_map/ppermute | solution.py:382
  162.2 10.6 %collective-permute-start.33 = (bf16[208,384]{1,0:T(8,128)(2,1)S(1)}, bf16[208,384]{1,0:T(8,128)(2,1)S(1)}, u32[]{:S(2)}, u32[]{:S(2)}) collective-permute-start(bf16[208,384]{1,0:T(8,128)(2,1)S(1)} %convolution_convert_fusion.6), channel_id=1, source_target_pairs={{0,18},{2,20},{4,22},{6,24},{8,26},{10,28},{12,30},{16,2},{18,4},{... | collective-permute-start | bytes 479240 | tf_op jit(solution)/shard_map/ppermute | solution.py:414
  166.3 9.1 %collective-permute-start.32 = (bf16[208,384]{1,0:T(8,128)(2,1)S(1)}, bf16[208,384]{1,0:T(8,128)(2,1)S(1)}, u32[]{:S(2)}, u32[]{:S(2)}) collective-permute-start(bf16[208,384]{1,0:T(8,128)(2,1)S(1)} %convolution_convert_fusion.7), channel_id=1, source_target_pairs={{0,2},{2,4},{4,6},{6,8},{8,10},{10,12},{12,14},{16,18},{18,20},{20... | collective-permute-start | bytes 479240 | tf_op jit(solution)/shard_map/ppermute | solution.py:414
  168.4 39.2 %collective-permute-start.26 = (bf16[2,512,384]{2,1,0:T(8,128)(2,1)S(1)}, bf16[2,512,384]{2,1,0:T(8,128)(2,1)S(1)}, u32[]{:S(2)}, u32[]{:S(2)}) collective-permute-start(bf16[2,512,384]{2,1,0:T(8,128)(2,1)S(1)} %maximum_select_fusion), channel_id=1, source_target_pairs={{0,1},{1,0},{2,3},{3,2},{4,5},{5,4},{6,7},{7,6},{8,9},{9,8},{10,11... | collective-permute-start | bytes 2359304 | tf_op jit(solution)/shard_map/ppermute | solution.py:379
  178.6 26.2 %collective-permute-start.34 = (bf16[2,512,384]{2,1,0:T(8,128)(2,1)S(1)}, bf16[2,512,384]{2,1,0:T(8,128)(2,1)S(1)}, u32[]{:S(2)}, u32[]{:S(2)}) collective-permute-start(bf16[2,512,384]{2,1,0:T(8,128)(2,1)S(1)} %maximum_select_fusion.1), channel_id=1, source_target_pairs={{0,1},{1,0},{2,3},{3,2},{4,5},{5,4},{6,7},{7,6},{8,9},{9,8},{10,11... | collective-permute-start | bytes 2359304 | tf_op jit(solution)/shard_map/ppermute | solution.py:379
  178.7 14.4 %collective-permute-start.35 = (bf16[4,48,1280]{2,1,0:T(8,128)(2,1)S(1)}, bf16[4,48,1280]{2,1,0:T(8,128)(2,1)S(1)}, u32[]{:S(2)}, u32[]{:S(2)}) collective-permute-start(bf16[4,48,1280]{2,1,0:T(8,128)(2,1)S(1)} %get-tuple-element.142), channel_id=1, source_target_pairs={{0,2},{2,0},{4,6},{6,4},{8,10},{10,8},{12,14},{14,12},{1,3},{3,1},... | collective-permute-start | bytes 1474568 | tf_op jit(solution)/shard_map/ppermute | solution.py:385
  181.2 14.1 %collective-permute-start.36 = (bf16[4,48,1280]{2,1,0:T(8,128)(2,1)S(1)}, bf16[4,48,1280]{2,1,0:T(8,128)(2,1)S(1)}, u32[]{:S(2)}, u32[]{:S(2)}) collective-permute-start(bf16[4,48,1280]{2,1,0:T(8,128)(2,1)S(1)} %get-tuple-element.143), channel_id=1, source_target_pairs={{0,16},{16,0},{1,17},{17,1},{2,18},{18,2},{3,19},{19,3},{4,20},{20... | collective-permute-start | bytes 1474568 | tf_op jit(solution)/shard_map/ppermute | solution.py:382
  182.4 22.3 %collective-permute-start.37 = (bf16[4,48,1280]{2,1,0:T(8,128)(2,1)S(1)}, bf16[4,48,1280]{2,1,0:T(8,128)(2,1)S(1)}, u32[]{:S(2)}, u32[]{:S(2)}) collective-permute-start(bf16[4,48,1280]{2,1,0:T(8,128)(2,1)S(1)} %get-tuple-element.144), channel_id=1, source_target_pairs={{0,18},{2,16},{4,22},{6,20},{8,26},{10,24},{12,30},{14,28},{16,2},... | collective-permute-start | bytes 1474568 | tf_op jit(solution)/shard_map/ppermute | solution.py:388
  193.0 14.1 %collective-permute-start.41 = (bf16[48,1280]{1,0:T(8,128)(2,1)S(1)}, bf16[48,1280]{1,0:T(8,128)(2,1)S(1)}, u32[]{:S(2)}, u32[]{:S(2)}) collective-permute-start(bf16[48,1280]{1,0:T(8,128)(2,1)S(1)} %get-tuple-element.207), channel_id=1, source_target_pairs={{0,4},{2,6},{4,8},{6,10},{8,12},{10,14},{12,0},{14,2},{1,5},{3,7},... | collective-permute-start | bytes 368648 | tf_op jit(solution)/shard_map/ppermute | solution.py:391
  195.3 16.1 %collective-permute-start.42 = (bf16[48,1280]{1,0:T(8,128)(2,1)S(1)}, bf16[48,1280]{1,0:T(8,128)(2,1)S(1)}, u32[]{:S(2)}, u32[]{:S(2)}) collective-permute-start(bf16[48,1280]{1,0:T(8,128)(2,1)S(1)} %get-tuple-element.209), channel_id=1, source_target_pairs={{0,8},{2,10},{4,12},{6,14},{8,0},{10,2},{12,4},{14,6},{1,9},{3,11}... | collective-permute-start | bytes 368648 | tf_op jit(solution)/shard_map/ppermute | solution.py:391
  204.7 7.9 %collective-permute-start.43 = (bf16[48,1280]{1,0:T(8,128)(2,1)S(1)}, bf16[48,1280]{1,0:T(8,128)(2,1)S(1)}, u32[]{:S(2)}, u32[]{:S(2)}) collective-permute-start(bf16[48,1280]{1,0:T(8,128)(2,1)S(1)} %get-tuple-element.208), channel_id=1, source_target_pairs={{0,12},{2,14},{4,0},{6,2},{8,4},{10,6},{12,8},{14,10},{1,13},{3,15... | collective-permute-start | bytes 368648 | tf_op jit(solution)/shard_map/ppermute | solution.py:391
  205.0 8.2 %collective-permute-start.38 = (bf16[48,1280]{1,0:T(8,128)(2,1)S(1)}, bf16[48,1280]{1,0:T(8,128)(2,1)S(1)}, u32[]{:S(2)}, u32[]{:S(2)}) collective-permute-start(bf16[48,1280]{1,0:T(8,128)(2,1)S(1)} %get-tuple-element.210), channel_id=1, source_target_pairs={{0,4},{2,6},{4,8},{6,10},{8,12},{10,14},{12,0},{14,2},{1,5},{3,7},... | collective-permute-start | bytes 368648 | tf_op jit(solution)/shard_map/ppermute | solution.py:391
  207.1 11.5 %collective-permute-start.39 = (bf16[48,1280]{1,0:T(8,128)(2,1)S(1)}, bf16[48,1280]{1,0:T(8,128)(2,1)S(1)}, u32[]{:S(2)}, u32[]{:S(2)}) collective-permute-start(bf16[48,1280]{1,0:T(8,128)(2,1)S(1)} %get-tuple-element.212), channel_id=1, source_target_pairs={{0,8},{2,10},{4,12},{6,14},{8,0},{10,2},{12,4},{14,6},{1,9},{3,11}... | collective-permute-start | bytes 368648 | tf_op jit(solution)/shard_map/ppermute | solution.py:391
  207.6 11.0 %collective-permute-start.40 = (bf16[48,1280]{1,0:T(8,128)(2,1)S(1)}, bf16[48,1280]{1,0:T(8,128)(2,1)S(1)}, u32[]{:S(2)}, u32[]{:S(2)}) collective-permute-start(bf16[48,1280]{1,0:T(8,128)(2,1)S(1)} %get-tuple-element.211), channel_id=1, source_target_pairs={{0,12},{2,14},{4,0},{6,2},{8,4},{10,6},{12,8},{14,10},{1,13},{3,15... | collective-permute-start | bytes 368648 | tf_op jit(solution)/shard_map/ppermute | solution.py:391
  218.7 4.9 %collective-permute-start.44 = (bf16[48,1280]{1,0:T(8,128)(2,1)S(1)}, bf16[48,1280]{1,0:T(8,128)(2,1)S(1)}, u32[]{:S(2)}, u32[]{:S(2)}) collective-permute-start(bf16[48,1280]{1,0:T(8,128)(2,1)S(1)} %get-tuple-element.186), channel_id=1, source_target_pairs={{0,16},{16,0},{1,17},{17,1},{2,18},{18,2},{3,19},{19,3},{4,20},{20... | collective-permute-start | bytes 368648 | tf_op jit(solution)/shard_map/ppermute | solution.py:382
  (16 other events, 18.9 us)

commit v5 on v4

--- a/solution.py
+++ b/solution.py
@@ -1,3 +1,4 @@
+import functools
 import math
 
 import jax
@@ -207,29 +208,30 @@
     in_ref[r, :] = res + norm_back(ig, xhat, kept["inv1"][r, :1], vec[0:1, :])
 
 
-def weight_grads(t, piece, kept, grad, small, bsum, g):
-    width = small.shape[0]
+def weight_grads(t, piece, kept, grad, g):
     ag, dg = grad["ag"][...], grad["dg"][...]
     ain, mlp_in = kept["ain"][...], kept["min"][...]
+    width = ag.shape[1]
     high = jnp.where(low_lanes(), 0.0, 1.0)
     d = grad["dqkv"][t]
-    g[t, 0, :, :OUT] = tn(ain, d[:, :OUT]).astype(BF16)
+    g[0, :, :OUT] = tn(ain, d[:, :OUT]).astype(BF16)
     out = tn(ag, kept["mx"][t])
-    g[t, 0, :, OUT:ATT] = (tn(ain, d[:, OUT:]) + out[:, :BLOCK] * high).astype(BF16)
-    g[t, 0, :, ATT:MISC] = out[:, BLOCK:].astype(BF16)
-    g[t, 0, :, MISC:UP0] = small
+    g[0, :, OUT:ATT] = (tn(ain, d[:, OUT:]) + out[:, :BLOCK] * high).astype(BF16)
+    g[0, :, ATT:MISC] = out[:, BLOCK:].astype(BF16)
+    sums = jnp.concatenate([grad["sums"][...], jnp.zeros((BLOCK - 8, width), F32)], 0)
+    g[0, :, MISC:UP0] = sums.T.astype(BF16)
     for j in range(2):
         c = pl.ds(pl.multiple_of((t * 2 + j) * CHUNK, BLOCK), CHUNK)
         up = tn(mlp_in, grad["up"][:, c]).astype(BF16)
         if j == 0:
-            g[t, 0, :, UP0:] = up
+            g[0, :, UP0:] = up
         else:
-            g[t, 1, :, :CHUNK] = up
-        g[t, 1, :, DOWN + j * CHUNK:DOWN + (j + 1) * CHUNK] = tn(dg, kept["hd"][:, c]).astype(BF16)
+            g[1, :, :CHUNK] = up
+        g[1, :, DOWN + j * CHUNK:DOWN + (j + 1) * CHUNK] = tn(dg, kept["hd"][:, c]).astype(BF16)
     if piece % 16 == 0:
-        rows = jnp.concatenate([bsum[t], jnp.zeros((piece - 16, BLOCK), F32)], 0).astype(BF16)
+        rows = jnp.concatenate([grad["bsum"][t], jnp.zeros((piece - 16, BLOCK), F32)], 0).astype(BF16)
         for i in range(width // piece):
-            g[t, 1, i * piece:(i + 1) * piece, ROWSB:] = rows
+            g[1, i * piece:(i + 1) * piece, ROWSB:] = rows
 
 
 def kept_shapes(total, width, ff):
@@ -242,40 +244,35 @@
 
 def grad_shapes(total, width, ff):
     return dict(dg=((total, width), BF16), up=((total, ff), BF16), res=((total, width), F32), sums=((8, width), F32),
-                bsum=((2, 16, BLOCK), F32))
+                bsum=((2, 16, BLOCK), F32), ag=((total, width), BF16), dqkv=((2, total, ATT), BF16))
 
 
 def layer_call(phases, sources, load, store, out_shapes, scalars, given, total, width, ff, piece):
     ks = kept_shapes(total, width, ff)
     gs = grad_shapes(total, width, ff)
-    need = {
-        "forward": ["x"], "mlp": ["u", "sl", "xh2", "inv2"],
-        "attention": list(gs) + ["ain", "qkv", "pr", "mx", "xh1", "inv1", "min", "hd"],
-    }
-    gives = {"forward": {"out": ((total, width), BF16), **ks}, "mlp": gs, "attention": {"in": ((total, width), F32)}}
+    weights = ["ain", "mx", "min", "hd"] + [n for n in gs if n != "res"]
+    need = {"forward": ["x"], "back": ["u"] + list(ks), "theirs": weights, "mine": weights}
+    gives = {"forward": {"out": ((total, width), BF16), **ks}, "back": {"in": ((total, width), F32), **gs},
+             "theirs": {}, "mine": {}}
     made = {}
     for p in phases:
         made.update(gives[p])
-    inputs = [n for p in phases for n in need[p] if n not in made]
-    inputs = list(dict.fromkeys(inputs))
-    last = phases[-1]
-    shown = {"forward": list(gives["forward"]), "mlp": list(gs), "attention": ["in"]}[last]
-    if last != "forward" and "forward" in phases:
-        shown = ["out"] + shown
-    if last == "mlp" and "forward" in phases:
-        shown += [n for n in ks if n in need["attention"]]
+    inputs = list(dict.fromkeys(n for p in phases for n in need[p] if n not in made))
+    if phases[-1] == "forward":
+        shown = list(made)
+    else:
+        shown = [n for n in made if n in weights or n in ("out", "in")]
     inner = [n for n in made if n not in shown]
-    end = last == "attention"
+    side = {"theirs": 0, "mine": 1}.get(phases[-1])
+    products = phases[0] != "mine"
     vmem = pl.BlockSpec(memory_space=pltpu.VMEM)
     anywhere = pl.BlockSpec(memory_space=pl.ANY)
-    ends = out_shapes if end else []
-    scratch = [pltpu.VMEM((2, 2, width, HALF), BF16), pltpu.VMEM((8, width), F32), pltpu.VMEM((2, 16, BLOCK), F32),
-               pltpu.SemaphoreType.DMA] + [pltpu.VMEM(*made[n]) for n in inner]
-    if end:
-        scratch += [pltpu.VMEM((total, width), BF16), pltpu.VMEM((2, total, ATT), BF16),
-                    pltpu.VMEM((2, 2, width, HALF), BF16)]
-        if "mlp" not in phases:
-            scratch += [pltpu.VMEM(*gs["sums"]), pltpu.VMEM(*gs["bsum"])]
+    ends = [] if side is None else out_shapes[side]
+    scratch = [pltpu.SemaphoreType.DMA] + [pltpu.VMEM(*made[n]) for n in inner]
+    if products:
+        scratch += [pltpu.VMEM((2, 2, width, HALF), BF16), pltpu.VMEM((8, width), F32), pltpu.VMEM((2, 16, BLOCK), F32)]
+    if ends:
+        scratch.append(pltpu.VMEM((2, width, HALF), BF16))
 
     def body(*refs):
         refs = list(refs)
@@ -289,60 +286,48 @@
         at = dict(zip(inputs, take(len(inputs))))
         src = take(len(sources))
         at.update(zip(shown, take(len(shown))))
-        if end:
-            bias = take(1)[0]
         dst = take(len(ends))
-        w, vec, brow, sem = take(4)
+        sem = take(1)[0]
         at.update(zip(inner, take(len(inner))))
-        if end:
-            at["ag"], at["dqkv"], g = take(3)
-            if "mlp" not in phases:
-                sums, bsum = take(2)
-                sums[...] = at["sums"][...]
-                bsum[...] = at["bsum"][...]
-                at["sums"], at["bsum"] = sums, bsum
-        copies = load(sc, src, w, sem)
-        for c in copies:
-            c.start()
-        for c in copies:
-            c.wait()
-        vec[...] = w[0, 0, :, MISC:UP0].astype(F32).T[:8, :]
-        for t in range(2):
-            brow[t] = w[t, 1, :16, ROWSB:].astype(F32)
+        if products:
+            w, vec, brow = take(3)
+            copies = load(sc, src, w, sem)
+            for c in copies:
+                c.start()
+            for c in copies:
+                c.wait()
+            vec[...] = w[0, 0, :, MISC:UP0].astype(F32).T[:8, :]
+            for t in range(2):
+                brow[t] = w[t, 1, :16, ROWSB:].astype(F32)
         if "forward" in phases:
             def step(n, carry):
                 forward_image(n, sc, at["x"], w, vec, brow, at["out"], at)
                 return carry
             lax.fori_loop(0, total // IMG_PAD, step, 0)
-        if "mlp" in phases:
-            at["sums"][...] = jnp.zeros_like(at["sums"])
-            at["bsum"][...] = jnp.zeros_like(at["bsum"])
-
-            def back_mlp(n, carry):
-                backward_mlp(n, sc, at["u"], w, vec, at, at, at["sums"], at["bsum"])
-                return carry
-            lax.fori_loop(0, total // IMG_PAD, back_mlp, 0)
-        if end:
+        if "back" in phases:
             sums, bsum = at["sums"], at["bsum"]
+            sums[...] = jnp.zeros_like(sums)
+            bsum[...] = jnp.zeros_like(bsum)
 
             def back(n, carry):
+                backward_mlp(n, sc, at["u"], w, vec, at, at, sums, bsum)
                 backward_attention(n, w, vec, at["in"], at, at, sums, bsum)
                 return carry
             lax.fori_loop(0, total // IMG_PAD, back, 0)
-            bias[...] = bsum[...]
-            small = jnp.concatenate([sums[...], jnp.zeros((BLOCK - 8, width), F32)], 0).T.astype(BF16)
-            copies = []
-            for side in range(2):
-                t = jnp.where(sc[1] == 0, 1 - side, side)
-                weight_grads(t, piece, at, at, small, bsum, g)
-                out = store(sc, side, t, g, dst, sem)
-                for c in out:
-                    c.start()
-                copies += out
+        if ends:
+            g = take(1)[0]
+            t = jnp.where(sc[1] == 0, 1 - side, side)
+            weight_grads(t, piece, at, at, g)
+            copies = store(sc, side, g, dst, sem)
+            for c in copies:
+                c.start()
             for c in copies:
                 c.wait()
 
-    outs = [made[n] for n in shown] + ([gs["bsum"]] if end else []) + ends
+    outs = [made[n] for n in shown] + ends
+    args = [scalars, *[given[n] for n in inputs], *(sources if products else [])]
+    if not products:
+        sources = []
     got = pl.pallas_call(
         body,
         out_shape=[jax.ShapeDtypeStruct(*o) for o in outs],
@@ -351,13 +336,10 @@
         scratch_shapes=scratch,
         compiler_params=pltpu.CompilerParams(vmem_limit_bytes=56 * 2 ** 20),
         cost_estimate=pl.CostEstimate(flops=COST * len(phases), transcendentals=0, bytes_accessed=2 ** 23),
-    )(scalars, *[given[n] for n in inputs], *sources)
+    )(*args)
     got = list(got)
     res = dict(zip(shown, got))
-    del got[:len(shown)]
-    if end:
-        res["bias"] = got.pop(0)
-        res["g"] = got
+    res["g"] = got[len(shown):]
     return res
 
 
@@ -397,7 +379,7 @@
         return sum(b.astype(F32) for b in a)
 
     def add_pair(g, got):
-        keep, to_y, to_x, to_d = [plus(a, b) for a, b in zip(g[1:], (got[0, 0], got[0, 1], got[1, 0], got[1, 1]))]
+        keep, to_y, to_x, to_d = [plus(a, b) for a, b in zip(g, (got[0, 0], got[0, 1], got[1, 0], got[1, 1]))]
         return [keep, to_y.astype(BF16), to_x.astype(BF16), to_d.astype(BF16)]
 
     def across(sent):
@@ -416,7 +398,8 @@
     def send_rows(a0, a1):
         keep, give = jnp.where(sec == 0, a0, a1), jnp.where(sec == 0, a1, a0)
         tail = select[:, local_rows:]
-        return [keep, px(give), pn(tn(tail, keep).astype(BF16), False), pn(tn(tail, give).astype(BF16), True)]
+        tails = [pn(tn(tail, keep).astype(BF16), False), pn(tn(tail, give).astype(BF16), True)]
+        return [keep, px(give)] + tails
 
     def place_rows(keep, got, tail, got_tail):
         def place(a, b):
@@ -463,24 +446,24 @@
     if direct:
         keep = jnp.where(sec == 0, part0, part1)
         give = jnp.where(sec == 0, part1, part0)
-        give, halo = after(give, halo)
-        got = px(give)
+        got, halo = after(px(give), halo)
         start = [jnp.where(sec == 0, keep, got), jnp.where(sec == 0, got, keep)]
 
-        def load(sc, src, w, sem):
+        def load(l, sc, src, w, sem):
             copies = []
             for side in range(2):
                 t = jnp.where(sc[1] == 0, side, 1 - side)
-                quad, qx, qy, qd = src[side * 4:side * 4 + 4]
+                own = src[side * 8:side * 8 + 8]
                 for kk in range(m):
                     z = lax.rem(sc[3] - kk + m, m)
                     near = pl.ds(pl.multiple_of((2 * z + sc[4]) * piece, 16), piece)
                     far = pl.ds(pl.multiple_of((2 * z + 1 - sc[4]) * piece, 16), piece)
-                    for a, h, r in ((quad, sc[2], near), (qx, 1 - sc[2], near), (qy, sc[2], far), (qd, 1 - sc[2], far)):
-                        copies.append(pltpu.make_async_copy(a.at[kk], w.at[t, h, r, :], sem))
+                    for i, (h, r) in enumerate(((sc[2], near), (1 - sc[2], near), (sc[2], far), (1 - sc[2], far))):
+                        a = own[i].at[l] if kk == 0 else own[4 + i].at[kk - 1]
+                        copies.append(pltpu.make_async_copy(a, w.at[t, h, r, :], sem))
             return copies
 
-        def store(sc, side, t, g, dst, sem):
+        def store(sc, side, g, dst, sem):
             copies = []
             for hr in range(2):
                 h = jnp.where(sc[2] == 0, hr, 1 - hr)
@@ -489,70 +472,72 @@
                     for kk in range(m):
                         z = lax.rem(sc[3] + kk, m)
                         r = pl.ds(pl.multiple_of((2 * z + y) * piece, 16), piece)
-                        out = dst[0].at[hr, yr, kk] if side == 0 else dst[1 + hr * 2 + yr].at[kk]
-                        copies.append(pltpu.make_async_copy(g.at[t, h, r, :], out, sem))
+                        out = dst[0].at[hr, yr, kk] if side == 0 else dst[hr * 2 + yr].at[kk]
+                        copies.append(pltpu.make_async_copy(g.at[h, r, :], out, sem))
             return copies
 
-        out_shapes = [((2, 2, m, piece, HALF), BF16)] + [((m, piece, HALF), BF16)] * 4
-
-        quads = [jnp.stack([a] + [pz(a, kk) for kk in range(1, m)]) for a in start]
-        mine = [quads[0], px(quads[0]), py(quads[0]), pd(quads[0])]
-        quads[1], mine[1] = after(quads[1], mine[1])
-        sources = [mine + [pt(b) for b in mine]]
-        mine = [quads[1], px(quads[1]), py(quads[1]), pd(quads[1])]
-        sources.append(mine)
+        out_shapes = [[((2, 2, m, piece, HALF), BF16)], [((m, piece, HALF), BF16)] * 4]
+        own = jnp.stack(start)
+        firsts = [own, px(own), py(own), pd(own)]
+        columns = [jnp.stack([pz(start[0], kk) for kk in range(1, m)])]
+        columns[0], start[1], *firsts = after(columns[0], start[1], *firsts)
+        columns.append(jnp.stack([pz(start[1], kk) for kk in range(1, m)]))
+        rest = [columns[0], px(columns[0]), py(columns[0]), pd(columns[0])]
+        columns[1], *rest = after(columns[1], *rest)
+        twins = [pt(a) for a in firsts]
+        sources = [firsts + rest + twins + [pt(a) for a in rest]]
+        sources.append(columns[1:] + [px(columns[1]), py(columns[1]), pd(columns[1])])
     else:
-        def load(sc, src, w, sem):
+        def load(l, sc, src, w, sem):
             return [pltpu.make_async_copy(src[0], w, sem)]
 
-        def store(sc, side, t, g, dst, sem):
-            return [pltpu.make_async_copy(g.at[t], dst[0].at[t], sem)]
-
-        out_shapes = [((2, 2, width, HALF), BF16)]
+        def store(sc, side, g, dst, sem):
+            return [pltpu.make_async_copy(g, dst[0], sem)]
+
+        out_shapes = [[((2, width, HALF), BF16)]] * 2
         a = lax.all_gather(jnp.stack([part0, part1]), "dp", axis=1, tiled=True)
         a = lax.all_gather(lax.all_gather(a, "tensor"), "section")
         sources = [[a[0]], [a[1]]]
 
-    both = jnp.concatenate([both, halo], 1)
-    x0 = nn(select, both[0]).astype(BF16)
-    cot = nn(select, both[1]).astype(BF16)
+    batch = jnp.concatenate([both, halo], 1)
+    x0 = nn(select, batch[0]).astype(BF16)
+    cot = nn(select, batch[1]).astype(BF16)
 
     def call(l, phases, **given):
-        return layer_call(phases, sources[l], load, store, out_shapes, scalars, given, total, width, ff, piece)
+        return layer_call(phases, sources[l], functools.partial(load, l), store, out_shapes, scalars, given, total,
+                          width, ff, piece)
 
     r0 = call(0, ["forward"], x=x0)
+    low0 = r0["out"]
     if direct:
-        low0, *mine = after(r0["out"], *sources[1])
-        sources[1] = mine + [pt(b) for b in mine]
-    else:
-        low0 = r0["out"]
-    r1 = call(1, ["forward", "mlp", "attention"], x=low0, u=cot)
+        low0, *rest = after(low0, *sources[1])
+        sources[1] = firsts + rest + twins + [pt(a) for a in rest]
+    r1 = call(1, ["forward", "back", "theirs"], x=low0, u=cot)
     if direct:
         got1 = pt(r1["g"][0])
-    rows = send_rows(r0["out"], r1["out"])
-    m0 = call(0, ["mlp"], **{**r0, "u": r1["in"]})
+    rows = send_rows(low0, r1["out"])
+    m1 = call(1, ["mine"], **r1)
     if direct:
-        m0["res"], *rows = after(m0["res"], *rows)
-        m0["res"], got1 = after(m0["res"], got1)
-        sent1 = add_pair(r1["g"], got1)
-        placed = place_rows(*rows)
-        m0["res"], placed, *sent1 = after(m0["res"], placed, *sent1)
-        other_core = pt(placed)
+        first, got1, *rows = after(m1["g"][0], got1, *rows)
+        sent1 = add_pair([first] + m1["g"][1:], got1)
+        u, *sent1 = after(r1["in"], *sent1)
         quad1 = across(sent1)
     else:
+        u = r1["in"]
+    placed = place_rows(*rows)
+    b0 = call(0, ["back", "theirs"], **{**r0, "u": u})
+    if direct:
+        b0["dg"], b0["g"][0], placed, *quad1 = after(b0["dg"], b0["g"][0], placed, *quad1)
+        got0 = pt(b0["g"][0])
+    layer_outputs = (placed + pt(placed))[None]
+    rows = send_rows(b0["in"].astype(BF16), r1["in"].astype(BF16))
+    m0 = call(0, ["mine"], **{**r0, **b0})
+
+    if direct:
+        first, got0 = after(m0["g"][0], got0)
+        sent0 = add_pair([first] + m0["g"][1:], got0)
+        rows[0], *sent0 = after(rows[0], *sent0)
         placed = place_rows(*rows)
-        other_core = pt(placed)
-    b0 = call(0, ["attention"], **{**r0, **m0})
-    layer_outputs = (placed + other_core)[None]
-
-    if direct:
-        out0, *quad1 = after(b0["g"][0], *quad1)
-        got0 = pt(out0)
-        rows = send_rows(b0["in"].astype(BF16), r1["in"].astype(BF16))
-        got0, *rows = after(got0, *rows)
-        placed = place_rows(*rows)
-        sent0 = add_pair(b0["g"], got0)
-        placed, *sent0 = after(placed, *sent0)
         other_core, *quad0 = after(pt(placed), *across(sent0))
         done = [along(quad1), along(quad0)]
         mine = jnp.where(sec == 0, done[1], done[0])
@@ -561,14 +546,18 @@
         final1 = jnp.where(sec == 0, other, mine)
         small = final1[:, ROWSB:]
     else:
-        placed = place_rows(*send_rows(b0["in"].astype(BF16), r1["in"].astype(BF16)))
+        placed = place_rows(*rows)
         other_core = pt(placed)
-        g = jnp.stack([b0["g"][0], r1["g"][0]])
+
+        def by_core(a, b):
+            return jnp.where(ten == 0, jnp.stack([b, a]), jnp.stack([a, b]))
+
+        g = jnp.stack([by_core(b0["g"][0], m0["g"][0]), by_core(r1["g"][0], m1["g"][0])])
         g = lax.psum_scatter(g.astype(F32), "section", scatter_dimension=0)
         g = lax.psum_scatter(g, "tensor", scatter_dimension=0)
         g = lax.psum_scatter(g, "dp", scatter_dimension=1, tiled=True)
         final0, final1 = g[0], g[1]
-        small = lax.psum(jnp.stack([b0["bias"], r1["bias"]]), ("section", "tensor", "dp"))
+        small = lax.psum(jnp.stack([b0["bsum"], r1["bsum"]]), ("section", "tensor", "dp"))
         small = lax.dynamic_index_in_dim(lax.dynamic_index_in_dim(small, sec, 0, False), ten, 0, False)
 
     input_grads = (placed + other_core).astype(F32)[None]

time: 230 us -> 223 us (0.970)
  waiting for transfers between devices: 83.1 us -> 56.6 us
  starting transfers between devices: 55.4 us -> 69.3 us
  Pallas kernels: 61.6 us -> 67.3 us
    ppermute x12, waiting for transfers between devices: 16.8 us -> 6.71 us  [pz(): lax.ppermute(a, 'dp', [(2 * z + y, 2 * ((z + k) % m) + y) for z in range(...]
    ppermute x4 -> x5, waiting for transfers between devices: 17.3 us -> 9.89 us  [pd(): lax.ppermute(a, ('section', 'dp'), [(i, (i + n_dp) % (2 * n_dp) ^ 1) for...]
    ppermute x1, waiting for transfers between devices: 10.5 us -> 4.13 us  [shards(): lax.ppermute(both[:, :IMG_PAD], 'dp', [(i + 1, i) for i in range(n_dp - 1)])]
    ppermute x4 -> x5, starting transfers between devices: 7.11 us -> 13.4 us  [py(): return lax.ppermute(a, 'dp', [(i, i ^ 1) for i in range(n_dp)])]
    pallas_call x4 -> x5, Pallas kernels: 61.6 us -> 67.3 us  [layer_call(): pl.pallas_call(body, out_shape=[jax.ShapeDtypeStruct(*o) for o in outs],...]
    ppermute x12, starting transfers between devices: 18.3 us -> 23.4 us  [pz(): lax.ppermute(a, 'dp', [(2 * z + y, 2 * ((z + k) % m) + y) for z in range(...]
    ppermute x4 -> x5, waiting for transfers between devices: 22.8 us -> 19 us  [py(): return lax.ppermute(a, 'dp', [(i, i ^ 1) for i in range(n_dp)])]
    ppermute x4, starting transfers between devices: 15.2 us -> 11.4 us  [pn(): return lax.ppermute(a, ('section', 'dp'), pairs)]
  transfers between devices with their start and end apart: 45 -> 52, of which waited for: 23 -> 19; matrix products, arithmetic and copies ran while one was open for 6% -> 7% of each run, Pallas kernels for 16% -> 19%
where the time goes in v5:
time: 223 us; the launch traced here: 222 us
  starting transfers between devices  69.3 us (31%)
  Pallas kernels  67.3 us (30%)
  waiting for transfers between devices  56.6 us (25%)
  other arithmetic  10.7 us (5%)
  local copies, waits for them, and re-layouts  10.3 us (5%)
  matrix products  5.96 us (3%)
  between operations  2.3 us (1%)
    pallas_call x5, Pallas kernels, layer_call(): pl.pallas_call(body, out_shape=[jax.ShapeDtypeStruct(*o) for o in outs],...  67.3 us
    ppermute x12, starting transfers between devices, pz(): lax.ppermute(a, 'dp', [(2 * z + y, 2 * ((z + k) % m) + y) for z in range(...  23.4 us
    ppermute x5, waiting for transfers between devices, py(): return lax.ppermute(a, 'dp', [(i, i ^ 1) for i in range(n_dp)])  19 us
    ppermute x5, starting transfers between devices, py(): return lax.ppermute(a, 'dp', [(i, i ^ 1) for i in range(n_dp)])  13.4 us
    ppermute x9, starting transfers between devices, px(): return lax.ppermute(a, 'section', [(0, 1), (1, 0)])  12.9 us
    ppermute x4, starting transfers between devices, pn(): return lax.ppermute(a, ('section', 'dp'), pairs)  11.4 us
    ppermute x5, waiting for transfers between devices, pd(): lax.ppermute(a, ('section', 'dp'), [(i, (i + n_dp) % (2 * n_dp) ^ 1) for...  9.89 us
    ppermute x9, waiting for transfers between devices, px(): return lax.ppermute(a, 'section', [(0, 1), (1, 0)])  8.96 us
  transfers between devices with their start and end apart: 52, of which 19 were waited for; matrix products, arithmetic and copies ran while one was open for 7% of the time, Pallas kernels for 19%

profile of v5, /device:TPU:0, one launch (start us, length us, event | category | flops | bytes accessed | tf_op | source)
XLA Modules:
  0.0 222.5 jit_solution(12461970811321390403)
XLA Ops:
  0.7 1.3 constant_dynamic-slice_fusion
  2.1 1.3 collective-permute-start.1
  4.0 3.0 %collective-permute-start = (bf16[48,1280]{1,0:T(8,128)(2,1)S(1)}, bf16[48,1280]{1,0:T(8,128)(2,1)S(1)}, u32[]{:S(2)}, u32[]{:S(2)}) collective-permute-start(bf16[48,1280]{1,0:T(8,128)(2,1)S(1)} %broadcast_select_fusion.8), channel_id=1, source_target_pairs={{0,16},{16,0},{1,17},{17,1},{2,18},{18,2},{3,19},{19,3},{4,20},{20... | collective-permute-start | bytes 368648 | tf_op jit(solution)/shard_map/ppermute | solution.py:364
  7.0 3.3 %collective-permute-done = bf16[48,1280]{1,0:T(8,128)(2,1)S(1)} collective-permute-done((bf16[48,1280]{1,0:T(8,128)(2,1)S(1)}, bf16[48,1280]{1,0:T(8,128)(2,1)S(1)}, u32[]{:S(2)}, u32[]{:S(2)}) %collective-permute-start) | collective-permute-done | bytes 122912 | tf_op jit(solution)/shard_map/ppermute | solution.py:364
  10.4 4.1 %collective-permute-done.1 = bf16[2,208,384]{2,1,0:T(8,128)(2,1)S(1)} collective-permute-done((bf16[2,208,384]{2,1,0:T(8,128)(2,1)S(1)}, bf16[2,208,384]{2,1,0:T(8,128)(2,1)S(1)}, u32[]{:S(2)}, u32[]{:S(2)}) %collective-permute-start.1) | collective-permute-done | bytes 319520 | tf_op jit(solution)/shard_map/ppermute | solution.py:432
  14.6 1.8 collective-permute-start.2
  16.4 2.6 %collective-permute-start.3 = (bf16[48,1280]{1,0:T(8,128)(2,1)S(1)}, bf16[48,1280]{1,0:T(8,128)(2,1)S(1)}, u32[]{:S(2)}, u32[]{:S(2)}) collective-permute-start(bf16[48,1280]{1,0:T(8,128)(2,1)S(1)} %get-tuple-element.248), channel_id=1, source_target_pairs={{0,8},{2,10},{4,12},{6,14},{8,0},{10,2},{12,4},{14,6},{1,9},{3,11}... | collective-permute-start | bytes 368648 | tf_op jit(solution)/shard_map/ppermute | solution.py:373
  19.0 1.3 collective-permute-start.4
  20.4 1.6 collective-permute-start.5
  21.9 2.4 %collective-permute-start.6 = (bf16[2,48,1280]{2,1,0:T(8,128)(2,1)S(1)}, bf16[2,48,1280]{2,1,0:T(8,128)(2,1)S(1)}, u32[]{:S(2)}, u32[]{:S(2)}) collective-permute-start(bf16[2,48,1280]{2,1,0:T(8,128)(2,1)S(1)} %pad_maximum_fusion.4.refs_2_.refs_3_.refs_13_), channel_id=1, source_target_pairs={{0,2},{2,0},{4,6},{6,4},{8,10},{10,8},{12,14},{14,12},{1,3},{3,1},... | collective-permute-start | bytes 737288 | tf_op jit(solution)/shard_map/ppermute | solution.py:367
  24.3 1.9 collective-permute-start.7
  26.5 2.5 %collective-permute-done.5.refs_3_.refs_4_.refs_14_ = bf16[2,48,1280]{2,1,0:T(8,128)(2,1)S(1)} collective-permute-done((bf16[2,48,1280]{2,1,0:T(8,128)(2,1)S(1)}, bf16[2,48,1280]{2,1,0:T(8,128)(2,1)S(1)}, u32[]{:S(2)}, u32[]{:S(2)}) %collective-permute-start.5) | collective-permute-done | bytes 245792 | tf_op jit(solution)/shard_map/ppermute | solution.py:364
  29.0 4.2 %collective-permute-done.6.refs_4_.refs_5_.refs_15_ = bf16[2,48,1280]{2,1,0:T(8,128)(2,1)S(1)} collective-permute-done((bf16[2,48,1280]{2,1,0:T(8,128)(2,1)S(1)}, bf16[2,48,1280]{2,1,0:T(8,128)(2,1)S(1)}, u32[]{:S(2)}, u32[]{:S(2)}) %collective-permute-start.6) | collective-permute-done | bytes 245792 | tf_op jit(solution)/shard_map/ppermute | solution.py:367
  33.2 0.8 collective-permute-done.7.refs_5_.refs_6_.refs_16_
  34.0 2.1 collective-permute-start.11
  36.1 3.0 %collective-permute-start.9 = (bf16[48,1280]{1,0:T(8,128)(2,1)S(1)}, bf16[48,1280]{1,0:T(8,128)(2,1)S(1)}, u32[]{:S(2)}, u32[]{:S(2)}) collective-permute-start(bf16[48,1280]{1,0:T(8,128)(2,1)S(1)} %get-tuple-element.105), channel_id=1, source_target_pairs={{0,8},{2,10},{4,12},{6,14},{8,0},{10,2},{12,4},{14,6},{1,9},{3,11}... | collective-permute-start | bytes 368648 | tf_op jit(solution)/shard_map/ppermute | solution.py:373
  39.1 2.9 %collective-permute-start.10 = (bf16[48,1280]{1,0:T(8,128)(2,1)S(1)}, bf16[48,1280]{1,0:T(8,128)(2,1)S(1)}, u32[]{:S(2)}, u32[]{:S(2)}) collective-permute-start(bf16[48,1280]{1,0:T(8,128)(2,1)S(1)} %get-tuple-element.105), channel_id=1, source_target_pairs={{0,12},{2,14},{4,0},{6,2},{8,4},{10,6},{12,8},{14,10},{1,13},{3,15... | collective-permute-start | bytes 368648 | tf_op jit(solution)/shard_map/ppermute | solution.py:373
  42.0 2.8 %collective-permute-start.12 = (bf16[3,48,1280]{2,1,0:T(8,128)(2,1)S(1)}, bf16[3,48,1280]{2,1,0:T(8,128)(2,1)S(1)}, u32[]{:S(2)}, u32[]{:S(2)}) collective-permute-start(bf16[3,48,1280]{2,1,0:T(8,128)(2,1)S(1)} %pad_maximum_fusion.1.refs_6_.refs_17_), channel_id=1, source_target_pairs={{0,2},{2,0},{4,6},{6,4},{8,10},{10,8},{12,14},{14,12},{1,3},{3,1},... | collective-permute-start | bytes 1105928 | tf_op jit(solution)/shard_map/ppermute | solution.py:367
  47.5 6.7 %collective-permute-done.12.refs_8_.refs_19_ = bf16[3,48,1280]{2,1,0:T(8,128)(2,1)S(1)} collective-permute-done((bf16[3,48,1280]{2,1,0:T(8,128)(2,1)S(1)}, bf16[3,48,1280]{2,1,0:T(8,128)(2,1)S(1)}, u32[]{:S(2)}, u32[]{:S(2)}) %collective-permute-start.12) | collective-permute-done | bytes 368672 | tf_op jit(solution)/shard_map/ppermute | solution.py:367
  55.5 1.3 convolution_convert_fusion.5.refs_1_
  56.8 1.0 collective-permute-done.17.refs_13_.refs_14_.refs_24_
  58.4 2.1 collective-permute-start.23
  60.6 0.8 collective-permute-start.24
  61.5 0.7 copy-done.22
  62.2 0.8 copy-done.23
  63.0 13.2 %shard_map.186 = (bf16[416,384]{1,0:T(8,128)(2,1)}, f32[416,384]{1,0:T(8,128)}, f32[416,128]{1,0:T(8,128)}, bf16[416,384]{1,0:T(8,128)(2,1)}, bf16[2,416,640]{2,...) custom-call(s32[5]{0:T(128)} %stack.98.refs_0_, ...), custom_call_target="tpu_custom_call" | custom-call | flops 10000000000 | bytes 8388608 | tf_op jit(solution)/shard_map/pallas_call | solution.py:331
  76.3 1.5 collective-permute-done.24.refs_10_
  78.8 1.3 convolution_convert_fusion.4.refs_2_
  81.3 0.8 copy-done.30
  82.1 24.9 %shard_map.187 = (bf16[416,384]{1,0:T(8,128)(2,1)}, bf16[416,384]{1,0:T(8,128)(2,1)}, bf16[2,416,256]{2,1,0:T(8,128)(2,1)}, bf16[416,384]{1,0:T(8,128)(2,1)}, bf...) custom-call(s32[5]{0:T(128)} %stack.98.refs_0_, ...), custom_call_target="tpu_custom_call" | custom-call | flops 30000001024 | bytes 8388608 | tf_op jit(solution)/shard_map/pallas_call | solution.py:331
  107.5 1.0 broadcast_select_fusion.2
  108.9 3.2 %collective-permute-start.31 = (bf16[208,384]{1,0:T(8,128)(2,1)S(1)}, bf16[208,384]{1,0:T(8,128)(2,1)S(1)}, u32[]{:S(2)}, u32[]{:S(2)}) collective-permute-start(bf16[208,384]{1,0:T(8,128)(2,1)S(1)} %convolution_convert_fusion.9), channel_id=1, source_target_pairs={{0,2},{2,4},{4,6},{6,8},{8,10},{10,12},{12,14},{16,18},{18,20},{20... | collective-permute-start | bytes 479240 | tf_op jit(solution)/shard_map/ppermute | solution.py:396
  112.1 1.4 collective-permute-start.30
  113.9 2.1 collective-permute-start.32
  116.0 5.3 %shard_map.188 = (bf16[4,48,1280]{2,1,0:T(8,128)(2,1)}, bf16[4,48,1280]{2,1,0:T(8,128)(2,1)}, bf16[4,48,1280]{2,1,0:T(8,128)(2,1)}, bf16[4,48,1280]{2,1,0:T(8,128)(2,1)}) custom-call(s32[5]{0:T(128)} %stack.98.refs_0_, bf16[416,384]{1,0:T(8,128)(2,1)} %get-tuple-element.119.refs_1_, bf16[2,416,256]{2,1,0:T(8,128)(2,1)} %get-tuple-element.120.refs_2_, ...), custom_call_target="tpu_custom_call" | custom-call | flops 10000000000 | bytes 8388608 | tf_op jit(solution)/shard_map/pallas_call | solution.py:331
  121.3 2.7 %collective-permute-done.32 = bf16[208,384]{1,0:T(8,128)(2,1)S(1)} collective-permute-done((bf16[208,384]{1,0:T(8,128)(2,1)S(1)}, bf16[208,384]{1,0:T(8,128)(2,1)S(1)}, u32[]{:S(2)}, u32[]{:S(2)}) %collective-permute-start.32) | collective-permute-done | bytes 159776 | tf_op jit(solution)/shard_map/ppermute | solution.py:396
  126.6 2.7 %collective-permute-start.33 = (bf16[4,48,1280]{2,1,0:T(8,128)(2,1)S(1)}, bf16[4,48,1280]{2,1,0:T(8,128)(2,1)S(1)}, u32[]{:S(2)}, u32[]{:S(2)}) collective-permute-start(bf16[4,48,1280]{2,1,0:T(8,128)(2,1)S(1)} %get-tuple-element.156), channel_id=1, source_target_pairs={{0,2},{2,0},{4,6},{6,4},{8,10},{10,8},{12,14},{14,12},{1,3},{3,1},... | collective-permute-start | bytes 1474568 | tf_op jit(solution)/shard_map/ppermute | solution.py:367
  129.3 1.3 collective-permute-start.34
  130.9 18.7 %shard_map.189 = (f32[416,384]{1,0:T(8,128)}, bf16[416,384]{1,0:T(8,128)(2,1)}, bf16[416,1536]{1,0:T(8,128)(2,1)}, f32[8,384]{1,0:T(8,128)}, f32[2,16,128]{2,1,0...) custom-call(s32[5]{0:T(128)} %stack.98.refs_0_, ...), custom_call_target="tpu_custom_call" | custom-call | flops 20000000000 | bytes 8388608 | tf_op jit(solution)/shard_map/pallas_call | solution.py:331
  149.5 1.2 broadcast_select_fusion.1
  150.7 1.4 collective-permute-start.39
  152.9 3.9 %collective-permute-start.38 = (bf16[208,384]{1,0:T(8,128)(2,1)S(1)}, bf16[208,384]{1,0:T(8,128)(2,1)S(1)}, u32[]{:S(2)}, u32[]{:S(2)}) collective-permute-start(bf16[208,384]{1,0:T(8,128)(2,1)S(1)} %convolution_convert_fusion.7), channel_id=1, source_target_pairs={{0,2},{2,4},{4,6},{6,8},{8,10},{10,12},{12,14},{16,18},{18,20},{20... | collective-permute-start | bytes 479240 | tf_op jit(solution)/shard_map/ppermute | solution.py:396
  157.1 2.3 %collective-permute-start.40 = (bf16[208,384]{1,0:T(8,128)(2,1)S(1)}, bf16[208,384]{1,0:T(8,128)(2,1)S(1)}, u32[]{:S(2)}, u32[]{:S(2)}) collective-permute-start(bf16[208,384]{1,0:T(8,128)(2,1)S(1)} %convolution_convert_fusion.6), channel_id=1, source_target_pairs={{0,18},{2,20},{4,22},{6,24},{8,26},{10,28},{12,30},{16,2},{18,4},{... | collective-permute-start | bytes 479240 | tf_op jit(solution)/shard_map/ppermute | solution.py:396
  160.0 3.2 %collective-permute-done.40 = bf16[208,384]{1,0:T(8,128)(2,1)S(1)} collective-permute-done((bf16[208,384]{1,0:T(8,128)(2,1)S(1)}, bf16[208,384]{1,0:T(8,128)(2,1)S(1)}, u32[]{:S(2)}, u32[]{:S(2)}) %collective-permute-start.40) | collective-permute-done | bytes 159776 | tf_op jit(solution)/shard_map/ppermute | solution.py:396
  163.3 5.3 %shard_map.190 = (bf16[4,48,1280]{2,1,0:T(8,128)(2,1)}, bf16[4,48,1280]{2,1,0:T(8,128)(2,1)}, bf16[4,48,1280]{2,1,0:T(8,128)(2,1)}, bf16[4,48,1280]{2,1,0:T(8,128)(2,1)}) custom-call(s32[5]{0:T(128)} %stack.98.refs_0_, bf16[416,384]{1,0:T(8,128)(2,1)} %get-tuple-element.140.refs_4_.refs_1_, bf16[2,416,256]{2,1,0:T(8,128)(2,1)} %get-tuple-element.143.refs_7_.refs_2_, ...), custom_call_target="tpu_custom_call" | custom-call | flops 10000000000 | bytes 8388608 | tf_op jit(solution)/shard_map/pallas_call | solution.py:331
  168.6 1.9 fusion.1
  171.4 3.4 %collective-permute-start.42 = (bf16[4,48,1280]{2,1,0:T(8,128)(2,1)S(1)}, bf16[4,48,1280]{2,1,0:T(8,128)(2,1)S(1)}, u32[]{:S(2)}, u32[]{:S(2)}) collective-permute-start(bf16[4,48,1280]{2,1,0:T(8,128)(2,1)S(1)} %get-tuple-element.176), channel_id=1, source_target_pairs={{0,2},{2,0},{4,6},{6,4},{8,10},{10,8},{12,14},{14,12},{1,3},{3,1},... | collective-permute-start | bytes 1474568 | tf_op jit(solution)/shard_map/ppermute | solution.py:367
  174.7 0.7 collective-permute-start.43
  175.5 0.8 collective-permute-start.44
  176.5 2.0 collective-permute-start.48
  178.6 8.0 %collective-permute-done.42 = bf16[4,48,1280]{2,1,0:T(8,128)(2,1)S(1)} collective-permute-done((bf16[4,48,1280]{2,1,0:T(8,128)(2,1)S(1)}, bf16[4,48,1280]{2,1,0:T(8,128)(2,1)S(1)}, u32[]{:S(2)}, u32[]{:S(2)}) %collective-permute-start.42) | collective-permute-done | bytes 491552 | tf_op jit(solution)/shard_map/ppermute | solution.py:367
  186.6 2.6 %collective-permute-start.49 = (bf16[48,1280]{1,0:T(8,128)(2,1)S(1)}, bf16[48,1280]{1,0:T(8,128)(2,1)S(1)}, u32[]{:S(2)}, u32[]{:S(2)}) collective-permute-start(bf16[48,1280]{1,0:T(8,128)(2,1)S(1)} %get-tuple-element.243), channel_id=1, source_target_pairs={{0,8},{2,10},{4,12},{6,14},{8,0},{10,2},{12,4},{14,6},{1,9},{3,11}... | collective-permute-start | bytes 368648 | tf_op jit(solution)/shard_map/ppermute | solution.py:373
  189.1 1.6 collective-permute-start.50
  190.7 7.6 %collective-permute-done.44 = bf16[4,48,1280]{2,1,0:T(8,128)(2,1)S(1)} collective-permute-done((bf16[4,48,1280]{2,1,0:T(8,128)(2,1)S(1)}, bf16[4,48,1280]{2,1,0:T(8,128)(2,1)S(1)}, u32[]{:S(2)}, u32[]{:S(2)}) %collective-permute-start.44) | collective-permute-done | bytes 491552 | tf_op jit(solution)/shard_map/ppermute | solution.py:370
  198.5 1.8 collective-permute-start.45
  200.4 1.1 collective-permute-start.46
  201.5 2.6 %collective-permute-start.47 = (bf16[48,1280]{1,0:T(8,128)(2,1)S(1)}, bf16[48,1280]{1,0:T(8,128)(2,1)S(1)}, u32[]{:S(2)}, u32[]{:S(2)}) collective-permute-start(bf16[48,1280]{1,0:T(8,128)(2,1)S(1)} %get-tuple-element.245), channel_id=1, source_target_pairs={{0,12},{2,14},{4,0},{6,2},{8,4},{10,6},{12,8},{14,10},{1,13},{3,15... | collective-permute-start | bytes 368648 | tf_op jit(solution)/shard_map/ppermute | solution.py:373
  204.1 1.0 add_bitcast_fusion
  205.1 1.6 collective-permute-done.45
  206.7 4.8 %collective-permute-done.46 = bf16[48,1280]{1,0:T(8,128)(2,1)S(1)} collective-permute-done((bf16[48,1280]{1,0:T(8,128)(2,1)S(1)}, bf16[48,1280]{1,0:T(8,128)(2,1)S(1)}, u32[]{:S(2)}, u32[]{:S(2)}) %collective-permute-start.46) | collective-permute-done | bytes 122912 | tf_op jit(solution)/shard_map/ppermute | solution.py:373
  211.6 0.8 collective-permute-start.51
  212.4 1.3 bitcast_convert_fusion
  213.7 3.1 %collective-permute-done.51 = bf16[48,1280]{1,0:T(8,128)(2,1)S(1)} collective-permute-done((bf16[48,1280]{1,0:T(8,128)(2,1)S(1)}, bf16[48,1280]{1,0:T(8,128)(2,1)S(1)}, u32[]{:S(2)}, u32[]{:S(2)}) %collective-permute-start.51) | collective-permute-done | bytes 122912 | tf_op jit(solution)/shard_map/ppermute | solution.py:364
  218.1 0.7 copy.34
  (204 shorter events, 19.2 us)
Async XLA Ops:
  2.1 12.4 %collective-permute-start.1 = (bf16[2,208,384]{2,1,0:T(8,128)(2,1)S(1)}, bf16[2,208,384]{2,1,0:T(8,128)(2,1)S(1)}, u32[]{:S(2)}, u32[]{:S(2)}) collective-permute-start(bf16[2,208,384]{2,1,0:T(8,128)(2,1)S(1)} %pad_maximum_fusion.3), channel_id=1, source_target_pairs={{2,0},{4,2},{6,4},{8,6},{10,8},{12,10},{14,12},{3,1},{5,3},{7,5},{... | collective-permute-start | bytes 958472 | tf_op jit(solution)/shard_map/ppermute | solution.py:432
  3.8 41.6 %copy-start.37 = (s32[2]{0:T(128)S(1)}, s32[2]{0:T(128)}, u32[]{:S(2)}) copy-start(s32[2]{0:T(128)} %param.12) | copy-start | bytes 28
  4.0 6.4 %collective-permute-start = (bf16[48,1280]{1,0:T(8,128)(2,1)S(1)}, bf16[48,1280]{1,0:T(8,128)(2,1)S(1)}, u32[]{:S(2)}, u32[]{:S(2)}) collective-permute-start(bf16[48,1280]{1,0:T(8,128)(2,1)S(1)} %broadcast_select_fusion.8), channel_id=1, source_target_pairs={{0,16},{16,0},{1,17},{17,1},{2,18},{18,2},{3,19},{19,3},{4,20},{20... | collective-permute-start | bytes 368648 | tf_op jit(solution)/shard_map/ppermute | solution.py:364
  14.6 9.8 %collective-permute-start.2 = (bf16[48,1280]{1,0:T(8,128)(2,1)S(1)}, bf16[48,1280]{1,0:T(8,128)(2,1)S(1)}, u32[]{:S(2)}, u32[]{:S(2)}) collective-permute-start(bf16[48,1280]{1,0:T(8,128)(2,1)S(1)} %get-tuple-element.248), channel_id=1, source_target_pairs={{0,4},{2,6},{4,8},{6,10},{8,12},{10,14},{12,0},{14,2},{1,5},{3,7},... | collective-permute-start | bytes 368648 | tf_op jit(solution)/shard_map/ppermute | solution.py:373
  16.4 9.9 %collective-permute-start.3 = (bf16[48,1280]{1,0:T(8,128)(2,1)S(1)}, bf16[48,1280]{1,0:T(8,128)(2,1)S(1)}, u32[]{:S(2)}, u32[]{:S(2)}) collective-permute-start(bf16[48,1280]{1,0:T(8,128)(2,1)S(1)} %get-tuple-element.248), channel_id=1, source_target_pairs={{0,8},{2,10},{4,12},{6,14},{8,0},{10,2},{12,4},{14,6},{1,9},{3,11}... | collective-permute-start | bytes 368648 | tf_op jit(solution)/shard_map/ppermute | solution.py:373
  19.0 7.5 %collective-permute-start.4 = (bf16[48,1280]{1,0:T(8,128)(2,1)S(1)}, bf16[48,1280]{1,0:T(8,128)(2,1)S(1)}, u32[]{:S(2)}, u32[]{:S(2)}) collective-permute-start(bf16[48,1280]{1,0:T(8,128)(2,1)S(1)} %get-tuple-element.248), channel_id=1, source_target_pairs={{0,12},{2,14},{4,0},{6,2},{8,4},{10,6},{12,8},{14,10},{1,13},{3,15... | collective-permute-start | bytes 368648 | tf_op jit(solution)/shard_map/ppermute | solution.py:373
  20.4 35.0 %copy-start.10 = (bf16[2,48,1280]{2,1,0:T(8,128)(2,1)}, bf16[2,48,1280]{2,1,0:T(8,128)(2,1)S(1)}, u32[]{:S(2)}) copy-start(bf16[2,48,1280]{2,1,0:T(8,128)(2,1)S(1)} %pad_maximum_fusion.4.refs_2_.refs_3_.refs_13_) | copy-start | bytes 737284
  20.4 8.6 %collective-permute-start.5 = (bf16[2,48,1280]{2,1,0:T(8,128)(2,1)S(1)}, bf16[2,48,1280]{2,1,0:T(8,128)(2,1)S(1)}, u32[]{:S(2)}, u32[]{:S(2)}) collective-permute-start(bf16[2,48,1280]{2,1,0:T(8,128)(2,1)S(1)} %pad_maximum_fusion.4.refs_2_.refs_3_.refs_13_), channel_id=1, source_target_pairs={{0,16},{16,0},{1,17},{17,1},{2,18},{18,2},{3,19},{19,3},{4,20},{20... | collective-permute-start | bytes 737288 | tf_op jit(solution)/shard_map/ppermute | solution.py:364
  21.9 11.2 %collective-permute-start.6 = (bf16[2,48,1280]{2,1,0:T(8,128)(2,1)S(1)}, bf16[2,48,1280]{2,1,0:T(8,128)(2,1)S(1)}, u32[]{:S(2)}, u32[]{:S(2)}) collective-permute-start(bf16[2,48,1280]{2,1,0:T(8,128)(2,1)S(1)} %pad_maximum_fusion.4.refs_2_.refs_3_.refs_13_), channel_id=1, source_target_pairs={{0,2},{2,0},{4,6},{6,4},{8,10},{10,8},{12,14},{14,12},{1,3},{3,1},... | collective-permute-start | bytes 737288 | tf_op jit(solution)/shard_map/ppermute | solution.py:367
  24.3 9.6 %collective-permute-start.7 = (bf16[2,48,1280]{2,1,0:T(8,128)(2,1)S(1)}, bf16[2,48,1280]{2,1,0:T(8,128)(2,1)S(1)}, u32[]{:S(2)}, u32[]{:S(2)}) collective-permute-start(bf16[2,48,1280]{2,1,0:T(8,128)(2,1)S(1)} %pad_maximum_fusion.4.refs_2_.refs_3_.refs_13_), channel_id=1, source_target_pairs={{0,18},{2,16},{4,22},{6,20},{8,26},{10,24},{12,30},{14,28},{16,2},... | collective-permute-start | bytes 737288 | tf_op jit(solution)/shard_map/ppermute | solution.py:370
  26.5 28.8 %copy-start.6 = (bf16[3,48,1280]{2,1,0:T(8,128)(2,1)}, bf16[3,48,1280]{2,1,0:T(8,128)(2,1)S(1)}, u32[]{:S(2)}) copy-start(bf16[3,48,1280]{2,1,0:T(8,128)(2,1)S(1)} %pad_maximum_fusion.1.refs_6_.refs_17_) | copy-start | bytes 1105924
  29.0 7.1 %copy-start.31 = (bf16[2,48,1280]{2,1,0:T(8,128)(2,1)}, bf16[2,48,1280]{2,1,0:T(8,128)(2,1)S(1)}, u32[]{:S(2)}) copy-start(bf16[2,48,1280]{2,1,0:T(8,128)(2,1)S(1)} %collective-permute-done.5.refs_3_.refs_4_.refs_14_) | copy-start | bytes 737284
  33.2 8.8 %copy-start.32 = (bf16[2,48,1280]{2,1,0:T(8,128)(2,1)}, bf16[2,48,1280]{2,1,0:T(8,128)(2,1)S(1)}, u32[]{:S(2)}) copy-start(bf16[2,48,1280]{2,1,0:T(8,128)(2,1)S(1)} %collective-permute-done.6.refs_4_.refs_5_.refs_15_) | copy-start | bytes 737284
  34.0 8.0 %copy-start.33 = (bf16[2,48,1280]{2,1,0:T(8,128)(2,1)}, bf16[2,48,1280]{2,1,0:T(8,128)(2,1)S(1)}, u32[]{:S(2)}) copy-start(bf16[2,48,1280]{2,1,0:T(8,128)(2,1)S(1)} %collective-permute-done.7.refs_5_.refs_6_.refs_16_) | copy-start | bytes 737284
  34.0 13.3 %collective-permute-start.11 = (bf16[3,48,1280]{2,1,0:T(8,128)(2,1)S(1)}, bf16[3,48,1280]{2,1,0:T(8,128)(2,1)S(1)}, u32[]{:S(2)}, u32[]{:S(2)}) collective-permute-start(bf16[3,48,1280]{2,1,0:T(8,128)(2,1)S(1)} %pad_maximum_fusion.1.refs_6_.refs_17_), channel_id=1, source_target_pairs={{0,16},{16,0},{1,17},{17,1},{2,18},{18,2},{3,19},{19,3},{4,20},{20... | collective-permute-start | bytes 1105928 | tf_op jit(solution)/shard_map/ppermute | solution.py:364
  36.1 8.7 %collective-permute-start.8 = (bf16[48,1280]{1,0:T(8,128)(2,1)S(1)}, bf16[48,1280]{1,0:T(8,128)(2,1)S(1)}, u32[]{:S(2)}, u32[]{:S(2)}) collective-permute-start(bf16[48,1280]{1,0:T(8,128)(2,1)S(1)} %get-tuple-element.105), channel_id=1, source_target_pairs={{0,4},{2,6},{4,8},{6,10},{8,12},{10,14},{12,0},{14,2},{1,5},{3,7},... | collective-permute-start | bytes 368648 | tf_op jit(solution)/shard_map/ppermute | solution.py:373
  36.1 8.7 %collective-permute-start.9 = (bf16[48,1280]{1,0:T(8,128)(2,1)S(1)}, bf16[48,1280]{1,0:T(8,128)(2,1)S(1)}, u32[]{:S(2)}, u32[]{:S(2)}) collective-permute-start(bf16[48,1280]{1,0:T(8,128)(2,1)S(1)} %get-tuple-element.105), channel_id=1, source_target_pairs={{0,8},{2,10},{4,12},{6,14},{8,0},{10,2},{12,4},{14,6},{1,9},{3,11}... | collective-permute-start | bytes 368648 | tf_op jit(solution)/shard_map/ppermute | solution.py:373
  39.1 5.9 %collective-permute-start.10 = (bf16[48,1280]{1,0:T(8,128)(2,1)S(1)}, bf16[48,1280]{1,0:T(8,128)(2,1)S(1)}, u32[]{:S(2)}, u32[]{:S(2)}) collective-permute-start(bf16[48,1280]{1,0:T(8,128)(2,1)S(1)} %get-tuple-element.105), channel_id=1, source_target_pairs={{0,12},{2,14},{4,0},{6,2},{8,4},{10,6},{12,8},{14,10},{1,13},{3,15... | collective-permute-start | bytes 368648 | tf_op jit(solution)/shard_map/ppermute | solution.py:373
  42.0 12.2 %collective-permute-start.12 = (bf16[3,48,1280]{2,1,0:T(8,128)(2,1)S(1)}, bf16[3,48,1280]{2,1,0:T(8,128)(2,1)S(1)}, u32[]{:S(2)}, u32[]{:S(2)}) collective-permute-start(bf16[3,48,1280]{2,1,0:T(8,128)(2,1)S(1)} %pad_maximum_fusion.1.refs_6_.refs_17_), channel_id=1, source_target_pairs={{0,2},{2,0},{4,6},{6,4},{8,10},{10,8},{12,14},{14,12},{1,3},{3,1},... | collective-permute-start | bytes 1105928 | tf_op jit(solution)/shard_map/ppermute | solution.py:367
  44.8 9.4 %collective-permute-start.13 = (bf16[3,48,1280]{2,1,0:T(8,128)(2,1)S(1)}, bf16[3,48,1280]{2,1,0:T(8,128)(2,1)}, u32[]{:S(2)}, u32[]{:S(2)}) collective-permute-start(bf16[3,48,1280]{2,1,0:T(8,128)(2,1)S(1)} %pad_maximum_fusion.1.refs_6_.refs_17_), channel_id=1, source_target_pairs={{0,18},{2,16},{4,22},{6,20},{8,26},{10,24},{12,30},{14,28},{16,2},... | collective-permute-start | bytes 1105928 | tf_op jit(solution)/shard_map/ppermute | solution.py:370
  44.8 9.9 %collective-permute-start.14 = (bf16[2,48,1280]{2,1,0:T(8,128)(2,1)S(1)}, bf16[2,48,1280]{2,1,0:T(8,128)(2,1)}, u32[]{:S(2)}, u32[]{:S(2)}) collective-permute-start(bf16[2,48,1280]{2,1,0:T(8,128)(2,1)S(1)} %pad_maximum_fusion.4.refs_2_.refs_3_.refs_13_), channel_id=1, source_target_pairs={{0,1},{1,0},{2,3},{3,2},{4,5},{5,4},{6,7},{7,6},{8,9},{9,8},{10,11... | collective-permute-start | bytes 737288 | tf_op jit(solution)/shard_map/ppermute | solution.py:361
  44.9 9.9 %collective-permute-start.15 = (bf16[2,48,1280]{2,1,0:T(8,128)(2,1)}, bf16[2,48,1280]{2,1,0:T(8,128)(2,1)}, u32[]{:S(2)}, u32[]{:S(2)}) collective-permute-start(bf16[2,48,1280]{2,1,0:T(8,128)(2,1)} %copy-done.31), channel_id=1, source_target_pairs={{0,1},{1,0},{2,3},{3,2},{4,5},{5,4},{6,7},{7,6},{8,9},{9,8},{10,11... | collective-permute-start | bytes 737288 | tf_op jit(solution)/shard_map/ppermute | solution.py:361
  47.3 8.0 %copy-start.18 = (bf16[3,48,1280]{2,1,0:T(8,128)(2,1)}, bf16[3,48,1280]{2,1,0:T(8,128)(2,1)S(1)}, u32[]{:S(2)}) copy-start(bf16[3,48,1280]{2,1,0:T(8,128)(2,1)S(1)} %collective-permute-done.11.refs_7_.refs_18_) | copy-start | bytes 1105924
  47.3 8.1 %collective-permute-start.16 = (bf16[2,48,1280]{2,1,0:T(8,128)(2,1)}, bf16[2,48,1280]{2,1,0:T(8,128)(2,1)S(1)}, u32[]{:S(2)}, u32[]{:S(2)}) collective-permute-start(bf16[2,48,1280]{2,1,0:T(8,128)(2,1)} %copy-done.32), channel_id=1, source_target_pairs={{0,1},{1,0},{2,3},{3,2},{4,5},{5,4},{6,7},{7,6},{8,9},{9,8},{10,11... | collective-permute-start | bytes 737288 | tf_op jit(solution)/shard_map/ppermute | solution.py:361
  47.5 30.4 %copy-start.7 = (bf16[3,48,1280]{2,1,0:T(8,128)(2,1)}, bf16[3,48,1280]{2,1,0:T(8,128)(2,1)S(1)}, u32[]{:S(2)}) copy-start(bf16[3,48,1280]{2,1,0:T(8,128)(2,1)S(1)} %pad_maximum_fusion.2.refs_7_) | copy-start | bytes 1105924
  47.5 7.9 %copy-start.34 = (bf16[2,48,1280]{2,1,0:T(8,128)(2,1)S(1)}, bf16[2,48,1280]{2,1,0:T(8,128)(2,1)}, u32[]{:S(2)}) copy-start(bf16[2,48,1280]{2,1,0:T(8,128)(2,1)} %copy-done.33) | copy-start | bytes 737284
  54.2 4.2 %collective-permute-start.18 = (bf16[3,48,1280]{2,1,0:T(8,128)(2,1)S(1)}, bf16[3,48,1280]{2,1,0:T(8,128)(2,1)S(1)}, u32[]{:S(2)}, u32[]{:S(2)}) collective-permute-start(bf16[3,48,1280]{2,1,0:T(8,128)(2,1)S(1)} %pad_maximum_fusion.1.refs_6_.refs_17_), channel_id=1, source_target_pairs={{0,1},{1,0},{2,3},{3,2},{4,5},{5,4},{6,7},{7,6},{8,9},{9,8},{10,11... | collective-permute-start | bytes 1105928 | tf_op jit(solution)/shard_map/ppermute | solution.py:361
  54.2 6.4 %collective-permute-start.19 = (bf16[3,48,1280]{2,1,0:T(8,128)(2,1)S(1)}, bf16[3,48,1280]{2,1,0:T(8,128)(2,1)S(1)}, u32[]{:S(2)}, u32[]{:S(2)}) collective-permute-start(bf16[3,48,1280]{2,1,0:T(8,128)(2,1)S(1)} %collective-permute-done.11.refs_7_.refs_18_), channel_id=1, source_target_pairs={{0,1},{1,0},{2,3},{3,2},{4,5},{5,4},{6,7},{7,6},{8,9},{9,8},{10,11... | collective-permute-start | bytes 1105928 | tf_op jit(solution)/shard_map/ppermute | solution.py:361
  54.7 6.7 %collective-permute-start.20 = (bf16[3,48,1280]{2,1,0:T(8,128)(2,1)S(1)}, bf16[3,48,1280]{2,1,0:T(8,128)(2,1)S(1)}, u32[]{:S(2)}, u32[]{:S(2)}) collective-permute-start(bf16[3,48,1280]{2,1,0:T(8,128)(2,1)S(1)} %collective-permute-done.12.refs_8_.refs_19_), channel_id=1, source_target_pairs={{0,1},{1,0},{2,3},{3,2},{4,5},{5,4},{6,7},{7,6},{8,9},{9,8},{10,11... | collective-permute-start | bytes 1105928 | tf_op jit(solution)/shard_map/ppermute | solution.py:361
  54.8 6.6 %collective-permute-start.21 = (bf16[3,48,1280]{2,1,0:T(8,128)(2,1)}, bf16[3,48,1280]{2,1,0:T(8,128)(2,1)S(1)}, u32[]{:S(2)}, u32[]{:S(2)}) collective-permute-start(bf16[3,48,1280]{2,1,0:T(8,128)(2,1)} %collective-permute-done.13.refs_9_.refs_20_), channel_id=1, source_target_pairs={{0,1},{1,0},{2,3},{3,2},{4,5},{5,4},{6,7},{7,6},{8,9},{9,8},{10,11... | collective-permute-start | bytes 1105928 | tf_op jit(solution)/shard_map/ppermute | solution.py:361
  55.4 6.0 %copy-start.35 = (bf16[2,48,1280]{2,1,0:T(8,128)(2,1)}, bf16[2,48,1280]{2,1,0:T(8,128)(2,1)S(1)}, u32[]{:S(2)}) copy-start(bf16[2,48,1280]{2,1,0:T(8,128)(2,1)S(1)} %collective-permute-done.16.refs_12_.refs_13_.refs_23_) | copy-start | bytes 737284
  55.4 2.4 %collective-permute-start.17 = (bf16[2,48,1280]{2,1,0:T(8,128)(2,1)S(1)}, bf16[2,48,1280]{2,1,0:T(8,128)(2,1)S(1)}, u32[]{:S(2)}, u32[]{:S(2)}) collective-permute-start(bf16[2,48,1280]{2,1,0:T(8,128)(2,1)S(1)} %copy-done.34), channel_id=1, source_target_pairs={{0,1},{1,0},{2,3},{3,2},{4,5},{5,4},{6,7},{7,6},{8,9},{9,8},{10,11... | collective-permute-start | bytes 737288 | tf_op jit(solution)/shard_map/ppermute | solution.py:361
  57.8 18.3 %collective-permute-start.22 = (bf16[3,48,1280]{2,1,0:T(8,128)(2,1)S(1)}, bf16[3,48,1280]{2,1,0:T(8,128)(2,1)S(1)}, u32[]{:S(2)}, u32[]{:S(2)}) collective-permute-start(bf16[3,48,1280]{2,1,0:T(8,128)(2,1)S(1)} %pad_maximum_fusion.2.refs_7_), channel_id=1, source_target_pairs={{0,16},{16,0},{1,17},{17,1},{2,18},{18,2},{3,19},{19,3},{4,20},{20... | collective-permute-start | bytes 1105928 | tf_op jit(solution)/shard_map/ppermute | solution.py:364
  58.4 17.9 %collective-permute-start.23 = (bf16[3,48,1280]{2,1,0:T(8,128)(2,1)S(1)}, bf16[3,48,1280]{2,1,0:T(8,128)(2,1)S(1)}, u32[]{:S(2)}, u32[]{:S(2)}) collective-permute-start(bf16[3,48,1280]{2,1,0:T(8,128)(2,1)S(1)} %pad_maximum_fusion.2.refs_7_), channel_id=1, source_target_pairs={{0,2},{2,0},{4,6},{6,4},{8,10},{10,8},{12,14},{14,12},{1,3},{3,1},... | collective-permute-start | bytes 1105928 | tf_op jit(solution)/shard_map/ppermute | solution.py:367
  60.6 17.2 %collective-permute-start.24 = (bf16[3,48,1280]{2,1,0:T(8,128)(2,1)S(1)}, bf16[3,48,1280]{2,1,0:T(8,128)(2,1)S(1)}, u32[]{:S(2)}, u32[]{:S(2)}) collective-permute-start(bf16[3,48,1280]{2,1,0:T(8,128)(2,1)S(1)} %pad_maximum_fusion.2.refs_7_), channel_id=1, source_target_pairs={{0,18},{2,16},{4,22},{6,20},{8,26},{10,24},{12,30},{14,28},{16,2},... | collective-permute-start | bytes 1105928 | tf_op jit(solution)/shard_map/ppermute | solution.py:370
  77.8 2.3 %collective-permute-start.25 = (bf16[3,48,1280]{2,1,0:T(8,128)(2,1)S(1)}, bf16[3,48,1280]{2,1,0:T(8,128)(2,1)S(1)}, u32[]{:S(2)}, u32[]{:S(2)}) collective-permute-start(bf16[3,48,1280]{2,1,0:T(8,128)(2,1)S(1)} %pad_maximum_fusion.2.refs_7_), channel_id=1, source_target_pairs={{0,1},{1,0},{2,3},{3,2},{4,5},{5,4},{6,7},{7,6},{8,9},{9,8},{10,11... | collective-permute-start | bytes 1105928 | tf_op jit(solution)/shard_map/ppermute | solution.py:361
  77.8 2.3 %collective-permute-start.26 = (bf16[3,48,1280]{2,1,0:T(8,128)(2,1)S(1)}, bf16[3,48,1280]{2,1,0:T(8,128)(2,1)S(1)}, u32[]{:S(2)}, u32[]{:S(2)}) collective-permute-start(bf16[3,48,1280]{2,1,0:T(8,128)(2,1)S(1)} %collective-permute-done.22.refs_8_), channel_id=1, source_target_pairs={{0,1},{1,0},{2,3},{3,2},{4,5},{5,4},{6,7},{7,6},{8,9},{9,8},{10,11... | collective-permute-start | bytes 1105928 | tf_op jit(solution)/shard_map/ppermute | solution.py:361
  78.3 2.2 %collective-permute-start.27 = (bf16[3,48,1280]{2,1,0:T(8,128)(2,1)S(1)}, bf16[3,48,1280]{2,1,0:T(8,128)(2,1)S(1)}, u32[]{:S(2)}, u32[]{:S(2)}) collective-permute-start(bf16[3,48,1280]{2,1,0:T(8,128)(2,1)S(1)} %collective-permute-done.23.refs_9_), channel_id=1, source_target_pairs={{0,1},{1,0},{2,3},{3,2},{4,5},{5,4},{6,7},{7,6},{8,9},{9,8},{10,11... | collective-permute-start | bytes 1105928 | tf_op jit(solution)/shard_map/ppermute | solution.py:361
  78.4 2.7 %collective-permute-start.28 = (bf16[3,48,1280]{2,1,0:T(8,128)(2,1)S(1)}, bf16[3,48,1280]{2,1,0:T(8,128)(2,1)S(1)}, u32[]{:S(2)}, u32[]{:S(2)}) collective-permute-start(bf16[3,48,1280]{2,1,0:T(8,128)(2,1)S(1)} %collective-permute-done.24.refs_10_), channel_id=1, source_target_pairs={{0,1},{1,0},{2,3},{3,2},{4,5},{5,4},{6,7},{7,6},{8,9},{9,8},{10,11... | collective-permute-start | bytes 1105928 | tf_op jit(solution)/shard_map/ppermute | solution.py:361
  80.1 27.4 %copy-start.8 = (bf16[416,384]{1,0:T(8,128)(2,1)S(1)}, bf16[416,384]{1,0:T(8,128)(2,1)}, u32[]{:S(2)}) copy-start(bf16[416,384]{1,0:T(8,128)(2,1)} %get-tuple-element.113.refs_1_) | copy-start | bytes 958468
  107.0 17.0 %collective-permute-start.29 = (bf16[2,2,4,48,1280]{4,3,2,1,0:T(8,128)(2,1)}, bf16[2,2,4,48,1280]{4,3,2,1,0:T(8,128)(2,1)S(1)}, u32[]{:S(2)}, u32[]{:S(2)}) collective-permute-start(bf16[2,2,4,48,1280]{4,3,2,1,0:T(8,128)(2,1)} %get-tuple-element.130), channel_id=1, source_target_pairs={{0,1},{1,0},{2,3},{3,2},{4,5},{5,4},{6,7},{7,6},{8,9},{9,8},{10,11... | collective-permute-start | bytes 5898248 | tf_op jit(solution)/shard_map/ppermute | solution.py:361
  108.9 12.4 %collective-permute-start.31 = (bf16[208,384]{1,0:T(8,128)(2,1)S(1)}, bf16[208,384]{1,0:T(8,128)(2,1)S(1)}, u32[]{:S(2)}, u32[]{:S(2)}) collective-permute-start(bf16[208,384]{1,0:T(8,128)(2,1)S(1)} %convolution_convert_fusion.9), channel_id=1, source_target_pairs={{0,2},{2,4},{4,6},{6,8},{8,10},{10,12},{12,14},{16,18},{18,20},{20... | collective-permute-start | bytes 479240 | tf_op jit(solution)/shard_map/ppermute | solution.py:396
  112.1 11.9 %collective-permute-start.30 = (bf16[416,384]{1,0:T(8,128)(2,1)S(1)}, bf16[416,384]{1,0:T(8,128)(2,1)S(1)}, u32[]{:S(2)}, u32[]{:S(2)}) collective-permute-start(bf16[416,384]{1,0:T(8,128)(2,1)S(1)} %get-tuple-element.237), channel_id=1, source_target_pairs={{0,16},{16,0},{1,17},{17,1},{2,18},{18,2},{3,19},{19,3},{4,20},{20... | collective-permute-start | bytes 958472 | tf_op jit(solution)/shard_map/ppermute | solution.py:364
  113.9 10.1 %collective-permute-start.32 = (bf16[208,384]{1,0:T(8,128)(2,1)S(1)}, bf16[208,384]{1,0:T(8,128)(2,1)S(1)}, u32[]{:S(2)}, u32[]{:S(2)}) collective-permute-start(bf16[208,384]{1,0:T(8,128)(2,1)S(1)} %convolution_convert_fusion.8), channel_id=1, source_target_pairs={{0,18},{2,20},{4,22},{6,24},{8,26},{10,28},{12,30},{16,2},{18,4},{... | collective-permute-start | bytes 479240 | tf_op jit(solution)/shard_map/ppermute | solution.py:396
  126.6 25.8 %collective-permute-start.33 = (bf16[4,48,1280]{2,1,0:T(8,128)(2,1)S(1)}, bf16[4,48,1280]{2,1,0:T(8,128)(2,1)S(1)}, u32[]{:S(2)}, u32[]{:S(2)}) collective-permute-start(bf16[4,48,1280]{2,1,0:T(8,128)(2,1)S(1)} %get-tuple-element.156), channel_id=1, source_target_pairs={{0,2},{2,0},{4,6},{6,4},{8,10},{10,8},{12,14},{14,12},{1,3},{3,1},... | collective-permute-start | bytes 1474568 | tf_op jit(solution)/shard_map/ppermute | solution.py:367
  129.3 23.1 %collective-permute-start.34 = (bf16[4,48,1280]{2,1,0:T(8,128)(2,1)S(1)}, bf16[4,48,1280]{2,1,0:T(8,128)(2,1)S(1)}, u32[]{:S(2)}, u32[]{:S(2)}) collective-permute-start(bf16[4,48,1280]{2,1,0:T(8,128)(2,1)S(1)} %get-tuple-element.157), channel_id=1, source_target_pairs={{0,16},{16,0},{1,17},{17,1},{2,18},{18,2},{3,19},{19,3},{4,20},{20... | collective-permute-start | bytes 1474568 | tf_op jit(solution)/shard_map/ppermute | solution.py:364
  130.6 21.8 %collective-permute-start.35 = (bf16[4,48,1280]{2,1,0:T(8,128)(2,1)S(1)}, bf16[4,48,1280]{2,1,0:T(8,128)(2,1)S(1)}, u32[]{:S(2)}, u32[]{:S(2)}) collective-permute-start(bf16[4,48,1280]{2,1,0:T(8,128)(2,1)S(1)} %get-tuple-element.158), channel_id=1, source_target_pairs={{0,18},{2,16},{4,22},{6,20},{8,26},{10,24},{12,30},{14,28},{16,2},... | collective-permute-start | bytes 1474568 | tf_op jit(solution)/shard_map/ppermute | solution.py:370
  130.8 18.7 %copy-start.1 = (f32[416,384]{1,0:T(8,128)S(1)}, f32[416,384]{1,0:T(8,128)}, u32[]{:S(2)}) copy-start(f32[416,384]{1,0:T(8,128)} %get-tuple-element.137.refs_1_) | copy-start | bytes 1916932
  150.7 8.7 %collective-permute-start.39 = (bf16[416,384]{1,0:T(8,128)(2,1)S(1)}, bf16[416,384]{1,0:T(8,128)(2,1)S(1)}, u32[]{:S(2)}, u32[]{:S(2)}) collective-permute-start(bf16[416,384]{1,0:T(8,128)(2,1)S(1)} %get-tuple-element.236), channel_id=1, source_target_pairs={{0,16},{16,0},{1,17},{17,1},{2,18},{18,2},{3,19},{19,3},{4,20},{20... | collective-permute-start | bytes 958472 | tf_op jit(solution)/shard_map/ppermute | solution.py:364
  152.5 16.1 %collective-permute-start.37 = (bf16[2,2,4,48,1280]{4,3,2,1,0:T(8,128)(2,1)}, bf16[2,2,4,48,1280]{4,3,2,1,0:T(8,128)(2,1)S(1)}, u32[]{:S(2)}, u32[]{:S(2)}) collective-permute-start(bf16[2,2,4,48,1280]{4,3,2,1,0:T(8,128)(2,1)} %get-tuple-element.168), channel_id=1, source_target_pairs={{0,1},{1,0},{2,3},{3,2},{4,5},{5,4},{6,7},{7,6},{8,9},{9,8},{10,11... | collective-permute-start | bytes 5898248 | tf_op jit(solution)/shard_map/ppermute | solution.py:361
  152.9 18.2 %collective-permute-start.38 = (bf16[208,384]{1,0:T(8,128)(2,1)S(1)}, bf16[208,384]{1,0:T(8,128)(2,1)S(1)}, u32[]{:S(2)}, u32[]{:S(2)}) collective-permute-start(bf16[208,384]{1,0:T(8,128)(2,1)S(1)} %convolution_convert_fusion.7), channel_id=1, source_target_pairs={{0,2},{2,4},{4,6},{6,8},{8,10},{10,12},{12,14},{16,18},{18,20},{20... | collective-permute-start | bytes 479240 | tf_op jit(solution)/shard_map/ppermute | solution.py:396
  157.1 6.1 %collective-permute-start.40 = (bf16[208,384]{1,0:T(8,128)(2,1)S(1)}, bf16[208,384]{1,0:T(8,128)(2,1)S(1)}, u32[]{:S(2)}, u32[]{:S(2)}) collective-permute-start(bf16[208,384]{1,0:T(8,128)(2,1)S(1)} %convolution_convert_fusion.6), channel_id=1, source_target_pairs={{0,18},{2,20},{4,22},{6,24},{8,26},{10,28},{12,30},{16,2},{18,4},{... | collective-permute-start | bytes 479240 | tf_op jit(solution)/shard_map/ppermute | solution.py:396
  171.3 27.0 %collective-permute-start.41 = (bf16[2,512,384]{2,1,0:T(8,128)(2,1)S(1)}, bf16[2,512,384]{2,1,0:T(8,128)(2,1)S(1)}, u32[]{:S(2)}, u32[]{:S(2)}) collective-permute-start(bf16[2,512,384]{2,1,0:T(8,128)(2,1)S(1)} %maximum_select_fusion.1), channel_id=1, source_target_pairs={{0,1},{1,0},{2,3},{3,2},{4,5},{5,4},{6,7},{7,6},{8,9},{9,8},{10,11... | collective-permute-start | bytes 2359304 | tf_op jit(solution)/shard_map/ppermute | solution.py:361
  171.4 15.2 %collective-permute-start.42 = (bf16[4,48,1280]{2,1,0:T(8,128)(2,1)S(1)}, bf16[4,48,1280]{2,1,0:T(8,128)(2,1)S(1)}, u32[]{:S(2)}, u32[]{:S(2)}) collective-permute-start(bf16[4,48,1280]{2,1,0:T(8,128)(2,1)S(1)} %get-tuple-element.176), channel_id=1, source_target_pairs={{0,2},{2,0},{4,6},{6,4},{8,10},{10,8},{12,14},{14,12},{1,3},{3,1},... | collective-permute-start | bytes 1474568 | tf_op jit(solution)/shard_map/ppermute | solution.py:367
  174.7 14.4 %collective-permute-start.43 = (bf16[4,48,1280]{2,1,0:T(8,128)(2,1)S(1)}, bf16[4,48,1280]{2,1,0:T(8,128)(2,1)S(1)}, u32[]{:S(2)}, u32[]{:S(2)}) collective-permute-start(bf16[4,48,1280]{2,1,0:T(8,128)(2,1)S(1)} %get-tuple-element.177), channel_id=1, source_target_pairs={{0,16},{16,0},{1,17},{17,1},{2,18},{18,2},{3,19},{19,3},{4,20},{20... | collective-permute-start | bytes 1474568 | tf_op jit(solution)/shard_map/ppermute | solution.py:364
  175.5 22.8 %collective-permute-start.44 = (bf16[4,48,1280]{2,1,0:T(8,128)(2,1)S(1)}, bf16[4,48,1280]{2,1,0:T(8,128)(2,1)S(1)}, u32[]{:S(2)}, u32[]{:S(2)}) collective-permute-start(bf16[4,48,1280]{2,1,0:T(8,128)(2,1)S(1)} %get-tuple-element.178), channel_id=1, source_target_pairs={{0,18},{2,16},{4,22},{6,20},{8,26},{10,24},{12,30},{14,28},{16,2},... | collective-permute-start | bytes 1474568 | tf_op jit(solution)/shard_map/ppermute | solution.py:370
  176.5 23.8 %collective-permute-start.48 = (bf16[48,1280]{1,0:T(8,128)(2,1)S(1)}, bf16[48,1280]{1,0:T(8,128)(2,1)S(1)}, u32[]{:S(2)}, u32[]{:S(2)}) collective-permute-start(bf16[48,1280]{1,0:T(8,128)(2,1)S(1)} %get-tuple-element.241), channel_id=1, source_target_pairs={{0,4},{2,6},{4,8},{6,10},{8,12},{10,14},{12,0},{14,2},{1,5},{3,7},... | collective-permute-start | bytes 368648 | tf_op jit(solution)/shard_map/ppermute | solution.py:373
  186.6 18.5 %collective-permute-start.49 = (bf16[48,1280]{1,0:T(8,128)(2,1)S(1)}, bf16[48,1280]{1,0:T(8,128)(2,1)S(1)}, u32[]{:S(2)}, u32[]{:S(2)}) collective-permute-start(bf16[48,1280]{1,0:T(8,128)(2,1)S(1)} %get-tuple-element.243), channel_id=1, source_target_pairs={{0,8},{2,10},{4,12},{6,14},{8,0},{10,2},{12,4},{14,6},{1,9},{3,11}... | collective-permute-start | bytes 368648 | tf_op jit(solution)/shard_map/ppermute | solution.py:373
  189.1 15.9 %collective-permute-start.50 = (bf16[48,1280]{1,0:T(8,128)(2,1)S(1)}, bf16[48,1280]{1,0:T(8,128)(2,1)S(1)}, u32[]{:S(2)}, u32[]{:S(2)}) collective-permute-start(bf16[48,1280]{1,0:T(8,128)(2,1)S(1)} %get-tuple-element.242), channel_id=1, source_target_pairs={{0,12},{2,14},{4,0},{6,2},{8,4},{10,6},{12,8},{14,10},{1,13},{3,15... | collective-permute-start | bytes 368648 | tf_op jit(solution)/shard_map/ppermute | solution.py:373
  198.3 3.2 %collective-permute-start.36 = (bf16[2,512,384]{2,1,0:T(8,128)(2,1)S(1)}, bf16[2,512,384]{2,1,0:T(8,128)(2,1)S(1)}, u32[]{:S(2)}, u32[]{:S(2)}) collective-permute-start(bf16[2,512,384]{2,1,0:T(8,128)(2,1)S(1)} %maximum_select_fusion), channel_id=1, source_target_pairs={{0,1},{1,0},{2,3},{3,2},{4,5},{5,4},{6,7},{7,6},{8,9},{9,8},{10,11... | collective-permute-start | bytes 2359304 | tf_op jit(solution)/shard_map/ppermute | solution.py:361
  198.5 8.2 %collective-permute-start.45 = (bf16[48,1280]{1,0:T(8,128)(2,1)S(1)}, bf16[48,1280]{1,0:T(8,128)(2,1)S(1)}, u32[]{:S(2)}, u32[]{:S(2)}) collective-permute-start(bf16[48,1280]{1,0:T(8,128)(2,1)S(1)} %get-tuple-element.244), channel_id=1, source_target_pairs={{0,4},{2,6},{4,8},{6,10},{8,12},{10,14},{12,0},{14,2},{1,5},{3,7},... | collective-permute-start | bytes 368648 | tf_op jit(solution)/shard_map/ppermute | solution.py:373
  200.4 11.1 %collective-permute-start.46 = (bf16[48,1280]{1,0:T(8,128)(2,1)S(1)}, bf16[48,1280]{1,0:T(8,128)(2,1)S(1)}, u32[]{:S(2)}, u32[]{:S(2)}) collective-permute-start(bf16[48,1280]{1,0:T(8,128)(2,1)S(1)} %get-tuple-element.246), channel_id=1, source_target_pairs={{0,8},{2,10},{4,12},{6,14},{8,0},{10,2},{12,4},{14,6},{1,9},{3,11}... | collective-permute-start | bytes 368648 | tf_op jit(solution)/shard_map/ppermute | solution.py:373
  201.5 10.0 %collective-permute-start.47 = (bf16[48,1280]{1,0:T(8,128)(2,1)S(1)}, bf16[48,1280]{1,0:T(8,128)(2,1)S(1)}, u32[]{:S(2)}, u32[]{:S(2)}) collective-permute-start(bf16[48,1280]{1,0:T(8,128)(2,1)S(1)} %get-tuple-element.245), channel_id=1, source_target_pairs={{0,12},{2,14},{4,0},{6,2},{8,4},{10,6},{12,8},{14,10},{1,13},{3,15... | collective-permute-start | bytes 368648 | tf_op jit(solution)/shard_map/ppermute | solution.py:373
  211.6 5.3 %collective-permute-start.51 = (bf16[48,1280]{1,0:T(8,128)(2,1)S(1)}, bf16[48,1280]{1,0:T(8,128)(2,1)S(1)}, u32[]{:S(2)}, u32[]{:S(2)}) collective-permute-start(bf16[48,1280]{1,0:T(8,128)(2,1)S(1)} %get-tuple-element.220), channel_id=1, source_target_pairs={{0,16},{16,0},{1,17},{17,1},{2,18},{18,2},{3,19},{19,3},{4,20},{20... | collective-permute-start | bytes 368648 | tf_op jit(solution)/shard_map/ppermute | solution.py:364
  (27 other events, 60.2 us)

commit v6 on v5

--- a/solution.py
+++ b/solution.py
@@ -252,7 +252,7 @@
     gs = grad_shapes(total, width, ff)
     weights = ["ain", "mx", "min", "hd"] + [n for n in gs if n != "res"]
     need = {"forward": ["x"], "back": ["u"] + list(ks), "theirs": weights, "mine": weights}
-    gives = {"forward": {"out": ((total, width), BF16), **ks}, "back": {"in": ((total, width), F32), **gs},
+    gives = {"forward": {"out": ((total, width), BF16), **ks}, "back": {"keep": ((total, width), BF16), "give": ((total, width), BF16), "in": ((total, width), F32), **gs},
              "theirs": {}, "mine": {}}
     made = {}
     for p in phases:
@@ -261,7 +261,9 @@
     if phases[-1] == "forward":
         shown = list(made)
     else:
-        shown = [n for n in made if n in weights or n in ("out", "in")]
+        shown = [n for n in made if n in weights or n in ("keep", "give")]
+        if "forward" in phases:
+            shown.append("in")
     inner = [n for n in made if n not in shown]
     side = {"theirs": 0, "mine": 1}.get(phases[-1])
     products = phases[0] != "mine"
@@ -314,6 +316,12 @@
                 backward_attention(n, w, vec, at["in"], at, at, sums, bsum)
                 return carry
             lax.fori_loop(0, total // IMG_PAD, back, 0)
+            rows = [at[n] for n in (("x", "out") if "forward" in phases else ("in", "u"))]
+            for here in range(2):
+                @pl.when(sc[2] == here)
+                def _():
+                    at["keep"][...] = rows[here][...].astype(BF16)
+                    at["give"][...] = rows[1 - here][...].astype(BF16)
         if ends:
             g = take(1)[0]
             t = jnp.where(sc[1] == 0, 1 - side, side)
@@ -355,7 +363,7 @@
     images = local_rows * n_dp // IMG_LEN
     piece = width // n_dp
     ff = 2 * up_weight.shape[2]
-    direct = piece % 16 == 0
+    direct = piece % 16 == 0 and m == 4
 
     def pt(a):
         return lax.ppermute(a, "tensor", [(0, 1), (1, 0)])
@@ -385,29 +393,37 @@
     def across(sent):
         return [sent[0], py(sent[1]), px(sent[2]), pd(sent[3])]
 
+    def pz_to(a, kk):
+        return lax.ppermute(a, "dp", [(i, i ^ (2 * kk)) for i in range(n_dp)])
+
     def along(quad):
         quad = plus(*quad)
         low = quad.astype(BF16)
-        return plus(quad[0], *[pz(low[kk], kk) for kk in range(1, m)])
-
-    def pn(a, flip):
-        other = n_dp if flip else 0
-        pairs = [(i, (i + other) % (2 * n_dp) + 1) for i in range(2 * n_dp) if i % n_dp < n_dp - 1]
-        return lax.ppermute(a, ("section", "dp"), pairs)
-
-    def send_rows(a0, a1):
-        keep, give = jnp.where(sec == 0, a0, a1), jnp.where(sec == 0, a1, a0)
+        return plus(quad[:, 0], *[pz_to(low[:, kk], kk) for kk in range(1, m)])
+
+    def along_steps(quad):
+        quad = plus(*quad)
+        got = pz_to(quad[:, 1::2].astype(BF16), 1)
+        quad = plus(quad[:, 0::2], got)
+        return plus(quad[:, 0], pz_to(quad[:, 1].astype(BF16), 2))
+
+    def pn(a):
+        return lax.ppermute(a, ("dp", "tensor"), [(2 * i + 1, 2 * i + 3) for i in range(n_dp - 1)])
+
+    def tails(keep, got):
         tail = select[:, local_rows:]
-        tails = [pn(tn(tail, keep).astype(BF16), False), pn(tn(tail, give).astype(BF16), True)]
-        return [keep, px(give)] + tails
-
-    def place_rows(keep, got, tail, got_tail):
+        return pn(jnp.stack([tn(tail, keep), tn(tail, got)]).astype(BF16))
+
+    def placed(keep, got, tail):
         def place(a, b):
             a = tn(select[:, :local_rows], a).astype(BF16)
             return jnp.concatenate([a[:IMG_PAD] + b, a[IMG_PAD:]], 0)
 
-        near, far = place(keep, tail), place(got, got_tail)
-        return jnp.where(sec == 0, jnp.stack([near, far]), jnp.stack([far, near]))
+        return jnp.stack([place(keep, tail[0]), place(got, tail[1])])
+
+    def ordered(a, b):
+        a = a + b
+        return jnp.where(sec == 0, a, a[::-1])[None]
 
     batch_tokens = lax.dynamic_index_in_dim(tokens, sec, 0, keepdims=False)
     batch_cot = lax.dynamic_index_in_dim(cotangent, sec, 0, keepdims=False)
@@ -429,7 +445,7 @@
     scalars = jnp.stack([jnp.minimum(own_count, jnp.maximum(count - own_first, 0)), ten, sec, zi, yi]).astype(jnp.int32)
 
     both = jnp.stack([batch_tokens, batch_cot])
-    halo = lax.ppermute(both[:, :IMG_PAD], "dp", [(i + 1, i) for i in range(n_dp - 1)])
+    halo = lax.ppermute(both[:, :IMG_PAD], ("dp", "tensor"), [(2 * i + 3, 2 * i + 1) for i in range(n_dp - 1)])
     q, k, v = [[qkv_weight[0, :, i, h * HD:(h + 1) * HD] for h in range(3)] for i in range(3)]
     o = out_weight[0].T
     o = [o[:, h * HD:(h + 1) * HD] for h in range(3)]
@@ -470,19 +486,22 @@
                 for yr in range(2):
                     y = jnp.where(sc[4] == 0, yr, 1 - yr)
                     for kk in range(m):
-                        z = lax.rem(sc[3] + kk, m)
+                        z = lax.bitwise_xor(sc[3], kk)
                         r = pl.ds(pl.multiple_of((2 * z + y) * piece, 16), piece)
-                        out = dst[0].at[hr, yr, kk] if side == 0 else dst[hr * 2 + yr].at[kk]
-                        copies.append(pltpu.make_async_copy(g.at[h, r, :], out, sem))
+                        out = dst[0].at[hr, yr] if side == 0 else dst[hr * 2 + yr]
+                        for c in range(2):
+                            a = g.at[h, r, c * part:(c + 1) * part]
+                            copies.append(pltpu.make_async_copy(a, out.at[c, kk], sem))
             return copies
 
-        out_shapes = [[((2, 2, m, piece, HALF), BF16)], [((m, piece, HALF), BF16)] * 4]
+        part = HALF // 2
+        out_shapes = [[((2, 2, 2, m, piece, part), BF16)], [((2, m, piece, part), BF16)] * 4]
         own = jnp.stack(start)
         firsts = [own, px(own), py(own), pd(own)]
         columns = [jnp.stack([pz(start[0], kk) for kk in range(1, m)])]
-        columns[0], start[1], *firsts = after(columns[0], start[1], *firsts)
+        rest = [columns[0], px(columns[0]), py(columns[0]), pd(columns[0])]
+        start[1], _, *firsts = after(start[1], columns[0], *firsts)
         columns.append(jnp.stack([pz(start[1], kk) for kk in range(1, m)]))
-        rest = [columns[0], px(columns[0]), py(columns[0]), pd(columns[0])]
         columns[1], *rest = after(columns[1], *rest)
         twins = [pt(a) for a in firsts]
         sources = [firsts + rest + twins + [pt(a) for a in rest]]
@@ -515,39 +534,48 @@
     r1 = call(1, ["forward", "back", "theirs"], x=low0, u=cot)
     if direct:
         got1 = pt(r1["g"][0])
-    rows = send_rows(low0, r1["out"])
+    low_got = px(r1["give"])
     m1 = call(1, ["mine"], **r1)
+    u = r1["in"]
     if direct:
-        first, got1, *rows = after(m1["g"][0], got1, *rows)
+        first, got1, low_got = after(m1["g"][0], got1, low_got)
         sent1 = add_pair([first] + m1["g"][1:], got1)
-        u, *sent1 = after(r1["in"], *sent1)
+        low_tails = tails(r1["keep"], low_got)
+        u, *sent1 = after(u, *sent1)
         quad1 = across(sent1)
     else:
-        u = r1["in"]
-    placed = place_rows(*rows)
+        low_tails = tails(r1["keep"], low_got)
     b0 = call(0, ["back", "theirs"], **{**r0, "u": u})
     if direct:
-        b0["dg"], b0["g"][0], placed, *quad1 = after(b0["dg"], b0["g"][0], placed, *quad1)
+        b0["dg"], b0["g"][0], low_tails, *quad1 = after(b0["dg"], b0["g"][0], low_tails, *quad1)
         got0 = pt(b0["g"][0])
-    layer_outputs = (placed + pt(placed))[None]
-    rows = send_rows(b0["in"].astype(BF16), r1["in"].astype(BF16))
+    low_rows = placed(r1["keep"], low_got, low_tails)
+    low_twin = pt(low_rows)
+    in_got = px(b0["give"])
     m0 = call(0, ["mine"], **{**r0, **b0})
 
     if direct:
-        first, got0 = after(m0["g"][0], got0)
+        first, got0, in_got, low_twin = after(m0["g"][0], got0, in_got, low_twin)
         sent0 = add_pair([first] + m0["g"][1:], got0)
-        rows[0], *sent0 = after(rows[0], *sent0)
-        placed = place_rows(*rows)
-        other_core, *quad0 = after(pt(placed), *across(sent0))
-        done = [along(quad1), along(quad0)]
-        mine = jnp.where(sec == 0, done[1], done[0])
-        other = px(jnp.where(sec == 0, done[0], done[1]).astype(BF16)).astype(F32)
+        both = after(in_got, *sent0, *quad1)
+        in_got, sent0, quad1 = both[0], both[1:5], both[5:]
+        in_tails = tails(b0["keep"], in_got)
+        quad0 = [across([a[c:c + 1] for a in sent0]) for c in range(2)]
+        in_rows = placed(b0["keep"], in_got, in_tails)
+        in_twin, *quad0[1] = after(pt(in_rows), *quad0[1])
+        done1 = along_steps(quad1)
+        done0 = [along_steps(quad0[0])]
+        done1, done0[0], *quad0[1] = after(done1, done0[0], *quad0[1])
+        done0 = jnp.concatenate(done0 + [along(quad0[1])])
+        mine = jnp.where(sec == 0, done0, done1)
+        other = px(jnp.where(sec == 0, done1, done0).astype(BF16)).astype(F32)
         final0 = jnp.where(sec == 0, mine, other)
         final1 = jnp.where(sec == 0, other, mine)
+        final0, final1 = [jnp.concatenate([a[0], a[1]], 1) for a in (final0, final1)]
         small = final1[:, ROWSB:]
     else:
-        placed = place_rows(*rows)
-        other_core = pt(placed)
+        in_rows = placed(b0["keep"], in_got, tails(b0["keep"], in_got))
+        in_twin = pt(in_rows)
 
         def by_core(a, b):
             return jnp.where(ten == 0, jnp.stack([b, a]), jnp.stack([a, b]))
@@ -560,7 +588,8 @@
         small = lax.psum(jnp.stack([b0["bsum"], r1["bsum"]]), ("section", "tensor", "dp"))
         small = lax.dynamic_index_in_dim(lax.dynamic_index_in_dim(small, sec, 0, False), ten, 0, False)
 
-    input_grads = (placed + other_core).astype(F32)[None]
+    layer_outputs = ordered(low_rows, low_twin)
+    input_grads = ordered(in_rows, in_twin).astype(F32)
 
     def heads(*starts):
         return [final0[:, s * HD:(s + 1) * HD] for s in starts]

time: 223 us -> 214 us (0.960)
  starting transfers between devices: 69.3 us -> 53.4 us
  waiting for transfers between devices: 56.6 us -> 60.8 us
    ppermute x12 -> x6, starting transfers between devices: 23.4 us -> 8.26 us  [pz(): lax.ppermute(a, 'dp', [(2 * z + y, 2 * ((z + k) % m) + y) for z in range(...]
    ppermute x5 -> x6, waiting for transfers between devices: 19 us -> 13.5 us  [py(): return lax.ppermute(a, 'dp', [(i, i ^ 1) for i in range(n_dp)])]
    ppermute x5 -> x10, waiting for transfers between devices: 10.1 us -> 14.9 us  [the longest x7 14.9 us: pz_to(): return lax.ppermute(a, 'dp', [(i, i ^ 2 * kk) for i in range(n_dp)])]
    ppermute x5 -> x6, starting transfers between devices: 13.4 us -> 9.3 us  [py(): return lax.ppermute(a, 'dp', [(i, i ^ 1) for i in range(n_dp)])]
    ppermute x9 -> x10, waiting for transfers between devices: 8.96 us -> 12.6 us  [px(): return lax.ppermute(a, 'section', [(0, 1), (1, 0)])]
    ppermute x5 -> x6, starting transfers between devices: 3.81 us -> 7.4 us  [pd(): lax.ppermute(a, ('section', 'dp'), [(i, (i + n_dp) % (2 * n_dp) ^ 1) for...]
    select_n x4 -> x0, other arithmetic: 2.53 us -> none  [the longest x2 2.25 us: send_rows(): keep, give = (jnp.where(sec == 0, a0, a1), jnp.where(sec == 0, a1, a0))]
    ppermute x5 -> x10, starting transfers between devices: 12.7 us -> 10.5 us  [the longest x7 8.45 us: pz_to(): return lax.ppermute(a, 'dp', [(i, i ^ 2 * kk) for i in range(n_dp)])]
  transfers between devices with their start and end apart: 52 -> 54, of which waited for: 19 -> 22; matrix products, arithmetic and copies ran while one was open for 7% -> 5% of each run, Pallas kernels for 19% -> 20%
where the time goes in v6:
time: 214 us; the launch traced here: 213 us
  Pallas kernels  68 us (32%)
  waiting for transfers between devices  60.8 us (28%)
  starting transfers between devices  53.4 us (25%)
  local copies, waits for them, and re-layouts  11.2 us (5%)
  other arithmetic  9.59 us (4%)
  matrix products  7.99 us (4%)
  between operations  2.41 us (1%)
    pallas_call x5, Pallas kernels, layer_call(): pl.pallas_call(body, out_shape=[jax.ShapeDtypeStruct(*o) for o in outs],...  68 us
    ppermute x7, waiting for transfers between devices, pz_to(): return lax.ppermute(a, 'dp', [(i, i ^ 2 * kk) for i in range(n_dp)])  14.9 us
    ppermute x10, starting transfers between devices, px(): return lax.ppermute(a, 'section', [(0, 1), (1, 0)])  14.7 us
    ppermute x6, waiting for transfers between devices, py(): return lax.ppermute(a, 'dp', [(i, i ^ 1) for i in range(n_dp)])  13.5 us
    ppermute x10, waiting for transfers between devices, px(): return lax.ppermute(a, 'section', [(0, 1), (1, 0)])  12.6 us
    ppermute x6, waiting for transfers between devices, pd(): lax.ppermute(a, ('section', 'dp'), [(i, (i + n_dp) % (2 * n_dp) ^ 1) for...  9.77 us
    ppermute x6, starting transfers between devices, py(): return lax.ppermute(a, 'dp', [(i, i ^ 1) for i in range(n_dp)])  9.3 us
    ppermute x7, starting transfers between devices, pz_to(): return lax.ppermute(a, 'dp', [(i, i ^ 2 * kk) for i in range(n_dp)])  8.45 us
  transfers between devices with their start and end apart: 54, of which 22 were waited for; matrix products, arithmetic and copies ran while one was open for 5% of the time, Pallas kernels for 20%

profile of v6, /device:TPU:0, one launch (start us, length us, event | category | flops | bytes accessed | tf_op | source)
XLA Modules:
  0.0 213.3 jit_solution(10222522283223369253)
XLA Ops:
  0.7 1.3 constant_dynamic-slice_fusion
  3.4 3.0 %collective-permute-start = (bf16[48,1280]{1,0:T(8,128)(2,1)S(1)}, bf16[48,1280]{1,0:T(8,128)(2,1)S(1)}, u32[]{:S(2)}, u32[]{:S(2)}) collective-permute-start(bf16[48,1280]{1,0:T(8,128)(2,1)S(1)} %broadcast_select_fusion.3), channel_id=1, source_target_pairs={{0,16},{16,0},{1,17},{17,1},{2,18},{18,2},{3,19},{19,3},{4,20},{20... | collective-permute-start | bytes 368648 | tf_op jit(solution)/shard_map/ppermute | solution.py:372
  6.4 3.9 %collective-permute-done = bf16[48,1280]{1,0:T(8,128)(2,1)S(1)} collective-permute-done((bf16[48,1280]{1,0:T(8,128)(2,1)S(1)}, bf16[48,1280]{1,0:T(8,128)(2,1)S(1)}, u32[]{:S(2)}, u32[]{:S(2)}) %collective-permute-start) | collective-permute-done | bytes 122912 | tf_op jit(solution)/shard_map/ppermute | solution.py:372
  10.4 1.2 collective-permute-start.2
  11.6 2.6 %collective-permute-start.3 = (bf16[48,1280]{1,0:T(8,128)(2,1)S(1)}, bf16[48,1280]{1,0:T(8,128)(2,1)S(1)}, u32[]{:S(2)}, u32[]{:S(2)}) collective-permute-start(bf16[48,1280]{1,0:T(8,128)(2,1)S(1)} %get-tuple-element.263), channel_id=1, source_target_pairs={{0,8},{2,10},{4,12},{6,14},{8,0},{10,2},{12,4},{14,6},{1,9},{3,11}... | collective-permute-start | bytes 368648 | tf_op jit(solution)/shard_map/ppermute | solution.py:381
  14.2 1.3 collective-permute-start.4
  15.6 1.6 collective-permute-start.5
  17.1 2.4 %collective-permute-start.6 = (bf16[2,48,1280]{2,1,0:T(8,128)(2,1)S(1)}, bf16[2,48,1280]{2,1,0:T(8,128)(2,1)}, u32[]{:S(2)}, u32[]{:S(2)}) collective-permute-start(bf16[2,48,1280]{2,1,0:T(8,128)(2,1)S(1)} %pad_maximum_fusion.8.refs_2_.refs_3_.refs_13_), channel_id=1, source_target_pairs={{0,2},{2,0},{4,6},{6,4},{8,10},{10,8},{12,14},{14,12},{1,3},{3,1},... | collective-permute-start | bytes 737288 | tf_op jit(solution)/shard_map/ppermute | solution.py:375
  19.6 1.8 collective-permute-start.7
  21.4 2.2 %collective-permute-done.3 = bf16[48,1280]{1,0:T(8,128)(2,1)S(1)} collective-permute-done((bf16[48,1280]{1,0:T(8,128)(2,1)S(1)}, bf16[48,1280]{1,0:T(8,128)(2,1)S(1)}, u32[]{:S(2)}, u32[]{:S(2)}) %collective-permute-start.3) | collective-permute-done | bytes 122912 | tf_op jit(solution)/shard_map/ppermute | solution.py:381
  23.6 1.6 collective-permute-start.11
  25.2 5.1 %collective-permute-done.6.refs_4_.refs_5_.refs_15_ = bf16[2,48,1280]{2,1,0:T(8,128)(2,1)} collective-permute-done((bf16[2,48,1280]{2,1,0:T(8,128)(2,1)S(1)}, bf16[2,48,1280]{2,1,0:T(8,128)(2,1)}, u32[]{:S(2)}, u32[]{:S(2)}) %collective-permute-start.6) | collective-permute-done | bytes 245792 | tf_op jit(solution)/shard_map/ppermute | solution.py:375
  30.3 1.3 collective-permute-done.7.refs_5_.refs_6_.refs_16_
  32.3 3.1 %collective-permute-start.10 = (bf16[48,1280]{1,0:T(8,128)(2,1)S(1)}, bf16[48,1280]{1,0:T(8,128)(2,1)S(1)}, u32[]{:S(2)}, u32[]{:S(2)}) collective-permute-start(bf16[48,1280]{1,0:T(8,128)(2,1)S(1)} %get-tuple-element.115), channel_id=1, source_target_pairs={{0,12},{2,14},{4,0},{6,2},{8,4},{10,6},{12,8},{14,10},{1,13},{3,15... | collective-permute-start | bytes 368648 | tf_op jit(solution)/shard_map/ppermute | solution.py:381
  35.4 1.3 collective-permute-start.12
  36.7 3.0 %collective-permute-done.8 = bf16[48,1280]{1,0:T(8,128)(2,1)S(1)} collective-permute-done((bf16[48,1280]{1,0:T(8,128)(2,1)S(1)}, bf16[48,1280]{1,0:T(8,128)(2,1)S(1)}, u32[]{:S(2)}, u32[]{:S(2)}) %collective-permute-start.8) | collective-permute-done | bytes 122912 | tf_op jit(solution)/shard_map/ppermute | solution.py:381
  40.0 2.9 %collective-permute-done.9 = bf16[48,1280]{1,0:T(8,128)(2,1)S(1)} collective-permute-done((bf16[48,1280]{1,0:T(8,128)(2,1)S(1)}, bf16[48,1280]{1,0:T(8,128)(2,1)S(1)}, u32[]{:S(2)}, u32[]{:S(2)}) %collective-permute-start.9) | collective-permute-done | bytes 122912 | tf_op jit(solution)/shard_map/ppermute | solution.py:381
  45.4 8.4 %collective-permute-done.12.refs_8_.refs_19_ = bf16[3,48,1280]{2,1,0:T(8,128)(2,1)S(1)} collective-permute-done((bf16[3,48,1280]{2,1,0:T(8,128)(2,1)S(1)}, bf16[3,48,1280]{2,1,0:T(8,128)(2,1)S(1)}, u32[]{:S(2)}, u32[]{:S(2)}) %collective-permute-start.12) | collective-permute-done | bytes 368672 | tf_op jit(solution)/shard_map/ppermute | solution.py:375
  55.2 1.3 convolution_convert_fusion.5.refs_1_
  56.5 1.0 collective-permute-done.17.refs_13_.refs_14_.refs_24_
  57.5 1.5 collective-permute-start.22
  59.0 0.9 collective-permute-start.23
  59.9 1.1 collective-permute-start.24
  61.8 0.8 copy-done.21
  62.5 13.2 %shard_map.186 = (bf16[416,384]{1,0:T(8,128)(2,1)}, f32[416,384]{1,0:T(8,128)}, f32[416,128]{1,0:T(8,128)}, bf16[416,384]{1,0:T(8,128)(2,1)}, bf16[2,416,640]{2,...) custom-call(s32[5]{0:T(128)} %stack.112.refs_0_, ...), custom_call_target="tpu_custom_call" | custom-call | flops 10000000000 | bytes 8388608 | tf_op jit(solution)/shard_map/pallas_call | solution.py:339
  75.8 1.5 collective-permute-done.24.refs_10_
  78.2 1.3 convolution_convert_fusion.4.refs_2_
  80.7 0.8 copy-done.28
  81.5 25.3 %shard_map.187 = (bf16[416,384]{1,0:T(8,128)(2,1)}, bf16[2,416,256]{2,1,0:T(8,128)(2,1)}, bf16[416,384]{1,0:T(8,128)(2,1)}, bf16[416,1536]{1,0:T(8,128)(2,1)}, b...) custom-call(s32[5]{0:T(128)} %stack.112.refs_0_, ...), custom_call_target="tpu_custom_call" | custom-call | flops 30000001024 | bytes 8388608 | tf_op jit(solution)/shard_map/pallas_call | solution.py:339
  106.8 1.8 copy.42
  109.1 0.8 collective-permute-start.30
  109.9 5.3 %shard_map.188 = (bf16[2,4,48,640]{3,2,1,0:T(8,128)(2,1)}, bf16[2,4,48,640]{3,2,1,0:T(8,128)(2,1)}, bf16[2,4,48,640]{3,2,1,0:T(8,128)(2,1)}, bf16[2,4,48,640]{3,2,1,0:T(8,128)(2,1)}) custom-call(s32[5]{0:T(128)} %stack.112.refs_0_, bf16[416,384]{1,0:T(8,128)(2,1)} %get-tuple-element.129.refs_1_, bf16[2,416,256]{2,1,0:T(8,128)(2,1)} %get-tuple-element.130.refs_2_, ...), custom_call_target="tpu_custom_call" | custom-call | flops 10000000000 | bytes 8388608 | tf_op jit(solution)/shard_map/pallas_call | solution.py:339
  116.1 2.8 %collective-permute-done.30 = bf16[416,384]{1,0:T(8,128)(2,1)S(1)} collective-permute-done((bf16[416,384]{1,0:T(8,128)(2,1)S(1)}, bf16[416,384]{1,0:T(8,128)(2,1)S(1)}, u32[]{:S(2)}, u32[]{:S(2)}) %collective-permute-start.30) | collective-permute-done | bytes 319520 | tf_op jit(solution)/shard_map/ppermute | solution.py:372
  120.6 1.1 collective-permute-start.32
  121.7 1.2 collective-permute-start.33
  123.0 1.2 collective-permute-start.34
  124.2 19.0 %shard_map.189 = (bf16[416,384]{1,0:T(8,128)(2,1)}, bf16[416,384]{1,0:T(8,128)(2,1)}, bf16[416,384]{1,0:T(8,128)(2,1)}, bf16[416,1536]{1,0:T(8,128)(2,1)}, f32[8...) custom-call(s32[5]{0:T(128)} %stack.112.refs_0_, ...), custom_call_target="tpu_custom_call" | custom-call | flops 20000000000 | bytes 8388608 | tf_op jit(solution)/shard_map/pallas_call | solution.py:339
  143.2 3.3 %collective-permute-done.34 = bf16[2,4,48,640]{3,2,0,1:T(8,128)(2,1)S(1)} collective-permute-done((bf16[2,4,48,640]{3,2,0,1:T(8,128)(2,1)S(1)}, bf16[2,4,48,640]{3,2,0,1:T(8,128)(2,1)S(1)}, u32[]{:S(2)}, u32[]{:S(2)}) %collective-permute-start.34) | collective-permute-done | bytes 491552 | tf_op jit(solution)/shard_map/ppermute | solution.py:378
  147.2 1.3 collective-permute-start.36
  149.7 5.3 %shard_map.190 = (bf16[2,4,48,640]{3,2,1,0:T(8,128)(2,1)}, bf16[2,4,48,640]{3,2,1,0:T(8,128)(2,1)}, bf16[2,4,48,640]{3,2,1,0:T(8,128)(2,1)}, bf16[2,4,48,640]{3,2,1,0:T(8,128)(2,1)}) custom-call(s32[5]{0:T(128)} %stack.112.refs_0_, bf16[416,384]{1,0:T(8,128)(2,1)} %get-tuple-element.150.refs_4_.refs_1_, ...), custom_call_target="tpu_custom_call" | custom-call | flops 10000000000 | bytes 8388608 | tf_op jit(solution)/shard_map/pallas_call | solution.py:339
  154.9 2.4 %collective-permute-done.36 = bf16[416,384]{1,0:T(8,128)(2,1)} collective-permute-done((bf16[416,384]{1,0:T(8,128)(2,1)}, bf16[416,384]{1,0:T(8,128)(2,1)}, u32[]{:S(2)}, u32[]{:S(2)}) %collective-permute-start.36) | collective-permute-done | bytes 319520 | tf_op jit(solution)/shard_map/ppermute | solution.py:372
  157.3 1.9 fusion.5
  159.3 1.3 fusion.4
  160.6 1.5 convolution_convert_fusion
  162.2 1.9 collective-permute-start.45
  164.2 1.3 collective-permute-start.46
  166.3 2.2 %collective-permute-start.43 = (bf16[2,2,48,640]{3,2,0,1:T(8,128)(2,1)S(1)}, bf16[2,2,48,640]{3,2,0,1:T(8,128)(2,1)S(1)}, u32[]{:S(2)}, u32[]{:S(2)}) collective-permute-start(bf16[2,2,48,640]{3,2,0,1:T(8,128)(2,1)S(1)} %slice.304), channel_id=1, source_target_pairs={{0,4},{2,6},{4,0},{6,2},{8,12},{10,14},{12,8},{14,10},{1,5},{3,7},... | collective-permute-start | bytes 737288 | tf_op jit(solution)/shard_map/ppermute | solution.py:397
  169.4 1.0 fusion.11
  170.4 1.7 collective-permute-start.40
  172.1 0.9 collective-permute-done.46
  173.1 1.2 collective-permute-start.41
  174.3 3.7 %collective-permute-done.47 = bf16[1,4,48,640]{3,2,1,0:T(8,128)(2,1)S(1)} collective-permute-done((bf16[1,4,48,640]{3,2,1,0:T(8,128)(2,1)S(1)}, bf16[1,4,48,640]{3,2,1,0:T(8,128)(2,1)S(1)}, u32[]{:S(2)}, u32[]{:S(2)}) %collective-permute-start.47) | collective-permute-done | bytes 245792 | tf_op jit(solution)/shard_map/ppermute | solution.py:378
  178.0 2.5 %collective-permute-start.42 = (bf16[1,4,48,640]{3,2,1,0:T(8,128)(2,1)S(1)}, bf16[1,4,48,640]{3,2,1,0:T(8,128)(2,1)S(1)}, u32[]{:S(2)}, u32[]{:S(2)}) collective-permute-start(bf16[1,4,48,640]{3,2,1,0:T(8,128)(2,1)S(1)} %get-tuple-element.262), channel_id=1, source_target_pairs={{0,18},{2,16},{4,22},{6,20},{8,26},{10,24},{12,30},{14,28},{16,2},... | collective-permute-start | bytes 737288 | tf_op jit(solution)/shard_map/ppermute | solution.py:378
  181.4 1.2 collective-permute-start.44
  182.8 4.5 %collective-permute-done.48 = bf16[1,2,48,640]{3,2,1,0:T(8,128)(2,1)S(1)} collective-permute-done((bf16[1,2,48,640]{3,2,1,0:T(8,128)(2,1)S(1)}, bf16[1,2,48,640]{3,2,1,0:T(8,128)(2,1)S(1)}, u32[]{:S(2)}, u32[]{:S(2)}) %collective-permute-start.48) | collective-permute-done | bytes 122912 | tf_op jit(solution)/shard_map/ppermute | solution.py:397
  187.3 1.4 collective-permute-done.44
  188.8 5.2 %collective-permute-done.49 = bf16[1,48,640]{2,1,0:T(8,128)(2,1)S(1)} collective-permute-done((bf16[1,48,640]{2,1,0:T(8,128)(2,1)S(1)}, bf16[1,48,640]{2,1,0:T(8,128)(2,1)S(1)}, u32[]{:S(2)}, u32[]{:S(2)}) %collective-permute-start.49) | collective-permute-done | bytes 61472 | tf_op jit(solution)/shard_map/ppermute | solution.py:397
  194.3 2.3 %collective-permute-start.51 = (bf16[1,48,640]{2,1,0:T(8,128)(2,1)S(1)}, bf16[1,48,640]{2,1,0:T(8,128)(2,1)S(1)}, u32[]{:S(2)}, u32[]{:S(2)}) collective-permute-start(bf16[1,48,640]{2,1,0:T(8,128)(2,1)S(1)} %get-tuple-element.275), channel_id=1, source_target_pairs={{0,8},{2,10},{4,12},{6,14},{8,0},{10,2},{12,4},{14,6},{1,9},{3,11}... | collective-permute-start | bytes 184328 | tf_op jit(solution)/shard_map/ppermute | solution.py:397
  196.6 2.1 collective-permute-start.52
  198.8 1.0 collective-permute-done.50
  199.8 2.8 %collective-permute-done.52 = bf16[1,48,640]{2,1,0:T(8,128)(2,1)S(1)} collective-permute-done((bf16[1,48,640]{2,1,0:T(8,128)(2,1)S(1)}, bf16[1,48,640]{2,1,0:T(8,128)(2,1)S(1)}, u32[]{:S(2)}, u32[]{:S(2)}) %collective-permute-start.52) | collective-permute-done | bytes 61472 | tf_op jit(solution)/shard_map/ppermute | solution.py:397
  202.7 1.3 collective-permute-start.53
  204.0 1.2 fusion.13
  205.2 2.4 %collective-permute-done.53 = bf16[2,48,640]{2,1,0:T(8,128)(2,1)S(1)} collective-permute-done((bf16[2,48,640]{2,1,0:T(8,128)(2,1)S(1)}, bf16[2,48,640]{2,1,0:T(8,128)(2,1)S(1)}, u32[]{:S(2)}, u32[]{:S(2)}) %collective-permute-start.53) | collective-permute-done | bytes 122912 | tf_op jit(solution)/shard_map/ppermute | solution.py:372
  (221 shorter events, 22.3 us)
Async XLA Ops:
  2.1 8.3 %collective-permute-start.1 = (bf16[2,208,384]{2,1,0:T(8,128)(2,1)S(1)}, bf16[2,208,384]{2,1,0:T(8,128)(2,1)S(1)}, u32[]{:S(2)}, u32[]{:S(2)}) collective-permute-start(bf16[2,208,384]{2,1,0:T(8,128)(2,1)S(1)} %pad_maximum_fusion.5), channel_id=1, source_target_pairs={{3,1},{5,3},{7,5},{9,7},{11,9},{13,11},{15,13},{19,17},{21,19},{23... | collective-permute-start | bytes 958472 | tf_op jit(solution)/shard_map/ppermute | solution.py:448
  3.2 40.2 %copy-start.34 = (s32[2]{0:T(128)S(1)}, s32[2]{0:T(128)}, u32[]{:S(2)}) copy-start(s32[2]{0:T(128)} %param.12) | copy-start | bytes 28
  3.4 7.0 %collective-permute-start = (bf16[48,1280]{1,0:T(8,128)(2,1)S(1)}, bf16[48,1280]{1,0:T(8,128)(2,1)S(1)}, u32[]{:S(2)}, u32[]{:S(2)}) collective-permute-start(bf16[48,1280]{1,0:T(8,128)(2,1)S(1)} %broadcast_select_fusion.3), channel_id=1, source_target_pairs={{0,16},{16,0},{1,17},{17,1},{2,18},{18,2},{3,19},{19,3},{4,20},{20... | collective-permute-start | bytes 368648 | tf_op jit(solution)/shard_map/ppermute | solution.py:372
  10.4 9.1 %collective-permute-start.2 = (bf16[48,1280]{1,0:T(8,128)(2,1)S(1)}, bf16[48,1280]{1,0:T(8,128)(2,1)S(1)}, u32[]{:S(2)}, u32[]{:S(2)}) collective-permute-start(bf16[48,1280]{1,0:T(8,128)(2,1)S(1)} %get-tuple-element.263), channel_id=1, source_target_pairs={{0,4},{2,6},{4,8},{6,10},{8,12},{10,14},{12,0},{14,2},{1,5},{3,7},... | collective-permute-start | bytes 368648 | tf_op jit(solution)/shard_map/ppermute | solution.py:381
  11.6 12.0 %collective-permute-start.3 = (bf16[48,1280]{1,0:T(8,128)(2,1)S(1)}, bf16[48,1280]{1,0:T(8,128)(2,1)S(1)}, u32[]{:S(2)}, u32[]{:S(2)}) collective-permute-start(bf16[48,1280]{1,0:T(8,128)(2,1)S(1)} %get-tuple-element.263), channel_id=1, source_target_pairs={{0,8},{2,10},{4,12},{6,14},{8,0},{10,2},{12,4},{14,6},{1,9},{3,11}... | collective-permute-start | bytes 368648 | tf_op jit(solution)/shard_map/ppermute | solution.py:381
  14.2 9.4 %collective-permute-start.4 = (bf16[48,1280]{1,0:T(8,128)(2,1)S(1)}, bf16[48,1280]{1,0:T(8,128)(2,1)S(1)}, u32[]{:S(2)}, u32[]{:S(2)}) collective-permute-start(bf16[48,1280]{1,0:T(8,128)(2,1)S(1)} %get-tuple-element.263), channel_id=1, source_target_pairs={{0,12},{2,14},{4,0},{6,2},{8,4},{10,6},{12,8},{14,10},{1,13},{3,15... | collective-permute-start | bytes 368648 | tf_op jit(solution)/shard_map/ppermute | solution.py:381
  15.6 39.4 %copy-start.7 = (bf16[2,48,1280]{2,1,0:T(8,128)(2,1)}, bf16[2,48,1280]{2,1,0:T(8,128)(2,1)S(1)}, u32[]{:S(2)}) copy-start(bf16[2,48,1280]{2,1,0:T(8,128)(2,1)S(1)} %pad_maximum_fusion.8.refs_2_.refs_3_.refs_13_) | copy-start | bytes 737284
  15.6 9.6 %collective-permute-start.5 = (bf16[2,48,1280]{2,1,0:T(8,128)(2,1)S(1)}, bf16[2,48,1280]{2,1,0:T(8,128)(2,1)}, u32[]{:S(2)}, u32[]{:S(2)}) collective-permute-start(bf16[2,48,1280]{2,1,0:T(8,128)(2,1)S(1)} %pad_maximum_fusion.8.refs_2_.refs_3_.refs_13_), channel_id=1, source_target_pairs={{0,16},{16,0},{1,17},{17,1},{2,18},{18,2},{3,19},{19,3},{4,20},{20... | collective-permute-start | bytes 737288 | tf_op jit(solution)/shard_map/ppermute | solution.py:372
  17.1 13.1 %collective-permute-start.6 = (bf16[2,48,1280]{2,1,0:T(8,128)(2,1)S(1)}, bf16[2,48,1280]{2,1,0:T(8,128)(2,1)}, u32[]{:S(2)}, u32[]{:S(2)}) collective-permute-start(bf16[2,48,1280]{2,1,0:T(8,128)(2,1)S(1)} %pad_maximum_fusion.8.refs_2_.refs_3_.refs_13_), channel_id=1, source_target_pairs={{0,2},{2,0},{4,6},{6,4},{8,10},{10,8},{12,14},{14,12},{1,3},{3,1},... | collective-permute-start | bytes 737288 | tf_op jit(solution)/shard_map/ppermute | solution.py:375
  19.6 12.0 %collective-permute-start.7 = (bf16[2,48,1280]{2,1,0:T(8,128)(2,1)S(1)}, bf16[2,48,1280]{2,1,0:T(8,128)(2,1)S(1)}, u32[]{:S(2)}, u32[]{:S(2)}) collective-permute-start(bf16[2,48,1280]{2,1,0:T(8,128)(2,1)S(1)} %pad_maximum_fusion.8.refs_2_.refs_3_.refs_13_), channel_id=1, source_target_pairs={{0,18},{2,16},{4,22},{6,20},{8,26},{10,24},{12,30},{14,28},{16,2},... | collective-permute-start | bytes 737288 | tf_op jit(solution)/shard_map/ppermute | solution.py:378
  23.6 31.4 %copy-start.4 = (bf16[3,48,1280]{2,1,0:T(8,128)(2,1)}, bf16[3,48,1280]{2,1,0:T(8,128)(2,1)S(1)}, u32[]{:S(2)}) copy-start(bf16[3,48,1280]{2,1,0:T(8,128)(2,1)S(1)} %pad_maximum_fusion.3.refs_6_.refs_17_) | copy-start | bytes 1105924
  23.6 21.7 %collective-permute-start.11 = (bf16[3,48,1280]{2,1,0:T(8,128)(2,1)S(1)}, bf16[3,48,1280]{2,1,0:T(8,128)(2,1)S(1)}, u32[]{:S(2)}, u32[]{:S(2)}) collective-permute-start(bf16[3,48,1280]{2,1,0:T(8,128)(2,1)S(1)} %pad_maximum_fusion.3.refs_6_.refs_17_), channel_id=1, source_target_pairs={{0,16},{16,0},{1,17},{17,1},{2,18},{18,2},{3,19},{19,3},{4,20},{20... | collective-permute-start | bytes 1105928 | tf_op jit(solution)/shard_map/ppermute | solution.py:372
  31.6 8.0 %collective-permute-start.8 = (bf16[48,1280]{1,0:T(8,128)(2,1)S(1)}, bf16[48,1280]{1,0:T(8,128)(2,1)S(1)}, u32[]{:S(2)}, u32[]{:S(2)}) collective-permute-start(bf16[48,1280]{1,0:T(8,128)(2,1)S(1)} %get-tuple-element.115), channel_id=1, source_target_pairs={{0,4},{2,6},{4,8},{6,10},{8,12},{10,14},{12,0},{14,2},{1,5},{3,7},... | collective-permute-start | bytes 368648 | tf_op jit(solution)/shard_map/ppermute | solution.py:381
  32.3 10.6 %collective-permute-start.9 = (bf16[48,1280]{1,0:T(8,128)(2,1)S(1)}, bf16[48,1280]{1,0:T(8,128)(2,1)S(1)}, u32[]{:S(2)}, u32[]{:S(2)}) collective-permute-start(bf16[48,1280]{1,0:T(8,128)(2,1)S(1)} %get-tuple-element.115), channel_id=1, source_target_pairs={{0,8},{2,10},{4,12},{6,14},{8,0},{10,2},{12,4},{14,6},{1,9},{3,11}... | collective-permute-start | bytes 368648 | tf_op jit(solution)/shard_map/ppermute | solution.py:381
  32.3 10.6 %collective-permute-start.10 = (bf16[48,1280]{1,0:T(8,128)(2,1)S(1)}, bf16[48,1280]{1,0:T(8,128)(2,1)S(1)}, u32[]{:S(2)}, u32[]{:S(2)}) collective-permute-start(bf16[48,1280]{1,0:T(8,128)(2,1)S(1)} %get-tuple-element.115), channel_id=1, source_target_pairs={{0,12},{2,14},{4,0},{6,2},{8,4},{10,6},{12,8},{14,10},{1,13},{3,15... | collective-permute-start | bytes 368648 | tf_op jit(solution)/shard_map/ppermute | solution.py:381
  35.4 18.3 %collective-permute-start.12 = (bf16[3,48,1280]{2,1,0:T(8,128)(2,1)S(1)}, bf16[3,48,1280]{2,1,0:T(8,128)(2,1)S(1)}, u32[]{:S(2)}, u32[]{:S(2)}) collective-permute-start(bf16[3,48,1280]{2,1,0:T(8,128)(2,1)S(1)} %pad_maximum_fusion.3.refs_6_.refs_17_), channel_id=1, source_target_pairs={{0,2},{2,0},{4,6},{6,4},{8,10},{10,8},{12,14},{14,12},{1,3},{3,1},... | collective-permute-start | bytes 1105928 | tf_op jit(solution)/shard_map/ppermute | solution.py:375
  39.6 14.1 %collective-permute-start.13 = (bf16[3,48,1280]{2,1,0:T(8,128)(2,1)S(1)}, bf16[3,48,1280]{2,1,0:T(8,128)(2,1)S(1)}, u32[]{:S(2)}, u32[]{:S(2)}) collective-permute-start(bf16[3,48,1280]{2,1,0:T(8,128)(2,1)S(1)} %pad_maximum_fusion.3.refs_6_.refs_17_), channel_id=1, source_target_pairs={{0,18},{2,16},{4,22},{6,20},{8,26},{10,24},{12,30},{14,28},{16,2},... | collective-permute-start | bytes 1105928 | tf_op jit(solution)/shard_map/ppermute | solution.py:378
  42.9 11.5 %collective-permute-start.14 = (bf16[2,48,1280]{2,1,0:T(8,128)(2,1)S(1)}, bf16[2,48,1280]{2,1,0:T(8,128)(2,1)}, u32[]{:S(2)}, u32[]{:S(2)}) collective-permute-start(bf16[2,48,1280]{2,1,0:T(8,128)(2,1)S(1)} %pad_maximum_fusion.8.refs_2_.refs_3_.refs_13_), channel_id=1, source_target_pairs={{0,1},{1,0},{2,3},{3,2},{4,5},{5,4},{6,7},{7,6},{8,9},{9,8},{10,11... | collective-permute-start | bytes 737288 | tf_op jit(solution)/shard_map/ppermute | solution.py:369
  42.9 11.5 %collective-permute-start.15 = (bf16[2,48,1280]{2,1,0:T(8,128)(2,1)}, bf16[2,48,1280]{2,1,0:T(8,128)(2,1)}, u32[]{:S(2)}, u32[]{:S(2)}) collective-permute-start(bf16[2,48,1280]{2,1,0:T(8,128)(2,1)} %collective-permute-done.5.refs_3_.refs_4_.refs_14_), channel_id=1, source_target_pairs={{0,1},{1,0},{2,3},{3,2},{4,5},{5,4},{6,7},{7,6},{8,9},{9,8},{10,11... | collective-permute-start | bytes 737288 | tf_op jit(solution)/shard_map/ppermute | solution.py:369
  45.3 9.7 %copy-start.15 = (bf16[3,48,1280]{2,1,0:T(8,128)(2,1)}, bf16[3,48,1280]{2,1,0:T(8,128)(2,1)S(1)}, u32[]{:S(2)}) copy-start(bf16[3,48,1280]{2,1,0:T(8,128)(2,1)S(1)} %collective-permute-done.11.refs_7_.refs_18_) | copy-start | bytes 1105924
  45.3 9.7 %collective-permute-start.16 = (bf16[2,48,1280]{2,1,0:T(8,128)(2,1)}, bf16[2,48,1280]{2,1,0:T(8,128)(2,1)S(1)}, u32[]{:S(2)}, u32[]{:S(2)}) collective-permute-start(bf16[2,48,1280]{2,1,0:T(8,128)(2,1)} %collective-permute-done.6.refs_4_.refs_5_.refs_15_), channel_id=1, source_target_pairs={{0,1},{1,0},{2,3},{3,2},{4,5},{5,4},{6,7},{7,6},{8,9},{9,8},{10,11... | collective-permute-start | bytes 737288 | tf_op jit(solution)/shard_map/ppermute | solution.py:369
  45.4 31.9 %copy-start.5 = (bf16[3,48,1280]{2,1,0:T(8,128)(2,1)}, bf16[3,48,1280]{2,1,0:T(8,128)(2,1)S(1)}, u32[]{:S(2)}) copy-start(bf16[3,48,1280]{2,1,0:T(8,128)(2,1)S(1)} %pad_maximum_fusion.4.refs_7_) | copy-start | bytes 1105924
  45.4 9.7 %copy-start.31 = (bf16[2,48,1280]{2,1,0:T(8,128)(2,1)S(1)}, bf16[2,48,1280]{2,1,0:T(8,128)(2,1)}, u32[]{:S(2)}) copy-start(bf16[2,48,1280]{2,1,0:T(8,128)(2,1)} %copy-done.30) | copy-start | bytes 737284
  53.8 5.2 %collective-permute-start.18 = (bf16[3,48,1280]{2,1,0:T(8,128)(2,1)S(1)}, bf16[3,48,1280]{2,1,0:T(8,128)(2,1)S(1)}, u32[]{:S(2)}, u32[]{:S(2)}) collective-permute-start(bf16[3,48,1280]{2,1,0:T(8,128)(2,1)S(1)} %pad_maximum_fusion.3.refs_6_.refs_17_), channel_id=1, source_target_pairs={{0,1},{1,0},{2,3},{3,2},{4,5},{5,4},{6,7},{7,6},{8,9},{9,8},{10,11... | collective-permute-start | bytes 1105928 | tf_op jit(solution)/shard_map/ppermute | solution.py:369
  53.9 6.0 %collective-permute-start.19 = (bf16[3,48,1280]{2,1,0:T(8,128)(2,1)S(1)}, bf16[3,48,1280]{2,1,0:T(8,128)(2,1)S(1)}, u32[]{:S(2)}, u32[]{:S(2)}) collective-permute-start(bf16[3,48,1280]{2,1,0:T(8,128)(2,1)S(1)} %collective-permute-done.11.refs_7_.refs_18_), channel_id=1, source_target_pairs={{0,1},{1,0},{2,3},{3,2},{4,5},{5,4},{6,7},{7,6},{8,9},{9,8},{10,11... | collective-permute-start | bytes 1105928 | tf_op jit(solution)/shard_map/ppermute | solution.py:369
  54.4 6.6 %collective-permute-start.20 = (bf16[3,48,1280]{2,1,0:T(8,128)(2,1)S(1)}, bf16[3,48,1280]{2,1,0:T(8,128)(2,1)S(1)}, u32[]{:S(2)}, u32[]{:S(2)}) collective-permute-start(bf16[3,48,1280]{2,1,0:T(8,128)(2,1)S(1)} %collective-permute-done.12.refs_8_.refs_19_), channel_id=1, source_target_pairs={{0,1},{1,0},{2,3},{3,2},{4,5},{5,4},{6,7},{7,6},{8,9},{9,8},{10,11... | collective-permute-start | bytes 1105928 | tf_op jit(solution)/shard_map/ppermute | solution.py:369
  54.4 6.5 %collective-permute-start.21 = (bf16[3,48,1280]{2,1,0:T(8,128)(2,1)S(1)}, bf16[3,48,1280]{2,1,0:T(8,128)(2,1)S(1)}, u32[]{:S(2)}, u32[]{:S(2)}) collective-permute-start(bf16[3,48,1280]{2,1,0:T(8,128)(2,1)S(1)} %collective-permute-done.13.refs_9_.refs_20_), channel_id=1, source_target_pairs={{0,1},{1,0},{2,3},{3,2},{4,5},{5,4},{6,7},{7,6},{8,9},{9,8},{10,11... | collective-permute-start | bytes 1105928 | tf_op jit(solution)/shard_map/ppermute | solution.py:369
  55.0 5.9 %copy-start.32 = (bf16[2,48,1280]{2,1,0:T(8,128)(2,1)}, bf16[2,48,1280]{2,1,0:T(8,128)(2,1)S(1)}, u32[]{:S(2)}) copy-start(bf16[2,48,1280]{2,1,0:T(8,128)(2,1)S(1)} %collective-permute-done.16.refs_12_.refs_13_.refs_23_) | copy-start | bytes 737284
  55.1 2.4 %collective-permute-start.17 = (bf16[2,48,1280]{2,1,0:T(8,128)(2,1)S(1)}, bf16[2,48,1280]{2,1,0:T(8,128)(2,1)S(1)}, u32[]{:S(2)}, u32[]{:S(2)}) collective-permute-start(bf16[2,48,1280]{2,1,0:T(8,128)(2,1)S(1)} %copy-done.31), channel_id=1, source_target_pairs={{0,1},{1,0},{2,3},{3,2},{4,5},{5,4},{6,7},{7,6},{8,9},{9,8},{10,11... | collective-permute-start | bytes 737288 | tf_op jit(solution)/shard_map/ppermute | solution.py:369
  57.5 18.2 %collective-permute-start.22 = (bf16[3,48,1280]{2,1,0:T(8,128)(2,1)S(1)}, bf16[3,48,1280]{2,1,0:T(8,128)(2,1)S(1)}, u32[]{:S(2)}, u32[]{:S(2)}) collective-permute-start(bf16[3,48,1280]{2,1,0:T(8,128)(2,1)S(1)} %pad_maximum_fusion.4.refs_7_), channel_id=1, source_target_pairs={{0,16},{16,0},{1,17},{17,1},{2,18},{18,2},{3,19},{19,3},{4,20},{20... | collective-permute-start | bytes 1105928 | tf_op jit(solution)/shard_map/ppermute | solution.py:372
  59.0 16.8 %collective-permute-start.23 = (bf16[3,48,1280]{2,1,0:T(8,128)(2,1)S(1)}, bf16[3,48,1280]{2,1,0:T(8,128)(2,1)S(1)}, u32[]{:S(2)}, u32[]{:S(2)}) collective-permute-start(bf16[3,48,1280]{2,1,0:T(8,128)(2,1)S(1)} %pad_maximum_fusion.4.refs_7_), channel_id=1, source_target_pairs={{0,2},{2,0},{4,6},{6,4},{8,10},{10,8},{12,14},{14,12},{1,3},{3,1},... | collective-permute-start | bytes 1105928 | tf_op jit(solution)/shard_map/ppermute | solution.py:375
  59.9 17.4 %collective-permute-start.24 = (bf16[3,48,1280]{2,1,0:T(8,128)(2,1)S(1)}, bf16[3,48,1280]{2,1,0:T(8,128)(2,1)S(1)}, u32[]{:S(2)}, u32[]{:S(2)}) collective-permute-start(bf16[3,48,1280]{2,1,0:T(8,128)(2,1)S(1)} %pad_maximum_fusion.4.refs_7_), channel_id=1, source_target_pairs={{0,18},{2,16},{4,22},{6,20},{8,26},{10,24},{12,30},{14,28},{16,2},... | collective-permute-start | bytes 1105928 | tf_op jit(solution)/shard_map/ppermute | solution.py:378
  75.7 4.8 %copy-start.22 = (bf16[3,48,1280]{2,1,0:T(8,128)(2,1)}, bf16[3,48,1280]{2,1,0:T(8,128)(2,1)S(1)}, u32[]{:S(2)}) copy-start(bf16[3,48,1280]{2,1,0:T(8,128)(2,1)S(1)} %collective-permute-done.22.refs_8_) | copy-start | bytes 1105924
  77.2 2.3 %collective-permute-start.25 = (bf16[3,48,1280]{2,1,0:T(8,128)(2,1)S(1)}, bf16[3,48,1280]{2,1,0:T(8,128)(2,1)S(1)}, u32[]{:S(2)}, u32[]{:S(2)}) collective-permute-start(bf16[3,48,1280]{2,1,0:T(8,128)(2,1)S(1)} %pad_maximum_fusion.4.refs_7_), channel_id=1, source_target_pairs={{0,1},{1,0},{2,3},{3,2},{4,5},{5,4},{6,7},{7,6},{8,9},{9,8},{10,11... | collective-permute-start | bytes 1105928 | tf_op jit(solution)/shard_map/ppermute | solution.py:369
  77.2 2.3 %collective-permute-start.26 = (bf16[3,48,1280]{2,1,0:T(8,128)(2,1)S(1)}, bf16[3,48,1280]{2,1,0:T(8,128)(2,1)S(1)}, u32[]{:S(2)}, u32[]{:S(2)}) collective-permute-start(bf16[3,48,1280]{2,1,0:T(8,128)(2,1)S(1)} %collective-permute-done.22.refs_8_), channel_id=1, source_target_pairs={{0,1},{1,0},{2,3},{3,2},{4,5},{5,4},{6,7},{7,6},{8,9},{9,8},{10,11... | collective-permute-start | bytes 1105928 | tf_op jit(solution)/shard_map/ppermute | solution.py:369
  77.7 2.2 %collective-permute-start.27 = (bf16[3,48,1280]{2,1,0:T(8,128)(2,1)S(1)}, bf16[3,48,1280]{2,1,0:T(8,128)(2,1)S(1)}, u32[]{:S(2)}, u32[]{:S(2)}) collective-permute-start(bf16[3,48,1280]{2,1,0:T(8,128)(2,1)S(1)} %collective-permute-done.23.refs_9_), channel_id=1, source_target_pairs={{0,1},{1,0},{2,3},{3,2},{4,5},{5,4},{6,7},{7,6},{8,9},{9,8},{10,11... | collective-permute-start | bytes 1105928 | tf_op jit(solution)/shard_map/ppermute | solution.py:369
  77.8 2.7 %collective-permute-start.28 = (bf16[3,48,1280]{2,1,0:T(8,128)(2,1)S(1)}, bf16[3,48,1280]{2,1,0:T(8,128)(2,1)S(1)}, u32[]{:S(2)}, u32[]{:S(2)}) collective-permute-start(bf16[3,48,1280]{2,1,0:T(8,128)(2,1)S(1)} %collective-permute-done.24.refs_10_), channel_id=1, source_target_pairs={{0,1},{1,0},{2,3},{3,2},{4,5},{5,4},{6,7},{7,6},{8,9},{9,8},{10,11... | collective-permute-start | bytes 1105928 | tf_op jit(solution)/shard_map/ppermute | solution.py:369
  108.6 10.4 %collective-permute-start.29 = (bf16[2,2,2,4,48,640]{5,4,2,3,1,0:T(8,128)(2,1)S(1)}, bf16[2,2,2,4,48,640]{5,4,2,3,1,0:T(8,128)(2,1)S(1)}, u32[]{:S(2)}, u32[]{:S(2)}) collective-permute-start(bf16[2,2,2,4,48,640]{5,4,2,3,1,0:T(8,128)(2,1)S(1)} %copy.42), channel_id=1, source_target_pairs={{0,1},{1,0},{2,3},{3,2},{4,5},{5,4},{6,7},{7,6},{8,9},{9,8},{10,11... | collective-permute-start | bytes 5898248 | tf_op jit(solution)/shard_map/ppermute | solution.py:369
  109.1 9.9 %collective-permute-start.30 = (bf16[416,384]{1,0:T(8,128)(2,1)S(1)}, bf16[416,384]{1,0:T(8,128)(2,1)S(1)}, u32[]{:S(2)}, u32[]{:S(2)}) collective-permute-start(bf16[416,384]{1,0:T(8,128)(2,1)S(1)} %copy-done.29), channel_id=1, source_target_pairs={{0,16},{16,0},{1,17},{17,1},{2,18},{18,2},{3,19},{19,3},{4,20},{20... | collective-permute-start | bytes 958472 | tf_op jit(solution)/shard_map/ppermute | solution.py:372
  109.9 5.3 %copy-start.36 = (bf16[416,384]{1,0:T(8,128)(2,1)S(1)}, bf16[416,384]{1,0:T(8,128)(2,1)}, u32[]{:S(2)}) copy-start(bf16[416,384]{1,0:T(8,128)(2,1)} %get-tuple-element.127) | copy-start | bytes 958468
  119.4 23.7 %collective-permute-start.31 = (bf16[2,208,384]{2,1,0:T(8,128)(2,1)S(1)}, bf16[2,208,384]{2,1,0:T(8,128)(2,1)S(1)}, u32[]{:S(2)}, u32[]{:S(2)}) collective-permute-start(bf16[2,208,384]{2,1,0:T(8,128)(2,1)S(1)} %pad_maximum_fusion.6), channel_id=1, source_target_pairs={{1,3},{3,5},{5,7},{7,9},{9,11},{11,13},{13,15},{17,19},{19,21},{21... | collective-permute-start | bytes 958472 | tf_op jit(solution)/shard_map/ppermute | solution.py:411
  120.6 22.5 %collective-permute-start.32 = (bf16[2,4,48,640]{3,2,0,1:T(8,128)(2,1)S(1)}, bf16[2,4,48,640]{3,2,0,1:T(8,128)(2,1)S(1)}, u32[]{:S(2)}, u32[]{:S(2)}) collective-permute-start(bf16[2,4,48,640]{3,2,0,1:T(8,128)(2,1)S(1)} %get-tuple-element.163), channel_id=1, source_target_pairs={{0,2},{2,0},{4,6},{6,4},{8,10},{10,8},{12,14},{14,12},{1,3},{3,1},... | collective-permute-start | bytes 1474568 | tf_op jit(solution)/shard_map/ppermute | solution.py:375
  121.7 21.4 %collective-permute-start.33 = (bf16[2,4,48,640]{3,2,0,1:T(8,128)(2,1)S(1)}, bf16[2,4,48,640]{3,2,0,1:T(8,128)(2,1)S(1)}, u32[]{:S(2)}, u32[]{:S(2)}) collective-permute-start(bf16[2,4,48,640]{3,2,0,1:T(8,128)(2,1)S(1)} %get-tuple-element.164), channel_id=1, source_target_pairs={{0,16},{16,0},{1,17},{17,1},{2,18},{18,2},{3,19},{19,3},{4,20},{20... | collective-permute-start | bytes 1474568 | tf_op jit(solution)/shard_map/ppermute | solution.py:372
  123.0 23.5 %collective-permute-start.34 = (bf16[2,4,48,640]{3,2,0,1:T(8,128)(2,1)S(1)}, bf16[2,4,48,640]{3,2,0,1:T(8,128)(2,1)S(1)}, u32[]{:S(2)}, u32[]{:S(2)}) collective-permute-start(bf16[2,4,48,640]{3,2,0,1:T(8,128)(2,1)S(1)} %get-tuple-element.165), channel_id=1, source_target_pairs={{0,18},{2,16},{4,22},{6,20},{8,26},{10,24},{12,30},{14,28},{16,2},... | collective-permute-start | bytes 1474568 | tf_op jit(solution)/shard_map/ppermute | solution.py:378
  143.1 5.3 %copy-start.35 = (bf16[416,384]{1,0:T(8,128)(2,1)S(1)}, bf16[416,384]{1,0:T(8,128)(2,1)}, u32[]{:S(2)}) copy-start(bf16[416,384]{1,0:T(8,128)(2,1)} %get-tuple-element.177) | copy-start | bytes 958468
  146.5 10.9 %collective-permute-start.35 = (bf16[2,2,2,4,48,640]{5,4,3,2,1,0:T(8,128)(2,1)}, bf16[2,2,2,4,48,640]{5,4,3,2,1,0:T(8,128)(2,1)S(1)}, u32[]{:S(2)}, u32[]{:S(2)}) collective-permute-start(bf16[2,2,2,4,48,640]{5,4,3,2,1,0:T(8,128)(2,1)} %get-tuple-element.174), channel_id=1, source_target_pairs={{0,1},{1,0},{2,3},{3,2},{4,5},{5,4},{6,7},{7,6},{8,9},{9,8},{10,11... | collective-permute-start | bytes 5898248 | tf_op jit(solution)/shard_map/ppermute | solution.py:369
  147.2 10.2 %collective-permute-start.36 = (bf16[416,384]{1,0:T(8,128)(2,1)}, bf16[416,384]{1,0:T(8,128)(2,1)}, u32[]{:S(2)}, u32[]{:S(2)}) collective-permute-start(bf16[416,384]{1,0:T(8,128)(2,1)} %get-tuple-element.175), channel_id=1, source_target_pairs={{0,16},{16,0},{1,17},{17,1},{2,18},{18,2},{3,19},{19,3},{4,20},{20... | collective-permute-start | bytes 958472 | tf_op jit(solution)/shard_map/ppermute | solution.py:372
  149.6 7.7 %collective-permute-start.37 = (bf16[2,512,384]{2,1,0:T(8,128)(2,1)S(1)}, bf16[2,512,384]{2,1,0:T(8,128)(2,1)S(1)}, u32[]{:S(2)}, u32[]{:S(2)}) collective-permute-start(bf16[2,512,384]{2,1,0:T(8,128)(2,1)S(1)} %pad_maximum_fusion.1), channel_id=1, source_target_pairs={{0,1},{1,0},{2,3},{3,2},{4,5},{5,4},{6,7},{7,6},{8,9},{9,8},{10,11... | collective-permute-start | bytes 2359304 | tf_op jit(solution)/shard_map/ppermute | solution.py:369
  162.2 8.2 %collective-permute-start.45 = (bf16[1,4,48,640]{3,2,1,0:T(8,128)(2,1)S(1)}, bf16[1,4,48,640]{3,2,1,0:T(8,128)(2,1)S(1)}, u32[]{:S(2)}, u32[]{:S(2)}) collective-permute-start(bf16[1,4,48,640]{3,2,1,0:T(8,128)(2,1)S(1)} %get-tuple-element.257), channel_id=1, source_target_pairs={{0,2},{2,0},{4,6},{6,4},{8,10},{10,8},{12,14},{14,12},{1,3},{3,1},... | collective-permute-start | bytes 737288 | tf_op jit(solution)/shard_map/ppermute | solution.py:375
  164.2 8.9 %collective-permute-start.46 = (bf16[1,4,48,640]{3,2,1,0:T(8,128)(2,1)S(1)}, bf16[1,4,48,640]{3,2,1,0:T(8,128)(2,1)S(1)}, u32[]{:S(2)}, u32[]{:S(2)}) collective-permute-start(bf16[1,4,48,640]{3,2,1,0:T(8,128)(2,1)S(1)} %get-tuple-element.259), channel_id=1, source_target_pairs={{0,16},{16,0},{1,17},{17,1},{2,18},{18,2},{3,19},{19,3},{4,20},{20... | collective-permute-start | bytes 737288 | tf_op jit(solution)/shard_map/ppermute | solution.py:372
  165.5 12.5 %collective-permute-start.47 = (bf16[1,4,48,640]{3,2,1,0:T(8,128)(2,1)S(1)}, bf16[1,4,48,640]{3,2,1,0:T(8,128)(2,1)S(1)}, u32[]{:S(2)}, u32[]{:S(2)}) collective-permute-start(bf16[1,4,48,640]{3,2,1,0:T(8,128)(2,1)S(1)} %get-tuple-element.261), channel_id=1, source_target_pairs={{0,18},{2,16},{4,22},{6,20},{8,26},{10,24},{12,30},{14,28},{16,2},... | collective-permute-start | bytes 737288 | tf_op jit(solution)/shard_map/ppermute | solution.py:378
  166.3 14.4 %collective-permute-start.43 = (bf16[2,2,48,640]{3,2,0,1:T(8,128)(2,1)S(1)}, bf16[2,2,48,640]{3,2,0,1:T(8,128)(2,1)S(1)}, u32[]{:S(2)}, u32[]{:S(2)}) collective-permute-start(bf16[2,2,48,640]{3,2,0,1:T(8,128)(2,1)S(1)} %slice.304), channel_id=1, source_target_pairs={{0,4},{2,6},{4,0},{6,2},{8,12},{10,14},{12,8},{14,10},{1,5},{3,7},... | collective-permute-start | bytes 737288 | tf_op jit(solution)/shard_map/ppermute | solution.py:397
  168.6 12.8 %collective-permute-start.38 = (bf16[2,208,384]{2,1,0:T(8,128)(2,1)S(1)}, bf16[2,208,384]{2,1,0:T(8,128)(2,1)S(1)}, u32[]{:S(2)}, u32[]{:S(2)}) collective-permute-start(bf16[2,208,384]{2,1,0:T(8,128)(2,1)S(1)} %pad_maximum_fusion.7), channel_id=1, source_target_pairs={{1,3},{3,5},{5,7},{7,9},{9,11},{11,13},{13,15},{17,19},{19,21},{21... | collective-permute-start | bytes 958472 | tf_op jit(solution)/shard_map/ppermute | solution.py:411
  170.4 23.6 %collective-permute-start.40 = (bf16[1,4,48,640]{3,2,1,0:T(8,128)(2,1)S(1)}, bf16[1,4,48,640]{3,2,1,0:T(8,128)(2,1)S(1)}, u32[]{:S(2)}, u32[]{:S(2)}) collective-permute-start(bf16[1,4,48,640]{3,2,1,0:T(8,128)(2,1)S(1)} %get-tuple-element.258), channel_id=1, source_target_pairs={{0,2},{2,0},{4,6},{6,4},{8,10},{10,8},{12,14},{14,12},{1,3},{3,1},... | collective-permute-start | bytes 737288 | tf_op jit(solution)/shard_map/ppermute | solution.py:375
  173.1 21.0 %collective-permute-start.41 = (bf16[1,4,48,640]{3,2,1,0:T(8,128)(2,1)S(1)}, bf16[1,4,48,640]{3,2,1,0:T(8,128)(2,1)S(1)}, u32[]{:S(2)}, u32[]{:S(2)}) collective-permute-start(bf16[1,4,48,640]{3,2,1,0:T(8,128)(2,1)S(1)} %get-tuple-element.260), channel_id=1, source_target_pairs={{0,16},{16,0},{1,17},{17,1},{2,18},{18,2},{3,19},{19,3},{4,20},{20... | collective-permute-start | bytes 737288 | tf_op jit(solution)/shard_map/ppermute | solution.py:372
  178.0 16.1 %collective-permute-start.42 = (bf16[1,4,48,640]{3,2,1,0:T(8,128)(2,1)S(1)}, bf16[1,4,48,640]{3,2,1,0:T(8,128)(2,1)S(1)}, u32[]{:S(2)}, u32[]{:S(2)}) collective-permute-start(bf16[1,4,48,640]{3,2,1,0:T(8,128)(2,1)S(1)} %get-tuple-element.262), channel_id=1, source_target_pairs={{0,18},{2,16},{4,22},{6,20},{8,26},{10,24},{12,30},{14,28},{16,2},... | collective-permute-start | bytes 737288 | tf_op jit(solution)/shard_map/ppermute | solution.py:378
  180.7 6.6 %collective-permute-start.48 = (bf16[1,2,48,640]{3,2,1,0:T(8,128)(2,1)S(1)}, bf16[1,2,48,640]{3,2,1,0:T(8,128)(2,1)S(1)}, u32[]{:S(2)}, u32[]{:S(2)}) collective-permute-start(bf16[1,2,48,640]{3,2,1,0:T(8,128)(2,1)S(1)} %slice.312), channel_id=1, source_target_pairs={{0,4},{2,6},{4,0},{6,2},{8,12},{10,14},{12,8},{14,10},{1,5},{3,7},... | collective-permute-start | bytes 368648 | tf_op jit(solution)/shard_map/ppermute | solution.py:397
  181.4 7.4 %collective-permute-start.44 = (bf16[2,48,640]{2,1,0:T(8,128)(2,1)S(1)}, bf16[2,48,640]{2,1,0:T(8,128)(2,1)S(1)}, u32[]{:S(2)}, u32[]{:S(2)}) collective-permute-start(bf16[2,48,640]{2,1,0:T(8,128)(2,1)S(1)} %fusion.29), channel_id=1, source_target_pairs={{0,8},{2,10},{4,12},{6,14},{8,0},{10,2},{12,4},{14,6},{1,9},{3,11}... | collective-permute-start | bytes 368648 | tf_op jit(solution)/shard_map/ppermute | solution.py:397
  187.3 6.8 %collective-permute-start.39 = (bf16[2,512,384]{2,1,0:T(8,128)(2,1)S(1)}, bf16[2,512,384]{2,1,0:T(8,128)(2,1)S(1)}, u32[]{:S(2)}, u32[]{:S(2)}) collective-permute-start(bf16[2,512,384]{2,1,0:T(8,128)(2,1)S(1)} %pad_maximum_fusion.2), channel_id=1, source_target_pairs={{0,1},{1,0},{2,3},{3,2},{4,5},{5,4},{6,7},{7,6},{8,9},{9,8},{10,11... | collective-permute-start | bytes 2359304 | tf_op jit(solution)/shard_map/ppermute | solution.py:369
  188.8 5.3 %collective-permute-start.49 = (bf16[1,48,640]{2,1,0:T(8,128)(2,1)S(1)}, bf16[1,48,640]{2,1,0:T(8,128)(2,1)S(1)}, u32[]{:S(2)}, u32[]{:S(2)}) collective-permute-start(bf16[1,48,640]{2,1,0:T(8,128)(2,1)S(1)} %fusion.34), channel_id=1, source_target_pairs={{0,8},{2,10},{4,12},{6,14},{8,0},{10,2},{12,4},{14,6},{1,9},{3,11}... | collective-permute-start | bytes 184328 | tf_op jit(solution)/shard_map/ppermute | solution.py:397
  194.2 5.6 %collective-permute-start.50 = (bf16[1,48,640]{2,1,0:T(8,128)(2,1)S(1)}, bf16[1,48,640]{2,1,0:T(8,128)(2,1)S(1)}, u32[]{:S(2)}, u32[]{:S(2)}) collective-permute-start(bf16[1,48,640]{2,1,0:T(8,128)(2,1)S(1)} %get-tuple-element.273), channel_id=1, source_target_pairs={{0,4},{2,6},{4,0},{6,2},{8,12},{10,14},{12,8},{14,10},{1,5},{3,7},... | collective-permute-start | bytes 184328 | tf_op jit(solution)/shard_map/ppermute | solution.py:397
  194.3 5.5 %collective-permute-start.51 = (bf16[1,48,640]{2,1,0:T(8,128)(2,1)S(1)}, bf16[1,48,640]{2,1,0:T(8,128)(2,1)S(1)}, u32[]{:S(2)}, u32[]{:S(2)}) collective-permute-start(bf16[1,48,640]{2,1,0:T(8,128)(2,1)S(1)} %get-tuple-element.275), channel_id=1, source_target_pairs={{0,8},{2,10},{4,12},{6,14},{8,0},{10,2},{12,4},{14,6},{1,9},{3,11}... | collective-permute-start | bytes 184328 | tf_op jit(solution)/shard_map/ppermute | solution.py:397
  196.6 6.0 %collective-permute-start.52 = (bf16[1,48,640]{2,1,0:T(8,128)(2,1)S(1)}, bf16[1,48,640]{2,1,0:T(8,128)(2,1)S(1)}, u32[]{:S(2)}, u32[]{:S(2)}) collective-permute-start(bf16[1,48,640]{2,1,0:T(8,128)(2,1)S(1)} %get-tuple-element.274), channel_id=1, source_target_pairs={{0,12},{2,14},{4,8},{6,10},{8,4},{10,6},{12,0},{14,2},{1,13},{3,15... | collective-permute-start | bytes 184328 | tf_op jit(solution)/shard_map/ppermute | solution.py:397
  202.7 4.9 %collective-permute-start.53 = (bf16[2,48,640]{2,1,0:T(8,128)(2,1)S(1)}, bf16[2,48,640]{2,1,0:T(8,128)(2,1)S(1)}, u32[]{:S(2)}, u32[]{:S(2)}) collective-permute-start(bf16[2,48,640]{2,1,0:T(8,128)(2,1)S(1)} %select_convert_fusion), channel_id=1, source_target_pairs={{0,16},{16,0},{1,17},{17,1},{2,18},{18,2},{3,19},{19,3},{4,20},{20... | collective-permute-start | bytes 368648 | tf_op jit(solution)/shard_map/ppermute | solution.py:372
  (27 other events, 62.7 us)

commit v7 on v6

--- a/solution.py
+++ b/solution.py
@@ -377,9 +377,6 @@
     def pd(a):
         return lax.ppermute(a, ("section", "dp"), [(i, (i + n_dp) % (2 * n_dp) ^ 1) for i in range(2 * n_dp)])
 
-    def pz(a, k):
-        return lax.ppermute(a, "dp", [(2 * z + y, 2 * ((z + k) % m) + y) for z in range(m) for y in range(2)])
-
     def after(a, *b):
         return lax.optimization_barrier((a, *b))
 
@@ -471,7 +468,7 @@
                 t = jnp.where(sc[1] == 0, side, 1 - side)
                 own = src[side * 8:side * 8 + 8]
                 for kk in range(m):
-                    z = lax.rem(sc[3] - kk + m, m)
+                    z = lax.bitwise_xor(sc[3], kk)
                     near = pl.ds(pl.multiple_of((2 * z + sc[4]) * piece, 16), piece)
                     far = pl.ds(pl.multiple_of((2 * z + 1 - sc[4]) * piece, 16), piece)
                     for i, (h, r) in enumerate(((sc[2], near), (1 - sc[2], near), (sc[2], far), (1 - sc[2], far))):
@@ -498,10 +495,12 @@
         out_shapes = [[((2, 2, 2, m, piece, part), BF16)], [((2, m, piece, part), BF16)] * 4]
         own = jnp.stack(start)
         firsts = [own, px(own), py(own), pd(own)]
-        columns = [jnp.stack([pz(start[0], kk) for kk in range(1, m)])]
+        columns = [jnp.stack([pz_to(start[0], kk) for kk in range(1, m)])]
+        start[1], columns[0] = after(start[1], columns[0])
+        columns[0], *firsts = after(columns[0], *firsts)
         rest = [columns[0], px(columns[0]), py(columns[0]), pd(columns[0])]
-        start[1], _, *firsts = after(start[1], columns[0], *firsts)
-        columns.append(jnp.stack([pz(start[1], kk) for kk in range(1, m)]))
+        near = pz_to(start[1], 1)
+        columns.append(jnp.concatenate([near[None], pz_to(jnp.stack([start[1], near]), 2)]))
         columns[1], *rest = after(columns[1], *rest)
         twins = [pt(a) for a in firsts]
         sources = [firsts + rest + twins + [pt(a) for a in rest]]
@@ -538,10 +537,10 @@
     m1 = call(1, ["mine"], **r1)
     u = r1["in"]
     if direct:
-        first, got1, low_got = after(m1["g"][0], got1, low_got)
+        first, got1 = after(m1["g"][0], got1)
         sent1 = add_pair([first] + m1["g"][1:], got1)
+        u, low_got, *sent1 = after(u, low_got, *sent1)
         low_tails = tails(r1["keep"], low_got)
-        u, *sent1 = after(u, *sent1)
         quad1 = across(sent1)
     else:
         low_tails = tails(r1["keep"], low_got)
@@ -555,7 +554,7 @@
     m0 = call(0, ["mine"], **{**r0, **b0})
 
     if direct:
-        first, got0, in_got, low_twin = after(m0["g"][0], got0, in_got, low_twin)
+        first, got0, low_twin = after(m0["g"][0], got0, low_twin)
         sent0 = add_pair([first] + m0["g"][1:], got0)
         both = after(in_got, *sent0, *quad1)
         in_got, sent0, quad1 = both[0], both[1:5], both[5:]
@@ -565,7 +564,6 @@
         in_twin, *quad0[1] = after(pt(in_rows), *quad0[1])
         done1 = along_steps(quad1)
         done0 = [along_steps(quad0[0])]
-        done1, done0[0], *quad0[1] = after(done1, done0[0], *quad0[1])
         done0 = jnp.concatenate(done0 + [along(quad0[1])])
         mine = jnp.where(sec == 0, done0, done1)
         other = px(jnp.where(sec == 0, done1, done0).astype(BF16)).astype(F32)

time: 214 us -> 209 us (0.977)
  waiting for transfers between devices: 60.8 us -> 49 us
  starting transfers between devices: 53.4 us -> 61 us
    ppermute x7 -> x12, starting transfers between devices: 8.45 us -> 22.5 us  [pz_to(): return lax.ppermute(a, 'dp', [(i, i ^ 2 * kk) for i in range(n_dp)])]
    ppermute x6 -> x0, starting transfers between devices: 8.26 us -> none  [pz(): lax.ppermute(a, 'dp', [(2 * z + y, 2 * ((z + k) % m) + y) for z in range(...]
    ppermute x6 -> x0, waiting for transfers between devices: 8.08 us -> none  [pz(): lax.ppermute(a, 'dp', [(2 * z + y, 2 * ((z + k) % m) + y) for z in range(...]
    ppermute x7 -> x12, waiting for transfers between devices: 14.9 us -> 21.9 us  [pz_to(): return lax.ppermute(a, 'dp', [(i, i ^ 2 * kk) for i in range(n_dp)])]
    ppermute x10, waiting for transfers between devices: 12.6 us -> 6.71 us  [px(): return lax.ppermute(a, 'section', [(0, 1), (1, 0)])]
    ppermute x6, waiting for transfers between devices: 13.5 us -> 9.62 us  [py(): return lax.ppermute(a, 'dp', [(i, i ^ 1) for i in range(n_dp)])]
    unnamed x78 -> x70, local copies, waits for them, and re-layouts: 5.22 us -> 4.52 us
  transfers between devices with their start and end apart: 54 -> 53, of which waited for: 22 -> 23; matrix products, arithmetic and copies ran while one was open for 5% -> 7% of each run, Pallas kernels for 20% -> 21%
where the time goes in v7:
time: 209 us; the launch traced here: 208 us
  Pallas kernels  68 us (33%)
  starting transfers between devices  61 us (29%)
  waiting for transfers between devices  49 us (23%)
  other arithmetic  11.1 us (5%)
  local copies, waits for them, and re-layouts  10.5 us (5%)
  matrix products  5.98 us (3%)
  between operations  2.38 us (1%)
    pallas_call x5, Pallas kernels, layer_call(): pl.pallas_call(body, out_shape=[jax.ShapeDtypeStruct(*o) for o in outs],...  68 us
    ppermute x12, starting transfers between devices, pz_to(): return lax.ppermute(a, 'dp', [(i, i ^ 2 * kk) for i in range(n_dp)])  22.5 us
    ppermute x12, waiting for transfers between devices, pz_to(): return lax.ppermute(a, 'dp', [(i, i ^ 2 * kk) for i in range(n_dp)])  21.9 us
    ppermute x10, starting transfers between devices, px(): return lax.ppermute(a, 'section', [(0, 1), (1, 0)])  14.3 us
    ppermute x6, starting transfers between devices, py(): return lax.ppermute(a, 'dp', [(i, i ^ 1) for i in range(n_dp)])  10.9 us
    ppermute x6, waiting for transfers between devices, py(): return lax.ppermute(a, 'dp', [(i, i ^ 1) for i in range(n_dp)])  9.62 us
    ppermute x6, waiting for transfers between devices, pd(): lax.ppermute(a, ('section', 'dp'), [(i, (i + n_dp) % (2 * n_dp) ^ 1) for...  8.78 us
    ppermute x10, waiting for transfers between devices, px(): return lax.ppermute(a, 'section', [(0, 1), (1, 0)])  6.71 us
  transfers between devices with their start and end apart: 53, of which 23 were waited for; matrix products, arithmetic and copies ran while one was open for 7% of the time, Pallas kernels for 21%

profile of v7, /device:TPU:0, one launch (start us, length us, event | category | flops | bytes accessed | tf_op | source)
XLA Modules:
  0.0 208.0 jit_solution(15670836149128364101)
XLA Ops:
  0.7 1.3 constant_dynamic-slice_fusion
  3.4 3.0 %collective-permute-start = (bf16[48,1280]{1,0:T(8,128)(2,1)S(1)}, bf16[48,1280]{1,0:T(8,128)(2,1)S(1)}, u32[]{:S(2)}, u32[]{:S(2)}) collective-permute-start(bf16[48,1280]{1,0:T(8,128)(2,1)S(1)} %broadcast_select_fusion.3), channel_id=1, source_target_pairs={{0,16},{16,0},{1,17},{17,1},{2,18},{18,2},{3,19},{19,3},{4,20},{20... | collective-permute-start | bytes 368648 | tf_op jit(solution)/shard_map/ppermute | solution.py:372
  6.4 3.9 %collective-permute-done = bf16[48,1280]{1,0:T(8,128)(2,1)S(1)} collective-permute-done((bf16[48,1280]{1,0:T(8,128)(2,1)S(1)}, bf16[48,1280]{1,0:T(8,128)(2,1)S(1)}, u32[]{:S(2)}, u32[]{:S(2)}) %collective-permute-start) | collective-permute-done | bytes 122912 | tf_op jit(solution)/shard_map/ppermute | solution.py:372
  10.4 1.2 collective-permute-start.2
  11.6 2.6 %collective-permute-start.3 = (bf16[48,1280]{1,0:T(8,128)(2,1)S(1)}, bf16[48,1280]{1,0:T(8,128)(2,1)S(1)}, u32[]{:S(2)}, u32[]{:S(2)}) collective-permute-start(bf16[48,1280]{1,0:T(8,128)(2,1)S(1)} %get-tuple-element.253), channel_id=1, source_target_pairs={{0,8},{2,10},{4,12},{6,14},{8,0},{10,2},{12,4},{14,6},{1,9},{3,11}... | collective-permute-start | bytes 368648 | tf_op jit(solution)/shard_map/ppermute | solution.py:394
  14.9 1.8 collective-permute-start.5
  16.7 1.7 collective-permute-start.6
  18.6 0.8 collective-permute-start.7
  19.4 4.6 %collective-permute-done.3 = bf16[48,1280]{1,0:T(8,128)(2,1)S(1)} collective-permute-done((bf16[48,1280]{1,0:T(8,128)(2,1)S(1)}, bf16[48,1280]{1,0:T(8,128)(2,1)S(1)}, u32[]{:S(2)}, u32[]{:S(2)}) %collective-permute-start.3) | collective-permute-done | bytes 122912 | tf_op jit(solution)/shard_map/ppermute | solution.py:394
  24.1 3.2 %collective-permute-start.8 = (bf16[48,1280]{1,0:T(8,128)(2,1)S(1)}, bf16[48,1280]{1,0:T(8,128)(2,1)S(1)}, u32[]{:S(2)}, u32[]{:S(2)}) collective-permute-start(bf16[48,1280]{1,0:T(8,128)(2,1)S(1)} %get-tuple-element.111), channel_id=1, source_target_pairs={{0,4},{2,6},{4,0},{6,2},{8,12},{10,14},{12,8},{14,10},{1,5},{3,7},... | collective-permute-start | bytes 368648 | tf_op jit(solution)/shard_map/ppermute | solution.py:394
  27.3 1.9 collective-permute-done.6.refs_4_.refs_5_.refs_15_
  29.2 0.7 collective-permute-done.7.refs_5_.refs_6_.refs_16_
  29.9 1.5 collective-permute-start.10
  31.4 2.3 %collective-permute-start.9 = (bf16[2,48,1280]{2,1,0:T(8,128)(2,1)S(1)}, bf16[2,48,1280]{2,1,0:T(8,128)(2,1)S(1)}, u32[]{:S(2)}, u32[]{:S(2)}) collective-permute-start(bf16[2,48,1280]{2,1,0:T(8,128)(2,1)S(1)} %pad_maximum_fusion.9), channel_id=1, source_target_pairs={{0,8},{2,10},{4,12},{6,14},{8,0},{10,2},{12,4},{14,6},{1,9},{3,11}... | collective-permute-start | bytes 737288 | tf_op jit(solution)/shard_map/ppermute | solution.py:394
  33.6 2.4 %collective-permute-start.11 = (bf16[3,48,1280]{2,1,0:T(8,128)(2,1)S(1)}, bf16[3,48,1280]{2,1,0:T(8,128)(2,1)}, u32[]{:S(2)}, u32[]{:S(2)}) collective-permute-start(bf16[3,48,1280]{2,1,0:T(8,128)(2,1)S(1)} %pad_maximum_fusion.3.refs_6_.refs_17_), channel_id=1, source_target_pairs={{0,2},{2,0},{4,6},{6,4},{8,10},{10,8},{12,14},{14,12},{1,3},{3,1},... | collective-permute-start | bytes 1105928 | tf_op jit(solution)/shard_map/ppermute | solution.py:375
  36.1 0.9 collective-permute-start.12
  37.1 7.6 %collective-permute-done.9 = bf16[2,48,1280]{2,1,0:T(8,128)(2,1)S(1)} collective-permute-done((bf16[2,48,1280]{2,1,0:T(8,128)(2,1)S(1)}, bf16[2,48,1280]{2,1,0:T(8,128)(2,1)S(1)}, u32[]{:S(2)}, u32[]{:S(2)}) %collective-permute-start.9) | collective-permute-done | bytes 245792 | tf_op jit(solution)/shard_map/ppermute | solution.py:394
  47.2 4.6 %collective-permute-done.11.refs_8_.refs_19_ = bf16[3,48,1280]{2,1,0:T(8,128)(2,1)} collective-permute-done((bf16[3,48,1280]{2,1,0:T(8,128)(2,1)S(1)}, bf16[3,48,1280]{2,1,0:T(8,128)(2,1)}, u32[]{:S(2)}, u32[]{:S(2)}) %collective-permute-start.11) | collective-permute-done | bytes 368672 | tf_op jit(solution)/shard_map/ppermute | solution.py:375
  53.1 1.3 convolution_convert_fusion.5.refs_1_
  54.4 1.0 collective-permute-done.16.refs_13_.refs_14_.refs_24_
  55.4 1.5 collective-permute-start.21
  56.8 1.7 collective-permute-start.22
  59.6 0.8 copy-done.15
  60.4 13.2 %shard_map.186 = (bf16[416,384]{1,0:T(8,128)(2,1)}, f32[416,384]{1,0:T(8,128)}, f32[416,128]{1,0:T(8,128)}, bf16[416,384]{1,0:T(8,128)(2,1)}, bf16[2,416,640]{2,...) custom-call(s32[5]{0:T(128)} %stack.107.refs_0_, ...), custom_call_target="tpu_custom_call" | custom-call | flops 10000000000 | bytes 8388608 | tf_op jit(solution)/shard_map/pallas_call | solution.py:339
  73.6 0.8 collective-permute-done.22.refs_9_
  74.4 0.7 collective-permute-done.23.refs_10_
  76.1 1.3 convolution_convert_fusion.4.refs_2_
  78.6 0.8 copy-done.22
  79.4 25.3 %shard_map.187 = (bf16[416,384]{1,0:T(8,128)(2,1)}, bf16[2,416,256]{2,1,0:T(8,128)(2,1)}, bf16[416,384]{1,0:T(8,128)(2,1)}, bf16[416,1536]{1,0:T(8,128)(2,1)}, b...) custom-call(s32[5]{0:T(128)} %stack.107.refs_0_, ...), custom_call_target="tpu_custom_call" | custom-call | flops 30000001024 | bytes 8388608 | tf_op jit(solution)/shard_map/pallas_call | solution.py:339
  104.7 1.8 copy.42
  107.0 1.5 collective-permute-start.28
  109.4 5.3 %shard_map.188 = (bf16[2,4,48,640]{3,2,1,0:T(8,128)(2,1)}, bf16[2,4,48,640]{3,2,1,0:T(8,128)(2,1)}, bf16[2,4,48,640]{3,2,1,0:T(8,128)(2,1)}, bf16[2,4,48,640]{3,2,1,0:T(8,128)(2,1)}) custom-call(s32[5]{0:T(128)} %stack.107.refs_0_, bf16[416,384]{1,0:T(8,128)(2,1)} %get-tuple-element.127.refs_1_, bf16[2,416,256]{2,1,0:T(8,128)(2,1)} %get-tuple-element.128.refs_2_, ...), custom_call_target="tpu_custom_call" | custom-call | flops 10000000000 | bytes 8388608 | tf_op jit(solution)/shard_map/pallas_call | solution.py:339
  114.8 1.9 fusion.8
  118.0 1.9 collective-permute-start.31
  120.4 1.2 collective-permute-start.33
  121.6 18.9 %shard_map.189 = (bf16[416,384]{1,0:T(8,128)(2,1)}, bf16[416,384]{1,0:T(8,128)(2,1)}, bf16[416,384]{1,0:T(8,128)(2,1)}, bf16[416,1536]{1,0:T(8,128)(2,1)}, f32[8...) custom-call(s32[5]{0:T(128)} %stack.107.refs_0_, ...), custom_call_target="tpu_custom_call" | custom-call | flops 20000000000 | bytes 8388608 | tf_op jit(solution)/shard_map/pallas_call | solution.py:339
  140.6 2.6 %collective-permute-done.33 = bf16[2,4,48,640]{3,2,0,1:T(8,128)(2,1)S(1)} collective-permute-done((bf16[2,4,48,640]{3,2,0,1:T(8,128)(2,1)S(1)}, bf16[2,4,48,640]{3,2,0,1:T(8,128)(2,1)S(1)}, u32[]{:S(2)}, u32[]{:S(2)}) %collective-permute-start.33) | collective-permute-done | bytes 491552 | tf_op jit(solution)/shard_map/ppermute | solution.py:378
  143.2 2.0 collective-permute-start.34
  145.8 1.0 collective-permute-start.36
  147.9 5.3 %shard_map.190 = (bf16[2,4,48,640]{3,2,1,0:T(8,128)(2,1)}, bf16[2,4,48,640]{3,2,1,0:T(8,128)(2,1)}, bf16[2,4,48,640]{3,2,1,0:T(8,128)(2,1)}, bf16[2,4,48,640]{3,2,1,0:T(8,128)(2,1)}) custom-call(s32[5]{0:T(128)} %stack.107.refs_0_, bf16[416,384]{1,0:T(8,128)(2,1)} %get-tuple-element.147.refs_4_.refs_1_, ...), custom_call_target="tpu_custom_call" | custom-call | flops 10000000000 | bytes 8388608 | tf_op jit(solution)/shard_map/pallas_call | solution.py:339
  153.2 1.9 fusion.5
  156.7 1.6 collective-permute-start.50
  158.3 1.3 collective-permute-start.42
  159.7 0.9 collective-permute-start.43
  160.7 1.5 collective-permute-start.44
  163.0 1.0 fusion.11
  164.1 2.4 %collective-permute-done.42 = bf16[1,4,48,640]{3,2,1,0:T(8,128)(2,1)S(1)} collective-permute-done((bf16[1,4,48,640]{3,2,1,0:T(8,128)(2,1)S(1)}, bf16[1,4,48,640]{3,2,1,0:T(8,128)(2,1)S(1)}, u32[]{:S(2)}, u32[]{:S(2)}) %collective-permute-start.42) | collective-permute-done | bytes 245792 | tf_op jit(solution)/shard_map/ppermute | solution.py:375
  166.5 1.9 collective-permute-start.39
  168.6 0.9 collective-permute-start.40
  169.4 4.7 %collective-permute-done.44 = bf16[1,4,48,640]{3,2,1,0:T(8,128)(2,1)S(1)} collective-permute-done((bf16[1,4,48,640]{3,2,1,0:T(8,128)(2,1)S(1)}, bf16[1,4,48,640]{3,2,1,0:T(8,128)(2,1)S(1)}, u32[]{:S(2)}, u32[]{:S(2)}) %collective-permute-start.44) | collective-permute-done | bytes 245792 | tf_op jit(solution)/shard_map/ppermute | solution.py:378
  174.1 1.5 collective-permute-start.41
  175.9 1.7 collective-permute-start.45
  177.9 2.9 %collective-permute-done.45 = bf16[1,2,48,640]{3,2,1,0:T(8,128)(2,1)S(1)} collective-permute-done((bf16[1,2,48,640]{3,2,1,0:T(8,128)(2,1)S(1)}, bf16[1,2,48,640]{3,2,1,0:T(8,128)(2,1)S(1)}, u32[]{:S(2)}, u32[]{:S(2)}) %collective-permute-start.45) | collective-permute-done | bytes 122912 | tf_op jit(solution)/shard_map/ppermute | solution.py:394
  180.8 2.4 %collective-permute-start.46 = (bf16[1,48,640]{2,1,0:T(8,128)(2,1)S(1)}, bf16[1,48,640]{2,1,0:T(8,128)(2,1)S(1)}, u32[]{:S(2)}, u32[]{:S(2)}) collective-permute-start(bf16[1,48,640]{2,1,0:T(8,128)(2,1)S(1)} %fusion.34), channel_id=1, source_target_pairs={{0,8},{2,10},{4,12},{6,14},{8,0},{10,2},{12,4},{14,6},{1,9},{3,11}... | collective-permute-start | bytes 184328 | tf_op jit(solution)/shard_map/ppermute | solution.py:394
  183.2 2.8 %collective-permute-done.46 = bf16[1,48,640]{2,1,0:T(8,128)(2,1)S(1)} collective-permute-done((bf16[1,48,640]{2,1,0:T(8,128)(2,1)S(1)}, bf16[1,48,640]{2,1,0:T(8,128)(2,1)S(1)}, u32[]{:S(2)}, u32[]{:S(2)}) %collective-permute-start.46) | collective-permute-done | bytes 61472 | tf_op jit(solution)/shard_map/ppermute | solution.py:394
  186.0 2.6 %collective-permute-start.51 = (bf16[2,48,640]{2,1,0:T(8,128)(2,1)S(1)}, bf16[2,48,640]{2,1,0:T(8,128)(2,1)S(1)}, u32[]{:S(2)}, u32[]{:S(2)}) collective-permute-start(bf16[2,48,640]{2,1,0:T(8,128)(2,1)S(1)} %fusion.29), channel_id=1, source_target_pairs={{0,8},{2,10},{4,12},{6,14},{8,0},{10,2},{12,4},{14,6},{1,9},{3,11}... | collective-permute-start | bytes 368648 | tf_op jit(solution)/shard_map/ppermute | solution.py:394
  189.2 2.0 collective-permute-start.48
  191.1 2.1 %collective-permute-start.49 = (bf16[1,48,640]{2,1,0:T(8,128)(2,1)S(1)}, bf16[1,48,640]{2,1,0:T(8,128)(2,1)S(1)}, u32[]{:S(2)}, u32[]{:S(2)}) collective-permute-start(bf16[1,48,640]{2,1,0:T(8,128)(2,1)S(1)} %get-tuple-element.264), channel_id=1, source_target_pairs={{0,12},{2,14},{4,8},{6,10},{8,4},{10,6},{12,0},{14,2},{1,13},{3,15... | collective-permute-start | bytes 184328 | tf_op jit(solution)/shard_map/ppermute | solution.py:394
  193.4 2.8 %collective-permute-done.48 = bf16[1,48,640]{2,1,0:T(8,128)(2,1)S(1)} collective-permute-done((bf16[1,48,640]{2,1,0:T(8,128)(2,1)S(1)}, bf16[1,48,640]{2,1,0:T(8,128)(2,1)S(1)}, u32[]{:S(2)}, u32[]{:S(2)}) %collective-permute-start.48) | collective-permute-done | bytes 61472 | tf_op jit(solution)/shard_map/ppermute | solution.py:394
  196.2 1.1 collective-permute-done.49
  197.4 1.7 collective-permute-start.52
  199.0 1.2 fusion.13
  200.3 2.0 collective-permute-done.52
  203.6 0.7 copy.49
  (211 shorter events, 22.5 us)
Async XLA Ops:
  2.1 8.3 %collective-permute-start.1 = (bf16[2,208,384]{2,1,0:T(8,128)(2,1)S(1)}, bf16[2,208,384]{2,1,0:T(8,128)(2,1)S(1)}, u32[]{:S(2)}, u32[]{:S(2)}) collective-permute-start(bf16[2,208,384]{2,1,0:T(8,128)(2,1)S(1)} %pad_maximum_fusion.5), channel_id=1, source_target_pairs={{3,1},{5,3},{7,5},{9,7},{11,9},{13,11},{15,13},{19,17},{21,19},{23... | collective-permute-start | bytes 958472 | tf_op jit(solution)/shard_map/ppermute | solution.py:445
  3.4 41.3 %copy-start.30 = (s32[2]{0:T(128)S(1)}, s32[2]{0:T(128)}, u32[]{:S(2)}) copy-start(s32[2]{0:T(128)} %param.12) | copy-start | bytes 28
  3.4 7.0 %collective-permute-start = (bf16[48,1280]{1,0:T(8,128)(2,1)S(1)}, bf16[48,1280]{1,0:T(8,128)(2,1)S(1)}, u32[]{:S(2)}, u32[]{:S(2)}) collective-permute-start(bf16[48,1280]{1,0:T(8,128)(2,1)S(1)} %broadcast_select_fusion.3), channel_id=1, source_target_pairs={{0,16},{16,0},{1,17},{17,1},{2,18},{18,2},{3,19},{19,3},{4,20},{20... | collective-permute-start | bytes 368648 | tf_op jit(solution)/shard_map/ppermute | solution.py:372
  10.4 8.2 %collective-permute-start.2 = (bf16[48,1280]{1,0:T(8,128)(2,1)S(1)}, bf16[48,1280]{1,0:T(8,128)(2,1)S(1)}, u32[]{:S(2)}, u32[]{:S(2)}) collective-permute-start(bf16[48,1280]{1,0:T(8,128)(2,1)S(1)} %get-tuple-element.253), channel_id=1, source_target_pairs={{0,4},{2,6},{4,0},{6,2},{8,12},{10,14},{12,8},{14,10},{1,5},{3,7},... | collective-permute-start | bytes 368648 | tf_op jit(solution)/shard_map/ppermute | solution.py:394
  11.6 12.4 %collective-permute-start.3 = (bf16[48,1280]{1,0:T(8,128)(2,1)S(1)}, bf16[48,1280]{1,0:T(8,128)(2,1)S(1)}, u32[]{:S(2)}, u32[]{:S(2)}) collective-permute-start(bf16[48,1280]{1,0:T(8,128)(2,1)S(1)} %get-tuple-element.253), channel_id=1, source_target_pairs={{0,8},{2,10},{4,12},{6,14},{8,0},{10,2},{12,4},{14,6},{1,9},{3,11}... | collective-permute-start | bytes 368648 | tf_op jit(solution)/shard_map/ppermute | solution.py:394
  14.2 9.8 %collective-permute-start.4 = (bf16[48,1280]{1,0:T(8,128)(2,1)S(1)}, bf16[48,1280]{1,0:T(8,128)(2,1)S(1)}, u32[]{:S(2)}, u32[]{:S(2)}) collective-permute-start(bf16[48,1280]{1,0:T(8,128)(2,1)S(1)} %get-tuple-element.253), channel_id=1, source_target_pairs={{0,12},{2,14},{4,8},{6,10},{8,4},{10,6},{12,0},{14,2},{1,13},{3,15... | collective-permute-start | bytes 368648 | tf_op jit(solution)/shard_map/ppermute | solution.py:394
  14.9 38.0 %copy-start.3 = (bf16[2,48,1280]{2,1,0:T(8,128)(2,1)}, bf16[2,48,1280]{2,1,0:T(8,128)(2,1)S(1)}, u32[]{:S(2)}) copy-start(bf16[2,48,1280]{2,1,0:T(8,128)(2,1)S(1)} %pad_maximum_fusion.8.refs_2_.refs_3_.refs_13_) | copy-start | bytes 737284
  14.9 12.4 %collective-permute-start.5 = (bf16[2,48,1280]{2,1,0:T(8,128)(2,1)S(1)}, bf16[2,48,1280]{2,1,0:T(8,128)(2,1)S(1)}, u32[]{:S(2)}, u32[]{:S(2)}) collective-permute-start(bf16[2,48,1280]{2,1,0:T(8,128)(2,1)S(1)} %pad_maximum_fusion.8.refs_2_.refs_3_.refs_13_), channel_id=1, source_target_pairs={{0,16},{16,0},{1,17},{17,1},{2,18},{18,2},{3,19},{19,3},{4,20},{20... | collective-permute-start | bytes 737288 | tf_op jit(solution)/shard_map/ppermute | solution.py:372
  16.7 12.4 %collective-permute-start.6 = (bf16[2,48,1280]{2,1,0:T(8,128)(2,1)S(1)}, bf16[2,48,1280]{2,1,0:T(8,128)(2,1)S(1)}, u32[]{:S(2)}, u32[]{:S(2)}) collective-permute-start(bf16[2,48,1280]{2,1,0:T(8,128)(2,1)S(1)} %pad_maximum_fusion.8.refs_2_.refs_3_.refs_13_), channel_id=1, source_target_pairs={{0,2},{2,0},{4,6},{6,4},{8,10},{10,8},{12,14},{14,12},{1,3},{3,1},... | collective-permute-start | bytes 737288 | tf_op jit(solution)/shard_map/ppermute | solution.py:375
  18.6 11.3 %collective-permute-start.7 = (bf16[2,48,1280]{2,1,0:T(8,128)(2,1)S(1)}, bf16[2,48,1280]{2,1,0:T(8,128)(2,1)S(1)}, u32[]{:S(2)}, u32[]{:S(2)}) collective-permute-start(bf16[2,48,1280]{2,1,0:T(8,128)(2,1)S(1)} %pad_maximum_fusion.8.refs_2_.refs_3_.refs_13_), channel_id=1, source_target_pairs={{0,18},{2,16},{4,22},{6,20},{8,26},{10,24},{12,30},{14,28},{16,2},... | collective-permute-start | bytes 737288 | tf_op jit(solution)/shard_map/ppermute | solution.py:378
  24.1 28.8 %copy-start = (bf16[3,48,1280]{2,1,0:T(8,128)(2,1)}, bf16[3,48,1280]{2,1,0:T(8,128)(2,1)S(1)}, u32[]{:S(2)}) copy-start(bf16[3,48,1280]{2,1,0:T(8,128)(2,1)S(1)} %pad_maximum_fusion.3.refs_6_.refs_17_) | copy-start | bytes 1105924
  24.1 7.3 %collective-permute-start.8 = (bf16[48,1280]{1,0:T(8,128)(2,1)S(1)}, bf16[48,1280]{1,0:T(8,128)(2,1)S(1)}, u32[]{:S(2)}, u32[]{:S(2)}) collective-permute-start(bf16[48,1280]{1,0:T(8,128)(2,1)S(1)} %get-tuple-element.111), channel_id=1, source_target_pairs={{0,4},{2,6},{4,0},{6,2},{8,12},{10,14},{12,8},{14,10},{1,5},{3,7},... | collective-permute-start | bytes 368648 | tf_op jit(solution)/shard_map/ppermute | solution.py:394
  27.3 25.6 %copy-start.24 = (bf16[2,48,1280]{2,1,0:T(8,128)(2,1)}, bf16[2,48,1280]{2,1,0:T(8,128)(2,1)S(1)}, u32[]{:S(2)}) copy-start(bf16[2,48,1280]{2,1,0:T(8,128)(2,1)S(1)} %collective-permute-done.5.refs_3_.refs_4_.refs_14_) | copy-start | bytes 737284
  29.2 23.7 %copy-start.25 = (bf16[2,48,1280]{2,1,0:T(8,128)(2,1)}, bf16[2,48,1280]{2,1,0:T(8,128)(2,1)S(1)}, u32[]{:S(2)}) copy-start(bf16[2,48,1280]{2,1,0:T(8,128)(2,1)S(1)} %collective-permute-done.6.refs_4_.refs_5_.refs_15_) | copy-start | bytes 737284
  29.9 16.7 %collective-permute-start.10 = (bf16[3,48,1280]{2,1,0:T(8,128)(2,1)S(1)}, bf16[3,48,1280]{2,1,0:T(8,128)(2,1)S(1)}, u32[]{:S(2)}, u32[]{:S(2)}) collective-permute-start(bf16[3,48,1280]{2,1,0:T(8,128)(2,1)S(1)} %pad_maximum_fusion.3.refs_6_.refs_17_), channel_id=1, source_target_pairs={{0,16},{16,0},{1,17},{17,1},{2,18},{18,2},{3,19},{19,3},{4,20},{20... | collective-permute-start | bytes 1105928 | tf_op jit(solution)/shard_map/ppermute | solution.py:372
  31.4 13.3 %collective-permute-start.9 = (bf16[2,48,1280]{2,1,0:T(8,128)(2,1)S(1)}, bf16[2,48,1280]{2,1,0:T(8,128)(2,1)S(1)}, u32[]{:S(2)}, u32[]{:S(2)}) collective-permute-start(bf16[2,48,1280]{2,1,0:T(8,128)(2,1)S(1)} %pad_maximum_fusion.9), channel_id=1, source_target_pairs={{0,8},{2,10},{4,12},{6,14},{8,0},{10,2},{12,4},{14,6},{1,9},{3,11}... | collective-permute-start | bytes 737288 | tf_op jit(solution)/shard_map/ppermute | solution.py:394
  33.6 18.1 %collective-permute-start.11 = (bf16[3,48,1280]{2,1,0:T(8,128)(2,1)S(1)}, bf16[3,48,1280]{2,1,0:T(8,128)(2,1)}, u32[]{:S(2)}, u32[]{:S(2)}) collective-permute-start(bf16[3,48,1280]{2,1,0:T(8,128)(2,1)S(1)} %pad_maximum_fusion.3.refs_6_.refs_17_), channel_id=1, source_target_pairs={{0,2},{2,0},{4,6},{6,4},{8,10},{10,8},{12,14},{14,12},{1,3},{3,1},... | collective-permute-start | bytes 1105928 | tf_op jit(solution)/shard_map/ppermute | solution.py:375
  36.1 15.7 %collective-permute-start.12 = (bf16[3,48,1280]{2,1,0:T(8,128)(2,1)S(1)}, bf16[3,48,1280]{2,1,0:T(8,128)(2,1)}, u32[]{:S(2)}, u32[]{:S(2)}) collective-permute-start(bf16[3,48,1280]{2,1,0:T(8,128)(2,1)S(1)} %pad_maximum_fusion.3.refs_6_.refs_17_), channel_id=1, source_target_pairs={{0,18},{2,16},{4,22},{6,20},{8,26},{10,24},{12,30},{14,28},{16,2},... | collective-permute-start | bytes 1105928 | tf_op jit(solution)/shard_map/ppermute | solution.py:378
  37.0 15.2 %collective-permute-start.13 = (bf16[2,48,1280]{2,1,0:T(8,128)(2,1)S(1)}, bf16[2,48,1280]{2,1,0:T(8,128)(2,1)}, u32[]{:S(2)}, u32[]{:S(2)}) collective-permute-start(bf16[2,48,1280]{2,1,0:T(8,128)(2,1)S(1)} %pad_maximum_fusion.8.refs_2_.refs_3_.refs_13_), channel_id=1, source_target_pairs={{0,1},{1,0},{2,3},{3,2},{4,5},{5,4},{6,7},{7,6},{8,9},{9,8},{10,11... | collective-permute-start | bytes 737288 | tf_op jit(solution)/shard_map/ppermute | solution.py:369
  44.7 7.6 %collective-permute-start.14 = (bf16[2,48,1280]{2,1,0:T(8,128)(2,1)S(1)}, bf16[2,48,1280]{2,1,0:T(8,128)(2,1)}, u32[]{:S(2)}, u32[]{:S(2)}) collective-permute-start(bf16[2,48,1280]{2,1,0:T(8,128)(2,1)S(1)} %collective-permute-done.5.refs_3_.refs_4_.refs_14_), channel_id=1, source_target_pairs={{0,1},{1,0},{2,3},{3,2},{4,5},{5,4},{6,7},{7,6},{8,9},{9,8},{10,11... | collective-permute-start | bytes 737288 | tf_op jit(solution)/shard_map/ppermute | solution.py:369
  46.6 6.3 %copy-start.11 = (bf16[3,48,1280]{2,1,0:T(8,128)(2,1)}, bf16[3,48,1280]{2,1,0:T(8,128)(2,1)S(1)}, u32[]{:S(2)}) copy-start(bf16[3,48,1280]{2,1,0:T(8,128)(2,1)S(1)} %collective-permute-done.10.refs_7_.refs_18_) | copy-start | bytes 1105924
  46.6 6.3 %collective-permute-start.15 = (bf16[2,48,1280]{2,1,0:T(8,128)(2,1)S(1)}, bf16[2,48,1280]{2,1,0:T(8,128)(2,1)S(1)}, u32[]{:S(2)}, u32[]{:S(2)}) collective-permute-start(bf16[2,48,1280]{2,1,0:T(8,128)(2,1)S(1)} %collective-permute-done.6.refs_4_.refs_5_.refs_15_), channel_id=1, source_target_pairs={{0,1},{1,0},{2,3},{3,2},{4,5},{5,4},{6,7},{7,6},{8,9},{9,8},{10,11... | collective-permute-start | bytes 737288 | tf_op jit(solution)/shard_map/ppermute | solution.py:369
  47.1 28.0 %copy-start.1 = (bf16[3,48,1280]{2,1,0:T(8,128)(2,1)}, bf16[3,48,1280]{2,1,0:T(8,128)(2,1)S(1)}, u32[]{:S(2)}) copy-start(bf16[3,48,1280]{2,1,0:T(8,128)(2,1)S(1)} %pad_maximum_fusion.4.refs_7_) | copy-start | bytes 1105924
  47.1 5.8 %copy-start.27 = (bf16[2,48,1280]{2,1,0:T(8,128)(2,1)S(1)}, bf16[2,48,1280]{2,1,0:T(8,128)(2,1)}, u32[]{:S(2)}) copy-start(bf16[2,48,1280]{2,1,0:T(8,128)(2,1)} %copy-done.26) | copy-start | bytes 737284
  51.7 5.1 %collective-permute-start.17 = (bf16[3,48,1280]{2,1,0:T(8,128)(2,1)S(1)}, bf16[3,48,1280]{2,1,0:T(8,128)(2,1)S(1)}, u32[]{:S(2)}, u32[]{:S(2)}) collective-permute-start(bf16[3,48,1280]{2,1,0:T(8,128)(2,1)S(1)} %pad_maximum_fusion.3.refs_6_.refs_17_), channel_id=1, source_target_pairs={{0,1},{1,0},{2,3},{3,2},{4,5},{5,4},{6,7},{7,6},{8,9},{9,8},{10,11... | collective-permute-start | bytes 1105928 | tf_op jit(solution)/shard_map/ppermute | solution.py:369
  51.7 6.9 %collective-permute-start.18 = (bf16[3,48,1280]{2,1,0:T(8,128)(2,1)S(1)}, bf16[3,48,1280]{2,1,0:T(8,128)(2,1)S(1)}, u32[]{:S(2)}, u32[]{:S(2)}) collective-permute-start(bf16[3,48,1280]{2,1,0:T(8,128)(2,1)S(1)} %collective-permute-done.10.refs_7_.refs_18_), channel_id=1, source_target_pairs={{0,1},{1,0},{2,3},{3,2},{4,5},{5,4},{6,7},{7,6},{8,9},{9,8},{10,11... | collective-permute-start | bytes 1105928 | tf_op jit(solution)/shard_map/ppermute | solution.py:369
  52.2 6.6 %collective-permute-start.19 = (bf16[3,48,1280]{2,1,0:T(8,128)(2,1)}, bf16[3,48,1280]{2,1,0:T(8,128)(2,1)S(1)}, u32[]{:S(2)}, u32[]{:S(2)}) collective-permute-start(bf16[3,48,1280]{2,1,0:T(8,128)(2,1)} %collective-permute-done.11.refs_8_.refs_19_), channel_id=1, source_target_pairs={{0,1},{1,0},{2,3},{3,2},{4,5},{5,4},{6,7},{7,6},{8,9},{9,8},{10,11... | collective-permute-start | bytes 1105928 | tf_op jit(solution)/shard_map/ppermute | solution.py:369
  52.2 6.6 %collective-permute-start.20 = (bf16[3,48,1280]{2,1,0:T(8,128)(2,1)}, bf16[3,48,1280]{2,1,0:T(8,128)(2,1)S(1)}, u32[]{:S(2)}, u32[]{:S(2)}) collective-permute-start(bf16[3,48,1280]{2,1,0:T(8,128)(2,1)} %collective-permute-done.12.refs_9_.refs_20_), channel_id=1, source_target_pairs={{0,1},{1,0},{2,3},{3,2},{4,5},{5,4},{6,7},{7,6},{8,9},{9,8},{10,11... | collective-permute-start | bytes 1105928 | tf_op jit(solution)/shard_map/ppermute | solution.py:369
  52.9 5.9 %copy-start.28 = (bf16[2,48,1280]{2,1,0:T(8,128)(2,1)}, bf16[2,48,1280]{2,1,0:T(8,128)(2,1)S(1)}, u32[]{:S(2)}) copy-start(bf16[2,48,1280]{2,1,0:T(8,128)(2,1)S(1)} %collective-permute-done.15.refs_12_.refs_13_.refs_23_) | copy-start | bytes 737284
  53.0 2.4 %collective-permute-start.16 = (bf16[2,48,1280]{2,1,0:T(8,128)(2,1)S(1)}, bf16[2,48,1280]{2,1,0:T(8,128)(2,1)S(1)}, u32[]{:S(2)}, u32[]{:S(2)}) collective-permute-start(bf16[2,48,1280]{2,1,0:T(8,128)(2,1)S(1)} %copy-done.27), channel_id=1, source_target_pairs={{0,1},{1,0},{2,3},{3,2},{4,5},{5,4},{6,7},{7,6},{8,9},{9,8},{10,11... | collective-permute-start | bytes 737288 | tf_op jit(solution)/shard_map/ppermute | solution.py:369
  55.4 18.2 %collective-permute-start.21 = (bf16[3,48,1280]{2,1,0:T(8,128)(2,1)S(1)}, bf16[3,48,1280]{2,1,0:T(8,128)(2,1)S(1)}, u32[]{:S(2)}, u32[]{:S(2)}) collective-permute-start(bf16[3,48,1280]{2,1,0:T(8,128)(2,1)S(1)} %pad_maximum_fusion.4.refs_7_), channel_id=1, source_target_pairs={{0,16},{16,0},{1,17},{17,1},{2,18},{18,2},{3,19},{19,3},{4,20},{20... | collective-permute-start | bytes 1105928 | tf_op jit(solution)/shard_map/ppermute | solution.py:372
  56.8 17.5 %collective-permute-start.22 = (bf16[3,48,1280]{2,1,0:T(8,128)(2,1)S(1)}, bf16[3,48,1280]{2,1,0:T(8,128)(2,1)S(1)}, u32[]{:S(2)}, u32[]{:S(2)}) collective-permute-start(bf16[3,48,1280]{2,1,0:T(8,128)(2,1)S(1)} %pad_maximum_fusion.4.refs_7_), channel_id=1, source_target_pairs={{0,2},{2,0},{4,6},{6,4},{8,10},{10,8},{12,14},{14,12},{1,3},{3,1},... | collective-permute-start | bytes 1105928 | tf_op jit(solution)/shard_map/ppermute | solution.py:375
  58.6 16.5 %collective-permute-start.23 = (bf16[3,48,1280]{2,1,0:T(8,128)(2,1)S(1)}, bf16[3,48,1280]{2,1,0:T(8,128)(2,1)S(1)}, u32[]{:S(2)}, u32[]{:S(2)}) collective-permute-start(bf16[3,48,1280]{2,1,0:T(8,128)(2,1)S(1)} %pad_maximum_fusion.4.refs_7_), channel_id=1, source_target_pairs={{0,18},{2,16},{4,22},{6,20},{8,26},{10,24},{12,30},{14,28},{16,2},... | collective-permute-start | bytes 1105928 | tf_op jit(solution)/shard_map/ppermute | solution.py:378
  73.6 4.8 %copy-start.16 = (bf16[3,48,1280]{2,1,0:T(8,128)(2,1)}, bf16[3,48,1280]{2,1,0:T(8,128)(2,1)S(1)}, u32[]{:S(2)}) copy-start(bf16[3,48,1280]{2,1,0:T(8,128)(2,1)S(1)} %collective-permute-done.21.refs_8_) | copy-start | bytes 1105924
  75.1 2.3 %collective-permute-start.24 = (bf16[3,48,1280]{2,1,0:T(8,128)(2,1)S(1)}, bf16[3,48,1280]{2,1,0:T(8,128)(2,1)S(1)}, u32[]{:S(2)}, u32[]{:S(2)}) collective-permute-start(bf16[3,48,1280]{2,1,0:T(8,128)(2,1)S(1)} %pad_maximum_fusion.4.refs_7_), channel_id=1, source_target_pairs={{0,1},{1,0},{2,3},{3,2},{4,5},{5,4},{6,7},{7,6},{8,9},{9,8},{10,11... | collective-permute-start | bytes 1105928 | tf_op jit(solution)/shard_map/ppermute | solution.py:369
  75.1 2.3 %collective-permute-start.25 = (bf16[3,48,1280]{2,1,0:T(8,128)(2,1)S(1)}, bf16[3,48,1280]{2,1,0:T(8,128)(2,1)S(1)}, u32[]{:S(2)}, u32[]{:S(2)}) collective-permute-start(bf16[3,48,1280]{2,1,0:T(8,128)(2,1)S(1)} %collective-permute-done.21.refs_8_), channel_id=1, source_target_pairs={{0,1},{1,0},{2,3},{3,2},{4,5},{5,4},{6,7},{7,6},{8,9},{9,8},{10,11... | collective-permute-start | bytes 1105928 | tf_op jit(solution)/shard_map/ppermute | solution.py:369
  75.6 2.2 %collective-permute-start.26 = (bf16[3,48,1280]{2,1,0:T(8,128)(2,1)S(1)}, bf16[3,48,1280]{2,1,0:T(8,128)(2,1)S(1)}, u32[]{:S(2)}, u32[]{:S(2)}) collective-permute-start(bf16[3,48,1280]{2,1,0:T(8,128)(2,1)S(1)} %collective-permute-done.22.refs_9_), channel_id=1, source_target_pairs={{0,1},{1,0},{2,3},{3,2},{4,5},{5,4},{6,7},{7,6},{8,9},{9,8},{10,11... | collective-permute-start | bytes 1105928 | tf_op jit(solution)/shard_map/ppermute | solution.py:369
  75.7 2.7 %collective-permute-start.27 = (bf16[3,48,1280]{2,1,0:T(8,128)(2,1)S(1)}, bf16[3,48,1280]{2,1,0:T(8,128)(2,1)S(1)}, u32[]{:S(2)}, u32[]{:S(2)}) collective-permute-start(bf16[3,48,1280]{2,1,0:T(8,128)(2,1)S(1)} %collective-permute-done.23.refs_10_), channel_id=1, source_target_pairs={{0,1},{1,0},{2,3},{3,2},{4,5},{5,4},{6,7},{7,6},{8,9},{9,8},{10,11... | collective-permute-start | bytes 1105928 | tf_op jit(solution)/shard_map/ppermute | solution.py:369
  106.5 8.2 %collective-permute-start.29 = (bf16[2,2,2,4,48,640]{5,4,2,3,1,0:T(8,128)(2,1)S(1)}, bf16[2,2,2,4,48,640]{5,4,2,3,1,0:T(8,128)(2,1)S(1)}, u32[]{:S(2)}, u32[]{:S(2)}) collective-permute-start(bf16[2,2,2,4,48,640]{5,4,2,3,1,0:T(8,128)(2,1)S(1)} %copy.42), channel_id=1, source_target_pairs={{0,1},{1,0},{2,3},{3,2},{4,5},{5,4},{6,7},{7,6},{8,9},{9,8},{10,11... | collective-permute-start | bytes 5898248 | tf_op jit(solution)/shard_map/ppermute | solution.py:369
  107.0 9.9 %collective-permute-start.28 = (bf16[416,384]{1,0:T(8,128)(2,1)S(1)}, bf16[416,384]{1,0:T(8,128)(2,1)S(1)}, u32[]{:S(2)}, u32[]{:S(2)}) collective-permute-start(bf16[416,384]{1,0:T(8,128)(2,1)S(1)} %copy-done.23), channel_id=1, source_target_pairs={{0,16},{16,0},{1,17},{17,1},{2,18},{18,2},{3,19},{19,3},{4,20},{20... | collective-permute-start | bytes 958472 | tf_op jit(solution)/shard_map/ppermute | solution.py:372
  117.3 23.2 %collective-permute-start.30 = (bf16[2,208,384]{2,1,0:T(8,128)(2,1)S(1)}, bf16[2,208,384]{2,1,0:T(8,128)(2,1)S(1)}, u32[]{:S(2)}, u32[]{:S(2)}) collective-permute-start(bf16[2,208,384]{2,1,0:T(8,128)(2,1)S(1)} %pad_maximum_fusion.6), channel_id=1, source_target_pairs={{1,3},{3,5},{5,7},{7,9},{9,11},{11,13},{13,15},{17,19},{19,21},{21... | collective-permute-start | bytes 958472 | tf_op jit(solution)/shard_map/ppermute | solution.py:408
  118.0 22.5 %collective-permute-start.31 = (bf16[2,4,48,640]{3,2,0,1:T(8,128)(2,1)S(1)}, bf16[2,4,48,640]{3,2,0,1:T(8,128)(2,1)S(1)}, u32[]{:S(2)}, u32[]{:S(2)}) collective-permute-start(bf16[2,4,48,640]{3,2,0,1:T(8,128)(2,1)S(1)} %get-tuple-element.160), channel_id=1, source_target_pairs={{0,2},{2,0},{4,6},{6,4},{8,10},{10,8},{12,14},{14,12},{1,3},{3,1},... | collective-permute-start | bytes 1474568 | tf_op jit(solution)/shard_map/ppermute | solution.py:375
  119.9 20.7 %collective-permute-start.32 = (bf16[2,4,48,640]{3,2,0,1:T(8,128)(2,1)S(1)}, bf16[2,4,48,640]{3,2,0,1:T(8,128)(2,1)S(1)}, u32[]{:S(2)}, u32[]{:S(2)}) collective-permute-start(bf16[2,4,48,640]{3,2,0,1:T(8,128)(2,1)S(1)} %get-tuple-element.161), channel_id=1, source_target_pairs={{0,16},{16,0},{1,17},{17,1},{2,18},{18,2},{3,19},{19,3},{4,20},{20... | collective-permute-start | bytes 1474568 | tf_op jit(solution)/shard_map/ppermute | solution.py:372
  120.4 22.8 %collective-permute-start.33 = (bf16[2,4,48,640]{3,2,0,1:T(8,128)(2,1)S(1)}, bf16[2,4,48,640]{3,2,0,1:T(8,128)(2,1)S(1)}, u32[]{:S(2)}, u32[]{:S(2)}) collective-permute-start(bf16[2,4,48,640]{3,2,0,1:T(8,128)(2,1)S(1)} %get-tuple-element.162), channel_id=1, source_target_pairs={{0,18},{2,16},{4,22},{6,20},{8,26},{10,24},{12,30},{14,28},{16,2},... | collective-permute-start | bytes 1474568 | tf_op jit(solution)/shard_map/ppermute | solution.py:378
  140.5 6.2 %copy-start.31 = (bf16[416,384]{1,0:T(8,128)(2,1)S(1)}, bf16[416,384]{1,0:T(8,128)(2,1)}, u32[]{:S(2)}) copy-start(bf16[416,384]{1,0:T(8,128)(2,1)} %get-tuple-element.173) | copy-start | bytes 958468
  143.2 10.0 %collective-permute-start.34 = (bf16[2,2,2,4,48,640]{5,4,3,2,1,0:T(8,128)(2,1)}, bf16[2,2,2,4,48,640]{5,4,3,2,1,0:T(8,128)(2,1)S(1)}, u32[]{:S(2)}, u32[]{:S(2)}) collective-permute-start(bf16[2,2,2,4,48,640]{5,4,3,2,1,0:T(8,128)(2,1)} %get-tuple-element.171), channel_id=1, source_target_pairs={{0,1},{1,0},{2,3},{3,2},{4,5},{5,4},{6,7},{7,6},{8,9},{9,8},{10,11... | collective-permute-start | bytes 5898248 | tf_op jit(solution)/shard_map/ppermute | solution.py:369
  145.8 9.7 %collective-permute-start.36 = (bf16[416,384]{1,0:T(8,128)(2,1)}, bf16[416,384]{1,0:T(8,128)(2,1)S(1)}, u32[]{:S(2)}, u32[]{:S(2)}) collective-permute-start(bf16[416,384]{1,0:T(8,128)(2,1)} %get-tuple-element.174), channel_id=1, source_target_pairs={{0,16},{16,0},{1,17},{17,1},{2,18},{18,2},{3,19},{19,3},{4,20},{20... | collective-permute-start | bytes 958472 | tf_op jit(solution)/shard_map/ppermute | solution.py:372
  147.9 5.3 %collective-permute-start.35 = (bf16[2,512,384]{2,1,0:T(8,128)(2,1)S(1)}, bf16[2,512,384]{2,1,0:T(8,128)(2,1)S(1)}, u32[]{:S(2)}, u32[]{:S(2)}) collective-permute-start(bf16[2,512,384]{2,1,0:T(8,128)(2,1)S(1)} %pad_maximum_fusion.1), channel_id=1, source_target_pairs={{0,1},{1,0},{2,3},{3,2},{4,5},{5,4},{6,7},{7,6},{8,9},{9,8},{10,11... | collective-permute-start | bytes 2359304 | tf_op jit(solution)/shard_map/ppermute | solution.py:369
  156.7 19.2 %collective-permute-start.50 = (bf16[2,2,48,640]{3,2,0,1:T(8,128)(2,1)S(1)}, bf16[2,2,48,640]{3,2,0,1:T(8,128)(2,1)S(1)}, u32[]{:S(2)}, u32[]{:S(2)}) collective-permute-start(bf16[2,2,48,640]{3,2,0,1:T(8,128)(2,1)S(1)} %slice.316), channel_id=1, source_target_pairs={{0,4},{2,6},{4,0},{6,2},{8,12},{10,14},{12,8},{14,10},{1,5},{3,7},... | collective-permute-start | bytes 737288 | tf_op jit(solution)/shard_map/ppermute | solution.py:394
  158.3 8.1 %collective-permute-start.42 = (bf16[1,4,48,640]{3,2,1,0:T(8,128)(2,1)S(1)}, bf16[1,4,48,640]{3,2,1,0:T(8,128)(2,1)S(1)}, u32[]{:S(2)}, u32[]{:S(2)}) collective-permute-start(bf16[1,4,48,640]{3,2,1,0:T(8,128)(2,1)S(1)} %get-tuple-element.247), channel_id=1, source_target_pairs={{0,2},{2,0},{4,6},{6,4},{8,10},{10,8},{12,14},{14,12},{1,3},{3,1},... | collective-permute-start | bytes 737288 | tf_op jit(solution)/shard_map/ppermute | solution.py:375
  159.7 8.9 %collective-permute-start.43 = (bf16[1,4,48,640]{3,2,1,0:T(8,128)(2,1)S(1)}, bf16[1,4,48,640]{3,2,1,0:T(8,128)(2,1)S(1)}, u32[]{:S(2)}, u32[]{:S(2)}) collective-permute-start(bf16[1,4,48,640]{3,2,1,0:T(8,128)(2,1)S(1)} %get-tuple-element.249), channel_id=1, source_target_pairs={{0,16},{16,0},{1,17},{17,1},{2,18},{18,2},{3,19},{19,3},{4,20},{20... | collective-permute-start | bytes 737288 | tf_op jit(solution)/shard_map/ppermute | solution.py:372
  160.7 13.5 %collective-permute-start.44 = (bf16[1,4,48,640]{3,2,1,0:T(8,128)(2,1)S(1)}, bf16[1,4,48,640]{3,2,1,0:T(8,128)(2,1)S(1)}, u32[]{:S(2)}, u32[]{:S(2)}) collective-permute-start(bf16[1,4,48,640]{3,2,1,0:T(8,128)(2,1)S(1)} %get-tuple-element.251), channel_id=1, source_target_pairs={{0,18},{2,16},{4,22},{6,20},{8,26},{10,24},{12,30},{14,28},{16,2},... | collective-permute-start | bytes 737288 | tf_op jit(solution)/shard_map/ppermute | solution.py:378
  162.2 15.4 %collective-permute-start.37 = (bf16[2,208,384]{2,1,0:T(8,128)(2,1)S(1)}, bf16[2,208,384]{2,1,0:T(8,128)(2,1)S(1)}, u32[]{:S(2)}, u32[]{:S(2)}) collective-permute-start(bf16[2,208,384]{2,1,0:T(8,128)(2,1)S(1)} %pad_maximum_fusion.7), channel_id=1, source_target_pairs={{1,3},{3,5},{5,7},{7,9},{9,11},{11,13},{13,15},{17,19},{19,21},{21... | collective-permute-start | bytes 958472 | tf_op jit(solution)/shard_map/ppermute | solution.py:408
  166.5 22.1 %collective-permute-start.39 = (bf16[1,4,48,640]{3,2,1,0:T(8,128)(2,1)S(1)}, bf16[1,4,48,640]{3,2,1,0:T(8,128)(2,1)S(1)}, u32[]{:S(2)}, u32[]{:S(2)}) collective-permute-start(bf16[1,4,48,640]{3,2,1,0:T(8,128)(2,1)S(1)} %get-tuple-element.248), channel_id=1, source_target_pairs={{0,2},{2,0},{4,6},{6,4},{8,10},{10,8},{12,14},{14,12},{1,3},{3,1},... | collective-permute-start | bytes 737288 | tf_op jit(solution)/shard_map/ppermute | solution.py:375
  168.6 20.1 %collective-permute-start.40 = (bf16[1,4,48,640]{3,2,1,0:T(8,128)(2,1)S(1)}, bf16[1,4,48,640]{3,2,1,0:T(8,128)(2,1)S(1)}, u32[]{:S(2)}, u32[]{:S(2)}) collective-permute-start(bf16[1,4,48,640]{3,2,1,0:T(8,128)(2,1)S(1)} %get-tuple-element.250), channel_id=1, source_target_pairs={{0,16},{16,0},{1,17},{17,1},{2,18},{18,2},{3,19},{19,3},{4,20},{20... | collective-permute-start | bytes 737288 | tf_op jit(solution)/shard_map/ppermute | solution.py:372
  174.1 14.5 %collective-permute-start.41 = (bf16[1,4,48,640]{3,2,1,0:T(8,128)(2,1)S(1)}, bf16[1,4,48,640]{3,2,1,0:T(8,128)(2,1)S(1)}, u32[]{:S(2)}, u32[]{:S(2)}) collective-permute-start(bf16[1,4,48,640]{3,2,1,0:T(8,128)(2,1)S(1)} %get-tuple-element.252), channel_id=1, source_target_pairs={{0,18},{2,16},{4,22},{6,20},{8,26},{10,24},{12,30},{14,28},{16,2},... | collective-permute-start | bytes 737288 | tf_op jit(solution)/shard_map/ppermute | solution.py:378
  175.9 4.9 %collective-permute-start.45 = (bf16[1,2,48,640]{3,2,1,0:T(8,128)(2,1)S(1)}, bf16[1,2,48,640]{3,2,1,0:T(8,128)(2,1)S(1)}, u32[]{:S(2)}, u32[]{:S(2)}) collective-permute-start(bf16[1,2,48,640]{3,2,1,0:T(8,128)(2,1)S(1)} %slice.308), channel_id=1, source_target_pairs={{0,4},{2,6},{4,0},{6,2},{8,12},{10,14},{12,8},{14,10},{1,5},{3,7},... | collective-permute-start | bytes 368648 | tf_op jit(solution)/shard_map/ppermute | solution.py:394
  177.8 10.8 %collective-permute-start.38 = (bf16[2,512,384]{2,1,0:T(8,128)(2,1)S(1)}, bf16[2,512,384]{2,1,0:T(8,128)(2,1)S(1)}, u32[]{:S(2)}, u32[]{:S(2)}) collective-permute-start(bf16[2,512,384]{2,1,0:T(8,128)(2,1)S(1)} %pad_maximum_fusion.2), channel_id=1, source_target_pairs={{0,1},{1,0},{2,3},{3,2},{4,5},{5,4},{6,7},{7,6},{8,9},{9,8},{10,11... | collective-permute-start | bytes 2359304 | tf_op jit(solution)/shard_map/ppermute | solution.py:369
  180.8 5.2 %collective-permute-start.46 = (bf16[1,48,640]{2,1,0:T(8,128)(2,1)S(1)}, bf16[1,48,640]{2,1,0:T(8,128)(2,1)S(1)}, u32[]{:S(2)}, u32[]{:S(2)}) collective-permute-start(bf16[1,48,640]{2,1,0:T(8,128)(2,1)S(1)} %fusion.34), channel_id=1, source_target_pairs={{0,8},{2,10},{4,12},{6,14},{8,0},{10,2},{12,4},{14,6},{1,9},{3,11}... | collective-permute-start | bytes 184328 | tf_op jit(solution)/shard_map/ppermute | solution.py:394
  186.0 11.3 %collective-permute-start.51 = (bf16[2,48,640]{2,1,0:T(8,128)(2,1)S(1)}, bf16[2,48,640]{2,1,0:T(8,128)(2,1)S(1)}, u32[]{:S(2)}, u32[]{:S(2)}) collective-permute-start(bf16[2,48,640]{2,1,0:T(8,128)(2,1)S(1)} %fusion.29), channel_id=1, source_target_pairs={{0,8},{2,10},{4,12},{6,14},{8,0},{10,2},{12,4},{14,6},{1,9},{3,11}... | collective-permute-start | bytes 368648 | tf_op jit(solution)/shard_map/ppermute | solution.py:394
  188.8 4.6 %collective-permute-start.47 = (bf16[1,48,640]{2,1,0:T(8,128)(2,1)S(1)}, bf16[1,48,640]{2,1,0:T(8,128)(2,1)S(1)}, u32[]{:S(2)}, u32[]{:S(2)}) collective-permute-start(bf16[1,48,640]{2,1,0:T(8,128)(2,1)S(1)} %get-tuple-element.263), channel_id=1, source_target_pairs={{0,4},{2,6},{4,0},{6,2},{8,12},{10,14},{12,8},{14,10},{1,5},{3,7},... | collective-permute-start | bytes 184328 | tf_op jit(solution)/shard_map/ppermute | solution.py:394
  189.2 7.0 %collective-permute-start.48 = (bf16[1,48,640]{2,1,0:T(8,128)(2,1)S(1)}, bf16[1,48,640]{2,1,0:T(8,128)(2,1)S(1)}, u32[]{:S(2)}, u32[]{:S(2)}) collective-permute-start(bf16[1,48,640]{2,1,0:T(8,128)(2,1)S(1)} %get-tuple-element.265), channel_id=1, source_target_pairs={{0,8},{2,10},{4,12},{6,14},{8,0},{10,2},{12,4},{14,6},{1,9},{3,11}... | collective-permute-start | bytes 184328 | tf_op jit(solution)/shard_map/ppermute | solution.py:394
  191.1 6.1 %collective-permute-start.49 = (bf16[1,48,640]{2,1,0:T(8,128)(2,1)S(1)}, bf16[1,48,640]{2,1,0:T(8,128)(2,1)S(1)}, u32[]{:S(2)}, u32[]{:S(2)}) collective-permute-start(bf16[1,48,640]{2,1,0:T(8,128)(2,1)S(1)} %get-tuple-element.264), channel_id=1, source_target_pairs={{0,12},{2,14},{4,8},{6,10},{8,4},{10,6},{12,0},{14,2},{1,13},{3,15... | collective-permute-start | bytes 184328 | tf_op jit(solution)/shard_map/ppermute | solution.py:394
  197.4 4.9 %collective-permute-start.52 = (bf16[2,48,640]{2,1,0:T(8,128)(2,1)S(1)}, bf16[2,48,640]{2,1,0:T(8,128)(2,1)S(1)}, u32[]{:S(2)}, u32[]{:S(2)}) collective-permute-start(bf16[2,48,640]{2,1,0:T(8,128)(2,1)S(1)} %select_convert_fusion), channel_id=1, source_target_pairs={{0,16},{16,0},{1,17},{17,1},{2,18},{18,2},{3,19},{19,3},{4,20},{20... | collective-permute-start | bytes 368648 | tf_op jit(solution)/shard_map/ppermute | solution.py:372
  (22 other events, 43.1 us)

commit v8 on v7

--- a/solution.py
+++ b/solution.py
@@ -56,21 +56,12 @@
     return u * cdf, cdf + u * pdf
 
 
-ATT = 640
-OUT = 512
-MISC = 768
-UP0 = 896
-DOWN = 384
-ROWSB = 1152
-CHUNK = 384
-
-
-def up_at(w, t, j):
-    return w[t, 0, :, UP0:] if j == 0 else w[t, 1, :, :CHUNK]
-
-
-def down_at(w, t, j):
-    return w[t, 1, :, DOWN + j * CHUNK:DOWN + (j + 1) * CHUNK]
+QK = 384
+V = 256
+OUT = 128
+MISC = 384
+MLP = 512
+ATT = QK + V
 
 
 def low_lanes():
@@ -90,7 +81,7 @@
     return pl.ds(pl.multiple_of(n * IMG_PAD, 16), IMG_PAD)
 
 
-def forward_image(n, sc, x_ref, w, vec, brow, out_ref, kept):
+def forward_image(n, sc, x_ref, w, vec, brow, out_ref, kept, ready):
     r = image_rows(n)
     x = x_ref[r, :].astype(F32)
     xhat, inv = normed(x)
@@ -105,7 +96,8 @@
     real = lax.broadcasted_iota(jnp.int32, (1, IMG_PAD), 1) < IMG_LEN
     for t in range(2):
         bias = jnp.concatenate([brow[t, i:i + 1, :] for i in range(5)], 1)
-        p = ((nn(attn_in, w[t, 0, :, :ATT]) + bias) * factor).astype(BF16)
+        p = jnp.concatenate([nn(attn_in, w[t, 0, :, :QK]), nn(attn_in, w[t, 1, :, :V])], 1)
+        p = ((p + bias) * factor).astype(BF16)
         kept["qkv"][t, r, :] = p
         q, qk, k, v, vx = [p[:, i * BLOCK:(i + 1) * BLOCK] for i in range(5)]
         kq, xv = turn(qk), turn(vx)
@@ -119,22 +111,22 @@
             outs.append(nn(pr, vv))
         mixed = jnp.concatenate([outs[2], jnp.where(low, outs[0], outs[1])], 1).astype(BF16)
         kept["mx"][t, r, :] = mixed
-        residual = residual + nt(mixed, w[t, 0, :, OUT:MISC])
+        residual = residual + nt(mixed, w[t, 1, :, OUT:MISC])
     xhat, inv = normed(residual)
     mlp_in = (xhat * vec[1:2, :] + vec[4:5, :]).astype(BF16)
     kept["xh2"][r, :] = xhat
     kept["inv2"][r, :] = jnp.broadcast_to(inv, (IMG_PAD, BLOCK))
     kept["min"][r, :] = mlp_in
     out = residual + vec[5:6, :]
+    ready(1)
+    ff = kept["hd"].shape[1] // 2
     for t in range(2):
-        for j in range(2):
-            bias = jnp.concatenate([brow[t, 5 + j * 3 + i:6 + j * 3 + i, :] for i in range(3)], 1)
-            hidden, slope = gelu_parts(nn(mlp_in, up_at(w, t, j)) + bias)
-            c = slice((t * 2 + j) * CHUNK, (t * 2 + j + 1) * CHUNK)
-            hidden = hidden.astype(BF16)
-            kept["hd"][r, c] = hidden
-            kept["sl"][r, c] = slope.astype(BF16)
-            out = out + nt(hidden, down_at(w, t, j))
+        bias = jnp.concatenate([brow[t, 5 + i:6 + i, :] for i in range(ff // BLOCK)], 1)
+        hidden, slope = gelu_parts(nn(mlp_in, w[t, 0, :, MLP:]) + bias)
+        hidden = hidden.astype(BF16)
+        kept["hd"][r, t * ff:(t + 1) * ff] = hidden
+        kept["sl"][r, t * ff:(t + 1) * ff] = slope.astype(BF16)
+        out = out + nt(hidden, w[t, 1, :, MLP:])
     out_ref[r, :] = (out * valid_rows(sc, n)).astype(BF16)
 
 
@@ -150,16 +142,15 @@
     dg = masked.astype(BF16)
     grad["dg"][r, :] = dg
     mg = jnp.zeros(masked.shape, F32)
+    ff = kept["hd"].shape[1] // 2
     for t in range(2):
-        for j in range(2):
-            c = slice((t * 2 + j) * CHUNK, (t * 2 + j + 1) * CHUNK)
-            up = nn(dg, down_at(w, t, j)) * kept["sl"][r, c].astype(F32)
-            up = up.astype(BF16)
-            grad["up"][r, c] = up
-            total = rsum(up.astype(F32))
-            for i in range(3):
-                bsum[t, 5 + j * 3 + i:6 + j * 3 + i, :] += total[:, i * BLOCK:(i + 1) * BLOCK]
-            mg = mg + nt(up, up_at(w, t, j))
+        c = slice(t * ff, (t + 1) * ff)
+        up = (nn(dg, w[t, 1, :, MLP:]) * kept["sl"][r, c].astype(F32)).astype(BF16)
+        grad["up"][r, c] = up
+        total = rsum(up.astype(F32))
+        for i in range(ff // BLOCK):
+            bsum[t, 5 + i:6 + i, :] += total[:, i * BLOCK:(i + 1) * BLOCK]
+        mg = mg + nt(up, w[t, 0, :, MLP:])
     xhat = kept["xh2"][r, :]
     sums[4:5, :] += rsum(mg)
     sums[1:2, :] += rsum(mg * xhat)
@@ -176,7 +167,7 @@
     low = low_lanes()
     ig = jnp.zeros(res.shape, F32)
     for t in range(2):
-        xg = nn(ag, w[t, 0, :, OUT:MISC]).astype(BF16)
+        xg = nn(ag, w[t, 1, :, OUT:MISC]).astype(BF16)
         gx = jnp.where(low, 0, xg[:, :BLOCK])
         g = xg[:, BLOCK:]
         p = kept["qkv"][t, r, :]
@@ -201,7 +192,7 @@
         total = rsum(d.astype(F32))
         for i in range(5):
             bsum[t, i:i + 1, :] += total[:, i * BLOCK:(i + 1) * BLOCK]
-        ig = ig + nt(d, w[t, 0, :, :ATT])
+        ig = ig + nt(d[:, :QK], w[t, 0, :, :QK]) + nt(d[:, QK:], w[t, 1, :, :V])
     xhat = kept["xh1"][r, :]
     sums[2:3, :] += rsum(ig)
     sums[0:1, :] += rsum(ig * xhat)
@@ -214,24 +205,22 @@
     width = ag.shape[1]
     high = jnp.where(low_lanes(), 0.0, 1.0)
     d = grad["dqkv"][t]
-    g[0, :, :OUT] = tn(ain, d[:, :OUT]).astype(BF16)
+    g[0, :, :QK] = tn(ain, d[:, :QK]).astype(BF16)
+    val = tn(ain, d[:, QK:])
     out = tn(ag, kept["mx"][t])
-    g[0, :, OUT:ATT] = (tn(ain, d[:, OUT:]) + out[:, :BLOCK] * high).astype(BF16)
-    g[0, :, ATT:MISC] = out[:, BLOCK:].astype(BF16)
+    g[1, :, :OUT] = val[:, :BLOCK].astype(BF16)
+    g[1, :, OUT:V] = (val[:, BLOCK:] + out[:, :BLOCK] * high).astype(BF16)
+    g[1, :, V:MISC] = out[:, BLOCK:].astype(BF16)
     sums = jnp.concatenate([grad["sums"][...], jnp.zeros((BLOCK - 8, width), F32)], 0)
-    g[0, :, MISC:UP0] = sums.T.astype(BF16)
-    for j in range(2):
-        c = pl.ds(pl.multiple_of((t * 2 + j) * CHUNK, BLOCK), CHUNK)
-        up = tn(mlp_in, grad["up"][:, c]).astype(BF16)
-        if j == 0:
-            g[0, :, UP0:] = up
-        else:
-            g[1, :, :CHUNK] = up
-        g[1, :, DOWN + j * CHUNK:DOWN + (j + 1) * CHUNK] = tn(dg, kept["hd"][:, c]).astype(BF16)
+    g[0, :, MISC:MLP] = sums.T.astype(BF16)
+    ff = kept["hd"].shape[1] // 2
+    c = pl.ds(pl.multiple_of(t * ff, BLOCK), ff)
+    g[0, :, MLP:] = tn(mlp_in, grad["up"][:, c]).astype(BF16)
+    g[1, :, MLP:] = tn(dg, kept["hd"][:, c]).astype(BF16)
     if piece % 16 == 0:
         rows = jnp.concatenate([grad["bsum"][t], jnp.zeros((piece - 16, BLOCK), F32)], 0).astype(BF16)
         for i in range(width // piece):
-            g[1, i * piece:(i + 1) * piece, ROWSB:] = rows
+            g[1, i * piece:(i + 1) * piece, MISC:MLP] = rows
 
 
 def kept_shapes(total, width, ff):
@@ -270,7 +259,7 @@
     vmem = pl.BlockSpec(memory_space=pltpu.VMEM)
     anywhere = pl.BlockSpec(memory_space=pl.ANY)
     ends = [] if side is None else out_shapes[side]
-    scratch = [pltpu.SemaphoreType.DMA] + [pltpu.VMEM(*made[n]) for n in inner]
+    scratch = [pltpu.SemaphoreType.DMA((2,))] + [pltpu.VMEM(*made[n]) for n in inner]
     if products:
         scratch += [pltpu.VMEM((2, 2, width, HALF), BF16), pltpu.VMEM((8, width), F32), pltpu.VMEM((2, 16, BLOCK), F32)]
     if ends:
@@ -293,23 +282,29 @@
         at.update(zip(inner, take(len(inner))))
         if products:
             w, vec, brow = take(3)
-            copies = load(sc, src, w, sem)
-            for c in copies:
-                c.start()
-            for c in copies:
-                c.wait()
-            vec[...] = w[0, 0, :, MISC:UP0].astype(F32).T[:8, :]
-            for t in range(2):
-                brow[t] = w[t, 1, :16, ROWSB:].astype(F32)
+            pending = [load(sc, src, w, sem, c) for c in range(2)]
+            for part in pending if "forward" in phases else pending[::-1]:
+                for c in part:
+                    c.start()
+
+            def ready(c):
+                for copy in pending[c]:
+                    copy.wait()
+                if c == 0 and pending[c]:
+                    vec[...] = w[0, 0, :, MISC:MLP].astype(F32).T[:8, :]
+                    for t in range(2):
+                        brow[t] = w[t, 1, :16, MISC:MLP].astype(F32)
+                pending[c] = []
+
+            ready(0 if "forward" in phases else 1)
         if "forward" in phases:
-            def step(n, carry):
-                forward_image(n, sc, at["x"], w, vec, brow, at["out"], at)
-                return carry
-            lax.fori_loop(0, total // IMG_PAD, step, 0)
+            for n in range(total // IMG_PAD):
+                forward_image(n, sc, at["x"], w, vec, brow, at["out"], at, ready)
         if "back" in phases:
             sums, bsum = at["sums"], at["bsum"]
             sums[...] = jnp.zeros_like(sums)
             bsum[...] = jnp.zeros_like(bsum)
+            ready(0)
 
             def back(n, carry):
                 backward_mlp(n, sc, at["u"], w, vec, at, at, sums, bsum)
@@ -326,7 +321,7 @@
             g = take(1)[0]
             t = jnp.where(sc[1] == 0, 1 - side, side)
             weight_grads(t, piece, at, at, g)
-            copies = store(sc, side, g, dst, sem)
+            copies = store(sc, side, g, dst, sem.at[0])
             for c in copies:
                 c.start()
             for c in copies:
@@ -452,9 +447,8 @@
     rows = jnp.concatenate([qv_bias[0, 0], gap, gap, gap, qv_bias[0, 1], gap, up_bias[0]]).reshape(-1, BLOCK)
     rows = jnp.pad(rows, ((0, piece - rows.shape[0]), (0, 0)))
     up, down = up_weight[0], down_weight[0].T
-    part0 = jnp.concatenate(
-        [q[0], q[1], q[2], k[2], k[0], k[1], v[0], v[1], v[2], o[2], o[0], o[1], misc, up[:, :CHUNK]], 1)
-    part1 = jnp.concatenate([up[:, CHUNK:], down, rows], 1)
+    part0 = jnp.concatenate([q[0], q[1], q[2], k[2], k[0], k[1], misc, up], 1)
+    part1 = jnp.concatenate([v[0], v[1], v[2], o[2], o[0], o[1], rows, down], 1)
 
     if direct:
         keep = jnp.where(sec == 0, part0, part1)
@@ -462,8 +456,9 @@
         got, halo = after(px(give), halo)
         start = [jnp.where(sec == 0, keep, got), jnp.where(sec == 0, got, keep)]
 
-        def load(l, sc, src, w, sem):
+        def load(l, sc, src, w, sem, c):
             copies = []
+            cols = slice(0, MLP) if c == 0 else slice(MLP, HALF)
             for side in range(2):
                 t = jnp.where(sc[1] == 0, side, 1 - side)
                 own = src[side * 8:side * 8 + 8]
@@ -472,8 +467,8 @@
                     near = pl.ds(pl.multiple_of((2 * z + sc[4]) * piece, 16), piece)
                     far = pl.ds(pl.multiple_of((2 * z + 1 - sc[4]) * piece, 16), piece)
                     for i, (h, r) in enumerate(((sc[2], near), (1 - sc[2], near), (sc[2], far), (1 - sc[2], far))):
-                        a = own[i].at[l] if kk == 0 else own[4 + i].at[kk - 1]
-                        copies.append(pltpu.make_async_copy(a, w.at[t, h, r, :], sem))
+                        a = own[i].at[l, :, cols] if kk == 0 else own[4 + i].at[kk - 1, :, cols]
+                        copies.append(pltpu.make_async_copy(a, w.at[t, h, r, cols], sem.at[c]))
             return copies
 
         def store(sc, side, g, dst, sem):
@@ -506,8 +501,8 @@
         sources = [firsts + rest + twins + [pt(a) for a in rest]]
         sources.append(columns[1:] + [px(columns[1]), py(columns[1]), pd(columns[1])])
     else:
-        def load(l, sc, src, w, sem):
-            return [pltpu.make_async_copy(src[0], w, sem)]
+        def load(l, sc, src, w, sem, c):
+            return [pltpu.make_async_copy(src[0], w, sem.at[c])] if c == 0 else []
 
         def store(sc, side, g, dst, sem):
             return [pltpu.make_async_copy(g, dst[0], sem)]
@@ -570,7 +565,7 @@
         final0 = jnp.where(sec == 0, mine, other)
         final1 = jnp.where(sec == 0, other, mine)
         final0, final1 = [jnp.concatenate([a[0], a[1]], 1) for a in (final0, final1)]
-        small = final1[:, ROWSB:]
+        small = final1[:, MISC:MLP]
     else:
         in_rows = placed(b0["keep"], in_got, tails(b0["keep"], in_got))
         in_twin = pt(in_rows)
@@ -589,11 +584,11 @@
     layer_outputs = ordered(low_rows, low_twin)
     input_grads = ordered(in_rows, in_twin).astype(F32)
 
-    def heads(*starts):
-        return [final0[:, s * HD:(s + 1) * HD] for s in starts]
+    def heads(a, *starts):
+        return [a[:, s * HD:(s + 1) * HD] for s in starts]
 
     small = small.reshape(-1)
-    qkv = jnp.concatenate(heads(0, 1, 2, 4, 5, 3, 6, 7, 8), 1).reshape(1, piece, 3, 3 * HD)
+    qkv = jnp.concatenate(heads(final0, 0, 1, 2, 4, 5, 3) + heads(final1, 0, 1, 2), 1).reshape(1, piece, 3, 3 * HD)
     return (
         layer_outputs,
         input_grads,
@@ -601,10 +596,10 @@
         final0[:, MISC + 2:MISC + 6].T[None],
         qkv,
         jnp.stack([small[:3 * HD], small[6 * HD:9 * HD]])[None],
-        jnp.concatenate(heads(10, 11, 9), 1).T[None],
-        jnp.concatenate([final0[:, UP0:], final1[:, :DOWN]], 1)[None],
+        jnp.concatenate(heads(final1, 4, 5, 3), 1).T[None],
+        final0[:, MLP:][None],
         small[ATT:ATT + ff // 2][None],
-        final1[:, DOWN:ROWSB].T[None],
+        final1[:, MLP:].T[None],
     )
 
 

time: 209 us -> 207 us (level)
  Pallas kernels: 68 us -> 61.8 us
  starting transfers between devices: 61 us -> 65.8 us
    pallas_call x5, Pallas kernels: 68 us -> 61.8 us  [layer_call(): pl.pallas_call(body, out_shape=[jax.ShapeDtypeStruct(*o) for o in outs],...]
    ppermute x12, waiting for transfers between devices: 21.9 us -> 18.4 us  [pz_to(): return lax.ppermute(a, 'dp', [(i, i ^ 2 * kk) for i in range(n_dp)])]
    ppermute x6, starting transfers between devices: 6.12 us -> 8.39 us  [pd(): lax.ppermute(a, ('section', 'dp'), [(i, (i + n_dp) % (2 * n_dp) ^ 1) for...]
    ppermute x6, waiting for transfers between devices: 9.62 us -> 11.8 us  [py(): return lax.ppermute(a, 'dp', [(i, i ^ 1) for i in range(n_dp)])]
  transfers between devices with their start and end apart: 53 -> 53, of which waited for: 23 -> 23; matrix products, arithmetic and copies ran while one was open for 7% -> 7% of each run, Pallas kernels for 21% -> 19%
where the time goes in v8:
time: 207 us; the launch traced here: 206 us
  starting transfers between devices  65.8 us (32%)
  Pallas kernels  61.8 us (30%)
  waiting for transfers between devices  48.6 us (23%)
  other arithmetic  11 us (5%)
  local copies, waits for them, and re-layouts  10.6 us (5%)
  matrix products  6 us (3%)
  between operations  2.35 us (1%)
    pallas_call x5, Pallas kernels, layer_call(): pl.pallas_call(body, out_shape=[jax.ShapeDtypeStruct(*o) for o in outs],...  61.8 us
    ppermute x12, starting transfers between devices, pz_to(): return lax.ppermute(a, 'dp', [(i, i ^ 2 * kk) for i in range(n_dp)])  23.9 us
    ppermute x12, waiting for transfers between devices, pz_to(): return lax.ppermute(a, 'dp', [(i, i ^ 2 * kk) for i in range(n_dp)])  18.4 us
    ppermute x10, starting transfers between devices, px(): return lax.ppermute(a, 'section', [(0, 1), (1, 0)])  15.1 us
    ppermute x6, waiting for transfers between devices, py(): return lax.ppermute(a, 'dp', [(i, i ^ 1) for i in range(n_dp)])  11.8 us
    ppermute x6, starting transfers between devices, py(): return lax.ppermute(a, 'dp', [(i, i ^ 1) for i in range(n_dp)])  10.9 us
    ppermute x6, waiting for transfers between devices, pd(): lax.ppermute(a, ('section', 'dp'), [(i, (i + n_dp) % (2 * n_dp) ^ 1) for...  9.67 us
    ppermute x6, starting transfers between devices, pd(): lax.ppermute(a, ('section', 'dp'), [(i, (i + n_dp) % (2 * n_dp) ^ 1) for...  8.39 us
  transfers between devices with their start and end apart: 53, of which 23 were waited for; matrix products, arithmetic and copies ran while one was open for 7% of the time, Pallas kernels for 19%

profile of v8, /device:TPU:0, one launch (start us, length us, event | category | flops | bytes accessed | tf_op | source)
XLA Modules:
  0.0 206.1 jit_solution(10677512993322759536)
XLA Ops:
  0.7 1.3 constant_dynamic-slice_fusion
  3.5 3.0 %collective-permute-start = (bf16[48,1280]{1,0:T(8,128)(2,1)S(1)}, bf16[48,1280]{1,0:T(8,128)(2,1)S(1)}, u32[]{:S(2)}, u32[]{:S(2)}) collective-permute-start(bf16[48,1280]{1,0:T(8,128)(2,1)S(1)} %broadcast_select_fusion.3), channel_id=1, source_target_pairs={{0,16},{16,0},{1,17},{17,1},{2,18},{18,2},{3,19},{19,3},{4,20},{20... | collective-permute-start | bytes 368648 | tf_op jit(solution)/shard_map/ppermute | solution.py:367
  6.5 3.9 %collective-permute-done = bf16[48,1280]{1,0:T(8,128)(2,1)S(1)} collective-permute-done((bf16[48,1280]{1,0:T(8,128)(2,1)S(1)}, bf16[48,1280]{1,0:T(8,128)(2,1)S(1)}, u32[]{:S(2)}, u32[]{:S(2)}) %collective-permute-start) | collective-permute-done | bytes 122912 | tf_op jit(solution)/shard_map/ppermute | solution.py:367
  10.5 1.2 collective-permute-start.2
  11.7 2.6 %collective-permute-start.3 = (bf16[48,1280]{1,0:T(8,128)(2,1)S(1)}, bf16[48,1280]{1,0:T(8,128)(2,1)S(1)}, u32[]{:S(2)}, u32[]{:S(2)}) collective-permute-start(bf16[48,1280]{1,0:T(8,128)(2,1)S(1)} %get-tuple-element.253), channel_id=1, source_target_pairs={{0,8},{2,10},{4,12},{6,14},{8,0},{10,2},{12,4},{14,6},{1,9},{3,11}... | collective-permute-start | bytes 368648 | tf_op jit(solution)/shard_map/ppermute | solution.py:389
  15.0 1.8 collective-permute-start.5
  16.8 1.7 collective-permute-start.6
  18.6 3.1 %collective-permute-start.7 = (bf16[2,48,1280]{2,1,0:T(8,128)(2,1)S(1)}, bf16[2,48,1280]{2,1,0:T(8,128)(2,1)S(1)}, u32[]{:S(2)}, u32[]{:S(2)}) collective-permute-start(bf16[2,48,1280]{2,1,0:T(8,128)(2,1)S(1)} %pad_maximum_fusion.8.refs_2_.refs_3_.refs_13_), channel_id=1, source_target_pairs={{0,18},{2,16},{4,22},{6,20},{8,26},{10,24},{12,30},{14,28},{16,2},... | collective-permute-start | bytes 737288 | tf_op jit(solution)/shard_map/ppermute | solution.py:373
  21.7 2.4 %collective-permute-done.3 = bf16[48,1280]{1,0:T(8,128)(2,1)S(1)} collective-permute-done((bf16[48,1280]{1,0:T(8,128)(2,1)S(1)}, bf16[48,1280]{1,0:T(8,128)(2,1)S(1)}, u32[]{:S(2)}, u32[]{:S(2)}) %collective-permute-start.3) | collective-permute-done | bytes 122912 | tf_op jit(solution)/shard_map/ppermute | solution.py:389
  24.1 3.1 %collective-permute-start.8 = (bf16[48,1280]{1,0:T(8,128)(2,1)S(1)}, bf16[48,1280]{1,0:T(8,128)(2,1)S(1)}, u32[]{:S(2)}, u32[]{:S(2)}) collective-permute-start(bf16[48,1280]{1,0:T(8,128)(2,1)S(1)} %get-tuple-element.111), channel_id=1, source_target_pairs={{0,4},{2,6},{4,0},{6,2},{8,12},{10,14},{12,8},{14,10},{1,5},{3,7},... | collective-permute-start | bytes 368648 | tf_op jit(solution)/shard_map/ppermute | solution.py:389
  27.3 1.9 collective-permute-done.6.refs_4_.refs_5_.refs_15_
  29.1 0.7 collective-permute-done.7.refs_5_.refs_6_.refs_16_
  29.9 1.5 collective-permute-start.10
  31.4 2.2 %collective-permute-start.9 = (bf16[2,48,1280]{2,1,0:T(8,128)(2,1)S(1)}, bf16[2,48,1280]{2,1,0:T(8,128)(2,1)S(1)}, u32[]{:S(2)}, u32[]{:S(2)}) collective-permute-start(bf16[2,48,1280]{2,1,0:T(8,128)(2,1)S(1)} %pad_maximum_fusion.9), channel_id=1, source_target_pairs={{0,8},{2,10},{4,12},{6,14},{8,0},{10,2},{12,4},{14,6},{1,9},{3,11}... | collective-permute-start | bytes 737288 | tf_op jit(solution)/shard_map/ppermute | solution.py:389
  33.6 2.4 %collective-permute-start.11 = (bf16[3,48,1280]{2,1,0:T(8,128)(2,1)S(1)}, bf16[3,48,1280]{2,1,0:T(8,128)(2,1)}, u32[]{:S(2)}, u32[]{:S(2)}) collective-permute-start(bf16[3,48,1280]{2,1,0:T(8,128)(2,1)S(1)} %pad_maximum_fusion.3.refs_6_.refs_17_), channel_id=1, source_target_pairs={{0,2},{2,0},{4,6},{6,4},{8,10},{10,8},{12,14},{14,12},{1,3},{3,1},... | collective-permute-start | bytes 1105928 | tf_op jit(solution)/shard_map/ppermute | solution.py:370
  36.0 0.9 collective-permute-start.12
  37.0 7.6 %collective-permute-done.9 = bf16[2,48,1280]{2,1,0:T(8,128)(2,1)S(1)} collective-permute-done((bf16[2,48,1280]{2,1,0:T(8,128)(2,1)S(1)}, bf16[2,48,1280]{2,1,0:T(8,128)(2,1)S(1)}, u32[]{:S(2)}, u32[]{:S(2)}) %collective-permute-start.9) | collective-permute-done | bytes 245792 | tf_op jit(solution)/shard_map/ppermute | solution.py:389
  47.1 4.5 %collective-permute-done.11.refs_8_.refs_19_ = bf16[3,48,1280]{2,1,0:T(8,128)(2,1)} collective-permute-done((bf16[3,48,1280]{2,1,0:T(8,128)(2,1)S(1)}, bf16[3,48,1280]{2,1,0:T(8,128)(2,1)}, u32[]{:S(2)}, u32[]{:S(2)}) %collective-permute-start.11) | collective-permute-done | bytes 368672 | tf_op jit(solution)/shard_map/ppermute | solution.py:370
  53.0 1.3 convolution_convert_fusion.5.refs_1_
  54.2 1.0 collective-permute-done.16.refs_13_.refs_14_.refs_24_
  55.2 1.5 collective-permute-start.21
  56.7 1.7 collective-permute-start.22
  59.5 0.8 copy-done.15
  60.2 10.7 %shard_map.186 = (bf16[416,384]{1,0:T(8,128)(2,1)}, f32[416,384]{1,0:T(8,128)}, f32[416,128]{1,0:T(8,128)}, bf16[416,384]{1,0:T(8,128)(2,1)}, bf16[2,416,640]{2,...) custom-call(s32[5]{0:T(128)} %stack.107.refs_0_, ...), custom_call_target="tpu_custom_call" | custom-call | flops 10000000000 | bytes 8388608 | tf_op jit(solution)/shard_map/pallas_call | solution.py:334
  71.0 3.3 %collective-permute-done.22.refs_9_ = bf16[3,48,1280]{2,1,0:T(8,128)(2,1)S(1)} collective-permute-done((bf16[3,48,1280]{2,1,0:T(8,128)(2,1)S(1)}, bf16[3,48,1280]{2,1,0:T(8,128)(2,1)S(1)}, u32[]{:S(2)}, u32[]{:S(2)}) %collective-permute-start.22) | collective-permute-done | bytes 368672 | tf_op jit(solution)/shard_map/ppermute | solution.py:370
  74.2 0.7 collective-permute-done.23.refs_10_
  76.0 1.3 convolution_convert_fusion.4.refs_2_
  78.5 0.8 copy-done.22
  79.2 22.8 %shard_map.187 = (bf16[416,384]{1,0:T(8,128)(2,1)}, bf16[2,416,256]{2,1,0:T(8,128)(2,1)}, bf16[416,384]{1,0:T(8,128)(2,1)}, bf16[416,1536]{1,0:T(8,128)(2,1)}, b...) custom-call(s32[5]{0:T(128)} %stack.107.refs_0_, ...), custom_call_target="tpu_custom_call" | custom-call | flops 30000001024 | bytes 8388608 | tf_op jit(solution)/shard_map/pallas_call | solution.py:334
  102.1 1.8 copy.42
  104.4 1.5 collective-permute-start.28
  106.8 5.1 %shard_map.188 = (bf16[2,4,48,640]{3,2,1,0:T(8,128)(2,1)}, bf16[2,4,48,640]{3,2,1,0:T(8,128)(2,1)}, bf16[2,4,48,640]{3,2,1,0:T(8,128)(2,1)}, bf16[2,4,48,640]{3,2,1,0:T(8,128)(2,1)}) custom-call(s32[5]{0:T(128)} %stack.107.refs_0_, bf16[416,384]{1,0:T(8,128)(2,1)} %get-tuple-element.127.refs_1_, bf16[2,416,256]{2,1,0:T(8,128)(2,1)} %get-tuple-element.128.refs_2_, ...), custom_call_target="tpu_custom_call" | custom-call | flops 10000000000 | bytes 8388608 | tf_op jit(solution)/shard_map/pallas_call | solution.py:334
  111.9 1.9 fusion.8
  114.6 0.9 collective-permute-start.30
  115.5 1.9 collective-permute-start.31
  118.0 1.1 collective-permute-start.33
  119.1 18.1 %shard_map.189 = (bf16[416,384]{1,0:T(8,128)(2,1)}, bf16[416,384]{1,0:T(8,128)(2,1)}, bf16[416,384]{1,0:T(8,128)(2,1)}, bf16[416,1536]{1,0:T(8,128)(2,1)}, f32[8...) custom-call(s32[5]{0:T(128)} %stack.107.refs_0_, ...), custom_call_target="tpu_custom_call" | custom-call | flops 20000000000 | bytes 8388608 | tf_op jit(solution)/shard_map/pallas_call | solution.py:334
  137.3 3.4 %collective-permute-done.33 = bf16[2,4,48,640]{3,2,0,1:T(8,128)(2,1)S(1)} collective-permute-done((bf16[2,4,48,640]{3,2,0,1:T(8,128)(2,1)S(1)}, bf16[2,4,48,640]{3,2,0,1:T(8,128)(2,1)S(1)}, u32[]{:S(2)}, u32[]{:S(2)}) %collective-permute-start.33) | collective-permute-done | bytes 491552 | tf_op jit(solution)/shard_map/ppermute | solution.py:373
  140.7 1.9 collective-permute-start.34
  143.1 0.8 collective-permute-start.36
  145.2 5.1 %shard_map.190 = (bf16[2,4,48,640]{3,2,1,0:T(8,128)(2,1)}, bf16[2,4,48,640]{3,2,1,0:T(8,128)(2,1)}, bf16[2,4,48,640]{3,2,1,0:T(8,128)(2,1)}, bf16[2,4,48,640]{3,2,1,0:T(8,128)(2,1)}) custom-call(s32[5]{0:T(128)} %stack.107.refs_0_, bf16[416,384]{1,0:T(8,128)(2,1)} %get-tuple-element.147.refs_4_.refs_1_, ...), custom_call_target="tpu_custom_call" | custom-call | flops 10000000000 | bytes 8388608 | tf_op jit(solution)/shard_map/pallas_call | solution.py:334
  150.3 1.9 fusion.5
  154.0 1.6 collective-permute-start.50
  155.7 1.3 collective-permute-start.42
  157.0 0.9 collective-permute-start.43
  157.9 1.6 collective-permute-start.44
  159.5 0.9 collective-permute-start.37
  160.6 1.0 fusion.11
  161.6 2.2 %collective-permute-done.42 = bf16[1,4,48,640]{3,2,1,0:T(8,128)(2,1)S(1)} collective-permute-done((bf16[1,4,48,640]{3,2,1,0:T(8,128)(2,1)S(1)}, bf16[1,4,48,640]{3,2,1,0:T(8,128)(2,1)S(1)}, u32[]{:S(2)}, u32[]{:S(2)}) %collective-permute-start.42) | collective-permute-done | bytes 245792 | tf_op jit(solution)/shard_map/ppermute | solution.py:370
  163.8 1.8 collective-permute-start.39
  165.9 0.8 collective-permute-start.40
  166.7 4.8 %collective-permute-done.44 = bf16[1,4,48,640]{3,2,1,0:T(8,128)(2,1)S(1)} collective-permute-done((bf16[1,4,48,640]{3,2,1,0:T(8,128)(2,1)S(1)}, bf16[1,4,48,640]{3,2,1,0:T(8,128)(2,1)S(1)}, u32[]{:S(2)}, u32[]{:S(2)}) %collective-permute-start.44) | collective-permute-done | bytes 245792 | tf_op jit(solution)/shard_map/ppermute | solution.py:373
  171.4 1.4 collective-permute-start.41
  173.1 1.5 collective-permute-start.45
  175.0 3.0 %collective-permute-done.45 = bf16[1,2,48,640]{3,2,1,0:T(8,128)(2,1)S(1)} collective-permute-done((bf16[1,2,48,640]{3,2,1,0:T(8,128)(2,1)S(1)}, bf16[1,2,48,640]{3,2,1,0:T(8,128)(2,1)S(1)}, u32[]{:S(2)}, u32[]{:S(2)}) %collective-permute-start.45) | collective-permute-done | bytes 122912 | tf_op jit(solution)/shard_map/ppermute | solution.py:389
  178.1 3.1 %collective-permute-start.46 = (bf16[1,48,640]{2,1,0:T(8,128)(2,1)S(1)}, bf16[1,48,640]{2,1,0:T(8,128)(2,1)S(1)}, u32[]{:S(2)}, u32[]{:S(2)}) collective-permute-start(bf16[1,48,640]{2,1,0:T(8,128)(2,1)S(1)} %fusion.33), channel_id=1, source_target_pairs={{0,8},{2,10},{4,12},{6,14},{8,0},{10,2},{12,4},{14,6},{1,9},{3,11}... | collective-permute-start | bytes 184328 | tf_op jit(solution)/shard_map/ppermute | solution.py:389
  181.2 2.4 %collective-permute-done.46 = bf16[1,48,640]{2,1,0:T(8,128)(2,1)S(1)} collective-permute-done((bf16[1,48,640]{2,1,0:T(8,128)(2,1)S(1)}, bf16[1,48,640]{2,1,0:T(8,128)(2,1)S(1)}, u32[]{:S(2)}, u32[]{:S(2)}) %collective-permute-start.46) | collective-permute-done | bytes 61472 | tf_op jit(solution)/shard_map/ppermute | solution.py:389
  183.7 3.4 %collective-permute-start.51 = (bf16[2,48,640]{2,1,0:T(8,128)(2,1)S(1)}, bf16[2,48,640]{2,1,0:T(8,128)(2,1)S(1)}, u32[]{:S(2)}, u32[]{:S(2)}) collective-permute-start(bf16[2,48,640]{2,1,0:T(8,128)(2,1)S(1)} %fusion.28), channel_id=1, source_target_pairs={{0,8},{2,10},{4,12},{6,14},{8,0},{10,2},{12,4},{14,6},{1,9},{3,11}... | collective-permute-start | bytes 368648 | tf_op jit(solution)/shard_map/ppermute | solution.py:389
  188.1 3.7 %collective-permute-start.49 = (bf16[1,48,640]{2,1,0:T(8,128)(2,1)S(1)}, bf16[1,48,640]{2,1,0:T(8,128)(2,1)S(1)}, u32[]{:S(2)}, u32[]{:S(2)}) collective-permute-start(bf16[1,48,640]{2,1,0:T(8,128)(2,1)S(1)} %get-tuple-element.264), channel_id=1, source_target_pairs={{0,12},{2,14},{4,8},{6,10},{8,4},{10,6},{12,0},{14,2},{1,13},{3,15... | collective-permute-start | bytes 184328 | tf_op jit(solution)/shard_map/ppermute | solution.py:389
  191.9 1.2 collective-permute-done.47
  193.1 1.6 collective-permute-done.49
  194.8 2.7 %collective-permute-start.52 = (bf16[2,48,640]{2,1,0:T(8,128)(2,1)S(1)}, bf16[2,48,640]{2,1,0:T(8,128)(2,1)S(1)}, u32[]{:S(2)}, u32[]{:S(2)}) collective-permute-start(bf16[2,48,640]{2,1,0:T(8,128)(2,1)S(1)} %select_convert_fusion), channel_id=1, source_target_pairs={{0,16},{16,0},{1,17},{17,1},{2,18},{18,2},{3,19},{19,3},{4,20},{20... | collective-permute-start | bytes 368648 | tf_op jit(solution)/shard_map/ppermute | solution.py:367
  197.5 1.2 fusion.13
  198.8 1.6 collective-permute-done.52
  (211 shorter events, 22.8 us)
Async XLA Ops:
  2.1 8.4 %collective-permute-start.1 = (bf16[2,208,384]{2,1,0:T(8,128)(2,1)S(1)}, bf16[2,208,384]{2,1,0:T(8,128)(2,1)S(1)}, u32[]{:S(2)}, u32[]{:S(2)}) collective-permute-start(bf16[2,208,384]{2,1,0:T(8,128)(2,1)S(1)} %pad_maximum_fusion.5), channel_id=1, source_target_pairs={{3,1},{5,3},{7,5},{9,7},{11,9},{13,11},{15,13},{19,17},{21,19},{23... | collective-permute-start | bytes 958472 | tf_op jit(solution)/shard_map/ppermute | solution.py:440
  3.5 41.2 %copy-start.30 = (s32[2]{0:T(128)S(1)}, s32[2]{0:T(128)}, u32[]{:S(2)}) copy-start(s32[2]{0:T(128)} %param.12) | copy-start | bytes 28
  3.5 7.0 %collective-permute-start = (bf16[48,1280]{1,0:T(8,128)(2,1)S(1)}, bf16[48,1280]{1,0:T(8,128)(2,1)S(1)}, u32[]{:S(2)}, u32[]{:S(2)}) collective-permute-start(bf16[48,1280]{1,0:T(8,128)(2,1)S(1)} %broadcast_select_fusion.3), channel_id=1, source_target_pairs={{0,16},{16,0},{1,17},{17,1},{2,18},{18,2},{3,19},{19,3},{4,20},{20... | collective-permute-start | bytes 368648 | tf_op jit(solution)/shard_map/ppermute | solution.py:367
  10.5 8.2 %collective-permute-start.2 = (bf16[48,1280]{1,0:T(8,128)(2,1)S(1)}, bf16[48,1280]{1,0:T(8,128)(2,1)S(1)}, u32[]{:S(2)}, u32[]{:S(2)}) collective-permute-start(bf16[48,1280]{1,0:T(8,128)(2,1)S(1)} %get-tuple-element.253), channel_id=1, source_target_pairs={{0,4},{2,6},{4,0},{6,2},{8,12},{10,14},{12,8},{14,10},{1,5},{3,7},... | collective-permute-start | bytes 368648 | tf_op jit(solution)/shard_map/ppermute | solution.py:389
  11.7 12.4 %collective-permute-start.3 = (bf16[48,1280]{1,0:T(8,128)(2,1)S(1)}, bf16[48,1280]{1,0:T(8,128)(2,1)S(1)}, u32[]{:S(2)}, u32[]{:S(2)}) collective-permute-start(bf16[48,1280]{1,0:T(8,128)(2,1)S(1)} %get-tuple-element.253), channel_id=1, source_target_pairs={{0,8},{2,10},{4,12},{6,14},{8,0},{10,2},{12,4},{14,6},{1,9},{3,11}... | collective-permute-start | bytes 368648 | tf_op jit(solution)/shard_map/ppermute | solution.py:389
  14.3 9.8 %collective-permute-start.4 = (bf16[48,1280]{1,0:T(8,128)(2,1)S(1)}, bf16[48,1280]{1,0:T(8,128)(2,1)S(1)}, u32[]{:S(2)}, u32[]{:S(2)}) collective-permute-start(bf16[48,1280]{1,0:T(8,128)(2,1)S(1)} %get-tuple-element.253), channel_id=1, source_target_pairs={{0,12},{2,14},{4,8},{6,10},{8,4},{10,6},{12,0},{14,2},{1,13},{3,15... | collective-permute-start | bytes 368648 | tf_op jit(solution)/shard_map/ppermute | solution.py:389
  15.0 37.8 %copy-start.2 = (bf16[2,48,1280]{2,1,0:T(8,128)(2,1)}, bf16[2,48,1280]{2,1,0:T(8,128)(2,1)S(1)}, u32[]{:S(2)}) copy-start(bf16[2,48,1280]{2,1,0:T(8,128)(2,1)S(1)} %pad_maximum_fusion.8.refs_2_.refs_3_.refs_13_) | copy-start | bytes 737284
  15.0 12.3 %collective-permute-start.5 = (bf16[2,48,1280]{2,1,0:T(8,128)(2,1)S(1)}, bf16[2,48,1280]{2,1,0:T(8,128)(2,1)S(1)}, u32[]{:S(2)}, u32[]{:S(2)}) collective-permute-start(bf16[2,48,1280]{2,1,0:T(8,128)(2,1)S(1)} %pad_maximum_fusion.8.refs_2_.refs_3_.refs_13_), channel_id=1, source_target_pairs={{0,16},{16,0},{1,17},{17,1},{2,18},{18,2},{3,19},{19,3},{4,20},{20... | collective-permute-start | bytes 737288 | tf_op jit(solution)/shard_map/ppermute | solution.py:367
  16.8 12.4 %collective-permute-start.6 = (bf16[2,48,1280]{2,1,0:T(8,128)(2,1)S(1)}, bf16[2,48,1280]{2,1,0:T(8,128)(2,1)S(1)}, u32[]{:S(2)}, u32[]{:S(2)}) collective-permute-start(bf16[2,48,1280]{2,1,0:T(8,128)(2,1)S(1)} %pad_maximum_fusion.8.refs_2_.refs_3_.refs_13_), channel_id=1, source_target_pairs={{0,2},{2,0},{4,6},{6,4},{8,10},{10,8},{12,14},{14,12},{1,3},{3,1},... | collective-permute-start | bytes 737288 | tf_op jit(solution)/shard_map/ppermute | solution.py:370
  18.6 11.2 %collective-permute-start.7 = (bf16[2,48,1280]{2,1,0:T(8,128)(2,1)S(1)}, bf16[2,48,1280]{2,1,0:T(8,128)(2,1)S(1)}, u32[]{:S(2)}, u32[]{:S(2)}) collective-permute-start(bf16[2,48,1280]{2,1,0:T(8,128)(2,1)S(1)} %pad_maximum_fusion.8.refs_2_.refs_3_.refs_13_), channel_id=1, source_target_pairs={{0,18},{2,16},{4,22},{6,20},{8,26},{10,24},{12,30},{14,28},{16,2},... | collective-permute-start | bytes 737288 | tf_op jit(solution)/shard_map/ppermute | solution.py:373
  24.1 28.6 %copy-start = (bf16[3,48,1280]{2,1,0:T(8,128)(2,1)}, bf16[3,48,1280]{2,1,0:T(8,128)(2,1)S(1)}, u32[]{:S(2)}) copy-start(bf16[3,48,1280]{2,1,0:T(8,128)(2,1)S(1)} %pad_maximum_fusion.3.refs_6_.refs_17_) | copy-start | bytes 1105924
  24.1 7.2 %collective-permute-start.8 = (bf16[48,1280]{1,0:T(8,128)(2,1)S(1)}, bf16[48,1280]{1,0:T(8,128)(2,1)S(1)}, u32[]{:S(2)}, u32[]{:S(2)}) collective-permute-start(bf16[48,1280]{1,0:T(8,128)(2,1)S(1)} %get-tuple-element.111), channel_id=1, source_target_pairs={{0,4},{2,6},{4,0},{6,2},{8,12},{10,14},{12,8},{14,10},{1,5},{3,7},... | collective-permute-start | bytes 368648 | tf_op jit(solution)/shard_map/ppermute | solution.py:389
  27.3 25.5 %copy-start.24 = (bf16[2,48,1280]{2,1,0:T(8,128)(2,1)}, bf16[2,48,1280]{2,1,0:T(8,128)(2,1)S(1)}, u32[]{:S(2)}) copy-start(bf16[2,48,1280]{2,1,0:T(8,128)(2,1)S(1)} %collective-permute-done.5.refs_3_.refs_4_.refs_14_) | copy-start | bytes 737284
  29.1 23.6 %copy-start.25 = (bf16[2,48,1280]{2,1,0:T(8,128)(2,1)}, bf16[2,48,1280]{2,1,0:T(8,128)(2,1)S(1)}, u32[]{:S(2)}) copy-start(bf16[2,48,1280]{2,1,0:T(8,128)(2,1)S(1)} %collective-permute-done.6.refs_4_.refs_5_.refs_15_) | copy-start | bytes 737284
  29.9 16.6 %collective-permute-start.10 = (bf16[3,48,1280]{2,1,0:T(8,128)(2,1)S(1)}, bf16[3,48,1280]{2,1,0:T(8,128)(2,1)S(1)}, u32[]{:S(2)}, u32[]{:S(2)}) collective-permute-start(bf16[3,48,1280]{2,1,0:T(8,128)(2,1)S(1)} %pad_maximum_fusion.3.refs_6_.refs_17_), channel_id=1, source_target_pairs={{0,16},{16,0},{1,17},{17,1},{2,18},{18,2},{3,19},{19,3},{4,20},{20... | collective-permute-start | bytes 1105928 | tf_op jit(solution)/shard_map/ppermute | solution.py:367
  31.4 13.2 %collective-permute-start.9 = (bf16[2,48,1280]{2,1,0:T(8,128)(2,1)S(1)}, bf16[2,48,1280]{2,1,0:T(8,128)(2,1)S(1)}, u32[]{:S(2)}, u32[]{:S(2)}) collective-permute-start(bf16[2,48,1280]{2,1,0:T(8,128)(2,1)S(1)} %pad_maximum_fusion.9), channel_id=1, source_target_pairs={{0,8},{2,10},{4,12},{6,14},{8,0},{10,2},{12,4},{14,6},{1,9},{3,11}... | collective-permute-start | bytes 737288 | tf_op jit(solution)/shard_map/ppermute | solution.py:389
  33.6 18.0 %collective-permute-start.11 = (bf16[3,48,1280]{2,1,0:T(8,128)(2,1)S(1)}, bf16[3,48,1280]{2,1,0:T(8,128)(2,1)}, u32[]{:S(2)}, u32[]{:S(2)}) collective-permute-start(bf16[3,48,1280]{2,1,0:T(8,128)(2,1)S(1)} %pad_maximum_fusion.3.refs_6_.refs_17_), channel_id=1, source_target_pairs={{0,2},{2,0},{4,6},{6,4},{8,10},{10,8},{12,14},{14,12},{1,3},{3,1},... | collective-permute-start | bytes 1105928 | tf_op jit(solution)/shard_map/ppermute | solution.py:370
  36.0 15.6 %collective-permute-start.12 = (bf16[3,48,1280]{2,1,0:T(8,128)(2,1)S(1)}, bf16[3,48,1280]{2,1,0:T(8,128)(2,1)}, u32[]{:S(2)}, u32[]{:S(2)}) collective-permute-start(bf16[3,48,1280]{2,1,0:T(8,128)(2,1)S(1)} %pad_maximum_fusion.3.refs_6_.refs_17_), channel_id=1, source_target_pairs={{0,18},{2,16},{4,22},{6,20},{8,26},{10,24},{12,30},{14,28},{16,2},... | collective-permute-start | bytes 1105928 | tf_op jit(solution)/shard_map/ppermute | solution.py:373
  36.9 15.2 %collective-permute-start.13 = (bf16[2,48,1280]{2,1,0:T(8,128)(2,1)S(1)}, bf16[2,48,1280]{2,1,0:T(8,128)(2,1)}, u32[]{:S(2)}, u32[]{:S(2)}) collective-permute-start(bf16[2,48,1280]{2,1,0:T(8,128)(2,1)S(1)} %pad_maximum_fusion.8.refs_2_.refs_3_.refs_13_), channel_id=1, source_target_pairs={{0,1},{1,0},{2,3},{3,2},{4,5},{5,4},{6,7},{7,6},{8,9},{9,8},{10,11... | collective-permute-start | bytes 737288 | tf_op jit(solution)/shard_map/ppermute | solution.py:364
  44.6 7.5 %collective-permute-start.14 = (bf16[2,48,1280]{2,1,0:T(8,128)(2,1)S(1)}, bf16[2,48,1280]{2,1,0:T(8,128)(2,1)}, u32[]{:S(2)}, u32[]{:S(2)}) collective-permute-start(bf16[2,48,1280]{2,1,0:T(8,128)(2,1)S(1)} %collective-permute-done.5.refs_3_.refs_4_.refs_14_), channel_id=1, source_target_pairs={{0,1},{1,0},{2,3},{3,2},{4,5},{5,4},{6,7},{7,6},{8,9},{9,8},{10,11... | collective-permute-start | bytes 737288 | tf_op jit(solution)/shard_map/ppermute | solution.py:364
  46.5 6.3 %copy-start.11 = (bf16[3,48,1280]{2,1,0:T(8,128)(2,1)}, bf16[3,48,1280]{2,1,0:T(8,128)(2,1)S(1)}, u32[]{:S(2)}) copy-start(bf16[3,48,1280]{2,1,0:T(8,128)(2,1)S(1)} %collective-permute-done.10.refs_7_.refs_18_) | copy-start | bytes 1105924
  46.5 6.3 %collective-permute-start.15 = (bf16[2,48,1280]{2,1,0:T(8,128)(2,1)S(1)}, bf16[2,48,1280]{2,1,0:T(8,128)(2,1)S(1)}, u32[]{:S(2)}, u32[]{:S(2)}) collective-permute-start(bf16[2,48,1280]{2,1,0:T(8,128)(2,1)S(1)} %collective-permute-done.6.refs_4_.refs_5_.refs_15_), channel_id=1, source_target_pairs={{0,1},{1,0},{2,3},{3,2},{4,5},{5,4},{6,7},{7,6},{8,9},{9,8},{10,11... | collective-permute-start | bytes 737288 | tf_op jit(solution)/shard_map/ppermute | solution.py:364
  47.1 27.9 %copy-start.1 = (bf16[3,48,1280]{2,1,0:T(8,128)(2,1)}, bf16[3,48,1280]{2,1,0:T(8,128)(2,1)S(1)}, u32[]{:S(2)}) copy-start(bf16[3,48,1280]{2,1,0:T(8,128)(2,1)S(1)} %pad_maximum_fusion.4.refs_7_) | copy-start | bytes 1105924
  47.1 5.7 %copy-start.27 = (bf16[2,48,1280]{2,1,0:T(8,128)(2,1)S(1)}, bf16[2,48,1280]{2,1,0:T(8,128)(2,1)}, u32[]{:S(2)}) copy-start(bf16[2,48,1280]{2,1,0:T(8,128)(2,1)} %copy-done.26) | copy-start | bytes 737284
  51.6 5.1 %collective-permute-start.17 = (bf16[3,48,1280]{2,1,0:T(8,128)(2,1)S(1)}, bf16[3,48,1280]{2,1,0:T(8,128)(2,1)S(1)}, u32[]{:S(2)}, u32[]{:S(2)}) collective-permute-start(bf16[3,48,1280]{2,1,0:T(8,128)(2,1)S(1)} %pad_maximum_fusion.3.refs_6_.refs_17_), channel_id=1, source_target_pairs={{0,1},{1,0},{2,3},{3,2},{4,5},{5,4},{6,7},{7,6},{8,9},{9,8},{10,11... | collective-permute-start | bytes 1105928 | tf_op jit(solution)/shard_map/ppermute | solution.py:364
  51.6 6.9 %collective-permute-start.18 = (bf16[3,48,1280]{2,1,0:T(8,128)(2,1)S(1)}, bf16[3,48,1280]{2,1,0:T(8,128)(2,1)S(1)}, u32[]{:S(2)}, u32[]{:S(2)}) collective-permute-start(bf16[3,48,1280]{2,1,0:T(8,128)(2,1)S(1)} %collective-permute-done.10.refs_7_.refs_18_), channel_id=1, source_target_pairs={{0,1},{1,0},{2,3},{3,2},{4,5},{5,4},{6,7},{7,6},{8,9},{9,8},{10,11... | collective-permute-start | bytes 1105928 | tf_op jit(solution)/shard_map/ppermute | solution.py:364
  52.1 6.6 %collective-permute-start.19 = (bf16[3,48,1280]{2,1,0:T(8,128)(2,1)}, bf16[3,48,1280]{2,1,0:T(8,128)(2,1)S(1)}, u32[]{:S(2)}, u32[]{:S(2)}) collective-permute-start(bf16[3,48,1280]{2,1,0:T(8,128)(2,1)} %collective-permute-done.11.refs_8_.refs_19_), channel_id=1, source_target_pairs={{0,1},{1,0},{2,3},{3,2},{4,5},{5,4},{6,7},{7,6},{8,9},{9,8},{10,11... | collective-permute-start | bytes 1105928 | tf_op jit(solution)/shard_map/ppermute | solution.py:364
  52.1 6.6 %collective-permute-start.20 = (bf16[3,48,1280]{2,1,0:T(8,128)(2,1)}, bf16[3,48,1280]{2,1,0:T(8,128)(2,1)S(1)}, u32[]{:S(2)}, u32[]{:S(2)}) collective-permute-start(bf16[3,48,1280]{2,1,0:T(8,128)(2,1)} %collective-permute-done.12.refs_9_.refs_20_), channel_id=1, source_target_pairs={{0,1},{1,0},{2,3},{3,2},{4,5},{5,4},{6,7},{7,6},{8,9},{9,8},{10,11... | collective-permute-start | bytes 1105928 | tf_op jit(solution)/shard_map/ppermute | solution.py:364
  52.8 5.9 %copy-start.28 = (bf16[2,48,1280]{2,1,0:T(8,128)(2,1)}, bf16[2,48,1280]{2,1,0:T(8,128)(2,1)S(1)}, u32[]{:S(2)}) copy-start(bf16[2,48,1280]{2,1,0:T(8,128)(2,1)S(1)} %collective-permute-done.15.refs_12_.refs_13_.refs_23_) | copy-start | bytes 737284
  52.8 2.4 %collective-permute-start.16 = (bf16[2,48,1280]{2,1,0:T(8,128)(2,1)S(1)}, bf16[2,48,1280]{2,1,0:T(8,128)(2,1)S(1)}, u32[]{:S(2)}, u32[]{:S(2)}) collective-permute-start(bf16[2,48,1280]{2,1,0:T(8,128)(2,1)S(1)} %copy-done.27), channel_id=1, source_target_pairs={{0,1},{1,0},{2,3},{3,2},{4,5},{5,4},{6,7},{7,6},{8,9},{9,8},{10,11... | collective-permute-start | bytes 737288 | tf_op jit(solution)/shard_map/ppermute | solution.py:364
  55.2 15.7 %collective-permute-start.21 = (bf16[3,48,1280]{2,1,0:T(8,128)(2,1)S(1)}, bf16[3,48,1280]{2,1,0:T(8,128)(2,1)S(1)}, u32[]{:S(2)}, u32[]{:S(2)}) collective-permute-start(bf16[3,48,1280]{2,1,0:T(8,128)(2,1)S(1)} %pad_maximum_fusion.4.refs_7_), channel_id=1, source_target_pairs={{0,16},{16,0},{1,17},{17,1},{2,18},{18,2},{3,19},{19,3},{4,20},{20... | collective-permute-start | bytes 1105928 | tf_op jit(solution)/shard_map/ppermute | solution.py:367
  56.7 17.5 %collective-permute-start.22 = (bf16[3,48,1280]{2,1,0:T(8,128)(2,1)S(1)}, bf16[3,48,1280]{2,1,0:T(8,128)(2,1)S(1)}, u32[]{:S(2)}, u32[]{:S(2)}) collective-permute-start(bf16[3,48,1280]{2,1,0:T(8,128)(2,1)S(1)} %pad_maximum_fusion.4.refs_7_), channel_id=1, source_target_pairs={{0,2},{2,0},{4,6},{6,4},{8,10},{10,8},{12,14},{14,12},{1,3},{3,1},... | collective-permute-start | bytes 1105928 | tf_op jit(solution)/shard_map/ppermute | solution.py:370
  58.5 16.5 %collective-permute-start.23 = (bf16[3,48,1280]{2,1,0:T(8,128)(2,1)S(1)}, bf16[3,48,1280]{2,1,0:T(8,128)(2,1)S(1)}, u32[]{:S(2)}, u32[]{:S(2)}) collective-permute-start(bf16[3,48,1280]{2,1,0:T(8,128)(2,1)S(1)} %pad_maximum_fusion.4.refs_7_), channel_id=1, source_target_pairs={{0,18},{2,16},{4,22},{6,20},{8,26},{10,24},{12,30},{14,28},{16,2},... | collective-permute-start | bytes 1105928 | tf_op jit(solution)/shard_map/ppermute | solution.py:373
  71.0 7.3 %copy-start.16 = (bf16[3,48,1280]{2,1,0:T(8,128)(2,1)}, bf16[3,48,1280]{2,1,0:T(8,128)(2,1)S(1)}, u32[]{:S(2)}) copy-start(bf16[3,48,1280]{2,1,0:T(8,128)(2,1)S(1)} %collective-permute-done.21.refs_8_) | copy-start | bytes 1105924
  75.0 2.3 %collective-permute-start.24 = (bf16[3,48,1280]{2,1,0:T(8,128)(2,1)S(1)}, bf16[3,48,1280]{2,1,0:T(8,128)(2,1)S(1)}, u32[]{:S(2)}, u32[]{:S(2)}) collective-permute-start(bf16[3,48,1280]{2,1,0:T(8,128)(2,1)S(1)} %pad_maximum_fusion.4.refs_7_), channel_id=1, source_target_pairs={{0,1},{1,0},{2,3},{3,2},{4,5},{5,4},{6,7},{7,6},{8,9},{9,8},{10,11... | collective-permute-start | bytes 1105928 | tf_op jit(solution)/shard_map/ppermute | solution.py:364
  75.0 2.3 %collective-permute-start.25 = (bf16[3,48,1280]{2,1,0:T(8,128)(2,1)S(1)}, bf16[3,48,1280]{2,1,0:T(8,128)(2,1)S(1)}, u32[]{:S(2)}, u32[]{:S(2)}) collective-permute-start(bf16[3,48,1280]{2,1,0:T(8,128)(2,1)S(1)} %collective-permute-done.21.refs_8_), channel_id=1, source_target_pairs={{0,1},{1,0},{2,3},{3,2},{4,5},{5,4},{6,7},{7,6},{8,9},{9,8},{10,11... | collective-permute-start | bytes 1105928 | tf_op jit(solution)/shard_map/ppermute | solution.py:364
  75.5 2.2 %collective-permute-start.26 = (bf16[3,48,1280]{2,1,0:T(8,128)(2,1)S(1)}, bf16[3,48,1280]{2,1,0:T(8,128)(2,1)S(1)}, u32[]{:S(2)}, u32[]{:S(2)}) collective-permute-start(bf16[3,48,1280]{2,1,0:T(8,128)(2,1)S(1)} %collective-permute-done.22.refs_9_), channel_id=1, source_target_pairs={{0,1},{1,0},{2,3},{3,2},{4,5},{5,4},{6,7},{7,6},{8,9},{9,8},{10,11... | collective-permute-start | bytes 1105928 | tf_op jit(solution)/shard_map/ppermute | solution.py:364
  75.5 2.7 %collective-permute-start.27 = (bf16[3,48,1280]{2,1,0:T(8,128)(2,1)S(1)}, bf16[3,48,1280]{2,1,0:T(8,128)(2,1)S(1)}, u32[]{:S(2)}, u32[]{:S(2)}) collective-permute-start(bf16[3,48,1280]{2,1,0:T(8,128)(2,1)S(1)} %collective-permute-done.23.refs_10_), channel_id=1, source_target_pairs={{0,1},{1,0},{2,3},{3,2},{4,5},{5,4},{6,7},{7,6},{8,9},{9,8},{10,11... | collective-permute-start | bytes 1105928 | tf_op jit(solution)/shard_map/ppermute | solution.py:364
  103.8 8.1 %collective-permute-start.29 = (bf16[2,2,2,4,48,640]{5,4,2,3,1,0:T(8,128)(2,1)S(1)}, bf16[2,2,2,4,48,640]{5,4,2,3,1,0:T(8,128)(2,1)S(1)}, u32[]{:S(2)}, u32[]{:S(2)}) collective-permute-start(bf16[2,2,2,4,48,640]{5,4,2,3,1,0:T(8,128)(2,1)S(1)} %copy.42), channel_id=1, source_target_pairs={{0,1},{1,0},{2,3},{3,2},{4,5},{5,4},{6,7},{7,6},{8,9},{9,8},{10,11... | collective-permute-start | bytes 5898248 | tf_op jit(solution)/shard_map/ppermute | solution.py:364
  104.4 9.9 %collective-permute-start.28 = (bf16[416,384]{1,0:T(8,128)(2,1)S(1)}, bf16[416,384]{1,0:T(8,128)(2,1)S(1)}, u32[]{:S(2)}, u32[]{:S(2)}) collective-permute-start(bf16[416,384]{1,0:T(8,128)(2,1)S(1)} %copy-done.23), channel_id=1, source_target_pairs={{0,16},{16,0},{1,17},{17,1},{2,18},{18,2},{3,19},{19,3},{4,20},{20... | collective-permute-start | bytes 958472 | tf_op jit(solution)/shard_map/ppermute | solution.py:367
  114.6 22.6 %collective-permute-start.30 = (bf16[2,208,384]{2,1,0:T(8,128)(2,1)S(1)}, bf16[2,208,384]{2,1,0:T(8,128)(2,1)S(1)}, u32[]{:S(2)}, u32[]{:S(2)}) collective-permute-start(bf16[2,208,384]{2,1,0:T(8,128)(2,1)S(1)} %pad_maximum_fusion.6), channel_id=1, source_target_pairs={{1,3},{3,5},{5,7},{7,9},{9,11},{11,13},{13,15},{17,19},{19,21},{21... | collective-permute-start | bytes 958472 | tf_op jit(solution)/shard_map/ppermute | solution.py:403
  115.5 21.7 %collective-permute-start.31 = (bf16[2,4,48,640]{3,2,0,1:T(8,128)(2,1)S(1)}, bf16[2,4,48,640]{3,2,0,1:T(8,128)(2,1)S(1)}, u32[]{:S(2)}, u32[]{:S(2)}) collective-permute-start(bf16[2,4,48,640]{3,2,0,1:T(8,128)(2,1)S(1)} %get-tuple-element.160), channel_id=1, source_target_pairs={{0,2},{2,0},{4,6},{6,4},{8,10},{10,8},{12,14},{14,12},{1,3},{3,1},... | collective-permute-start | bytes 1474568 | tf_op jit(solution)/shard_map/ppermute | solution.py:370
  117.4 19.8 %collective-permute-start.32 = (bf16[2,4,48,640]{3,2,0,1:T(8,128)(2,1)S(1)}, bf16[2,4,48,640]{3,2,0,1:T(8,128)(2,1)S(1)}, u32[]{:S(2)}, u32[]{:S(2)}) collective-permute-start(bf16[2,4,48,640]{3,2,0,1:T(8,128)(2,1)S(1)} %get-tuple-element.161), channel_id=1, source_target_pairs={{0,16},{16,0},{1,17},{17,1},{2,18},{18,2},{3,19},{19,3},{4,20},{20... | collective-permute-start | bytes 1474568 | tf_op jit(solution)/shard_map/ppermute | solution.py:367
  118.0 22.7 %collective-permute-start.33 = (bf16[2,4,48,640]{3,2,0,1:T(8,128)(2,1)S(1)}, bf16[2,4,48,640]{3,2,0,1:T(8,128)(2,1)S(1)}, u32[]{:S(2)}, u32[]{:S(2)}) collective-permute-start(bf16[2,4,48,640]{3,2,0,1:T(8,128)(2,1)S(1)} %get-tuple-element.162), channel_id=1, source_target_pairs={{0,18},{2,16},{4,22},{6,20},{8,26},{10,24},{12,30},{14,28},{16,2},... | collective-permute-start | bytes 1474568 | tf_op jit(solution)/shard_map/ppermute | solution.py:373
  137.2 6.8 %copy-start.31 = (bf16[416,384]{1,0:T(8,128)(2,1)S(1)}, bf16[416,384]{1,0:T(8,128)(2,1)}, u32[]{:S(2)}) copy-start(bf16[416,384]{1,0:T(8,128)(2,1)} %get-tuple-element.173) | copy-start | bytes 958468
  140.7 9.6 %collective-permute-start.34 = (bf16[2,2,2,4,48,640]{5,4,3,2,1,0:T(8,128)(2,1)}, bf16[2,2,2,4,48,640]{5,4,3,2,1,0:T(8,128)(2,1)S(1)}, u32[]{:S(2)}, u32[]{:S(2)}) collective-permute-start(bf16[2,2,2,4,48,640]{5,4,3,2,1,0:T(8,128)(2,1)} %get-tuple-element.171), channel_id=1, source_target_pairs={{0,1},{1,0},{2,3},{3,2},{4,5},{5,4},{6,7},{7,6},{8,9},{9,8},{10,11... | collective-permute-start | bytes 5898248 | tf_op jit(solution)/shard_map/ppermute | solution.py:364
  143.1 9.7 %collective-permute-start.36 = (bf16[416,384]{1,0:T(8,128)(2,1)}, bf16[416,384]{1,0:T(8,128)(2,1)S(1)}, u32[]{:S(2)}, u32[]{:S(2)}) collective-permute-start(bf16[416,384]{1,0:T(8,128)(2,1)} %get-tuple-element.174), channel_id=1, source_target_pairs={{0,16},{16,0},{1,17},{17,1},{2,18},{18,2},{3,19},{19,3},{4,20},{20... | collective-permute-start | bytes 958472 | tf_op jit(solution)/shard_map/ppermute | solution.py:367
  145.1 5.1 %collective-permute-start.35 = (bf16[2,512,384]{2,1,0:T(8,128)(2,1)S(1)}, bf16[2,512,384]{2,1,0:T(8,128)(2,1)S(1)}, u32[]{:S(2)}, u32[]{:S(2)}) collective-permute-start(bf16[2,512,384]{2,1,0:T(8,128)(2,1)S(1)} %pad_maximum_fusion.1), channel_id=1, source_target_pairs={{0,1},{1,0},{2,3},{3,2},{4,5},{5,4},{6,7},{7,6},{8,9},{9,8},{10,11... | collective-permute-start | bytes 2359304 | tf_op jit(solution)/shard_map/ppermute | solution.py:364
  154.0 19.1 %collective-permute-start.50 = (bf16[2,2,48,640]{3,2,0,1:T(8,128)(2,1)S(1)}, bf16[2,2,48,640]{3,2,0,1:T(8,128)(2,1)S(1)}, u32[]{:S(2)}, u32[]{:S(2)}) collective-permute-start(bf16[2,2,48,640]{3,2,0,1:T(8,128)(2,1)S(1)} %slice.305), channel_id=1, source_target_pairs={{0,4},{2,6},{4,0},{6,2},{8,12},{10,14},{12,8},{14,10},{1,5},{3,7},... | collective-permute-start | bytes 737288 | tf_op jit(solution)/shard_map/ppermute | solution.py:389
  155.7 8.1 %collective-permute-start.42 = (bf16[1,4,48,640]{3,2,1,0:T(8,128)(2,1)S(1)}, bf16[1,4,48,640]{3,2,1,0:T(8,128)(2,1)S(1)}, u32[]{:S(2)}, u32[]{:S(2)}) collective-permute-start(bf16[1,4,48,640]{3,2,1,0:T(8,128)(2,1)S(1)} %get-tuple-element.247), channel_id=1, source_target_pairs={{0,2},{2,0},{4,6},{6,4},{8,10},{10,8},{12,14},{14,12},{1,3},{3,1},... | collective-permute-start | bytes 737288 | tf_op jit(solution)/shard_map/ppermute | solution.py:370
  157.0 8.9 %collective-permute-start.43 = (bf16[1,4,48,640]{3,2,1,0:T(8,128)(2,1)S(1)}, bf16[1,4,48,640]{3,2,1,0:T(8,128)(2,1)S(1)}, u32[]{:S(2)}, u32[]{:S(2)}) collective-permute-start(bf16[1,4,48,640]{3,2,1,0:T(8,128)(2,1)S(1)} %get-tuple-element.249), channel_id=1, source_target_pairs={{0,16},{16,0},{1,17},{17,1},{2,18},{18,2},{3,19},{19,3},{4,20},{20... | collective-permute-start | bytes 737288 | tf_op jit(solution)/shard_map/ppermute | solution.py:367
  157.9 13.6 %collective-permute-start.44 = (bf16[1,4,48,640]{3,2,1,0:T(8,128)(2,1)S(1)}, bf16[1,4,48,640]{3,2,1,0:T(8,128)(2,1)S(1)}, u32[]{:S(2)}, u32[]{:S(2)}) collective-permute-start(bf16[1,4,48,640]{3,2,1,0:T(8,128)(2,1)S(1)} %get-tuple-element.251), channel_id=1, source_target_pairs={{0,18},{2,16},{4,22},{6,20},{8,26},{10,24},{12,30},{14,28},{16,2},... | collective-permute-start | bytes 737288 | tf_op jit(solution)/shard_map/ppermute | solution.py:373
  159.5 15.2 %collective-permute-start.37 = (bf16[2,208,384]{2,1,0:T(8,128)(2,1)S(1)}, bf16[2,208,384]{2,1,0:T(8,128)(2,1)S(1)}, u32[]{:S(2)}, u32[]{:S(2)}) collective-permute-start(bf16[2,208,384]{2,1,0:T(8,128)(2,1)S(1)} %pad_maximum_fusion.7), channel_id=1, source_target_pairs={{1,3},{3,5},{5,7},{7,9},{9,11},{11,13},{13,15},{17,19},{19,21},{21... | collective-permute-start | bytes 958472 | tf_op jit(solution)/shard_map/ppermute | solution.py:403
  163.8 23.3 %collective-permute-start.39 = (bf16[1,4,48,640]{3,2,1,0:T(8,128)(2,1)S(1)}, bf16[1,4,48,640]{3,2,1,0:T(8,128)(2,1)S(1)}, u32[]{:S(2)}, u32[]{:S(2)}) collective-permute-start(bf16[1,4,48,640]{3,2,1,0:T(8,128)(2,1)S(1)} %get-tuple-element.248), channel_id=1, source_target_pairs={{0,2},{2,0},{4,6},{6,4},{8,10},{10,8},{12,14},{14,12},{1,3},{3,1},... | collective-permute-start | bytes 737288 | tf_op jit(solution)/shard_map/ppermute | solution.py:370
  165.9 21.3 %collective-permute-start.40 = (bf16[1,4,48,640]{3,2,1,0:T(8,128)(2,1)S(1)}, bf16[1,4,48,640]{3,2,1,0:T(8,128)(2,1)S(1)}, u32[]{:S(2)}, u32[]{:S(2)}) collective-permute-start(bf16[1,4,48,640]{3,2,1,0:T(8,128)(2,1)S(1)} %get-tuple-element.250), channel_id=1, source_target_pairs={{0,16},{16,0},{1,17},{17,1},{2,18},{18,2},{3,19},{19,3},{4,20},{20... | collective-permute-start | bytes 737288 | tf_op jit(solution)/shard_map/ppermute | solution.py:367
  171.4 15.7 %collective-permute-start.41 = (bf16[1,4,48,640]{3,2,1,0:T(8,128)(2,1)S(1)}, bf16[1,4,48,640]{3,2,1,0:T(8,128)(2,1)S(1)}, u32[]{:S(2)}, u32[]{:S(2)}) collective-permute-start(bf16[1,4,48,640]{3,2,1,0:T(8,128)(2,1)S(1)} %get-tuple-element.252), channel_id=1, source_target_pairs={{0,18},{2,16},{4,22},{6,20},{8,26},{10,24},{12,30},{14,28},{16,2},... | collective-permute-start | bytes 737288 | tf_op jit(solution)/shard_map/ppermute | solution.py:373
  173.1 4.9 %collective-permute-start.45 = (bf16[1,2,48,640]{3,2,1,0:T(8,128)(2,1)S(1)}, bf16[1,2,48,640]{3,2,1,0:T(8,128)(2,1)S(1)}, u32[]{:S(2)}, u32[]{:S(2)}) collective-permute-start(bf16[1,2,48,640]{3,2,1,0:T(8,128)(2,1)S(1)} %slice.297), channel_id=1, source_target_pairs={{0,4},{2,6},{4,0},{6,2},{8,12},{10,14},{12,8},{14,10},{1,5},{3,7},... | collective-permute-start | bytes 368648 | tf_op jit(solution)/shard_map/ppermute | solution.py:389
  174.9 12.2 %collective-permute-start.38 = (bf16[2,512,384]{2,1,0:T(8,128)(2,1)S(1)}, bf16[2,512,384]{2,1,0:T(8,128)(2,1)S(1)}, u32[]{:S(2)}, u32[]{:S(2)}) collective-permute-start(bf16[2,512,384]{2,1,0:T(8,128)(2,1)S(1)} %pad_maximum_fusion.2), channel_id=1, source_target_pairs={{0,1},{1,0},{2,3},{3,2},{4,5},{5,4},{6,7},{7,6},{8,9},{9,8},{10,11... | collective-permute-start | bytes 2359304 | tf_op jit(solution)/shard_map/ppermute | solution.py:364
  178.1 5.6 %collective-permute-start.46 = (bf16[1,48,640]{2,1,0:T(8,128)(2,1)S(1)}, bf16[1,48,640]{2,1,0:T(8,128)(2,1)S(1)}, u32[]{:S(2)}, u32[]{:S(2)}) collective-permute-start(bf16[1,48,640]{2,1,0:T(8,128)(2,1)S(1)} %fusion.33), channel_id=1, source_target_pairs={{0,8},{2,10},{4,12},{6,14},{8,0},{10,2},{12,4},{14,6},{1,9},{3,11}... | collective-permute-start | bytes 184328 | tf_op jit(solution)/shard_map/ppermute | solution.py:389
  183.7 11.1 %collective-permute-start.51 = (bf16[2,48,640]{2,1,0:T(8,128)(2,1)S(1)}, bf16[2,48,640]{2,1,0:T(8,128)(2,1)S(1)}, u32[]{:S(2)}, u32[]{:S(2)}) collective-permute-start(bf16[2,48,640]{2,1,0:T(8,128)(2,1)S(1)} %fusion.28), channel_id=1, source_target_pairs={{0,8},{2,10},{4,12},{6,14},{8,0},{10,2},{12,4},{14,6},{1,9},{3,11}... | collective-permute-start | bytes 368648 | tf_op jit(solution)/shard_map/ppermute | solution.py:389
  187.3 5.8 %collective-permute-start.47 = (bf16[1,48,640]{2,1,0:T(8,128)(2,1)S(1)}, bf16[1,48,640]{2,1,0:T(8,128)(2,1)S(1)}, u32[]{:S(2)}, u32[]{:S(2)}) collective-permute-start(bf16[1,48,640]{2,1,0:T(8,128)(2,1)S(1)} %get-tuple-element.263), channel_id=1, source_target_pairs={{0,4},{2,6},{4,0},{6,2},{8,12},{10,14},{12,8},{14,10},{1,5},{3,7},... | collective-permute-start | bytes 184328 | tf_op jit(solution)/shard_map/ppermute | solution.py:389
  187.4 5.7 %collective-permute-start.48 = (bf16[1,48,640]{2,1,0:T(8,128)(2,1)S(1)}, bf16[1,48,640]{2,1,0:T(8,128)(2,1)S(1)}, u32[]{:S(2)}, u32[]{:S(2)}) collective-permute-start(bf16[1,48,640]{2,1,0:T(8,128)(2,1)S(1)} %get-tuple-element.265), channel_id=1, source_target_pairs={{0,8},{2,10},{4,12},{6,14},{8,0},{10,2},{12,4},{14,6},{1,9},{3,11}... | collective-permute-start | bytes 184328 | tf_op jit(solution)/shard_map/ppermute | solution.py:389
  188.1 6.6 %collective-permute-start.49 = (bf16[1,48,640]{2,1,0:T(8,128)(2,1)S(1)}, bf16[1,48,640]{2,1,0:T(8,128)(2,1)S(1)}, u32[]{:S(2)}, u32[]{:S(2)}) collective-permute-start(bf16[1,48,640]{2,1,0:T(8,128)(2,1)S(1)} %get-tuple-element.264), channel_id=1, source_target_pairs={{0,12},{2,14},{4,8},{6,10},{8,4},{10,6},{12,0},{14,2},{1,13},{3,15... | collective-permute-start | bytes 184328 | tf_op jit(solution)/shard_map/ppermute | solution.py:389
  194.8 5.6 %collective-permute-start.52 = (bf16[2,48,640]{2,1,0:T(8,128)(2,1)S(1)}, bf16[2,48,640]{2,1,0:T(8,128)(2,1)S(1)}, u32[]{:S(2)}, u32[]{:S(2)}) collective-permute-start(bf16[2,48,640]{2,1,0:T(8,128)(2,1)S(1)} %select_convert_fusion), channel_id=1, source_target_pairs={{0,16},{16,0},{1,17},{17,1},{2,18},{18,2},{3,19},{19,3},{4,20},{20... | collective-permute-start | bytes 368648 | tf_op jit(solution)/shard_map/ppermute | solution.py:367
  (22 other events, 44.7 us)
